TPU v7x, 32 devices: a whole 2x2x4 slice. The times are simulated.
32 devices in a mesh: tile: 4 (over y, core), pos: 8 (over z, x).
Axes of the slice: x: 2, y: 2, z: 4, core: 2. Of those that a mesh axis runs over, the one named last changes fastest.
Arguments:
- object_field: float32 [2048, 2, 512], P('tile'), may hold values from -5 to 5
- illumination: float32 [256, 2, 256], replicated, may hold values from -5 to 5
- amplitudes: bfloat16 [64, 256, 256], P(('tile', 'pos')), may hold values from 0.19921875 to 3
- row_offset: int32 [64], P(('tile', 'pos')), may hold values from 0 to 1792, as said below
- col_offset: int32 [64], P(('tile', 'pos')), may hold values from 0 to 256
Outputs:
- object_gradient: float32 [2048, 2, 512], P(('tile', 'pos'))
Inputs may be any that keep to these rules, and one draw needn't show every extreme that they name: Position i lies in band b = i // 16: b * 512 <= row_offset[i] < (b + 1) * 512, and every window lies inside the object. Among the 2 positions of one device (an aligned block), at most 1 have row_offset[i] > (b + 1) * 512 - 256, so that their window reaches into band b + 1; in every draw some device has exactly 1 such positions; positions of the last band have none.
All inputs are finite; a program needn't handle non-finite values.
Results may differ from a plain program's by a relative error of at most 0.0003.
Values sent between devices are 32-bit elements; how exact they have to be, the bound alone decides.
No kernel may reach another device: no remote copies, remote signals or barrier semaphores. Data moves between devices by JAX's collectives and lax.ppermute only.
A program may use at most 64 MiB of HBM per device.

v0:
```python
import math

import jax
import jax.numpy as jnp
from jax import lax
from jax.sharding import PartitionSpec as P


def shifted(block, axis, distance):
    devices = range(lax.axis_size(axis))
    route = [(i - distance, i) for i in devices if i - distance in devices]
    return lax.ppermute(block, axis, route)


def dft_tables(length):
    indices = jnp.arange(length, dtype=jnp.int32)
    product = indices[:, None] * indices[None, :] % length
    angles = product.astype(jnp.float32) * (2.0 * math.pi / length)
    factor = 1.0 / math.sqrt(length)
    return (jnp.cos(angles) * factor, jnp.sin(angles) * factor)


def apply_right(matrix, factor):
    return jnp.einsum("bij,jk->bik", matrix, factor, precision=lax.Precision.HIGHEST)


def apply_left(factor, matrix):
    return jnp.einsum("ij,bjk->bik", factor, matrix, precision=lax.Precision.HIGHEST)


def transform(real_part, imag_part, cos_table, sin_table, signum):
    mid_real = apply_right(real_part, cos_table) + signum * apply_right(imag_part, sin_table)
    mid_imag = apply_right(imag_part, cos_table) - signum * apply_right(real_part, sin_table)
    out_real = apply_left(cos_table, mid_real) + signum * apply_left(sin_table, mid_imag)
    out_imag = apply_left(cos_table, mid_imag) - signum * apply_left(sin_table, mid_real)
    return (out_real, out_imag)


def modulus(real_part, imag_part, amplitude):
    magnitude = jnp.sqrt(real_part * real_part + imag_part * imag_part)
    retain = 1.0 - amplitude.astype(jnp.float32) / jnp.maximum(magnitude, 0.25)
    return (real_part * retain, imag_part * retain)


def exit_wave(windows, illumination):
    obj_real = windows[:, :, 0, :]
    obj_imag = windows[:, :, 1, :]
    probe_real = illumination[:, 0, :]
    probe_imag = illumination[:, 1, :]
    return (
        probe_real * obj_real - probe_imag * obj_imag,
        probe_real * obj_imag + probe_imag * obj_real,
    )


def far_gradient(exit_real, exit_imag, illumination, amplitude, cos_table, sin_table):
    far_real, far_imag = transform(exit_real, exit_imag, cos_table, sin_table, 1.0)
    diff_real, diff_imag = modulus(far_real, far_imag, amplitude)
    back_real, back_imag = transform(diff_real, diff_imag, cos_table, sin_table, -1.0)
    probe_real = illumination[:, 0, :]
    probe_imag = illumination[:, 1, :]
    grad_real = probe_real * back_real + probe_imag * back_imag
    grad_imag = probe_real * back_imag - probe_imag * back_real
    return jnp.stack([grad_real, grad_imag], axis=2)


def add_windows(buffer, gradients, row_list, col_list, number):
    window = gradients.shape[1]
    anchor = jnp.zeros((), jnp.int32)

    def add_one(position, current):
        corner = (row_list[position], anchor, col_list[position])
        updated = lax.dynamic_slice(current, corner, (window, 2, window)) + gradients[position]
        return lax.dynamic_update_slice(current, updated, corner)

    return lax.fori_loop(0, number, add_one, buffer)


def on_device(object_field, illumination, amplitudes, row_offset, col_offset):
    band_rows = object_field.shape[0]
    columns = object_field.shape[2]
    window = illumination.shape[0]
    number = row_offset.shape[0]
    cos_table, sin_table = dft_tables(window)
    anchor = jnp.zeros((), jnp.int32)
    local_rows = row_offset - lax.axis_index("tile") * band_rows
    rim_rows = shifted(object_field[:window], "tile", -1)
    extended = jnp.concatenate([object_field, rim_rows], axis=0)

    def single(row_start, col_start):
        return lax.dynamic_slice(extended, (row_start, anchor, col_start), (window, 2, window))

    exit_real, exit_imag = exit_wave(jax.vmap(single)(local_rows, col_offset), illumination)
    gradients = far_gradient(exit_real, exit_imag, illumination, amplitudes, cos_table, sin_table)
    ext_grad = add_windows(
        jnp.zeros((band_rows + window, 2, columns), jnp.float32),
        gradients,
        local_rows,
        col_offset,
        number,
    )
    spilled = shifted(ext_grad[band_rows:], "tile", 1)
    band_grad = ext_grad[:band_rows] + jnp.pad(spilled, ((0, band_rows - window), (0, 0), (0, 0)))
    result = lax.psum_scatter(band_grad, "pos", scatter_dimension=0, tiled=True)
    return result


def solution(mesh):
    in_specs = (
        P("tile", None, None),
        P(),
        P(("tile", "pos"), None, None),
        P(("tile", "pos")),
        P(("tile", "pos")),
    )
    out_specs = P(("tile", "pos"), None, None)
    return jax.shard_map(
        on_device, mesh=mesh, in_specs=in_specs, out_specs=out_specs, check_vma=False
    )
```

profile of v0, /device:TPU:0, one launch (start us, length us, event | category | flops | bytes accessed | tf_op | source)
XLA Modules:
  0.0 313.3 jit_solution(16311259551840081868)
XLA Ops:
  6.6 2.7 slice.24
  14.2 4.2 %pad_maximum_fusion = f32[768,2,512]{2,1,0:T(2,128)} fusion(f32[256,2,512]{2,1,0:T(2,128)} %collective-permute-done, f32[512,2,512]{2,1,0:T(2,128)S(1)} %copy-done), kind=kLoop, calls=%fused_computation.5 | loop fusion | flops 786432 | bytes 6291456 | tf_op jit(solution)/shard_map/concatenate | solution.py:88
  18.4 9.1 %while.15 = (s32[]{:T(128)}, f32[768,2,512]{2,1,0:T(2,128)}, s32[2,3]{1,0:T(2,128)S(1)}, f32[2,256,2,256]{1,3,0,2:T(8,128)}, s32[]{:T(128)}) while((s32[]{:T(128)}, f32[768,2,512]{2,1,0:T(2,128)}, s32[2,3]{1,0:T(2,128)S(1)}, f32[2,256,2,256]{1,3,0,2:T(8,128)}, s32[]{:T(128)}) %tuple.51), condition=%wide.while_cond, body=%wide.while_body.sunk | while | flops 2 | bytes 3146353 | solution.py:91
  19.0 2.9 dynamic-slice_bitcast_fusion.2
  23.5 2.9 dynamic-slice_bitcast_fusion.2
  27.6 3.2 %fusion.37 = f32[2,256,256]{2,1,0:T(8,128)S(1)} fusion(f32[2,256,2,256]{1,3,0,2:T(8,128)} %get-tuple-element.107, f32[256,256]{0,1:T(8,128)S(1)} %bitcast.115, f32[256,256]{0,1:T(8,128)S(1)} %bitcast.110), kind=kOutput, calls=%fused_computation.63 | convolution fusion | flops 404029440 | bytes 2097152 | tf_op jit(solution)/shard_map/bij,jk->bik/dot_general | solution.py:24
  30.7 3.1 fusion.33
  33.8 1.9 convolution_add_fusion.1
  35.7 1.8 fusion.35
  37.5 1.9 convolution_subtract_fusion.1
  39.4 1.8 fusion.31
  41.2 2.0 fusion.7
  43.3 1.8 fusion.6
  45.1 2.1 fusion.29
  47.2 2.1 fusion.25
  49.3 2.1 fusion.5
  51.4 2.1 fusion.4
  53.5 2.1 fusion.23
  55.6 1.8 fusion.27
  57.4 1.8 fusion.1
  59.3 1.9 add_bitcast_fusion
  61.2 2.4 broadcast_in_dim.11
  63.7 104.1 %while.14 = (s32[]{:T(128)}, f32[768,2,512]{2,1,0:T(2,128)}, s32[2]{0:T(128)S(1)}, s32[2]{0:T(128)S(1)}, f32[2,256,2,256]{1,3,0,2:T(8,128)S(1)}, /*index=5*/s32[]{:T(128)}, s32[]{:T(128)}, s32[]{:T(128)}, s32[]{:T(128)}) while((s32[]{:T(128)}, f32[768,2,512]{2,1,0:T(2,128)}, s32[2]{0:T(128)S(1)}, s32[2]{0:T(128)S(1)}, ...), condition=%wide.region_1.2_spmd, body=%wide.region_0.1_spmd.sunk | while | flops 131080 | bytes 4718793 | solution.py:76
  69.0 1.8 bitcast_add_fusion.2
  70.7 45.0 %dynamic_update_slice.8 = f32[768,2,512]{2,1,0:T(2,128)} dynamic-update-slice(f32[768,2,512]{2,1,0:T(2,128)} %get-tuple-element.246, f32[256,2,256]{2,1,0:T(2,128)S(1)} %bitcast_add_fusion.2, s32[]{:T(128)S(6)} %select_n.136, s32[]{:T(128)} %constant.63.clone.1..sunk, s32[]{:T(128)S(6)} %select_n.137) | dynamic-update-slice | bytes 1048580 | tf_op jit(solution)/shard_map/while/body/eval_jaxpr/dynamic_update_slice | solution.py:74
  121.0 1.8 bitcast_add_fusion.2
  122.8 45.0 %dynamic_update_slice.8 = f32[768,2,512]{2,1,0:T(2,128)} dynamic-update-slice(f32[768,2,512]{2,1,0:T(2,128)} %get-tuple-element.246, f32[256,2,256]{2,1,0:T(2,128)S(1)} %bitcast_add_fusion.2, s32[]{:T(128)S(6)} %select_n.136, s32[]{:T(128)} %constant.63.clone.1..sunk, s32[]{:T(128)S(6)} %select_n.137) | dynamic-update-slice | bytes 1048580 | tf_op jit(solution)/shard_map/while/body/eval_jaxpr/dynamic_update_slice | solution.py:74
  169.3 14.9 %collective-permute-start.1 = (f32[256,2,512]{2,1,0:T(2,128)S(1)}, f32[256,2,512]{2,1,0:T(2,128)S(1)}, u32[]{:S(2)}, u32[]{:S(2)}) collective-permute-start(f32[256,2,512]{2,1,0:T(2,128)S(1)} %slice.29), channel_id=1, source_target_pairs={{0,8},{8,16},{16,24},{1,9},{9,17},{17,25},{2,10},{10,18},{18,26},{... | collective-permute-start | bytes 3145736 | tf_op jit(solution)/shard_map/ppermute | solution.py:12
  184.2 2.2 collective-permute-done.1
  186.4 3.9 %pad_add_fusion = f32[512,2,512]{2,1,0:T(2,128)} fusion(f32[256,2,512]{2,1,0:T(2,128)S(1)} %collective-permute-done.1, f32[768,2,512]{2,1,0:T(2,128)} %get-tuple-element.99), kind=kLoop, calls=%fused_computation.6 | loop fusion | flops 524288 | bytes 5242880 | tf_op jit(solution)/shard_map/add | solution.py:103
  191.5 112.8 %all-reduce.4.cloned.1.call-done = f32[512,2,512]{2,1,0:T(2,128)} async-done(((f32[512,2,512]{2,1,0:T(2,128)}), f32[512,2,512]{2,1,0:T(2,128)}) %all-reduce.4.cloned.1.call-update) | async-done | bytes 2097168
  304.3 1.7 constant_dynamic-slice_fusion.2
  (45 shorter events, 13.5 us)
Async XLA Ops:
  6.5 7.7 %copy-start = (f32[512,2,512]{2,1,0:T(2,128)S(1)}, f32[512,2,512]{2,1,0:T(2,128)}, u32[]{:S(2)}) copy-start(f32[512,2,512]{2,1,0:T(2,128)} %param.7) | copy-start | bytes 6291460
  6.5 6.1 %copy-start.4 = (s32[2]{0:T(128)S(1)}, s32[2]{0:T(128)}, u32[]{:S(2)}) copy-start(s32[2]{0:T(128)} %param.11) | copy-start | bytes 28
  6.5 6.1 %copy-start.3 = (s32[2]{0:T(128)S(1)}, s32[2]{0:T(128)}, u32[]{:S(2)}) copy-start(s32[2]{0:T(128)} %param.10) | copy-start | bytes 28
  6.5 6.3 %copy-start.2 = (bf16[2,256,256]{2,1,0:T(8,128)(2,1)S(1)}, bf16[2,256,256]{2,1,0:T(8,128)(2,1)}, u32[]{:S(2)}) copy-start(bf16[2,256,256]{2,1,0:T(8,128)(2,1)} %param.9) | copy-start | bytes 786436
  6.5 297.8 %all-reduce.4.cloned.1.call-start = ((), (), s32[]{:S(2)}) async-start(), calls=%async_computation | async-start | bytes 4194304
  9.3 4.9 %collective-permute-start = (f32[256,2,512]{2,1,0:T(2,128)}, f32[256,2,512]{2,1,0:T(2,128)}, u32[]{:S(2)}, u32[]{:S(2)}) collective-permute-start(f32[256,2,512]{2,1,0:T(2,128)} %slice.24), channel_id=1, source_target_pairs={{8,0},{16,8},{24,16},{9,1},{17,9},{25,17},{10,2},{18,10},{26,18},{... | collective-permute-start | bytes 3145736 | tf_op jit(solution)/shard_map/ppermute | solution.py:12
  27.6 6.3 %copy-start.1 = (f32[2,256,2,256]{1,3,0,2:T(8,128)S(1)}, f32[2,256,2,256]{1,3,0,2:T(8,128)}, u32[]{:S(2)}) copy-start(f32[2,256,2,256]{1,3,0,2:T(8,128)} %get-tuple-element.107) | copy-start | bytes 3145732
  169.3 21.0 %copy-start.5 = (u32[32]{0:T(128)S(1)}, u32[32]{0:T(128)}, u32[]{:S(2)}) copy-start(u32[32]{0:T(128)} %constant.97) | copy-start | bytes 388
  169.3 17.1 %collective-permute-start.1 = (f32[256,2,512]{2,1,0:T(2,128)S(1)}, f32[256,2,512]{2,1,0:T(2,128)S(1)}, u32[]{:S(2)}, u32[]{:S(2)}) collective-permute-start(f32[256,2,512]{2,1,0:T(2,128)S(1)} %slice.29), channel_id=1, source_target_pairs={{0,8},{8,16},{16,24},{1,9},{9,17},{17,25},{2,10},{10,18},{18,26},{... | collective-permute-start | bytes 3145736 | tf_op jit(solution)/shard_map/ppermute | solution.py:12
Sparse Core Ops, SparseCore 0:
  190.4 113.8 all-reduce.3
where the time goes:
time: 318 us; the launch traced here: 313 us
  waiting for transfers between devices  116 us (36%)
  local copies, waits for them, and re-layouts  113 us (36%)
  matrix products  33.5 us (11%)
  starting transfers between devices  16.2 us (5%)
  between operations  14.7 us (5%)
  other arithmetic  11.7 us (4%)
  loops' own time  7.66 us (2%)
    unnamed x2, waiting for transfers between devices  113 us
    dynamic_update_slice x2, local copies, waits for them, and re-layouts, add_one(): return lax.dynamic_update_slice(current, updated, corner)  90 us
    dot_general x8, matrix products, apply_right(): jnp.einsum('bij,jk->bik', matrix, factor, precision=lax.Precision.HIGHEST)  18.4 us
    ppermute x2, starting transfers between devices, shifted(): return lax.ppermute(block, axis, route)  16.1 us
    dot_general x8, matrix products, apply_left(): jnp.einsum('ij,bjk->bik', factor, matrix, precision=lax.Precision.HIGHEST)  15.1 us
    gather x10, local copies, waits for them, and re-layouts  8.98 us
    another operation x1, loops' own time, add_windows(): return lax.fori_loop(0, number, add_one, buffer)  7.5 us
  transfers between devices with their start and end apart: 3, of which 3 were waited for; matrix products, arithmetic and copies ran while one was open for 1% of the time, Pallas kernels for 0%

commit v1 on v0

v1 whole, which is shorter than its diff:
```python
import functools
import math

import jax
import jax.numpy as jnp
import numpy as np
from jax import lax
from jax.experimental import pallas as pl
from jax.experimental.pallas import tpu as pltpu
from jax.sharding import PartitionSpec as P

LANES = 128
F32 = jnp.float32
BF16 = jnp.bfloat16


def shifted(block, axis, distance):
    devices = range(lax.axis_size(axis))
    route = [(i - distance, i) for i in devices if i - distance in devices]
    return lax.ppermute(block, axis, route)


def exchanged(block, axis, flip):
    return lax.ppermute(block, axis, [(i, i ^ flip) for i in range(lax.axis_size(axis))])


def split_tables(length):
    indices = np.arange(length, dtype=np.int64)
    angles = (indices[:, None] * indices[None, :] % length) * (2.0 * math.pi / length)
    factor = 1.0 / math.sqrt(length)
    whole = np.concatenate([np.cos(angles), np.sin(angles)], axis=0) * factor
    high = whole.astype(BF16)
    low = (whole - high.astype(np.float64)).astype(BF16)
    return jnp.asarray(np.concatenate([high, low], axis=0))


def linear(array):
    rows, parts, columns = array.shape
    tiles = columns // LANES
    return array.reshape(rows, parts, tiles, LANES).transpose(0, 2, 1, 3).reshape(rows * tiles * parts, LANES)


def unlinear(array, rows, columns):
    tiles = columns // LANES
    return array.reshape(rows, tiles, 2, LANES).transpose(0, 2, 1, 3).reshape(rows, 2, columns)


def halves(value):
    high = value.astype(BF16)
    return high, (value - high.astype(F32)).astype(BF16)


def dot3(high_left, low_left, high_right, low_right):
    dot = functools.partial(jnp.dot, preferred_element_type=F32)
    return dot(high_left, high_right) + (dot(low_left, high_right) + dot(high_left, low_right))


def rim_kernel(window, info, obj_ref, out_ref):
    offset = info[0]
    tiles = window // LANES
    shape = (window, 2 * tiles, LANES)
    column = lax.broadcasted_iota(jnp.int32, shape, 1) // 2 * LANES + lax.broadcasted_iota(jnp.int32, shape, 2)
    near = obj_ref[:, : 2 * tiles, :]
    beyond = obj_ref[:, 2 * tiles :, :]
    out_ref[...] = jnp.where(column < offset, beyond, near)


def wave_kernel(slot, window, classes, with_rim, *refs):
    info, obj_hbm, ill_hbm, amp_hbm, table_hbm = refs[:5]
    refs = refs[5:]
    if with_rim:
        rim_hbm, refs = refs[0], refs[1:]
    outs, refs = refs[:classes], refs[classes:]
    obj, ill, amp, table, probe, xh, xl, far, sem = refs[:9]
    rim = refs[9] if with_rim else None
    row, column, index, own = info[3 * slot], info[3 * slot + 1], info[3 * slot + 2], info[6]
    tiles = window // LANES
    ill_rows = window * 2 * tiles
    copies = [
        pltpu.make_async_copy(ill_hbm, ill.at[pl.ds(0, ill_rows)], sem.at[0]),
        pltpu.make_async_copy(ill_hbm, ill.at[pl.ds(ill_rows, ill_rows)], sem.at[1]),
        pltpu.make_async_copy(obj_hbm, obj, sem.at[2]),
        pltpu.make_async_copy(table_hbm, table, sem.at[3]),
        pltpu.make_async_copy(amp_hbm.at[index], amp, sem.at[4]),
    ]
    if with_rim:
        copies.append(pltpu.make_async_copy(rim_hbm, rim, sem.at[5]))
    for copy in copies:
        copy.start()
    for copy in copies:
        copy.wait()

    size = 32
    start = (window - lax.rem(row, window)) * (2 * tiles)

    def store_pair(first, real, imag):
        here = pl.ds(first, size)
        below = pl.ds(window + first, size)
        left, right = pl.ds(0, window), pl.ds(window, window)
        for part, ref in zip(range(2), (xh, xl)):
            r, i, n = (halves(v)[part] for v in (real, imag, -real))
            ref[here, left] = r
            ref[here, right] = i
            ref[below, left] = i
            ref[below, right] = n

    for first in range(0, window, size):
        place = lax.broadcasted_iota(jnp.int32, (size, window), 0) + first
        across = lax.broadcasted_iota(jnp.int32, (size, window), 1)
        pair = []
        for part in range(2):
            rolled = jnp.concatenate(
                [
                    ill[pl.ds(start + first * 2 * tiles + tile * 2 + part, size, stride=2 * tiles), :]
                    for tile in range(tiles)
                ],
                axis=1,
            )
            rolled = pltpu.roll(rolled, column, 1)
            probe[part, pl.ds(first, size), :] = rolled

            def block(base):
                def tile_at(tile):
                    return obj[pl.ds((base + first) * 4 * tiles + tile * 2 + part, size, stride=4 * tiles), :]

                near = jnp.concatenate([tile_at(t) for t in range(tiles)], axis=1)
                beyond = jnp.concatenate([tile_at(t + tiles) for t in range(tiles)], axis=1)
                return jnp.where(across < column, beyond, near)

            seen = jnp.where(place < row, block(window), block(0))
            if with_rim:
                edge = jnp.concatenate(
                    [
                        rim[pl.ds(first * 2 * tiles + tile * 2 + part, size, stride=2 * tiles), :]
                        for tile in range(tiles)
                    ],
                    axis=1,
                )
                seen = jnp.where(place + window < row, edge, seen)
            pair.append((rolled, seen))
        (probe_real, obj_real), (probe_imag, obj_imag) = pair
        store_pair(
            first,
            probe_real * obj_real - probe_imag * obj_imag,
            probe_real * obj_imag + probe_imag * obj_real,
        )

    high = table[pl.ds(0, 2 * window), :]
    low = table[pl.ds(2 * window, 2 * window), :]
    left_high = jnp.concatenate([table[pl.ds(0, window), :], table[pl.ds(window, window), :]], axis=1)
    left_low = jnp.concatenate([table[pl.ds(2 * window, window), :], table[pl.ds(3 * window, window), :]], axis=1)

    def both_sides():
        mid = dot3(xh[...], xl[...], high, low)
        for first in range(0, window, size):
            store_pair(first, mid[first : first + size], mid[window + first : window + first + size])
        far[...] = dot3(left_high, left_low, xh[...], xl[...])

    both_sides()
    for first in range(0, window, size):
        real = far[pl.ds(first, size), pl.ds(0, window)]
        imag = far[pl.ds(first, size), pl.ds(window, window)]
        inverse = jnp.minimum(lax.rsqrt(real * real + imag * imag), 4.0)
        scaled = amp[pl.ds(first, size), :].astype(F32) * inverse
        store_pair(first, real * (1.0 - scaled), imag * (scaled - 1.0))
    both_sides()

    share = window // classes
    for flip in range(classes):
        base = pl.multiple_of((own ^ flip) * share, share)
        here = pl.ds(base, share)
        real = far[here, pl.ds(0, window)]
        imag = far[here, pl.ds(window, window)]
        probe_real = probe[0, here, :]
        probe_imag = probe[1, here, :]
        outs[flip][pl.ds(0, share), :] = probe_real * real - probe_imag * imag
        outs[flip][pl.ds(share, share), :] = -(probe_real * imag + probe_imag * real)
        line = lax.broadcasted_iota(jnp.int32, (8, window), 0)
        outs[flip][pl.ds(2 * share, 8), :] = jnp.where(line == 0, row, column).astype(F32)


def wave(slot, window, classes, info, obj, ill, amp, table, rim=None):
    share = window // classes
    any_spec = pl.BlockSpec(memory_space=pl.ANY)
    ins = [obj, ill, amp, table] + ([rim] if rim is not None else [])
    out = jax.ShapeDtypeStruct((2 * share + 8, window), F32)
    scratch = [
        pltpu.VMEM(obj.shape, F32),
        pltpu.VMEM((2 * ill.shape[0], LANES), F32),
        pltpu.VMEM((window, window), BF16),
        pltpu.VMEM(table.shape, BF16),
        pltpu.VMEM((2, window, window), F32),
        pltpu.VMEM((2 * window, 2 * window), BF16),
        pltpu.VMEM((2 * window, 2 * window), BF16),
        pltpu.VMEM((window, 2 * window), F32),
        pltpu.SemaphoreType.DMA((6,)),
    ] + ([pltpu.VMEM(rim.shape, F32)] if rim is not None else [])
    return pl.pallas_call(
        functools.partial(wave_kernel, slot, window, classes, rim is not None),
        out_shape=[out] * classes,
        in_specs=[pl.BlockSpec(memory_space=pltpu.SMEM)] + [any_spec] * len(ins),
        out_specs=[pl.BlockSpec(memory_space=pltpu.VMEM)] * classes,
        scratch_shapes=scratch,
        cost_estimate=pl.CostEstimate(flops=96 * window**3, transcendentals=window**2, bytes_accessed=5 << 20),
        name="wave" + str(slot),
    )(info, *ins)


def placed(piece_ref, own, share, window):
    row = piece_ref[pl.ds(2 * share, 1), :]
    column = piece_ref[pl.ds(2 * share + 1, 1), :]
    place = (lax.broadcasted_iota(jnp.int32, (share, window), 0) + own * share).astype(F32)
    across = lax.broadcasted_iota(jnp.int32, (share, window), 1).astype(F32)
    upper = across < column
    below = place < row
    lowest = place + float(window) < row
    return upper, below, lowest


def first_sum_kernel(window, classes, info, *refs):
    pieces, acc = refs[:classes], refs[classes]
    share = window // classes
    for part in range(2):
        total = [[jnp.zeros((share, window), F32) for _ in range(2)] for _ in range(2)]
        for piece in pieces:
            upper, below, _ = placed(piece, info[6], share, window)
            value = piece[pl.ds(part * share, share), :]
            for k, wanted in enumerate((~below, below)):
                kept = jnp.where(wanted, value, 0.0)
                total[k][0] += jnp.where(upper, 0.0, kept)
                total[k][1] += jnp.where(upper, kept, 0.0)
        for k in range(2):
            for half in range(2):
                acc[k, part, :, pl.ds(half * window, window)] = total[k][half]


def second_sum_kernel(window, classes, info, acc, *refs):
    pieces, outs = refs[:classes], refs[classes:]
    share = window // classes
    tiles = window // LANES
    for part in range(2):
        total = [[acc[k, part, :, pl.ds(h * window, window)] for h in range(2)] for k in range(2)]
        total.append([jnp.zeros((share, window), F32) for _ in range(2)])
        for piece in pieces:
            upper, below, lowest = placed(piece, info[6], share, window)
            value = piece[pl.ds(part * share, share), :]
            for k, wanted in enumerate((~below, below & ~lowest, lowest)):
                kept = jnp.where(wanted, value, 0.0)
                total[k][0] += jnp.where(upper, 0.0, kept)
                total[k][1] += jnp.where(upper, kept, 0.0)
        for k in range(3):
            for half in range(2):
                for tile in range(tiles):
                    outs[k][pl.ds((half * tiles + tile) * 2 + part, share, stride=4 * tiles), :] = total[k][half][
                        :, tile * LANES : (tile + 1) * LANES
                    ]


def on_device(object_field, illumination, amplitudes, row_offset, col_offset):
    band_rows, _, columns = object_field.shape
    window = illumination.shape[0]
    ways = lax.axis_size("pos")
    assert band_rows == 2 * window and columns == 2 * window and row_offset.shape[0] == 2
    classes = ways // 2
    share = window // classes
    tiles = window // LANES
    pos = lax.axis_index("pos")
    tile = lax.axis_index("tile")
    own, upper = lax.rem(pos, classes), pos // classes
    table = split_tables(window)

    local = row_offset - tile * band_rows
    swap = local[0] > window
    first = swap.astype(jnp.int32)
    rows = jnp.where(swap, local[::-1], local)
    cols = jnp.where(swap, col_offset[::-1], col_offset)
    info = jnp.stack([rows[0], cols[0], first, rows[1], cols[1], 1 - first, own, upper])

    wanted = shifted(cols[1:], "tile", 1)
    obj = linear(object_field)
    ill = linear(illumination)
    obj_rows = obj.reshape(band_rows, 4 * tiles, LANES)
    smem = pl.BlockSpec(memory_space=pltpu.SMEM)
    vmem = pl.BlockSpec(memory_space=pltpu.VMEM)
    rim = pl.pallas_call(
        functools.partial(rim_kernel, window),
        grid_spec=pltpu.PrefetchScalarGridSpec(
            num_scalar_prefetch=1,
            grid=(1,),
            in_specs=[pl.BlockSpec((window, 4 * tiles, LANES), lambda i, s: (0, 0, 0))],
            out_specs=pl.BlockSpec((window, 2 * tiles, LANES), lambda i, s: (0, 0, 0)),
        ),
        out_shape=jax.ShapeDtypeStruct((window, 2 * tiles, LANES), F32),
        name="rim",
    )(wanted, obj_rows)
    rim = shifted(rim, "tile", -1).reshape(window * 2 * tiles, LANES)

    def spread(pieces):
        return [pieces[0]] + [exchanged(pieces[d], "pos", d) for d in range(1, classes)]

    near = spread(wave(0, window, classes, info, obj, ill, amplitudes, table))
    acc = pl.pallas_call(
        functools.partial(first_sum_kernel, window, classes),
        out_shape=jax.ShapeDtypeStruct((2, 2, share, columns), F32),
        in_specs=[smem] + [vmem] * classes,
        out_specs=vmem,
        name="sum0",
    )(info, *near)
    late = spread(wave(1, window, classes, info, obj, ill, amplitudes, table, rim))
    block = jax.ShapeDtypeStruct((share * 4 * tiles, LANES), F32)
    top, middle, spilled = pl.pallas_call(
        functools.partial(second_sum_kernel, window, classes),
        out_shape=[block] * 3,
        in_specs=[smem] + [vmem] * (classes + 1),
        out_specs=[vmem] * 3,
        name="sum1",
    )(info, acc, *late)
    top = top + shifted(spilled, "tile", 1)
    is_upper = upper == 1
    received = exchanged(jnp.where(is_upper, top, middle), "pos", classes)
    result = jnp.where(is_upper, middle, top) + received
    return unlinear(result, share, columns)


def solution(mesh):
    in_specs = (
        P("tile", None, None),
        P(),
        P(("tile", "pos"), None, None),
        P(("tile", "pos")),
        P(("tile", "pos")),
    )
    out_specs = P(("tile", "pos"), None, None)
    return jax.shard_map(
        on_device, mesh=mesh, in_specs=in_specs, out_specs=out_specs, check_vma=False
    )
```

time: 318 us -> 71.1 us (0.22)
  the two profiles are of different devices: /device:TPU:0 before, /device:TPU:4 now
where the time goes in v1:
time: 71.1 us; the launch traced here: 70.7 us
  Pallas kernels  22.4 us (32%)
  waiting for transfers between devices  20.4 us (29%)
  starting transfers between devices  15.4 us (22%)
  local copies, waits for them, and re-layouts  8.15 us (11%)
  other arithmetic  4.14 us (6%)
    pallas_call x2, Pallas kernels, wave(): pl.pallas_call(functools.partial(wave_kernel, slot, window, classes, rim...  15 us
    ppermute x7, waiting for transfers between devices, exchanged(): lax.ppermute(block, axis, [(i, i ^ flip) for i in range(lax.axis_size(axi...  11.3 us
    ppermute x7, starting transfers between devices, exchanged(): lax.ppermute(block, axis, [(i, i ^ flip) for i in range(lax.axis_size(axi...  9.67 us
    ppermute x3, waiting for transfers between devices, shifted(): return lax.ppermute(block, axis, route)  9.09 us
    ppermute x3, starting transfers between devices, shifted(): return lax.ppermute(block, axis, route)  5.73 us
    another operation x1, local copies, waits for them, and re-layouts, on_device(): jnp.stack([rows[0], cols[0], first, rows[1], cols[1], 1 - first, own, upp...  3.26 us
    pallas_call x1, Pallas kernels, on_device(): pl.pallas_call(functools.partial(rim_kernel, window), grid_spec=pltpu.Pre...  2.84 us
    pallas_call x1, Pallas kernels, on_device(): pl.pallas_call(functools.partial(second_sum_kernel, window, classes), out...  2.44 us
  transfers between devices with their start and end apart: 10, of which 5 were waited for; matrix products, arithmetic and copies ran while one was open for 5% of the time, Pallas kernels for 24%

profile of v1, /device:TPU:4, one launch (start us, length us, event | category | flops | bytes accessed | tf_op | source)
XLA Modules:
  0.0 70.7 jit_solution(14771499856318806762)
XLA Ops:
  0.0 0.7 %rev.7 = s32[2]{0:T(128)S(1)} reverse(s32[2]{0:T(128)} %param.10), dimensions={0} | reverse | bytes 16 | tf_op jit(solution)/shard_map/rev | solution.py:276
  0.7 0.7 %reverse.3 = s32[2]{0:T(128)S(1)} reverse(s32[2]{0:T(128)} %param.9), dimensions={0} | reverse | bytes 16 | tf_op jit(solution)/shard_map/reverse
  1.5 0.7 broadcast_subtract_fusion
  2.2 0.7 broadcast_select_fusion.1
  2.9 0.6 fusion
  3.5 1.9 %collective-permute-start.3 = (s32[1]{0:T(128)}, s32[1]{0:T(128)}, u32[]{:S(2)}, u32[]{:S(2)}) collective-permute-start(s32[1]{0:T(128)} %get-tuple-element.27), channel_id=1, source_target_pairs={{0,8},{8,16},{16,24},{1,9},{9,17},{17,25},{2,10},{10,18},{18,26},{... | collective-permute-start | bytes 20 | tf_op jit(solution)/shard_map/ppermute | solution.py:20
  5.5 3.1 %collective-permute-done.3.info = s32[1]{0:T(128)} collective-permute-done((s32[1]{0:T(128)}, s32[1]{0:T(128)}, u32[]{:S(2)}, u32[]{:S(2)}) %collective-permute-start.3) | collective-permute-done | bytes 36 | tf_op jit(solution)/shard_map/ppermute | solution.py:20
  8.6 2.8 %rim.1 = f32[256,4,128]{2,1,0:T(4,128)} custom-call(s32[1]{0:T(128)} %collective-permute-done.3.info, f32[512,8,128]{2,1,0:T(8,128)} %bitcast.24), custom_call_target="tpu_custom_call" | custom-call | tf_op jit(solution)/shard_map/rim/pallas_call | solution.py:285
  11.4 1.9 %collective-permute-start.4 = (f32[256,4,128]{2,1,0:T(4,128)}, f32[256,4,128]{2,1,0:T(4,128)S(1)}, u32[]{:S(2)}, u32[]{:S(2)}) collective-permute-start(f32[256,4,128]{2,1,0:T(4,128)} %rim.1), channel_id=1, source_target_pairs={{8,0},{16,8},{24,16},{9,1},{17,9},{25,17},{10,2},{18,10},{26,18},{... | collective-permute-start | bytes 1572872 | tf_op jit(solution)/shard_map/ppermute | solution.py:20
  13.3 0.6 fusion.1
  13.9 3.3 %stack.19.refs_0_.info = s32[8]{0:T(128)} concatenate(s32[1]{0:T(128)} %get-tuple-element.30, s32[1]{0:T(128)} %get-tuple-element.28, s32[1]{0:T(128)} %bitcast.1, s32[1]{0:T(128)} %get-tuple-element.29, s32[1]{0:T(128)} %get-tuple-element.27, s32[1]{0:T(128)} %bitcast.2, s32[1]{0:T(128)} %bitcast.3, s32[1]{0:T(128)} %bitcast.4), dimensions={0} | concatenate | bytes 64 | tf_op jit(solution)/shard_map/stack | solution.py:277
  17.2 7.4 %wave0.1 = (f32[136,256]{1,0:T(8,128)}, f32[136,256]{1,0:T(8,128)}, f32[136,256]{1,0:T(8,128)}, f32[136,256]{1,0:T(8,128)}) custom-call(s32[8]{0:T(128)} %stack.19.refs_0_.info, f32[4096,128]{1,0:T(8,128)} %bitcast.25, f32[1024,128]{1,0:T(8,128)} %bitcast.27, bf16[2,256,256]{2,1,0:T(8,128)(2,1)} %refs_3_.3, bf16[1024,256]{1,0:T(8,128)(2,1)} %constant.32.clone.refs_4_), custom_call_target="tpu_custom_call" | custom-call | flops 1610612736 | bytes 5242880 | tf_op jit(solution)/shard_map/wave0/pallas_call | solution.py:198
  24.6 1.6 %collective-permute-start = (f32[136,256]{1,0:T(8,128)}, f32[136,256]{1,0:T(8,128)S(1)}, u32[]{:S(2)}, u32[]{:S(2)}) collective-permute-start(f32[136,256]{1,0:T(8,128)} %get-tuple-element.17), channel_id=1, source_target_pairs={{0,1},{1,0},{2,3},{3,2},{4,5},{5,4},{6,7},{7,6},{8,9},{9,8},{10,11... | collective-permute-start | bytes 417800 | tf_op jit(solution)/shard_map/ppermute | solution.py:24
  26.2 1.6 %collective-permute-start.1 = (f32[136,256]{1,0:T(8,128)}, f32[136,256]{1,0:T(8,128)S(1)}, u32[]{:S(2)}, u32[]{:S(2)}) collective-permute-start(f32[136,256]{1,0:T(8,128)} %get-tuple-element.18), channel_id=1, source_target_pairs={{0,2},{1,3},{2,0},{3,1},{4,6},{5,7},{6,4},{7,5},{8,10},{9,11},{10,... | collective-permute-start | bytes 417800 | tf_op jit(solution)/shard_map/ppermute | solution.py:24
  27.7 0.4 collective-permute-start.2
  28.2 0.8 %copy-done.6 = f32[256,4,128]{2,1,0:T(4,128)} copy-done((f32[256,4,128]{2,1,0:T(4,128)}, f32[256,4,128]{2,1,0:T(4,128)S(1)}, u32[]{:S(2)}) %copy-start.6) | copy-done | bytes 524312
  29.0 7.6 %wave1.1 = (f32[136,256]{1,0:T(8,128)}, f32[136,256]{1,0:T(8,128)}, f32[136,256]{1,0:T(8,128)}, f32[136,256]{1,0:T(8,128)}) custom-call(s32[8]{0:T(128)} %stack.19.refs_0_.info, f32[4096,128]{1,0:T(8,128)} %bitcast.26, f32[1024,128]{1,0:T(8,128)} %bitcast.28, bf16[2,256,256]{2,1,0:T(8,128)(2,1)} %refs_3_.3, bf16[1024,256]{1,0:T(8,128)(2,1)} %constant.32.clone.refs_4_, ...), custom_call_target="tpu_custom_call" | custom-call | flops 1610612736 | bytes 5242880 | tf_op jit(solution)/shard_map/wave1/pallas_call | solution.py:198
  36.6 1.6 %collective-permute-start.5 = (f32[136,256]{1,0:T(8,128)}, f32[136,256]{1,0:T(8,128)S(1)}, u32[]{:S(2)}, u32[]{:S(2)}) collective-permute-start(f32[136,256]{1,0:T(8,128)} %get-tuple-element.21), channel_id=1, source_target_pairs={{0,1},{1,0},{2,3},{3,2},{4,5},{5,4},{6,7},{7,6},{8,9},{9,8},{10,11... | collective-permute-start | bytes 417800 | tf_op jit(solution)/shard_map/ppermute | solution.py:24
  38.1 1.6 %collective-permute-start.6 = (f32[136,256]{1,0:T(8,128)}, f32[136,256]{1,0:T(8,128)S(1)}, u32[]{:S(2)}, u32[]{:S(2)}) collective-permute-start(f32[136,256]{1,0:T(8,128)} %get-tuple-element.22), channel_id=1, source_target_pairs={{0,2},{1,3},{2,0},{3,1},{4,6},{5,7},{6,4},{7,5},{8,10},{9,11},{10,... | collective-permute-start | bytes 417800 | tf_op jit(solution)/shard_map/ppermute | solution.py:24
  39.7 0.4 collective-permute-start.7
  40.4 0.4 copy-done.2
  40.9 2.1 %sum0.1.acc = f32[2,2,64,512]{3,2,1,0:T(8,128)} custom-call(s32[8]{0:T(128)} %stack.19.refs_0_.info, f32[136,256]{1,0:T(8,128)} %get-tuple-element.16.refs_0_, f32[136,256]{1,0:T(8,128)} %copy-done, f32[136,256]{1,0:T(8,128)} %copy-done.2, f32[136,256]{1,0:T(8,128)} %copy-done.4), custom_call_target="tpu_custom_call" | custom-call | tf_op jit(solution)/shard_map/sum0/pallas_call | solution.py:302
  43.0 1.8 %collective-permute-done.6.refs_2_ = f32[136,256]{1,0:T(8,128)S(1)} collective-permute-done((f32[136,256]{1,0:T(8,128)}, f32[136,256]{1,0:T(8,128)S(1)}, u32[]{:S(2)}, u32[]{:S(2)}) %collective-permute-start.6) | collective-permute-done | bytes 139296 | tf_op jit(solution)/shard_map/ppermute | solution.py:24
  44.8 1.5 %collective-permute-done.7.refs_3_ = f32[136,256]{1,0:T(8,128)S(1)} collective-permute-done((f32[136,256]{1,0:T(8,128)}, f32[136,256]{1,0:T(8,128)S(1)}, u32[]{:S(2)}, u32[]{:S(2)}) %collective-permute-start.7) | collective-permute-done | bytes 139296 | tf_op jit(solution)/shard_map/ppermute | solution.py:24
  46.4 0.7 copy-done.5
  47.0 2.4 %sum1.1 = (f32[512,128]{1,0:T(8,128)}, f32[512,128]{1,0:T(8,128)}, f32[512,128]{1,0:T(8,128)}) custom-call(s32[8]{0:T(128)} %stack.19.refs_0_.info, f32[2,2,64,512]{3,2,1,0:T(8,128)} %sum0.1.acc, f32[136,256]{1,0:T(8,128)} %get-tuple-element.20.refs_0_, f32[136,256]{1,0:T(8,128)} %copy-done.1, f32[136,256]{1,0:T(8,128)} %copy-done.3, f32[136,256]{1,0:T(8,128)} %copy-done.5), custom_call_target="tpu_custom_call" | custom-call | tf_op jit(solution)/shard_map/sum1/pallas_call | solution.py:311
  49.5 1.9 %collective-permute-start.8 = (f32[512,128]{1,0:T(8,128)}, f32[512,128]{1,0:T(8,128)S(1)}, u32[]{:S(2)}, u32[]{:S(2)}) collective-permute-start(f32[512,128]{1,0:T(8,128)} %get-tuple-element.26), channel_id=1, source_target_pairs={{0,8},{8,16},{16,24},{1,9},{9,17},{17,25},{2,10},{10,18},{18,26},{... | collective-permute-start | bytes 786440 | tf_op jit(solution)/shard_map/ppermute | solution.py:20
  51.4 6.0 %collective-permute-done.8 = f32[512,128]{1,0:T(8,128)S(1)} collective-permute-done((f32[512,128]{1,0:T(8,128)}, f32[512,128]{1,0:T(8,128)S(1)}, u32[]{:S(2)}, u32[]{:S(2)}) %collective-permute-start.8) | collective-permute-done | bytes 262176 | tf_op jit(solution)/shard_map/ppermute | solution.py:20
  57.4 1.1 %broadcast_select_fusion = f32[512,128]{1,0:T(8,128)S(1)} fusion(f32[512,128]{1,0:T(8,128)} %get-tuple-element.24, pred[]{:T(512)S(6)} %eq.3, f32[512,128]{1,0:T(8,128)} %get-tuple-element.25, f32[512,128]{1,0:T(8,128)S(1)} %collective-permute-done.8), kind=kLoop, calls=%fused_computation.1 | loop fusion | flops 131072 | bytes 1048577 | tf_op jit(solution)/shard_map/jit(_where)/select_n | solution.py:320
  58.4 2.6 %collective-permute-start.9 = (f32[512,128]{1,0:T(8,128)S(1)}, f32[512,128]{1,0:T(8,128)S(1)}, u32[]{:S(2)}, u32[]{:S(2)}) collective-permute-start(f32[512,128]{1,0:T(8,128)S(1)} %broadcast_select_fusion), channel_id=1, source_target_pairs={{0,4},{1,5},{2,6},{3,7},{4,0},{5,1},{6,2},{7,3},{8,12},{9,13},{10,... | collective-permute-start | bytes 786440 | tf_op jit(solution)/shard_map/ppermute | solution.py:24
  61.0 8.0 %collective-permute-done.9 = f32[512,128]{1,0:T(8,128)S(1)} collective-permute-done((f32[512,128]{1,0:T(8,128)S(1)}, f32[512,128]{1,0:T(8,128)S(1)}, u32[]{:S(2)}, u32[]{:S(2)}) %collective-permute-start.9) | collective-permute-done | bytes 262176 | tf_op jit(solution)/shard_map/ppermute | solution.py:24
  69.0 1.7 %select_add_fusion = f32[512,128]{1,0:T(8,128)} fusion(f32[512,128]{1,0:T(8,128)S(1)} %collective-permute-done.9, f32[512,128]{1,0:T(8,128)} %get-tuple-element.24, pred[]{:T(512)S(6)} %eq.3, f32[512,128]{1,0:T(8,128)} %get-tuple-element.25, f32[512,128]{1,0:T(8,128)S(1)} %collective-permute-done.8), kind=kLoop, calls=%fused_computation | loop fusion | flops 196608 | bytes 1310721 | tf_op jit(solution)/shard_map/add | solution.py:321
  (16 shorter events, 0.3 us)
Async XLA Ops:
  3.5 5.0 %collective-permute-start.3 = (s32[1]{0:T(128)}, s32[1]{0:T(128)}, u32[]{:S(2)}, u32[]{:S(2)}) collective-permute-start(s32[1]{0:T(128)} %get-tuple-element.27), channel_id=1, source_target_pairs={{0,8},{8,16},{16,24},{1,9},{9,17},{17,25},{2,10},{10,18},{18,26},{... | collective-permute-start | bytes 20 | tf_op jit(solution)/shard_map/ppermute | solution.py:20
  11.4 16.7 %collective-permute-start.4 = (f32[256,4,128]{2,1,0:T(4,128)}, f32[256,4,128]{2,1,0:T(4,128)S(1)}, u32[]{:S(2)}, u32[]{:S(2)}) collective-permute-start(f32[256,4,128]{2,1,0:T(4,128)} %rim.1), channel_id=1, source_target_pairs={{8,0},{16,8},{24,16},{9,1},{17,9},{25,17},{10,2},{18,10},{26,18},{... | collective-permute-start | bytes 1572872 | tf_op jit(solution)/shard_map/ppermute | solution.py:20
  24.6 15.1 %collective-permute-start = (f32[136,256]{1,0:T(8,128)}, f32[136,256]{1,0:T(8,128)S(1)}, u32[]{:S(2)}, u32[]{:S(2)}) collective-permute-start(f32[136,256]{1,0:T(8,128)} %get-tuple-element.17), channel_id=1, source_target_pairs={{0,1},{1,0},{2,3},{3,2},{4,5},{5,4},{6,7},{7,6},{8,9},{9,8},{10,11... | collective-permute-start | bytes 417800 | tf_op jit(solution)/shard_map/ppermute | solution.py:24
  26.2 14.0 %collective-permute-start.1 = (f32[136,256]{1,0:T(8,128)}, f32[136,256]{1,0:T(8,128)S(1)}, u32[]{:S(2)}, u32[]{:S(2)}) collective-permute-start(f32[136,256]{1,0:T(8,128)} %get-tuple-element.18), channel_id=1, source_target_pairs={{0,2},{1,3},{2,0},{3,1},{4,6},{5,7},{6,4},{7,5},{8,10},{9,11},{10,... | collective-permute-start | bytes 417800 | tf_op jit(solution)/shard_map/ppermute | solution.py:24
  27.7 12.4 %collective-permute-start.2 = (f32[136,256]{1,0:T(8,128)}, f32[136,256]{1,0:T(8,128)S(1)}, u32[]{:S(2)}, u32[]{:S(2)}) collective-permute-start(f32[136,256]{1,0:T(8,128)} %get-tuple-element.19), channel_id=1, source_target_pairs={{0,3},{1,2},{2,1},{3,0},{4,7},{5,6},{6,5},{7,4},{8,11},{9,10},{10,... | collective-permute-start | bytes 417800 | tf_op jit(solution)/shard_map/ppermute | solution.py:24
  28.2 0.8 %copy-start.6 = (f32[256,4,128]{2,1,0:T(4,128)}, f32[256,4,128]{2,1,0:T(4,128)S(1)}, u32[]{:S(2)}) copy-start(f32[256,4,128]{2,1,0:T(4,128)S(1)} %collective-permute-done.4) | copy-start | bytes 1572868
  36.6 6.4 %collective-permute-start.5 = (f32[136,256]{1,0:T(8,128)}, f32[136,256]{1,0:T(8,128)S(1)}, u32[]{:S(2)}, u32[]{:S(2)}) collective-permute-start(f32[136,256]{1,0:T(8,128)} %get-tuple-element.21), channel_id=1, source_target_pairs={{0,1},{1,0},{2,3},{3,2},{4,5},{5,4},{6,7},{7,6},{8,9},{9,8},{10,11... | collective-permute-start | bytes 417800 | tf_op jit(solution)/shard_map/ppermute | solution.py:24
  38.1 6.7 %collective-permute-start.6 = (f32[136,256]{1,0:T(8,128)}, f32[136,256]{1,0:T(8,128)S(1)}, u32[]{:S(2)}, u32[]{:S(2)}) collective-permute-start(f32[136,256]{1,0:T(8,128)} %get-tuple-element.22), channel_id=1, source_target_pairs={{0,2},{1,3},{2,0},{3,1},{4,6},{5,7},{6,4},{7,5},{8,10},{9,11},{10,... | collective-permute-start | bytes 417800 | tf_op jit(solution)/shard_map/ppermute | solution.py:24
  39.7 0.7 copy-start
  39.7 6.6 %collective-permute-start.7 = (f32[136,256]{1,0:T(8,128)}, f32[136,256]{1,0:T(8,128)S(1)}, u32[]{:S(2)}, u32[]{:S(2)}) collective-permute-start(f32[136,256]{1,0:T(8,128)} %get-tuple-element.23), channel_id=1, source_target_pairs={{0,3},{1,2},{2,1},{3,0},{4,7},{5,6},{6,5},{7,4},{8,11},{9,10},{10,... | collective-permute-start | bytes 417800 | tf_op jit(solution)/shard_map/ppermute | solution.py:24
  40.1 0.7 copy-start.2
  40.1 0.7 copy-start.4
  43.0 3.4 %copy-start.1 = (f32[136,256]{1,0:T(8,128)}, f32[136,256]{1,0:T(8,128)S(1)}, u32[]{:S(2)}) copy-start(f32[136,256]{1,0:T(8,128)S(1)} %collective-permute-done.5.refs_1_) | copy-start | bytes 417796
  44.8 1.5 %copy-start.3 = (f32[136,256]{1,0:T(8,128)}, f32[136,256]{1,0:T(8,128)S(1)}, u32[]{:S(2)}) copy-start(f32[136,256]{1,0:T(8,128)S(1)} %collective-permute-done.6.refs_2_) | copy-start | bytes 417796
  46.4 0.7 copy-start.5
  49.5 7.9 %collective-permute-start.8 = (f32[512,128]{1,0:T(8,128)}, f32[512,128]{1,0:T(8,128)S(1)}, u32[]{:S(2)}, u32[]{:S(2)}) collective-permute-start(f32[512,128]{1,0:T(8,128)} %get-tuple-element.26), channel_id=1, source_target_pairs={{0,8},{8,16},{16,24},{1,9},{9,17},{17,25},{2,10},{10,18},{18,26},{... | collective-permute-start | bytes 786440 | tf_op jit(solution)/shard_map/ppermute | solution.py:20
  58.4 10.5 %collective-permute-start.9 = (f32[512,128]{1,0:T(8,128)S(1)}, f32[512,128]{1,0:T(8,128)S(1)}, u32[]{:S(2)}, u32[]{:S(2)}) collective-permute-start(f32[512,128]{1,0:T(8,128)S(1)} %broadcast_select_fusion), channel_id=1, source_target_pairs={{0,4},{1,5},{2,6},{3,7},{4,0},{5,1},{6,2},{7,3},{8,12},{9,13},{10,... | collective-permute-start | bytes 786440 | tf_op jit(solution)/shard_map/ppermute | solution.py:24

commit v2 on v1

v2 whole, which is shorter than its diff:
```python
import functools
import math

import jax
import jax.numpy as jnp
import numpy as np
from jax import lax
from jax.experimental import pallas as pl
from jax.experimental.pallas import tpu as pltpu
from jax.sharding import PartitionSpec as P

LANES = 128
F32 = jnp.float32
BF16 = jnp.bfloat16


def shifted(block, axis, distance):
    devices = range(lax.axis_size(axis))
    route = [(i - distance, i) for i in devices if i - distance in devices]
    return lax.ppermute(block, axis, route)


def exchanged(block, axis, flip):
    return lax.ppermute(block, axis, [(i, i ^ flip) for i in range(lax.axis_size(axis))])


def split_tables(length):
    indices = np.arange(length, dtype=np.int64)
    angles = (indices[:, None] * indices[None, :] % length) * (2.0 * math.pi / length)
    factor = 1.0 / math.sqrt(length)
    whole = np.concatenate([np.cos(angles), np.sin(angles)], axis=0) * factor
    high = whole.astype(BF16)
    low = (whole - high.astype(np.float64)).astype(BF16)
    return jnp.asarray(np.concatenate([high, low], axis=0))


def linear(array):
    rows, parts, columns = array.shape
    tiles = columns // LANES
    return array.reshape(rows, parts, tiles, LANES).transpose(0, 2, 1, 3).reshape(rows * tiles * parts, LANES)


def unlinear(array, rows, columns):
    tiles = columns // LANES
    return array.reshape(rows, tiles, 2, LANES).transpose(0, 2, 1, 3).reshape(rows, 2, columns)


def halves(value):
    high = value.astype(BF16)
    return high, (value - high.astype(F32)).astype(BF16)


def dot3(high_left, low_left, high_right, low_right):
    left = jnp.concatenate([low_left, high_left, high_left], axis=1)
    right = jnp.concatenate([high_right, low_right, high_right], axis=0)
    return jnp.dot(left, right, preferred_element_type=F32)


def in_vmem(array):
    return pltpu.with_memory_space_constraint(array, pltpu.VMEM)


def kernel_call(body, name, out_shapes, scalars, arrays, scratch=(), flops=0):
    smem = pl.BlockSpec(memory_space=pltpu.SMEM)
    vmem = pl.BlockSpec(memory_space=pltpu.VMEM)
    moved = sum(4 * math.prod(shape) for shape in out_shapes)
    return pl.pallas_call(
        body,
        out_shape=[pltpu.VMEM(shape, F32) for shape in out_shapes],
        in_specs=[smem] * len(scalars) + [vmem] * len(arrays),
        out_specs=[vmem] * len(out_shapes),
        scratch_shapes=scratch,
        cost_estimate=pl.CostEstimate(flops=flops, transcendentals=0, bytes_accessed=2 * moved),
        compiler_params=pltpu.CompilerParams(vmem_limit_bytes=16 << 20),
        name=name,
    )(*scalars, *[in_vmem(array) for array in arrays])


def chosen(slot, rows, cols, band_start, window):
    crossing = (rows[0] - band_start > window).astype(jnp.int32)
    index = crossing if slot == 0 else 1 - crossing
    return rows[index] - band_start, cols[index], index


def rim_kernel(window, rows, cols, obj, out):
    band_start = (lax.axis_index("tile") - 1) * (2 * window)
    _, offset, _ = chosen(1, rows, cols, band_start, window)
    tiles = window // LANES
    for tile in range(tiles):
        column = lax.broadcasted_iota(jnp.int32, (window, LANES), 1) + tile * LANES
        for part in range(2):
            near = obj[pl.ds(tile * 2 + part, window, stride=4 * tiles), :]
            beyond = obj[pl.ds((tiles + tile) * 2 + part, window, stride=4 * tiles), :]
            out[part, :, pl.ds(tile * LANES, LANES)] = jnp.where(column < offset, beyond, near)


def wave_kernel(slot, window, classes, with_rim, rows, cols, obj, ill, amps, table, *refs):
    if with_rim:
        rim, refs = refs[0], refs[1:]
    outs, refs = refs[:classes], refs[classes:]
    doubled, probe, xh, xl, far = refs
    tiles = window // LANES
    row, column, index = chosen(slot, rows, cols, lax.axis_index("tile") * (2 * window), window)
    own = lax.rem(lax.axis_index("pos"), classes)
    size = 32
    step = 2 * tiles
    whole = window * step
    doubled[pl.ds(0, whole), :] = ill[...]
    doubled[pl.ds(whole, size * step), :] = ill[pl.ds(0, size * step), :]
    turn = lax.rem(row, window)

    def store_pair(first, real, imag):
        here = pl.ds(first, size)
        below = pl.ds(window + first, size)
        left, right = pl.ds(0, window), pl.ds(window, window)
        for part, ref in zip(range(2), (xh, xl)):
            r, i, n = (halves(v)[part] for v in (real, imag, -real))
            ref[here, left] = r
            ref[here, right] = i
            ref[below, left] = i
            ref[below, right] = n

    for first in range(0, window, size):
        place = lax.broadcasted_iota(jnp.int32, (size, window), 0) + first
        across = lax.broadcasted_iota(jnp.int32, (size, window), 1)
        start = lax.rem(first + window - turn, window) * step
        pair = []
        for part in range(2):
            rolled = jnp.concatenate(
                [doubled[pl.ds(start + tile * 2 + part, size, stride=step), :] for tile in range(tiles)],
                axis=1,
            )
            rolled = pltpu.roll(rolled, column, 1)
            probe[part, pl.ds(first, size), :] = rolled

            def block(base):
                def tile_at(tile):
                    return obj[pl.ds((base + first) * 2 * step + tile * 2 + part, size, stride=2 * step), :]

                near = jnp.concatenate([tile_at(t) for t in range(tiles)], axis=1)
                beyond = jnp.concatenate([tile_at(t + tiles) for t in range(tiles)], axis=1)
                return jnp.where(across < column, beyond, near)

            seen = jnp.where(place < row, block(window), block(0))
            if with_rim:
                seen = jnp.where(place + window < row, rim[part, pl.ds(first, size), :], seen)
            pair.append((rolled, seen))
        (probe_real, obj_real), (probe_imag, obj_imag) = pair
        store_pair(
            first,
            probe_real * obj_real - probe_imag * obj_imag,
            probe_real * obj_imag + probe_imag * obj_real,
        )

    high = table[pl.ds(0, 2 * window), :]
    low = table[pl.ds(2 * window, 2 * window), :]
    left_high = jnp.concatenate([table[pl.ds(0, window), :], table[pl.ds(window, window), :]], axis=1)
    left_low = jnp.concatenate([table[pl.ds(2 * window, window), :], table[pl.ds(3 * window, window), :]], axis=1)

    def both_sides():
        mid = dot3(xh[...], xl[...], high, low)
        for first in range(0, window, size):
            store_pair(first, mid[first : first + size], mid[window + first : window + first + size])
        far[...] = dot3(left_high, left_low, xh[...], xl[...])

    both_sides()
    for first in range(0, window, size):
        real = far[pl.ds(first, size), pl.ds(0, window)]
        imag = far[pl.ds(first, size), pl.ds(window, window)]
        inverse = jnp.minimum(lax.rsqrt(real * real + imag * imag), 4.0)
        scaled = amps[index, pl.ds(first, size), :].astype(F32) * inverse
        store_pair(first, real * (1.0 - scaled), imag * (scaled - 1.0))
    both_sides()

    share = window // classes
    for flip in range(classes):
        base = pl.multiple_of((own ^ flip) * share, share)
        here = pl.ds(base, share)
        real = far[here, pl.ds(0, window)]
        imag = far[here, pl.ds(window, window)]
        probe_real = probe[0, here, :]
        probe_imag = probe[1, here, :]
        outs[flip][pl.ds(0, share), :] = probe_real * real - probe_imag * imag
        outs[flip][pl.ds(share, share), :] = -(probe_real * imag + probe_imag * real)
        line = lax.broadcasted_iota(jnp.int32, (8, window), 0)
        outs[flip][pl.ds(2 * share, 8), :] = jnp.where(line == 0, row, column).astype(F32)


def wave(slot, window, classes, scalars, arrays):
    share = window // classes
    tiles = window // LANES
    scratch = [
        pltpu.VMEM(((window + 32) * 2 * tiles + 8, LANES), F32),
        pltpu.VMEM((2, window, window), F32),
        pltpu.VMEM((2 * window, 2 * window), BF16),
        pltpu.VMEM((2 * window, 2 * window), BF16),
        pltpu.VMEM((window, 2 * window), F32),
    ]
    return kernel_call(
        functools.partial(wave_kernel, slot, window, classes, len(arrays) == 5),
        "wave" + str(slot),
        [(2 * share + 8, window)] * classes,
        scalars,
        arrays,
        scratch,
        96 * window**3,
    )


def placed(piece, own, share, window):
    row = piece[pl.ds(2 * share, 1), :]
    column = piece[pl.ds(2 * share + 1, 1), :]
    place = (lax.broadcasted_iota(jnp.int32, (share, window), 0) + own * share).astype(F32)
    across = lax.broadcasted_iota(jnp.int32, (share, window), 1).astype(F32)
    return across < column, place < row, place + float(window) < row


def first_sum_kernel(window, classes, *refs):
    pieces, acc = refs[:classes], refs[classes]
    share = window // classes
    own = lax.rem(lax.axis_index("pos"), classes)
    for part in range(2):
        total = [[jnp.zeros((share, window), F32) for _ in range(2)] for _ in range(2)]
        for piece in pieces:
            upper, below, _ = placed(piece, own, share, window)
            value = piece[pl.ds(part * share, share), :]
            for k, wanted in enumerate((~below, below)):
                kept = jnp.where(wanted, value, 0.0)
                total[k][0] += jnp.where(upper, 0.0, kept)
                total[k][1] += jnp.where(upper, kept, 0.0)
        for k in range(2):
            for half in range(2):
                acc[k, part, :, pl.ds(half * window, window)] = total[k][half]


def second_sum_kernel(window, classes, acc, *refs):
    pieces, outs = refs[:classes], refs[classes:]
    share = window // classes
    tiles = window // LANES
    own = lax.rem(lax.axis_index("pos"), classes)
    for part in range(2):
        total = [[acc[k, part, :, pl.ds(h * window, window)] for h in range(2)] for k in range(2)]
        total.append([jnp.zeros((share, window), F32) for _ in range(2)])
        for piece in pieces:
            upper, below, lowest = placed(piece, own, share, window)
            value = piece[pl.ds(part * share, share), :]
            for k, wanted in enumerate((~below, below & ~lowest, lowest)):
                kept = jnp.where(wanted, value, 0.0)
                total[k][0] += jnp.where(upper, 0.0, kept)
                total[k][1] += jnp.where(upper, kept, 0.0)
        for k in range(3):
            for half in range(2):
                for tile in range(tiles):
                    outs[k][pl.ds((half * tiles + tile) * 2 + part, share, stride=4 * tiles), :] = total[k][half][
                        :, tile * LANES : (tile + 1) * LANES
                    ]


def on_device(object_field, illumination, amplitudes, row_offset, col_offset):
    band_rows, _, columns = object_field.shape
    window = illumination.shape[0]
    ways = lax.axis_size("pos")
    assert band_rows == 2 * window and columns == 2 * window and row_offset.shape[0] == 2
    classes = ways // 2
    share = window // classes
    tiles = window // LANES
    table = split_tables(window)
    obj = linear(object_field)
    ill = linear(illumination)
    scalars = (row_offset, col_offset)

    wanted = [shifted(scalar, "tile", 1) for scalar in scalars]
    (rim,) = kernel_call(functools.partial(rim_kernel, window), "rim", [(2, window, window)], wanted, [obj])
    rim = shifted(rim, "tile", -1)

    def spread(pieces):
        return [pieces[0]] + [exchanged(pieces[d], "pos", d) for d in range(1, classes)]

    near = spread(wave(0, window, classes, scalars, [obj, ill, amplitudes, table]))
    (acc,) = kernel_call(
        functools.partial(first_sum_kernel, window, classes), "sum0", [(2, 2, share, columns)], (), near
    )
    late = spread(wave(1, window, classes, scalars, [obj, ill, amplitudes, table, rim]))
    top, middle, spilled = kernel_call(
        functools.partial(second_sum_kernel, window, classes),
        "sum1",
        [(share * 4 * tiles, LANES)] * 3,
        (),
        [acc, *late],
    )
    top = top + shifted(spilled, "tile", 1)
    is_upper = lax.axis_index("pos") >= classes
    received = exchanged(jnp.where(is_upper, top, middle), "pos", classes)
    result = jnp.where(is_upper, middle, top) + received
    return unlinear(result, share, columns)


def solution(mesh):
    in_specs = (
        P("tile", None, None),
        P(),
        P(("tile", "pos"), None, None),
        P(("tile", "pos")),
        P(("tile", "pos")),
    )
    out_specs = P(("tile", "pos"), None, None)
    return jax.shard_map(
        on_device, mesh=mesh, in_specs=in_specs, out_specs=out_specs, check_vma=False
    )
```

time: 71.1 us -> 55.8 us (0.78)
  the two profiles are of different devices: /device:TPU:4 before, /device:TPU:0 now
where the time goes in v2:
time: 55.8 us; the launch traced here: 54.9 us
  waiting for transfers between devices  20.2 us (36%)
  starting transfers between devices  19.5 us (35%)
  Pallas kernels  10.7 us (19%)
  local copies, waits for them, and re-layouts  3.6 us (6%)
  other arithmetic  0.79 us (1%)
    ppermute x7, waiting for transfers between devices, exchanged(): lax.ppermute(block, axis, [(i, i ^ flip) for i in range(lax.axis_size(axi...  18.1 us
    pallas_call x5, Pallas kernels, kernel_call(): pl.pallas_call(body, out_shape=[pltpu.VMEM(shape, F32) for shape in out_s...  10.7 us
    ppermute x4, starting transfers between devices, shifted(): return lax.ppermute(block, axis, route)  9.77 us
    ppermute x7, starting transfers between devices, exchanged(): lax.ppermute(block, axis, [(i, i ^ flip) for i in range(lax.axis_size(axi...  9.76 us
    unnamed x16, local copies, waits for them, and re-layouts  3.6 us
    ppermute x4, waiting for transfers between devices, shifted(): return lax.ppermute(block, axis, route)  2.05 us
  transfers between devices with their start and end apart: 11, of which 6 were waited for; matrix products, arithmetic and copies ran while one was open for 0% of the time, Pallas kernels for 17%

profile of v2, /device:TPU:0, one launch (start us, length us, event | category | flops | bytes accessed | tf_op | source)
XLA Modules:
  0.0 54.9 jit_solution(5208113832446608591)
XLA Ops:
  0.0 2.5 %collective-permute-start.3 = (s32[2]{0:T(128)}, s32[2]{0:T(128)S(1)}, u32[]{:S(2)}, u32[]{:S(2)}) collective-permute-start(s32[2]{0:T(128)} %rows.3), channel_id=1, source_target_pairs={{0,8},{8,16},{16,24},{1,9},{9,17},{17,25},{2,10},{10,18},{18,26},{... | collective-permute-start | bytes 32 | tf_op jit(solution)/shard_map/ppermute | solution.py:20
  2.5 4.5 %collective-permute-start.4 = (s32[2]{0:T(128)}, s32[2]{0:T(128)S(1)}, u32[]{:S(2)}, u32[]{:S(2)}) collective-permute-start(s32[2]{0:T(128)} %cols.3), channel_id=1, source_target_pairs={{0,8},{8,16},{16,24},{1,9},{9,17},{17,25},{2,10},{10,18},{18,26},{... | collective-permute-start | bytes 32 | tf_op jit(solution)/shard_map/ppermute | solution.py:20
  7.1 0.0 collective-permute-done.3.rows
  7.1 0.9 %collective-permute-done.4.cols = s32[2]{0:T(128)S(1)} collective-permute-done((s32[2]{0:T(128)}, s32[2]{0:T(128)S(1)}, u32[]{:S(2)}, u32[]{:S(2)}) %collective-permute-start.4) | collective-permute-done | bytes 40 | tf_op jit(solution)/shard_map/ppermute | solution.py:20
  8.0 1.6 %copy-done = f32[512,2,512]{2,1,0:T(2,128)S(1)} copy-done((f32[512,2,512]{2,1,0:T(2,128)S(1)}, f32[512,2,512]{2,1,0:T(2,128)}, u32[]{:S(2)}) %copy-start) | copy-done | bytes 2097176
  9.6 0.7 %rim.1 = f32[2,256,256]{2,1,0:T(8,128)S(1)} custom-call(s32[2]{0:T(128)S(1)} %collective-permute-done.3.rows, s32[2]{0:T(128)S(1)} %collective-permute-done.4.cols, f32[4096,128]{1,0:T(8,128)S(1)} %bitcast.15), custom_call_target="tpu_custom_call" | custom-call | bytes 1048576 | tf_op jit(solution)/shard_map/rim/pallas_call | solution.py:67
  10.3 1.4 %collective-permute-start.5 = (f32[2,256,256]{2,1,0:T(8,128)S(1)}, f32[2,256,256]{2,1,0:T(8,128)S(1)}, u32[]{:S(2)}, u32[]{:S(2)}) collective-permute-start(f32[2,256,256]{2,1,0:T(8,128)S(1)} %rim.1), channel_id=1, source_target_pairs={{8,0},{16,8},{24,16},{9,1},{17,9},{25,17},{10,2},{18,10},{26,18},{... | collective-permute-start | bytes 1572872 | tf_op jit(solution)/shard_map/ppermute | solution.py:20
  11.8 0.0 copy-start.3
  11.8 0.9 %copy-done.3 = bf16[2,256,256]{2,1,0:T(8,128)(2,1)S(1)} copy-done((bf16[2,256,256]{2,1,0:T(8,128)(2,1)S(1)}, bf16[2,256,256]{2,1,0:T(8,128)(2,1)}, u32[]{:S(2)}) %copy-start.3) | copy-done | bytes 262168
  12.7 1.0 %copy-done.7 = bf16[1024,256]{1,0:T(8,128)(2,1)S(1)} copy-done((bf16[1024,256]{1,0:T(8,128)(2,1)S(1)}, bf16[1024,256]{1,0:T(8,128)(2,1)}, u32[]{:S(2)}) %copy-start.7) | copy-done | bytes 524312
  13.8 4.6 %wave0.1 = (f32[136,256]{1,0:T(8,128)S(1)}, f32[136,256]{1,0:T(8,128)S(1)}, f32[136,256]{1,0:T(8,128)S(1)}, f32[136,256]{1,0:T(8,128)S(1)}) custom-call(s32[2]{0:T(128)S(1)} %copy-done.5, s32[2]{0:T(128)S(1)} %copy-done.6, f32[4096,128]{1,0:T(8,128)S(1)} %bitcast.16, f32[1024,128]{1,0:T(8,128)S(1)} %bitcast.18, bf16[2,256,256]{2,1,0:T(8,128)(2,1)S(1)} %copy-done.3, ...), custom_call_target="tpu_custom_call" | custom-call | flops 1610612736 | bytes 1114112 | tf_op jit(solution)/shard_map/wave0/pallas_call | solution.py:67
  18.4 1.6 %collective-permute-start = (f32[136,256]{1,0:T(8,128)S(1)}, f32[136,256]{1,0:T(8,128)S(1)}, u32[]{:S(2)}, u32[]{:S(2)}) collective-permute-start(f32[136,256]{1,0:T(8,128)S(1)} %get-tuple-element.17), channel_id=1, source_target_pairs={{0,1},{1,0},{2,3},{3,2},{4,5},{5,4},{6,7},{7,6},{8,9},{9,8},{10,11... | collective-permute-start | bytes 417800 | tf_op jit(solution)/shard_map/ppermute | solution.py:24
  20.0 1.6 %collective-permute-start.1 = (f32[136,256]{1,0:T(8,128)S(1)}, f32[136,256]{1,0:T(8,128)S(1)}, u32[]{:S(2)}, u32[]{:S(2)}) collective-permute-start(f32[136,256]{1,0:T(8,128)S(1)} %get-tuple-element.18), channel_id=1, source_target_pairs={{0,2},{1,3},{2,0},{3,1},{4,6},{5,7},{6,4},{7,5},{8,10},{9,11},{10,... | collective-permute-start | bytes 417800 | tf_op jit(solution)/shard_map/ppermute | solution.py:24
  21.5 0.4 collective-permute-start.2
  22.0 0.0 collective-permute-done.5.refs_0_
  22.0 4.7 %wave1.1 = (f32[136,256]{1,0:T(8,128)S(1)}, f32[136,256]{1,0:T(8,128)S(1)}, f32[136,256]{1,0:T(8,128)S(1)}, f32[136,256]{1,0:T(8,128)S(1)}) custom-call(s32[2]{0:T(128)S(1)} %copy-done.5, s32[2]{0:T(128)S(1)} %copy-done.6, f32[4096,128]{1,0:T(8,128)S(1)} %bitcast.17, f32[1024,128]{1,0:T(8,128)S(1)} %bitcast.19, bf16[2,256,256]{2,1,0:T(8,128)(2,1)S(1)} %copy-done.4, ...), custom_call_target="tpu_custom_call" | custom-call | flops 1610612736 | bytes 1114112 | tf_op jit(solution)/shard_map/wave1/pallas_call | solution.py:67
  26.6 1.6 %collective-permute-start.6 = (f32[136,256]{1,0:T(8,128)S(1)}, f32[136,256]{1,0:T(8,128)S(1)}, u32[]{:S(2)}, u32[]{:S(2)}) collective-permute-start(f32[136,256]{1,0:T(8,128)S(1)} %get-tuple-element.21), channel_id=1, source_target_pairs={{0,1},{1,0},{2,3},{3,2},{4,5},{5,4},{6,7},{7,6},{8,9},{9,8},{10,11... | collective-permute-start | bytes 417800 | tf_op jit(solution)/shard_map/ppermute | solution.py:24
  28.2 1.6 %collective-permute-start.7 = (f32[136,256]{1,0:T(8,128)S(1)}, f32[136,256]{1,0:T(8,128)S(1)}, u32[]{:S(2)}, u32[]{:S(2)}) collective-permute-start(f32[136,256]{1,0:T(8,128)S(1)} %get-tuple-element.22), channel_id=1, source_target_pairs={{0,2},{1,3},{2,0},{3,1},{4,6},{5,7},{6,4},{7,5},{8,10},{9,11},{10,... | collective-permute-start | bytes 417800 | tf_op jit(solution)/shard_map/ppermute | solution.py:24
  29.8 0.0 collective-permute-done.refs_1_
  29.8 0.4 collective-permute-start.8
  30.2 0.0 collective-permute-done.1.refs_2_
  30.2 0.0 collective-permute-done.2.refs_3_
  30.2 0.2 sum0.1.acc
  30.4 2.1 %collective-permute-done.6.refs_1_ = f32[136,256]{1,0:T(8,128)S(1)} collective-permute-done((f32[136,256]{1,0:T(8,128)S(1)}, f32[136,256]{1,0:T(8,128)S(1)}, u32[]{:S(2)}, u32[]{:S(2)}) %collective-permute-start.6) | collective-permute-done | bytes 139296 | tf_op jit(solution)/shard_map/ppermute | solution.py:24
  32.6 2.2 %collective-permute-done.7.refs_2_ = f32[136,256]{1,0:T(8,128)S(1)} collective-permute-done((f32[136,256]{1,0:T(8,128)S(1)}, f32[136,256]{1,0:T(8,128)S(1)}, u32[]{:S(2)}, u32[]{:S(2)}) %collective-permute-start.7) | collective-permute-done | bytes 139296 | tf_op jit(solution)/shard_map/ppermute | solution.py:24
  34.7 2.0 %collective-permute-done.8.refs_3_ = f32[136,256]{1,0:T(8,128)S(1)} collective-permute-done((f32[136,256]{1,0:T(8,128)S(1)}, f32[136,256]{1,0:T(8,128)S(1)}, u32[]{:S(2)}, u32[]{:S(2)}) %collective-permute-start.8) | collective-permute-done | bytes 139296 | tf_op jit(solution)/shard_map/ppermute | solution.py:24
  36.7 0.4 sum1.1
  37.2 1.3 %collective-permute-start.9 = (f32[512,128]{1,0:T(8,128)S(1)}, f32[512,128]{1,0:T(8,128)S(1)}, u32[]{:S(2)}, u32[]{:S(2)}) collective-permute-start(f32[512,128]{1,0:T(8,128)S(1)} %get-tuple-element.26), channel_id=1, source_target_pairs={{0,8},{8,16},{16,24},{1,9},{9,17},{17,25},{2,10},{10,18},{18,26},{... | collective-permute-start | bytes 786440 | tf_op jit(solution)/shard_map/ppermute | solution.py:20
  38.5 1.1 %collective-permute-done.9 = f32[512,128]{1,0:T(8,128)S(1)} collective-permute-done((f32[512,128]{1,0:T(8,128)S(1)}, f32[512,128]{1,0:T(8,128)S(1)}, u32[]{:S(2)}, u32[]{:S(2)}) %collective-permute-start.9) | collective-permute-done | bytes 262176 | tf_op jit(solution)/shard_map/ppermute | solution.py:20
  39.7 2.7 %collective-permute-start.10 = (f32[512,128]{1,0:T(8,128)S(1)}, f32[512,128]{1,0:T(8,128)S(1)}, u32[]{:S(2)}, u32[]{:S(2)}) collective-permute-start(f32[512,128]{1,0:T(8,128)S(1)} %broadcast_select_fusion), channel_id=1, source_target_pairs={{0,4},{1,5},{2,6},{3,7},{4,0},{5,1},{6,2},{7,3},{8,12},{9,13},{10,... | collective-permute-start | bytes 786440 | tf_op jit(solution)/shard_map/ppermute | solution.py:24
  42.3 11.8 %collective-permute-done.10 = f32[512,128]{1,0:T(8,128)S(1)} collective-permute-done((f32[512,128]{1,0:T(8,128)S(1)}, f32[512,128]{1,0:T(8,128)S(1)}, u32[]{:S(2)}, u32[]{:S(2)}) %collective-permute-start.10) | collective-permute-done | bytes 262176 | tf_op jit(solution)/shard_map/ppermute | solution.py:24
  54.2 0.8 %select_add_fusion = f32[512,128]{1,0:T(8,128)} fusion(f32[512,128]{1,0:T(8,128)S(1)} %collective-permute-done.10, f32[512,128]{1,0:T(8,128)S(1)} %get-tuple-element.24, pred[]{:T(512)S(6)} %ge.3, f32[512,128]{1,0:T(8,128)S(1)} %get-tuple-element.25, f32[512,128]{1,0:T(8,128)S(1)} %collective-permute-done.9), kind=kLoop, calls=%fused_computation | loop fusion | flops 196608 | bytes 1310721 | tf_op jit(solution)/shard_map/add | solution.py:294
  (13 shorter events, 0.1 us)
Async XLA Ops:
  0.0 11.7 %copy-start.5 = (s32[2]{0:T(128)S(1)}, s32[2]{0:T(128)}, u32[]{:S(2)}) copy-start(s32[2]{0:T(128)} %rows.3) | copy-start | bytes 28
  0.0 11.8 %copy-start.6 = (s32[2]{0:T(128)S(1)}, s32[2]{0:T(128)}, u32[]{:S(2)}) copy-start(s32[2]{0:T(128)} %cols.3) | copy-start | bytes 28
  0.0 7.1 %collective-permute-start.3 = (s32[2]{0:T(128)}, s32[2]{0:T(128)S(1)}, u32[]{:S(2)}, u32[]{:S(2)}) collective-permute-start(s32[2]{0:T(128)} %rows.3), channel_id=1, source_target_pairs={{0,8},{8,16},{16,24},{1,9},{9,17},{17,25},{2,10},{10,18},{18,26},{... | collective-permute-start | bytes 32 | tf_op jit(solution)/shard_map/ppermute | solution.py:20
  2.5 5.5 %collective-permute-start.4 = (s32[2]{0:T(128)}, s32[2]{0:T(128)S(1)}, u32[]{:S(2)}, u32[]{:S(2)}) collective-permute-start(s32[2]{0:T(128)} %cols.3), channel_id=1, source_target_pairs={{0,8},{8,16},{16,24},{1,9},{9,17},{17,25},{2,10},{10,18},{18,26},{... | collective-permute-start | bytes 32 | tf_op jit(solution)/shard_map/ppermute | solution.py:20
  8.0 1.6 %copy-start = (f32[512,2,512]{2,1,0:T(2,128)S(1)}, f32[512,2,512]{2,1,0:T(2,128)}, u32[]{:S(2)}) copy-start(f32[512,2,512]{2,1,0:T(2,128)} %param.6) | copy-start | bytes 6291460
  9.6 2.2 %copy-start.1 = (f32[512,2,512]{2,1,0:T(2,128)S(1)}, f32[512,2,512]{2,1,0:T(2,128)}, u32[]{:S(2)}) copy-start(f32[512,2,512]{2,1,0:T(2,128)} %param.6) | copy-start | bytes 6291460
  9.6 2.2 %copy-start.2 = (f32[256,2,256]{2,1,0:T(2,128)S(1)}, f32[256,2,256]{2,1,0:T(2,128)}, u32[]{:S(2)}) copy-start(f32[256,2,256]{2,1,0:T(2,128)} %param.7) | copy-start | bytes 1572868
  10.3 11.7 %collective-permute-start.5 = (f32[2,256,256]{2,1,0:T(8,128)S(1)}, f32[2,256,256]{2,1,0:T(8,128)S(1)}, u32[]{:S(2)}, u32[]{:S(2)}) collective-permute-start(f32[2,256,256]{2,1,0:T(8,128)S(1)} %rim.1), channel_id=1, source_target_pairs={{8,0},{16,8},{24,16},{9,1},{17,9},{25,17},{10,2},{18,10},{26,18},{... | collective-permute-start | bytes 1572872 | tf_op jit(solution)/shard_map/ppermute | solution.py:20
  11.8 1.0 %copy-start.3 = (bf16[2,256,256]{2,1,0:T(8,128)(2,1)S(1)}, bf16[2,256,256]{2,1,0:T(8,128)(2,1)}, u32[]{:S(2)}) copy-start(bf16[2,256,256]{2,1,0:T(8,128)(2,1)} %amps.3) | copy-start | bytes 786436
  12.7 1.0 %copy-start.7 = (bf16[1024,256]{1,0:T(8,128)(2,1)S(1)}, bf16[1024,256]{1,0:T(8,128)(2,1)}, u32[]{:S(2)}) copy-start(bf16[1024,256]{1,0:T(8,128)(2,1)} %constant.8.clone.table) | copy-start | bytes 1572868
  13.8 8.2 %copy-start.4 = (bf16[2,256,256]{2,1,0:T(8,128)(2,1)S(1)}, bf16[2,256,256]{2,1,0:T(8,128)(2,1)}, u32[]{:S(2)}) copy-start(bf16[2,256,256]{2,1,0:T(8,128)(2,1)} %amps.3) | copy-start | bytes 786436
  18.4 11.4 %collective-permute-start = (f32[136,256]{1,0:T(8,128)S(1)}, f32[136,256]{1,0:T(8,128)S(1)}, u32[]{:S(2)}, u32[]{:S(2)}) collective-permute-start(f32[136,256]{1,0:T(8,128)S(1)} %get-tuple-element.17), channel_id=1, source_target_pairs={{0,1},{1,0},{2,3},{3,2},{4,5},{5,4},{6,7},{7,6},{8,9},{9,8},{10,11... | collective-permute-start | bytes 417800 | tf_op jit(solution)/shard_map/ppermute | solution.py:24
  20.0 10.2 %collective-permute-start.1 = (f32[136,256]{1,0:T(8,128)S(1)}, f32[136,256]{1,0:T(8,128)S(1)}, u32[]{:S(2)}, u32[]{:S(2)}) collective-permute-start(f32[136,256]{1,0:T(8,128)S(1)} %get-tuple-element.18), channel_id=1, source_target_pairs={{0,2},{1,3},{2,0},{3,1},{4,6},{5,7},{6,4},{7,5},{8,10},{9,11},{10,... | collective-permute-start | bytes 417800 | tf_op jit(solution)/shard_map/ppermute | solution.py:24
  21.5 8.7 %collective-permute-start.2 = (f32[136,256]{1,0:T(8,128)S(1)}, f32[136,256]{1,0:T(8,128)S(1)}, u32[]{:S(2)}, u32[]{:S(2)}) collective-permute-start(f32[136,256]{1,0:T(8,128)S(1)} %get-tuple-element.19), channel_id=1, source_target_pairs={{0,3},{1,2},{2,1},{3,0},{4,7},{5,6},{6,5},{7,4},{8,11},{9,10},{10,... | collective-permute-start | bytes 417800 | tf_op jit(solution)/shard_map/ppermute | solution.py:24
  26.6 5.9 %collective-permute-start.6 = (f32[136,256]{1,0:T(8,128)S(1)}, f32[136,256]{1,0:T(8,128)S(1)}, u32[]{:S(2)}, u32[]{:S(2)}) collective-permute-start(f32[136,256]{1,0:T(8,128)S(1)} %get-tuple-element.21), channel_id=1, source_target_pairs={{0,1},{1,0},{2,3},{3,2},{4,5},{5,4},{6,7},{7,6},{8,9},{9,8},{10,11... | collective-permute-start | bytes 417800 | tf_op jit(solution)/shard_map/ppermute | solution.py:24
  28.2 6.5 %collective-permute-start.7 = (f32[136,256]{1,0:T(8,128)S(1)}, f32[136,256]{1,0:T(8,128)S(1)}, u32[]{:S(2)}, u32[]{:S(2)}) collective-permute-start(f32[136,256]{1,0:T(8,128)S(1)} %get-tuple-element.22), channel_id=1, source_target_pairs={{0,2},{1,3},{2,0},{3,1},{4,6},{5,7},{6,4},{7,5},{8,10},{9,11},{10,... | collective-permute-start | bytes 417800 | tf_op jit(solution)/shard_map/ppermute | solution.py:24
  29.8 6.9 %collective-permute-start.8 = (f32[136,256]{1,0:T(8,128)S(1)}, f32[136,256]{1,0:T(8,128)S(1)}, u32[]{:S(2)}, u32[]{:S(2)}) collective-permute-start(f32[136,256]{1,0:T(8,128)S(1)} %get-tuple-element.23), channel_id=1, source_target_pairs={{0,3},{1,2},{2,1},{3,0},{4,7},{5,6},{6,5},{7,4},{8,11},{9,10},{10,... | collective-permute-start | bytes 417800 | tf_op jit(solution)/shard_map/ppermute | solution.py:24
  37.2 2.4 %collective-permute-start.9 = (f32[512,128]{1,0:T(8,128)S(1)}, f32[512,128]{1,0:T(8,128)S(1)}, u32[]{:S(2)}, u32[]{:S(2)}) collective-permute-start(f32[512,128]{1,0:T(8,128)S(1)} %get-tuple-element.26), channel_id=1, source_target_pairs={{0,8},{8,16},{16,24},{1,9},{9,17},{17,25},{2,10},{10,18},{18,26},{... | collective-permute-start | bytes 786440 | tf_op jit(solution)/shard_map/ppermute | solution.py:20
  39.7 14.5 %collective-permute-start.10 = (f32[512,128]{1,0:T(8,128)S(1)}, f32[512,128]{1,0:T(8,128)S(1)}, u32[]{:S(2)}, u32[]{:S(2)}) collective-permute-start(f32[512,128]{1,0:T(8,128)S(1)} %broadcast_select_fusion), channel_id=1, source_target_pairs={{0,4},{1,5},{2,6},{3,7},{4,0},{5,1},{6,2},{7,3},{8,12},{9,13},{10,... | collective-permute-start | bytes 786440 | tf_op jit(solution)/shard_map/ppermute | solution.py:24

commit v3 on v2

--- a/solution.py
+++ b/solution.py
@@ -82,9 +82,29 @@
     return rows[index] - band_start, cols[index], index
 
 
-def rim_kernel(window, rows, cols, obj, out):
-    band_start = (lax.axis_index("tile") - 1) * (2 * window)
-    _, offset, _ = chosen(1, rows, cols, band_start, window)
+def load_kernel(number, *refs):
+    sources, targets, sem = refs[:number], refs[number : 2 * number], refs[2 * number]
+    copies = [pltpu.make_async_copy(a, b, sem.at[i]) for i, (a, b) in enumerate(zip(sources, targets))]
+    for copy in copies:
+        copy.start()
+    for copy in copies:
+        copy.wait()
+
+
+def loaded(arrays):
+    return pl.pallas_call(
+        functools.partial(load_kernel, len(arrays)),
+        out_shape=[pltpu.VMEM(array.shape, array.dtype) for array in arrays],
+        in_specs=[pl.BlockSpec(memory_space=pl.ANY)] * len(arrays),
+        out_specs=[pl.BlockSpec(memory_space=pltpu.VMEM)] * len(arrays),
+        scratch_shapes=[pltpu.SemaphoreType.DMA((len(arrays),))],
+        compiler_params=pltpu.CompilerParams(vmem_limit_bytes=16 << 20),
+        name="load",
+    )(*[pltpu.with_memory_space_constraint(array, pltpu.HBM) for array in arrays])
+
+
+def rim_kernel(window, wanted, obj, out):
+    offset = wanted[0]
     tiles = window // LANES
     for tile in range(tiles):
         column = lax.broadcasted_iota(jnp.int32, (window, LANES), 1) + tile * LANES
@@ -264,23 +284,23 @@
     classes = ways // 2
     share = window // classes
     tiles = window // LANES
-    table = split_tables(window)
-    obj = linear(object_field)
-    ill = linear(illumination)
     scalars = (row_offset, col_offset)
 
-    wanted = [shifted(scalar, "tile", 1) for scalar in scalars]
-    (rim,) = kernel_call(functools.partial(rim_kernel, window), "rim", [(2, window, window)], wanted, [obj])
+    crossing = row_offset[:1] - lax.axis_index("tile") * band_rows > window
+    wanted = shifted(jnp.where(crossing, col_offset[:1], col_offset[1:]), "tile", 1)
+    obj, ill, amps, table = loaded([linear(object_field), linear(illumination), amplitudes, split_tables(window)])
+    (rim,) = kernel_call(functools.partial(rim_kernel, window), "rim", [(2, window, window)], [wanted], [obj])
     rim = shifted(rim, "tile", -1)
 
     def spread(pieces):
-        return [pieces[0]] + [exchanged(pieces[d], "pos", d) for d in range(1, classes)]
-
-    near = spread(wave(0, window, classes, scalars, [obj, ill, amplitudes, table]))
+        moved = {d: exchanged(pieces[d], "pos", d) for d in reversed(range(1, classes))}
+        return [pieces[0]] + [moved[d] for d in range(1, classes)]
+
+    near = spread(wave(0, window, classes, scalars, [obj, ill, amps, table]))
     (acc,) = kernel_call(
         functools.partial(first_sum_kernel, window, classes), "sum0", [(2, 2, share, columns)], (), near
     )
-    late = spread(wave(1, window, classes, scalars, [obj, ill, amplitudes, table, rim]))
+    late = spread(wave(1, window, classes, scalars, [obj, ill, amps, table, rim]))
     top, middle, spilled = kernel_call(
         functools.partial(second_sum_kernel, window, classes),
         "sum1",

time: 55.8 us -> 54.9 us (0.984)
  starting transfers between devices: 19.5 us -> 17.2 us
  local copies, waits for them, and re-layouts: 3.6 us -> 1.35 us
  Pallas kernels: 10.7 us -> 12.6 us
  between operations: 0.14 us -> 1.96 us
    unnamed x16 -> x4, local copies, waits for them, and re-layouts: 3.6 us -> 0.01 us
    ppermute x4 -> x3, starting transfers between devices: 9.77 us -> 6.99 us  [shifted(): return lax.ppermute(block, axis, route)]
    pallas_call x0 -> x1, Pallas kernels: none -> 1.94 us  [loaded(): pl.pallas_call(functools.partial(load_kernel, len(arrays)), out_shape=[pl...]
    slice x0 -> x1, local copies, waits for them, and re-layouts: none -> 1.33 us  [on_device(): col_offset[1:]]
    ppermute x7, waiting for transfers between devices: 18.1 us -> 19.4 us  [exchanged(): lax.ppermute(block, axis, [(i, i ^ flip) for i in range(lax.axis_size(axi...]
    ppermute x4 -> x3, waiting for transfers between devices: 2.05 us -> 1.13 us  [shifted(): return lax.ppermute(block, axis, route)]
  transfers between devices with their start and end apart: 11 -> 10, of which waited for: 6 -> 5; matrix products, arithmetic and copies ran while one was open for 0% -> 0% of each run, Pallas kernels for 17% -> 21%
where the time goes in v3:
time: 54.9 us; the launch traced here: 54.4 us
  waiting for transfers between devices  20.5 us (37%)
  starting transfers between devices  17.2 us (31%)
  Pallas kernels  12.6 us (23%)
  between operations  1.96 us (4%)
  local copies, waits for them, and re-layouts  1.35 us (2%)
  other arithmetic  0.79 us (1%)
    ppermute x7, waiting for transfers between devices, exchanged(): lax.ppermute(block, axis, [(i, i ^ flip) for i in range(lax.axis_size(axi...  19.4 us
    pallas_call x5, Pallas kernels, kernel_call(): pl.pallas_call(body, out_shape=[pltpu.VMEM(shape, F32) for shape in out_s...  10.7 us
    ppermute x7, starting transfers between devices, exchanged(): lax.ppermute(block, axis, [(i, i ^ flip) for i in range(lax.axis_size(axi...  10.2 us
    ppermute x3, starting transfers between devices, shifted(): return lax.ppermute(block, axis, route)  6.99 us
    pallas_call x1, Pallas kernels, loaded(): pl.pallas_call(functools.partial(load_kernel, len(arrays)), out_shape=[pl...  1.94 us
    slice x1, local copies, waits for them, and re-layouts, on_device(): col_offset[1:]  1.33 us
    ppermute x3, waiting for transfers between devices, shifted(): return lax.ppermute(block, axis, route)  1.13 us
  transfers between devices with their start and end apart: 10, of which 5 were waited for; matrix products, arithmetic and copies ran while one was open for 0% of the time, Pallas kernels for 21%

profile of v3, /device:TPU:0, one launch (start us, length us, event | category | flops | bytes accessed | tf_op | source)
XLA Modules:
  0.0 54.4 jit_solution(777766295820645654)
XLA Ops:
  0.0 1.3 %fusion = (s32[1]{0:T(128)}, s32[1]{0:T(128)}) fusion(s32[2]{0:T(128)} %cols.3), kind=kLoop, calls=%fused_computation.2 | loop fusion | bytes 16 | tf_op jit(solution)/shard_map/slice | solution.py:290
  3.2 3.3 %collective-permute-start.3 = (s32[1]{0:T(128)}, s32[1]{0:T(128)}, u32[]{:S(2)}, u32[]{:S(2)}) collective-permute-start(s32[1]{0:T(128)} %select_n.19), channel_id=1, source_target_pairs={{0,8},{8,16},{16,24},{1,9},{9,17},{17,25},{2,10},{10,18},{18,26},{... | collective-permute-start | bytes 20 | tf_op jit(solution)/shard_map/ppermute | solution.py:20
  6.5 1.9 %load.1 = (f32[4096,128]{1,0:T(8,128)S(1)}, f32[1024,128]{1,0:T(8,128)S(1)}, bf16[2,256,256]{2,1,0:T(8,128)(2,1)S(1)}, bf16[1024,256]{1,0:T(8,128)(2,1)S(1)}) custom-call(f32[4096,128]{1,0:T(8,128)} %bitcast.18, f32[1024,128]{1,0:T(8,128)} %bitcast.19, bf16[2,256,256]{2,1,0:T(8,128)(2,1)} %refs_2_.1, bf16[1024,256]{1,0:T(8,128)(2,1)} %constant.16.clone.refs_3_), custom_call_target="tpu_custom_call" | custom-call | tf_op jit(solution)/shard_map/load/pallas_call | solution.py:95
  8.5 0.0 copy-start
  8.5 0.0 copy-start.1
  8.5 0.0 collective-permute-done.3.wanted
  8.5 0.8 %rim.1 = f32[2,256,256]{2,1,0:T(8,128)S(1)} custom-call(s32[1]{0:T(128)} %collective-permute-done.3.wanted, f32[4096,128]{1,0:T(8,128)S(1)} %get-tuple-element.20.obj), custom_call_target="tpu_custom_call" | custom-call | bytes 1048576 | tf_op jit(solution)/shard_map/rim/pallas_call | solution.py:67
  9.3 1.3 %collective-permute-start.4 = (f32[2,256,256]{2,1,0:T(8,128)S(1)}, f32[2,256,256]{2,1,0:T(8,128)S(1)}, u32[]{:S(2)}, u32[]{:S(2)}) collective-permute-start(f32[2,256,256]{2,1,0:T(8,128)S(1)} %rim.1), channel_id=1, source_target_pairs={{8,0},{16,8},{24,16},{9,1},{17,9},{25,17},{10,2},{18,10},{26,18},{... | collective-permute-start | bytes 1572872 | tf_op jit(solution)/shard_map/ppermute | solution.py:20
  10.6 0.0 copy-done
  10.6 0.0 copy-done.1
  10.6 4.6 %wave0.1 = (f32[136,256]{1,0:T(8,128)S(1)}, f32[136,256]{1,0:T(8,128)S(1)}, f32[136,256]{1,0:T(8,128)S(1)}, f32[136,256]{1,0:T(8,128)S(1)}) custom-call(s32[2]{0:T(128)S(1)} %copy-done.1, s32[2]{0:T(128)S(1)} %copy-done, f32[4096,128]{1,0:T(8,128)S(1)} %get-tuple-element.20.obj, f32[1024,128]{1,0:T(8,128)S(1)} %get-tuple-element.21.ill, ...), custom_call_target="tpu_custom_call" | custom-call | flops 1610612736 | bytes 1114112 | tf_op jit(solution)/shard_map/wave0/pallas_call | solution.py:67
  15.2 2.4 %collective-permute-start = (f32[136,256]{1,0:T(8,128)S(1)}, f32[136,256]{1,0:T(8,128)S(1)}, u32[]{:S(2)}, u32[]{:S(2)}) collective-permute-start(f32[136,256]{1,0:T(8,128)S(1)} %get-tuple-element.25), channel_id=1, source_target_pairs={{0,1},{1,0},{2,3},{3,2},{4,5},{5,4},{6,7},{7,6},{8,9},{9,8},{10,11... | collective-permute-start | bytes 417800 | tf_op jit(solution)/shard_map/ppermute | solution.py:24
  17.6 1.6 %collective-permute-start.1 = (f32[136,256]{1,0:T(8,128)S(1)}, f32[136,256]{1,0:T(8,128)S(1)}, u32[]{:S(2)}, u32[]{:S(2)}) collective-permute-start(f32[136,256]{1,0:T(8,128)S(1)} %get-tuple-element.26), channel_id=1, source_target_pairs={{0,2},{1,3},{2,0},{3,1},{4,6},{5,7},{6,4},{7,5},{8,10},{9,11},{10,... | collective-permute-start | bytes 417800 | tf_op jit(solution)/shard_map/ppermute | solution.py:24
  19.2 0.0 collective-permute-start.2
  19.2 0.0 collective-permute-done.4.refs_0_
  19.2 4.6 %wave1.1 = (f32[136,256]{1,0:T(8,128)S(1)}, f32[136,256]{1,0:T(8,128)S(1)}, f32[136,256]{1,0:T(8,128)S(1)}, f32[136,256]{1,0:T(8,128)S(1)}) custom-call(s32[2]{0:T(128)S(1)} %copy-done.1, s32[2]{0:T(128)S(1)} %copy-done, f32[4096,128]{1,0:T(8,128)S(1)} %get-tuple-element.20.obj, f32[1024,128]{1,0:T(8,128)S(1)} %get-tuple-element.21.ill, ...), custom_call_target="tpu_custom_call" | custom-call | flops 1610612736 | bytes 1114112 | tf_op jit(solution)/shard_map/wave1/pallas_call | solution.py:67
  23.8 2.0 %collective-permute-start.5 = (f32[136,256]{1,0:T(8,128)S(1)}, f32[136,256]{1,0:T(8,128)S(1)}, u32[]{:S(2)}, u32[]{:S(2)}) collective-permute-start(f32[136,256]{1,0:T(8,128)S(1)} %get-tuple-element.29), channel_id=1, source_target_pairs={{0,1},{1,0},{2,3},{3,2},{4,5},{5,4},{6,7},{7,6},{8,9},{9,8},{10,11... | collective-permute-start | bytes 417800 | tf_op jit(solution)/shard_map/ppermute | solution.py:24
  25.8 1.6 %collective-permute-start.6 = (f32[136,256]{1,0:T(8,128)S(1)}, f32[136,256]{1,0:T(8,128)S(1)}, u32[]{:S(2)}, u32[]{:S(2)}) collective-permute-start(f32[136,256]{1,0:T(8,128)S(1)} %get-tuple-element.30), channel_id=1, source_target_pairs={{0,2},{1,3},{2,0},{3,1},{4,6},{5,7},{6,4},{7,5},{8,10},{9,11},{10,... | collective-permute-start | bytes 417800 | tf_op jit(solution)/shard_map/ppermute | solution.py:24
  27.4 0.0 collective-permute-done.refs_1_
  27.4 0.0 collective-permute-start.7
  27.4 0.0 collective-permute-done.1.refs_2_
  27.4 0.0 collective-permute-done.2.refs_3_
  27.4 0.2 sum0.1.acc
  27.6 1.3 %collective-permute-done.5.refs_1_ = f32[136,256]{1,0:T(8,128)S(1)} collective-permute-done((f32[136,256]{1,0:T(8,128)S(1)}, f32[136,256]{1,0:T(8,128)S(1)}, u32[]{:S(2)}, u32[]{:S(2)}) %collective-permute-start.5) | collective-permute-done | bytes 139296 | tf_op jit(solution)/shard_map/ppermute | solution.py:24
  28.9 2.1 %collective-permute-done.6.refs_2_ = f32[136,256]{1,0:T(8,128)S(1)} collective-permute-done((f32[136,256]{1,0:T(8,128)S(1)}, f32[136,256]{1,0:T(8,128)S(1)}, u32[]{:S(2)}, u32[]{:S(2)}) %collective-permute-start.6) | collective-permute-done | bytes 139296 | tf_op jit(solution)/shard_map/ppermute | solution.py:24
  31.0 3.8 %collective-permute-done.7.refs_3_ = f32[136,256]{1,0:T(8,128)S(1)} collective-permute-done((f32[136,256]{1,0:T(8,128)S(1)}, f32[136,256]{1,0:T(8,128)S(1)}, u32[]{:S(2)}, u32[]{:S(2)}) %collective-permute-start.7) | collective-permute-done | bytes 139296 | tf_op jit(solution)/shard_map/ppermute | solution.py:24
  34.8 0.5 sum1.1
  35.3 2.4 %collective-permute-start.8 = (f32[512,128]{1,0:T(8,128)S(1)}, f32[512,128]{1,0:T(8,128)S(1)}, u32[]{:S(2)}, u32[]{:S(2)}) collective-permute-start(f32[512,128]{1,0:T(8,128)S(1)} %get-tuple-element.34), channel_id=1, source_target_pairs={{0,8},{8,16},{16,24},{1,9},{9,17},{17,25},{2,10},{10,18},{18,26},{... | collective-permute-start | bytes 786440 | tf_op jit(solution)/shard_map/ppermute | solution.py:20
  37.6 1.1 %collective-permute-done.8 = f32[512,128]{1,0:T(8,128)S(1)} collective-permute-done((f32[512,128]{1,0:T(8,128)S(1)}, f32[512,128]{1,0:T(8,128)S(1)}, u32[]{:S(2)}, u32[]{:S(2)}) %collective-permute-start.8) | collective-permute-done | bytes 262176 | tf_op jit(solution)/shard_map/ppermute | solution.py:20
  38.8 2.7 %collective-permute-start.9 = (f32[512,128]{1,0:T(8,128)S(1)}, f32[512,128]{1,0:T(8,128)S(1)}, u32[]{:S(2)}, u32[]{:S(2)}) collective-permute-start(f32[512,128]{1,0:T(8,128)S(1)} %broadcast_select_fusion), channel_id=1, source_target_pairs={{0,4},{1,5},{2,6},{3,7},{4,0},{5,1},{6,2},{7,3},{8,12},{9,13},{10,... | collective-permute-start | bytes 786440 | tf_op jit(solution)/shard_map/ppermute | solution.py:24
  41.5 12.1 %collective-permute-done.9 = f32[512,128]{1,0:T(8,128)S(1)} collective-permute-done((f32[512,128]{1,0:T(8,128)S(1)}, f32[512,128]{1,0:T(8,128)S(1)}, u32[]{:S(2)}, u32[]{:S(2)}) %collective-permute-start.9) | collective-permute-done | bytes 262176 | tf_op jit(solution)/shard_map/ppermute | solution.py:24
  53.6 0.8 %select_add_fusion = f32[512,128]{1,0:T(8,128)} fusion(f32[512,128]{1,0:T(8,128)S(1)} %collective-permute-done.9, f32[512,128]{1,0:T(8,128)S(1)} %get-tuple-element.32, pred[]{:T(512)S(6)} %ge.3, f32[512,128]{1,0:T(8,128)S(1)} %get-tuple-element.33, f32[512,128]{1,0:T(8,128)S(1)} %collective-permute-done.8), kind=kLoop, calls=%fused_computation | loop fusion | flops 196608 | bytes 1310721 | tf_op jit(solution)/shard_map/add | solution.py:314
  (1 shorter events, 0.0 us)
Async XLA Ops:
  3.2 5.3 %collective-permute-start.3 = (s32[1]{0:T(128)}, s32[1]{0:T(128)}, u32[]{:S(2)}, u32[]{:S(2)}) collective-permute-start(s32[1]{0:T(128)} %select_n.19), channel_id=1, source_target_pairs={{0,8},{8,16},{16,24},{1,9},{9,17},{17,25},{2,10},{10,18},{18,26},{... | collective-permute-start | bytes 20 | tf_op jit(solution)/shard_map/ppermute | solution.py:20
  8.5 2.1 %copy-start = (s32[2]{0:T(128)S(1)}, s32[2]{0:T(128)}, u32[]{:S(2)}) copy-start(s32[2]{0:T(128)} %cols.3) | copy-start | bytes 28
  8.5 2.1 %copy-start.1 = (s32[2]{0:T(128)S(1)}, s32[2]{0:T(128)}, u32[]{:S(2)}) copy-start(s32[2]{0:T(128)} %rows.3) | copy-start | bytes 28
  9.3 9.9 %collective-permute-start.4 = (f32[2,256,256]{2,1,0:T(8,128)S(1)}, f32[2,256,256]{2,1,0:T(8,128)S(1)}, u32[]{:S(2)}, u32[]{:S(2)}) collective-permute-start(f32[2,256,256]{2,1,0:T(8,128)S(1)} %rim.1), channel_id=1, source_target_pairs={{8,0},{16,8},{24,16},{9,1},{17,9},{25,17},{10,2},{18,10},{26,18},{... | collective-permute-start | bytes 1572872 | tf_op jit(solution)/shard_map/ppermute | solution.py:20
  15.2 12.2 %collective-permute-start = (f32[136,256]{1,0:T(8,128)S(1)}, f32[136,256]{1,0:T(8,128)S(1)}, u32[]{:S(2)}, u32[]{:S(2)}) collective-permute-start(f32[136,256]{1,0:T(8,128)S(1)} %get-tuple-element.25), channel_id=1, source_target_pairs={{0,1},{1,0},{2,3},{3,2},{4,5},{5,4},{6,7},{7,6},{8,9},{9,8},{10,11... | collective-permute-start | bytes 417800 | tf_op jit(solution)/shard_map/ppermute | solution.py:24
  17.6 9.8 %collective-permute-start.1 = (f32[136,256]{1,0:T(8,128)S(1)}, f32[136,256]{1,0:T(8,128)S(1)}, u32[]{:S(2)}, u32[]{:S(2)}) collective-permute-start(f32[136,256]{1,0:T(8,128)S(1)} %get-tuple-element.26), channel_id=1, source_target_pairs={{0,2},{1,3},{2,0},{3,1},{4,6},{5,7},{6,4},{7,5},{8,10},{9,11},{10,... | collective-permute-start | bytes 417800 | tf_op jit(solution)/shard_map/ppermute | solution.py:24
  19.2 8.2 %collective-permute-start.2 = (f32[136,256]{1,0:T(8,128)S(1)}, f32[136,256]{1,0:T(8,128)S(1)}, u32[]{:S(2)}, u32[]{:S(2)}) collective-permute-start(f32[136,256]{1,0:T(8,128)S(1)} %get-tuple-element.27), channel_id=1, source_target_pairs={{0,3},{1,2},{2,1},{3,0},{4,7},{5,6},{6,5},{7,4},{8,11},{9,10},{10,... | collective-permute-start | bytes 417800 | tf_op jit(solution)/shard_map/ppermute | solution.py:24
  23.8 5.1 %collective-permute-start.5 = (f32[136,256]{1,0:T(8,128)S(1)}, f32[136,256]{1,0:T(8,128)S(1)}, u32[]{:S(2)}, u32[]{:S(2)}) collective-permute-start(f32[136,256]{1,0:T(8,128)S(1)} %get-tuple-element.29), channel_id=1, source_target_pairs={{0,1},{1,0},{2,3},{3,2},{4,5},{5,4},{6,7},{7,6},{8,9},{9,8},{10,11... | collective-permute-start | bytes 417800 | tf_op jit(solution)/shard_map/ppermute | solution.py:24
  25.8 5.2 %collective-permute-start.6 = (f32[136,256]{1,0:T(8,128)S(1)}, f32[136,256]{1,0:T(8,128)S(1)}, u32[]{:S(2)}, u32[]{:S(2)}) collective-permute-start(f32[136,256]{1,0:T(8,128)S(1)} %get-tuple-element.30), channel_id=1, source_target_pairs={{0,2},{1,3},{2,0},{3,1},{4,6},{5,7},{6,4},{7,5},{8,10},{9,11},{10,... | collective-permute-start | bytes 417800 | tf_op jit(solution)/shard_map/ppermute | solution.py:24
  27.4 7.4 %collective-permute-start.7 = (f32[136,256]{1,0:T(8,128)S(1)}, f32[136,256]{1,0:T(8,128)S(1)}, u32[]{:S(2)}, u32[]{:S(2)}) collective-permute-start(f32[136,256]{1,0:T(8,128)S(1)} %get-tuple-element.31), channel_id=1, source_target_pairs={{0,3},{1,2},{2,1},{3,0},{4,7},{5,6},{6,5},{7,4},{8,11},{9,10},{10,... | collective-permute-start | bytes 417800 | tf_op jit(solution)/shard_map/ppermute | solution.py:24
  35.3 3.5 %collective-permute-start.8 = (f32[512,128]{1,0:T(8,128)S(1)}, f32[512,128]{1,0:T(8,128)S(1)}, u32[]{:S(2)}, u32[]{:S(2)}) collective-permute-start(f32[512,128]{1,0:T(8,128)S(1)} %get-tuple-element.34), channel_id=1, source_target_pairs={{0,8},{8,16},{16,24},{1,9},{9,17},{17,25},{2,10},{10,18},{18,26},{... | collective-permute-start | bytes 786440 | tf_op jit(solution)/shard_map/ppermute | solution.py:20
  38.8 14.8 %collective-permute-start.9 = (f32[512,128]{1,0:T(8,128)S(1)}, f32[512,128]{1,0:T(8,128)S(1)}, u32[]{:S(2)}, u32[]{:S(2)}) collective-permute-start(f32[512,128]{1,0:T(8,128)S(1)} %broadcast_select_fusion), channel_id=1, source_target_pairs={{0,4},{1,5},{2,6},{3,7},{4,0},{5,1},{6,2},{7,3},{8,12},{9,13},{10,... | collective-permute-start | bytes 786440 | tf_op jit(solution)/shard_map/ppermute | solution.py:24

commit v4 on v3

--- a/solution.py
+++ b/solution.py
@@ -8,6 +8,7 @@
 from jax.experimental import pallas as pl
 from jax.experimental.pallas import tpu as pltpu
 from jax.sharding import PartitionSpec as P
+
 
 LANES = 128
 F32 = jnp.float32
@@ -60,19 +61,19 @@
     return pltpu.with_memory_space_constraint(array, pltpu.VMEM)
 
 
-def kernel_call(body, name, out_shapes, scalars, arrays, scratch=(), flops=0):
+def kernel_call(body, out_shapes, scalars, arrays, scratch=(), flops=0):
     smem = pl.BlockSpec(memory_space=pltpu.SMEM)
     vmem = pl.BlockSpec(memory_space=pltpu.VMEM)
-    moved = sum(4 * math.prod(shape) for shape in out_shapes)
+    out_shapes = [shape if isinstance(shape, pl.MemoryRef) else pltpu.VMEM(shape, F32) for shape in out_shapes]
+    moved = sum(4 * math.prod(shape.shape) for shape in out_shapes)
     return pl.pallas_call(
         body,
-        out_shape=[pltpu.VMEM(shape, F32) for shape in out_shapes],
+        out_shape=out_shapes,
         in_specs=[smem] * len(scalars) + [vmem] * len(arrays),
         out_specs=[vmem] * len(out_shapes),
         scratch_shapes=scratch,
         cost_estimate=pl.CostEstimate(flops=flops, transcendentals=0, bytes_accessed=2 * moved),
         compiler_params=pltpu.CompilerParams(vmem_limit_bytes=16 << 20),
-        name=name,
     )(*scalars, *[in_vmem(array) for array in arrays])
 
 
@@ -103,11 +104,16 @@
     )(*[pltpu.with_memory_space_constraint(array, pltpu.HBM) for array in arrays])
 
 
+def pick_kernel(window, rows, cols, out):
+    _, column, _ = chosen(1, rows, cols, lax.axis_index("tile") * (2 * window), window)
+    out[...] = jnp.broadcast_to(column.astype(F32), out.shape)
+
+
 def rim_kernel(window, wanted, obj, out):
-    offset = wanted[0]
+    offset = wanted[pl.ds(0, 1), :]
     tiles = window // LANES
     for tile in range(tiles):
-        column = lax.broadcasted_iota(jnp.int32, (window, LANES), 1) + tile * LANES
+        column = (lax.broadcasted_iota(jnp.int32, (window, LANES), 1) + tile * LANES).astype(F32)
         for part in range(2):
             near = obj[pl.ds(tile * 2 + part, window, stride=4 * tiles), :]
             beyond = obj[pl.ds((tiles + tile) * 2 + part, window, stride=4 * tiles), :]
@@ -118,7 +124,10 @@
     if with_rim:
         rim, refs = refs[0], refs[1:]
     outs, refs = refs[:classes], refs[classes:]
-    doubled, probe, xh, xl, far = refs
+    if slot == 0:
+        doubled, far, probe, xh, xl = refs
+    else:
+        probe, xh, xl, doubled, far = refs
     tiles = window // LANES
     row, column, index = chosen(slot, rows, cols, lax.axis_index("tile") * (2 * window), window)
     own = lax.rem(lax.axis_index("pos"), classes)
@@ -177,61 +186,98 @@
     left_high = jnp.concatenate([table[pl.ds(0, window), :], table[pl.ds(window, window), :]], axis=1)
     left_low = jnp.concatenate([table[pl.ds(2 * window, window), :], table[pl.ds(3 * window, window), :]], axis=1)
 
-    def both_sides():
+    def right_side():
         mid = dot3(xh[...], xl[...], high, low)
         for first in range(0, window, size):
             store_pair(first, mid[first : first + size], mid[window + first : window + first + size])
-        far[...] = dot3(left_high, left_low, xh[...], xl[...])
-
-    both_sides()
+
+    right_side()
+    far[...] = dot3(left_high, left_low, xh[...], xl[...])
     for first in range(0, window, size):
         real = far[pl.ds(first, size), pl.ds(0, window)]
         imag = far[pl.ds(first, size), pl.ds(window, window)]
         inverse = jnp.minimum(lax.rsqrt(real * real + imag * imag), 4.0)
         scaled = amps[index, pl.ds(first, size), :].astype(F32) * inverse
         store_pair(first, real * (1.0 - scaled), imag * (scaled - 1.0))
-    both_sides()
-
-    share = window // classes
+    right_side()
+    if slot == 0:
+        finish(0, window, classes, row, column, table, probe, xh, xl, far, outs)
+    else:
+        finish(0, LANES, classes, row, column, table, probe, xh, xl, far, outs)
+
+
+def finish(start, width, classes, row, column, table, probe, xh, xl, far, outs):
+    window = probe.shape[1]
+    share = window // classes
+    own = lax.rem(lax.axis_index("pos"), classes)
+    left_high = jnp.concatenate([table[pl.ds(0, window), :], table[pl.ds(window, window), :]], axis=1)
+    left_low = jnp.concatenate([table[pl.ds(2 * window, window), :], table[pl.ds(3 * window, window), :]], axis=1)
+    across = pl.ds(start, width)
+
+    def columns_of(ref):
+        return jnp.concatenate([ref[:, across], ref[:, pl.ds(window + start, width)]], axis=1)
+
+    far[:, pl.ds(0, 2 * width)] = dot3(left_high, left_low, columns_of(xh), columns_of(xl))
     for flip in range(classes):
         base = pl.multiple_of((own ^ flip) * share, share)
         here = pl.ds(base, share)
-        real = far[here, pl.ds(0, window)]
-        imag = far[here, pl.ds(window, window)]
-        probe_real = probe[0, here, :]
-        probe_imag = probe[1, here, :]
+        real = far[here, pl.ds(0, width)]
+        imag = far[here, pl.ds(width, width)]
+        probe_real = probe[0, here, across]
+        probe_imag = probe[1, here, across]
         outs[flip][pl.ds(0, share), :] = probe_real * real - probe_imag * imag
         outs[flip][pl.ds(share, share), :] = -(probe_real * imag + probe_imag * real)
-        line = lax.broadcasted_iota(jnp.int32, (8, window), 0)
+        line = lax.broadcasted_iota(jnp.int32, (8, width), 0)
         outs[flip][pl.ds(2 * share, 8), :] = jnp.where(line == 0, row, column).astype(F32)
 
 
+def rest_kernel(start, window, classes, rows, cols, table, probe, xh, xl, *refs):
+    outs, far = refs[:classes], refs[classes]
+    row, column, _ = chosen(1, rows, cols, lax.axis_index("tile") * (2 * window), window)
+    finish(start, LANES, classes, row, column, table, probe, xh, xl, far, outs)
+
+
 def wave(slot, window, classes, scalars, arrays):
     share = window // classes
     tiles = window // LANES
-    scratch = [
-        pltpu.VMEM(((window + 32) * 2 * tiles + 8, LANES), F32),
+    width = window if slot == 0 else LANES
+    pieces = [pltpu.VMEM((2 * share + 8, width), F32)] * classes
+    state = [
         pltpu.VMEM((2, window, window), F32),
         pltpu.VMEM((2 * window, 2 * window), BF16),
         pltpu.VMEM((2 * window, 2 * window), BF16),
+    ]
+    scratch = [
+        pltpu.VMEM(((window + 32) * 2 * tiles + 8, LANES), F32),
         pltpu.VMEM((window, 2 * window), F32),
     ]
     return kernel_call(
-        functools.partial(wave_kernel, slot, window, classes, len(arrays) == 5),
-        "wave" + str(slot),
-        [(2 * share + 8, window)] * classes,
+        functools.partial(wave_kernel, slot, window, classes, slot == 1),
+        pieces + (state if slot == 1 else []),
         scalars,
         arrays,
-        scratch,
+        scratch + (state if slot == 0 else []),
         96 * window**3,
     )
 
 
-def placed(piece, own, share, window):
+def rest(tile, window, classes, scalars, arrays):
+    share = window // classes
+    return kernel_call(
+        functools.partial(rest_kernel, tile * LANES, window, classes),
+        [pltpu.VMEM((2 * share + 8, LANES), F32)] * classes,
+        scalars,
+        arrays,
+        [pltpu.VMEM((window, 2 * LANES), F32)],
+        12 * window**3,
+    )
+
+
+def placed(piece, start, width, own, share, window):
     row = piece[pl.ds(2 * share, 1), :]
     column = piece[pl.ds(2 * share + 1, 1), :]
-    place = (lax.broadcasted_iota(jnp.int32, (share, window), 0) + own * share).astype(F32)
-    across = lax.broadcasted_iota(jnp.int32, (share, window), 1).astype(F32)
+    place = (lax.broadcasted_iota(jnp.int32, (share, width), 0) + own * share).astype(F32)
+    across = (lax.broadcasted_iota(jnp.int32, (share, width), 1) + start).astype(F32)
     return across < column, place < row, place + float(window) < row
 
 
@@ -242,7 +288,7 @@
     for part in range(2):
         total = [[jnp.zeros((share, window), F32) for _ in range(2)] for _ in range(2)]
         for piece in pieces:
-            upper, below, _ = placed(piece, own, share, window)
+            upper, below, _ = placed(piece, 0, window, own, share, window)
             value = piece[pl.ds(part * share, share), :]
             for k, wanted in enumerate((~below, below)):
                 kept = jnp.where(wanted, value, 0.0)
@@ -253,16 +299,15 @@
                 acc[k, part, :, pl.ds(half * window, window)] = total[k][half]
 
 
-def second_sum_kernel(window, classes, acc, *refs):
+def second_sum_kernel(start, window, classes, acc, *refs):
     pieces, outs = refs[:classes], refs[classes:]
     share = window // classes
-    tiles = window // LANES
     own = lax.rem(lax.axis_index("pos"), classes)
     for part in range(2):
-        total = [[acc[k, part, :, pl.ds(h * window, window)] for h in range(2)] for k in range(2)]
-        total.append([jnp.zeros((share, window), F32) for _ in range(2)])
+        total = [[acc[k, part, :, pl.ds(h * window + start, LANES)] for h in range(2)] for k in range(2)]
+        total.append([jnp.zeros((share, LANES), F32) for _ in range(2)])
         for piece in pieces:
-            upper, below, lowest = placed(piece, own, share, window)
+            upper, below, lowest = placed(piece, start, LANES, own, share, window)
             value = piece[pl.ds(part * share, share), :]
             for k, wanted in enumerate((~below, below & ~lowest, lowest)):
                 kept = jnp.where(wanted, value, 0.0)
@@ -270,10 +315,17 @@
                 total[k][1] += jnp.where(upper, kept, 0.0)
         for k in range(3):
             for half in range(2):
-                for tile in range(tiles):
-                    outs[k][pl.ds((half * tiles + tile) * 2 + part, share, stride=4 * tiles), :] = total[k][half][
-                        :, tile * LANES : (tile + 1) * LANES
-                    ]
+                outs[k][pl.ds((half * 2 + part) * share, share), :] = total[k][half]
+
+
+def final_kernel(tiles, share, *refs):
+    kept, received, out = refs[:tiles], refs[tiles : 2 * tiles], refs[2 * tiles]
+    for tile in range(tiles):
+        for half in range(2):
+            for part in range(2):
+                here = pl.ds((half * 2 + part) * share, share)
+                line = (half * tiles + tile) * 2 + part
+                out[pl.ds(line, share, stride=4 * tiles), :] = kept[tile][here, :] + received[tile][here, :]
 
 
 def on_device(object_field, illumination, amplitudes, row_offset, col_offset):
@@ -286,10 +338,11 @@
     tiles = window // LANES
     scalars = (row_offset, col_offset)
 
-    crossing = row_offset[:1] - lax.axis_index("tile") * band_rows > window
-    wanted = shifted(jnp.where(crossing, col_offset[:1], col_offset[1:]), "tile", 1)
+    remote = tuple(pltpu.with_memory_space_constraint(scalar, pltpu.HBM) for scalar in scalars)
+    (wanted,) = kernel_call(functools.partial(pick_kernel, window), [(8, LANES)], remote, [])
+    wanted = shifted(wanted, "tile", 1)
     obj, ill, amps, table = loaded([linear(object_field), linear(illumination), amplitudes, split_tables(window)])
-    (rim,) = kernel_call(functools.partial(rim_kernel, window), "rim", [(2, window, window)], [wanted], [obj])
+    (rim,) = kernel_call(functools.partial(rim_kernel, window), [(2, window, window)], (), [wanted, obj])
     rim = shifted(rim, "tile", -1)
 
     def spread(pieces):
@@ -297,21 +350,34 @@
         return [pieces[0]] + [moved[d] for d in range(1, classes)]
 
     near = spread(wave(0, window, classes, scalars, [obj, ill, amps, table]))
-    (acc,) = kernel_call(
-        functools.partial(first_sum_kernel, window, classes), "sum0", [(2, 2, share, columns)], (), near
-    )
-    late = spread(wave(1, window, classes, scalars, [obj, ill, amps, table, rim]))
-    top, middle, spilled = kernel_call(
-        functools.partial(second_sum_kernel, window, classes),
-        "sum1",
-        [(share * 4 * tiles, LANES)] * 3,
-        (),
-        [acc, *late],
-    )
-    top = top + shifted(spilled, "tile", 1)
+    (acc,) = kernel_call(functools.partial(first_sum_kernel, window, classes), [(2, 2, share, columns)], (), near)
+    *pieces, probe, xh, xl = wave(1, window, classes, scalars, [obj, ill, amps, table, rim])
+    late = [spread(pieces)]
+    for lane_tile in range(1, tiles):
+        pieces = rest(lane_tile, window, classes, scalars, [table, probe, xh, xl])
+        late.append(spread(pieces))
     is_upper = lax.axis_index("pos") >= classes
-    received = exchanged(jnp.where(is_upper, top, middle), "pos", classes)
-    result = jnp.where(is_upper, middle, top) + received
+    kept, received = [], []
+    for lane_tile in range(tiles):
+        top, middle, spilled = kernel_call(
+            functools.partial(second_sum_kernel, lane_tile * LANES, window, classes),
+            [(4 * share, LANES)] * 3,
+            (),
+            [acc, *late[lane_tile]],
+        )
+        spilled = shifted(spilled, "tile", 1)
+        top = top + spilled
+        outgoing = jnp.where(is_upper, top, middle)
+        received.append(exchanged(outgoing, "pos", classes))
+        kept.append(jnp.where(is_upper, middle, top))
+    result = pl.pallas_call(
+        functools.partial(final_kernel, tiles, share),
+        out_shape=jax.ShapeDtypeStruct((share * 4 * tiles, LANES), F32),
+        in_specs=[pl.BlockSpec(memory_space=pltpu.VMEM)] * (2 * tiles),
+        out_specs=pl.BlockSpec(memory_space=pltpu.VMEM),
+        compiler_params=pltpu.CompilerParams(vmem_limit_bytes=16 << 20),
+        name="final",
+    )(*[in_vmem(array) for array in kept + received])
     return unlinear(result, share, columns)
 
 
@@ -324,6 +390,5 @@
         P(("tile", "pos")),
     )
     out_specs = P(("tile", "pos"), None, None)
-    return jax.shard_map(
-        on_device, mesh=mesh, in_specs=in_specs, out_specs=out_specs, check_vma=False
-    )
+
+    return jax.shard_map(on_device, mesh=mesh, in_specs=in_specs, out_specs=out_specs, check_vma=False)

time: 54.9 us -> 58.6 us (1.067)
  starting transfers between devices: 17.2 us -> 24.4 us
  between operations: 1.96 us -> 0.16 us
  Pallas kernels: 12.6 us -> 14 us
  local copies, waits for them, and re-layouts: 1.35 us -> 0.01 us
  other arithmetic: 0.79 us -> 0.06 us
  waiting for transfers between devices: 20.5 us -> 19.8 us
    ppermute x7 -> x11, starting transfers between devices: 10.2 us -> 14.7 us  [exchanged(): lax.ppermute(block, axis, [(i, i ^ flip) for i in range(lax.axis_size(axi...]
    ppermute x3 -> x4, starting transfers between devices: 6.99 us -> 9.71 us  [shifted(): return lax.ppermute(block, axis, route)]
    slice x1 -> x0, local copies, waits for them, and re-layouts: 1.33 us -> none  [on_device(): col_offset[1:]]
    pallas_call x5 -> x9, Pallas kernels: 10.7 us -> 12 us  [the longest x8 11.2 us: kernel_call(): pl.pallas_call(body, out_shape=out_shapes, in_specs=[smem] * len(scalars)...]
    ppermute x3 -> x4, waiting for transfers between devices: 1.13 us -> 0.01 us  [shifted(): return lax.ppermute(block, axis, route)]
    add x1 -> x0, other arithmetic: 0.75 us -> none  [on_device(): result = jnp.where(is_upper, middle, top) + received]
    ppermute x7 -> x11, waiting for transfers between devices: 19.4 us -> 19.8 us  [exchanged(): lax.ppermute(block, axis, [(i, i ^ flip) for i in range(lax.axis_size(axi...]
  transfers between devices with their start and end apart: 10 -> 15, of which waited for: 5 -> 8; matrix products, arithmetic and copies ran while one was open for 0% -> 0% of each run, Pallas kernels for 21% -> 21%
where the time goes in v4:
time: 58.6 us; the launch traced here: 58.4 us
  starting transfers between devices  24.4 us (42%)
  waiting for transfers between devices  19.8 us (34%)
  Pallas kernels  14 us (24%)
    ppermute x11, waiting for transfers between devices, exchanged(): lax.ppermute(block, axis, [(i, i ^ flip) for i in range(lax.axis_size(axi...  19.8 us
    ppermute x11, starting transfers between devices, exchanged(): lax.ppermute(block, axis, [(i, i ^ flip) for i in range(lax.axis_size(axi...  14.7 us
    pallas_call x8, Pallas kernels, kernel_call(): pl.pallas_call(body, out_shape=out_shapes, in_specs=[smem] * len(scalars)...  11.2 us
    ppermute x4, starting transfers between devices, shifted(): return lax.ppermute(block, axis, route)  9.71 us
    pallas_call x1, Pallas kernels, loaded(): pl.pallas_call(functools.partial(load_kernel, len(arrays)), out_shape=[pl...  1.95 us
  transfers between devices with their start and end apart: 15, of which 8 were waited for; matrix products, arithmetic and copies ran while one was open for 0% of the time, Pallas kernels for 21%

profile of v4, /device:TPU:0, one launch (start us, length us, event | category | flops | bytes accessed | tf_op | source)
XLA Modules:
  0.0 58.4 jit_solution(15817076664804976492)
XLA Ops:
  0.0 0.7 %shard_map.66 = f32[8,128]{1,0:T(8,128)S(1)} custom-call(s32[2]{0:T(128)} %rows.7, s32[2]{0:T(128)} %cols.7), custom_call_target="tpu_custom_call" | custom-call | bytes 8192 | tf_op jit(solution)/shard_map/pallas_call | solution.py:69
  0.7 2.4 %collective-permute-start.3 = (f32[8,128]{1,0:T(8,128)S(1)}, f32[8,128]{1,0:T(8,128)S(1)}, u32[]{:S(2)}, u32[]{:S(2)}) collective-permute-start(f32[8,128]{1,0:T(8,128)S(1)} %shard_map.66), channel_id=1, source_target_pairs={{0,8},{8,16},{16,24},{1,9},{9,17},{17,25},{2,10},{10,18},{18,26},{... | collective-permute-start | bytes 12296 | tf_op jit(solution)/shard_map/ppermute | solution.py:21
  3.1 1.9 %load.1 = (f32[4096,128]{1,0:T(8,128)S(1)}, f32[1024,128]{1,0:T(8,128)S(1)}, bf16[2,256,256]{2,1,0:T(8,128)(2,1)S(1)}, bf16[1024,256]{1,0:T(8,128)(2,1)S(1)}) custom-call(f32[4096,128]{1,0:T(8,128)} %bitcast.15, f32[1024,128]{1,0:T(8,128)} %bitcast.16, bf16[2,256,256]{2,1,0:T(8,128)(2,1)} %refs_2_.1, bf16[1024,256]{1,0:T(8,128)(2,1)} %constant.8.clone.refs_3_), custom_call_target="tpu_custom_call" | custom-call | tf_op jit(solution)/shard_map/load/pallas_call | solution.py:96
  5.1 0.2 shard_map.67
  5.3 1.3 %collective-permute-start.4 = (f32[2,256,256]{2,1,0:T(8,128)S(1)}, f32[2,256,256]{2,1,0:T(8,128)S(1)}, u32[]{:S(2)}, u32[]{:S(2)}) collective-permute-start(f32[2,256,256]{2,1,0:T(8,128)S(1)} %shard_map.67), channel_id=1, source_target_pairs={{8,0},{16,8},{24,16},{9,1},{17,9},{25,17},{10,2},{18,10},{26,18},{... | collective-permute-start | bytes 1572872 | tf_op jit(solution)/shard_map/ppermute | solution.py:21
  6.6 4.6 %shard_map.64 = (f32[136,256]{1,0:T(8,128)S(1)}, f32[136,256]{1,0:T(8,128)S(1)}, f32[136,256]{1,0:T(8,128)S(1)}, f32[136,256]{1,0:T(8,128)S(1)}) custom-call(s32[2]{0:T(128)S(1)} %copy-done, s32[2]{0:T(128)S(1)} %copy-done.1, f32[4096,128]{1,0:T(8,128)S(1)} %get-tuple-element.30.obj, f32[1024,128]{1,0:T(8,128)S(1)} %get-tuple-element.31.ill, ...), custom_call_target="tpu_custom_call" | custom-call | flops 1610612736 | bytes 1114112 | tf_op jit(solution)/shard_map/pallas_call | solution.py:69
  11.2 2.4 %collective-permute-start = (f32[136,256]{1,0:T(8,128)S(1)}, f32[136,256]{1,0:T(8,128)S(1)}, u32[]{:S(2)}, u32[]{:S(2)}) collective-permute-start(f32[136,256]{1,0:T(8,128)S(1)} %get-tuple-element.35), channel_id=1, source_target_pairs={{0,1},{1,0},{2,3},{3,2},{4,5},{5,4},{6,7},{7,6},{8,9},{9,8},{10,11... | collective-permute-start | bytes 417800 | tf_op jit(solution)/shard_map/ppermute | solution.py:25
  13.6 1.6 %collective-permute-start.1 = (f32[136,256]{1,0:T(8,128)S(1)}, f32[136,256]{1,0:T(8,128)S(1)}, u32[]{:S(2)}, u32[]{:S(2)}) collective-permute-start(f32[136,256]{1,0:T(8,128)S(1)} %get-tuple-element.36), channel_id=1, source_target_pairs={{0,2},{1,3},{2,0},{3,1},{4,6},{5,7},{6,4},{7,5},{8,10},{9,11},{10,... | collective-permute-start | bytes 417800 | tf_op jit(solution)/shard_map/ppermute | solution.py:25
  15.2 4.2 %shard_map.68 = (f32[136,128]{1,0:T(8,128)S(1)}, f32[136,128]{1,0:T(8,128)S(1)}, f32[136,128]{1,0:T(8,128)S(1)}, f32[136,128]{1,0:T(8,128)S(1)}, f32[2,256,256]{...) custom-call(s32[2]{0:T(128)S(1)} %copy-done, s32[2]{0:T(128)S(1)} %copy-done.1, ...), custom_call_target="tpu_custom_call" | custom-call | flops 1610612736 | bytes 5799936 | tf_op jit(solution)/shard_map/pallas_call | solution.py:69
  19.4 1.0 %shard_map.70 = (f32[136,128]{1,0:T(8,128)S(1)}, f32[136,128]{1,0:T(8,128)S(1)}, f32[136,128]{1,0:T(8,128)S(1)}, f32[136,128]{1,0:T(8,128)S(1)}) custom-call(s32[2]{0:T(128)S(1)} %copy-done, s32[2]{0:T(128)S(1)} %copy-done.1, bf16[1024,256]{1,0:T(8,128)(2,1)S(1)} %get-tuple-element.33.table, f32[2,256,256]{2,1,0:T(8,128)S(1)} %get-tuple-element.45.probe, ...), custom_call_target="tpu_custom_call" | custom-call | flops 201326592 | bytes 557056 | tf_op jit(solution)/shard_map/pallas_call | solution.py:69
  20.3 2.1 %collective-permute-start.10 = (f32[136,128]{1,0:T(8,128)S(1)}, f32[136,128]{1,0:T(8,128)S(1)}, u32[]{:S(2)}, u32[]{:S(2)}) collective-permute-start(f32[136,128]{1,0:T(8,128)S(1)} %get-tuple-element.50), channel_id=1, source_target_pairs={{0,2},{1,3},{2,0},{3,1},{4,6},{5,7},{6,4},{7,5},{8,10},{9,11},{10,... | collective-permute-start | bytes 208904 | tf_op jit(solution)/shard_map/ppermute | solution.py:25
  22.4 1.4 %collective-permute-start.11 = (f32[136,128]{1,0:T(8,128)S(1)}, f32[136,128]{1,0:T(8,128)S(1)}, u32[]{:S(2)}, u32[]{:S(2)}) collective-permute-start(f32[136,128]{1,0:T(8,128)S(1)} %get-tuple-element.51), channel_id=1, source_target_pairs={{0,3},{1,2},{2,1},{3,0},{4,7},{5,6},{6,5},{7,4},{8,11},{9,10},{10,... | collective-permute-start | bytes 208904 | tf_op jit(solution)/shard_map/ppermute | solution.py:25
  23.8 0.2 collective-permute-start.9
  23.9 0.2 shard_map.65.acc
  24.2 0.5 collective-permute-done.10.refs_2_
  24.7 3.4 %collective-permute-done.11.refs_3_ = f32[136,128]{1,0:T(8,128)S(1)} collective-permute-done((f32[136,128]{1,0:T(8,128)S(1)}, f32[136,128]{1,0:T(8,128)S(1)}, u32[]{:S(2)}, u32[]{:S(2)}) %collective-permute-start.11) | collective-permute-done | bytes 69664 | tf_op jit(solution)/shard_map/ppermute | solution.py:25
  28.1 0.4 collective-permute-done.9.refs_1_
  28.4 0.2 shard_map.71
  28.7 3.4 %collective-permute-start.12 = (f32[256,128]{1,0:T(8,128)S(1)}, f32[256,128]{1,0:T(8,128)S(1)}, u32[]{:S(2)}, u32[]{:S(2)}) collective-permute-start(f32[256,128]{1,0:T(8,128)S(1)} %get-tuple-element.54), channel_id=1, source_target_pairs={{0,8},{8,16},{16,24},{1,9},{9,17},{17,25},{2,10},{10,18},{18,26},{... | collective-permute-start | bytes 393224 | tf_op jit(solution)/shard_map/ppermute | solution.py:21
  32.0 0.9 %collective-permute-start.5 = (f32[136,128]{1,0:T(8,128)S(1)}, f32[136,128]{1,0:T(8,128)S(1)}, u32[]{:S(2)}, u32[]{:S(2)}) collective-permute-start(f32[136,128]{1,0:T(8,128)S(1)} %get-tuple-element.39), channel_id=1, source_target_pairs={{0,1},{1,0},{2,3},{3,2},{4,5},{5,4},{6,7},{7,6},{8,9},{9,8},{10,11... | collective-permute-start | bytes 208904 | tf_op jit(solution)/shard_map/ppermute | solution.py:25
  33.0 0.9 %collective-permute-start.6 = (f32[136,128]{1,0:T(8,128)S(1)}, f32[136,128]{1,0:T(8,128)S(1)}, u32[]{:S(2)}, u32[]{:S(2)}) collective-permute-start(f32[136,128]{1,0:T(8,128)S(1)} %get-tuple-element.40), channel_id=1, source_target_pairs={{0,2},{1,3},{2,0},{3,1},{4,6},{5,7},{6,4},{7,5},{8,10},{9,11},{10,... | collective-permute-start | bytes 208904 | tf_op jit(solution)/shard_map/ppermute | solution.py:25
  33.8 1.7 %collective-permute-start.7 = (f32[136,128]{1,0:T(8,128)S(1)}, f32[136,128]{1,0:T(8,128)S(1)}, u32[]{:S(2)}, u32[]{:S(2)}) collective-permute-start(f32[136,128]{1,0:T(8,128)S(1)} %get-tuple-element.41), channel_id=1, source_target_pairs={{0,3},{1,2},{2,1},{3,0},{4,7},{5,6},{6,5},{7,4},{8,11},{9,10},{10,... | collective-permute-start | bytes 208904 | tf_op jit(solution)/shard_map/ppermute | solution.py:25
  35.6 0.8 %collective-permute-done.5.refs_1_ = f32[136,128]{1,0:T(8,128)S(1)} collective-permute-done((f32[136,128]{1,0:T(8,128)S(1)}, f32[136,128]{1,0:T(8,128)S(1)}, u32[]{:S(2)}, u32[]{:S(2)}) %collective-permute-start.5) | collective-permute-done | bytes 69664 | tf_op jit(solution)/shard_map/ppermute | solution.py:25
  36.4 0.9 %collective-permute-done.6.refs_2_ = f32[136,128]{1,0:T(8,128)S(1)} collective-permute-done((f32[136,128]{1,0:T(8,128)S(1)}, f32[136,128]{1,0:T(8,128)S(1)}, u32[]{:S(2)}, u32[]{:S(2)}) %collective-permute-start.6) | collective-permute-done | bytes 69664 | tf_op jit(solution)/shard_map/ppermute | solution.py:25
  37.3 2.4 %collective-permute-done.7.refs_3_ = f32[136,128]{1,0:T(8,128)S(1)} collective-permute-done((f32[136,128]{1,0:T(8,128)S(1)}, f32[136,128]{1,0:T(8,128)S(1)}, u32[]{:S(2)}, u32[]{:S(2)}) %collective-permute-start.7) | collective-permute-done | bytes 69664 | tf_op jit(solution)/shard_map/ppermute | solution.py:25
  39.6 0.2 shard_map.69
  39.8 2.6 %collective-permute-start.8 = (f32[256,128]{1,0:T(8,128)S(1)}, f32[256,128]{1,0:T(8,128)S(1)}, u32[]{:S(2)}, u32[]{:S(2)}) collective-permute-start(f32[256,128]{1,0:T(8,128)S(1)} %get-tuple-element.44), channel_id=1, source_target_pairs={{0,8},{8,16},{16,24},{1,9},{9,17},{17,25},{2,10},{10,18},{18,26},{... | collective-permute-start | bytes 393224 | tf_op jit(solution)/shard_map/ppermute | solution.py:21
  42.5 2.7 %collective-permute-start.14 = (f32[256,128]{1,0:T(8,128)S(1)}, f32[256,128]{1,0:T(8,128)S(1)}, u32[]{:S(2)}, u32[]{:S(2)}) collective-permute-start(f32[256,128]{1,0:T(8,128)S(1)} %get-tuple-element.55), channel_id=1, source_target_pairs={{0,4},{1,5},{2,6},{3,7},{4,0},{5,1},{6,2},{7,3},{8,12},{9,13},{10,... | collective-permute-start | bytes 393224 | tf_op jit(solution)/shard_map/ppermute | solution.py:25
  45.2 0.9 %collective-permute-start.13 = (f32[256,128]{1,0:T(8,128)S(1)}, f32[256,128]{1,0:T(8,128)S(1)}, u32[]{:S(2)}, u32[]{:S(2)}) collective-permute-start(f32[256,128]{1,0:T(8,128)S(1)} %get-tuple-element.57), channel_id=1, source_target_pairs={{0,4},{1,5},{2,6},{3,7},{4,0},{5,1},{6,2},{7,3},{8,12},{9,13},{10,... | collective-permute-start | bytes 393224 | tf_op jit(solution)/shard_map/ppermute | solution.py:25
  46.1 8.7 %collective-permute-done.14.refs_3_ = f32[256,128]{1,0:T(8,128)S(1)} collective-permute-done((f32[256,128]{1,0:T(8,128)S(1)}, f32[256,128]{1,0:T(8,128)S(1)}, u32[]{:S(2)}, u32[]{:S(2)}) %collective-permute-start.14) | collective-permute-done | bytes 131104 | tf_op jit(solution)/shard_map/ppermute | solution.py:25
  54.8 2.8 %collective-permute-done.13.refs_2_ = f32[256,128]{1,0:T(8,128)S(1)} collective-permute-done((f32[256,128]{1,0:T(8,128)S(1)}, f32[256,128]{1,0:T(8,128)S(1)}, u32[]{:S(2)}, u32[]{:S(2)}) %collective-permute-start.13) | collective-permute-done | bytes 131104 | tf_op jit(solution)/shard_map/ppermute | solution.py:25
  57.6 0.8 %final.1 = f32[512,128]{1,0:T(8,128)} custom-call(f32[256,128]{1,0:T(8,128)S(1)} %get-tuple-element.58.refs_0_, f32[256,128]{1,0:T(8,128)S(1)} %get-tuple-element.56.refs_1_, f32[256,128]{1,0:T(8,128)S(1)} %collective-permute-done.13.refs_2_, f32[256,128]{1,0:T(8,128)S(1)} %collective-permute-done.14.refs_3_), custom_call_target="tpu_custom_call" | custom-call | tf_op jit(solution)/shard_map/final/pallas_call | solution.py:373
  (14 shorter events, 0.1 us)
Async XLA Ops:
  0.7 4.4 %collective-permute-start.3 = (f32[8,128]{1,0:T(8,128)S(1)}, f32[8,128]{1,0:T(8,128)S(1)}, u32[]{:S(2)}, u32[]{:S(2)}) collective-permute-start(f32[8,128]{1,0:T(8,128)S(1)} %shard_map.66), channel_id=1, source_target_pairs={{0,8},{8,16},{16,24},{1,9},{9,17},{17,25},{2,10},{10,18},{18,26},{... | collective-permute-start | bytes 12296 | tf_op jit(solution)/shard_map/ppermute | solution.py:21
  5.1 1.5 %copy-start = (s32[2]{0:T(128)S(1)}, s32[2]{0:T(128)}, u32[]{:S(2)}) copy-start(s32[2]{0:T(128)} %rows.7) | copy-start | bytes 28
  5.1 1.5 %copy-start.1 = (s32[2]{0:T(128)S(1)}, s32[2]{0:T(128)}, u32[]{:S(2)}) copy-start(s32[2]{0:T(128)} %cols.7) | copy-start | bytes 28
  5.3 9.9 %collective-permute-start.4 = (f32[2,256,256]{2,1,0:T(8,128)S(1)}, f32[2,256,256]{2,1,0:T(8,128)S(1)}, u32[]{:S(2)}, u32[]{:S(2)}) collective-permute-start(f32[2,256,256]{2,1,0:T(8,128)S(1)} %shard_map.67), channel_id=1, source_target_pairs={{8,0},{16,8},{24,16},{9,1},{17,9},{25,17},{10,2},{18,10},{26,18},{... | collective-permute-start | bytes 1572872 | tf_op jit(solution)/shard_map/ppermute | solution.py:21
  11.2 12.5 %collective-permute-start = (f32[136,256]{1,0:T(8,128)S(1)}, f32[136,256]{1,0:T(8,128)S(1)}, u32[]{:S(2)}, u32[]{:S(2)}) collective-permute-start(f32[136,256]{1,0:T(8,128)S(1)} %get-tuple-element.35), channel_id=1, source_target_pairs={{0,1},{1,0},{2,3},{3,2},{4,5},{5,4},{6,7},{7,6},{8,9},{9,8},{10,11... | collective-permute-start | bytes 417800 | tf_op jit(solution)/shard_map/ppermute | solution.py:25
  13.6 10.3 %collective-permute-start.1 = (f32[136,256]{1,0:T(8,128)S(1)}, f32[136,256]{1,0:T(8,128)S(1)}, u32[]{:S(2)}, u32[]{:S(2)}) collective-permute-start(f32[136,256]{1,0:T(8,128)S(1)} %get-tuple-element.36), channel_id=1, source_target_pairs={{0,2},{1,3},{2,0},{3,1},{4,6},{5,7},{6,4},{7,5},{8,10},{9,11},{10,... | collective-permute-start | bytes 417800 | tf_op jit(solution)/shard_map/ppermute | solution.py:25
  15.2 8.8 %collective-permute-start.2 = (f32[136,256]{1,0:T(8,128)S(1)}, f32[136,256]{1,0:T(8,128)S(1)}, u32[]{:S(2)}, u32[]{:S(2)}) collective-permute-start(f32[136,256]{1,0:T(8,128)S(1)} %get-tuple-element.37), channel_id=1, source_target_pairs={{0,3},{1,2},{2,1},{3,0},{4,7},{5,6},{6,5},{7,4},{8,11},{9,10},{10,... | collective-permute-start | bytes 417800 | tf_op jit(solution)/shard_map/ppermute | solution.py:25
  20.3 4.4 %collective-permute-start.10 = (f32[136,128]{1,0:T(8,128)S(1)}, f32[136,128]{1,0:T(8,128)S(1)}, u32[]{:S(2)}, u32[]{:S(2)}) collective-permute-start(f32[136,128]{1,0:T(8,128)S(1)} %get-tuple-element.50), channel_id=1, source_target_pairs={{0,2},{1,3},{2,0},{3,1},{4,6},{5,7},{6,4},{7,5},{8,10},{9,11},{10,... | collective-permute-start | bytes 208904 | tf_op jit(solution)/shard_map/ppermute | solution.py:25
  22.4 5.7 %collective-permute-start.11 = (f32[136,128]{1,0:T(8,128)S(1)}, f32[136,128]{1,0:T(8,128)S(1)}, u32[]{:S(2)}, u32[]{:S(2)}) collective-permute-start(f32[136,128]{1,0:T(8,128)S(1)} %get-tuple-element.51), channel_id=1, source_target_pairs={{0,3},{1,2},{2,1},{3,0},{4,7},{5,6},{6,5},{7,4},{8,11},{9,10},{10,... | collective-permute-start | bytes 208904 | tf_op jit(solution)/shard_map/ppermute | solution.py:25
  23.8 4.7 %collective-permute-start.9 = (f32[136,128]{1,0:T(8,128)S(1)}, f32[136,128]{1,0:T(8,128)S(1)}, u32[]{:S(2)}, u32[]{:S(2)}) collective-permute-start(f32[136,128]{1,0:T(8,128)S(1)} %get-tuple-element.49), channel_id=1, source_target_pairs={{0,1},{1,0},{2,3},{3,2},{4,5},{5,4},{6,7},{7,6},{8,9},{9,8},{10,11... | collective-permute-start | bytes 208904 | tf_op jit(solution)/shard_map/ppermute | solution.py:25
  28.7 13.8 %collective-permute-start.12 = (f32[256,128]{1,0:T(8,128)S(1)}, f32[256,128]{1,0:T(8,128)S(1)}, u32[]{:S(2)}, u32[]{:S(2)}) collective-permute-start(f32[256,128]{1,0:T(8,128)S(1)} %get-tuple-element.54), channel_id=1, source_target_pairs={{0,8},{8,16},{16,24},{1,9},{9,17},{17,25},{2,10},{10,18},{18,26},{... | collective-permute-start | bytes 393224 | tf_op jit(solution)/shard_map/ppermute | solution.py:21
  32.0 4.4 %collective-permute-start.5 = (f32[136,128]{1,0:T(8,128)S(1)}, f32[136,128]{1,0:T(8,128)S(1)}, u32[]{:S(2)}, u32[]{:S(2)}) collective-permute-start(f32[136,128]{1,0:T(8,128)S(1)} %get-tuple-element.39), channel_id=1, source_target_pairs={{0,1},{1,0},{2,3},{3,2},{4,5},{5,4},{6,7},{7,6},{8,9},{9,8},{10,11... | collective-permute-start | bytes 208904 | tf_op jit(solution)/shard_map/ppermute | solution.py:25
  33.0 4.3 %collective-permute-start.6 = (f32[136,128]{1,0:T(8,128)S(1)}, f32[136,128]{1,0:T(8,128)S(1)}, u32[]{:S(2)}, u32[]{:S(2)}) collective-permute-start(f32[136,128]{1,0:T(8,128)S(1)} %get-tuple-element.40), channel_id=1, source_target_pairs={{0,2},{1,3},{2,0},{3,1},{4,6},{5,7},{6,4},{7,5},{8,10},{9,11},{10,... | collective-permute-start | bytes 208904 | tf_op jit(solution)/shard_map/ppermute | solution.py:25
  33.8 5.8 %collective-permute-start.7 = (f32[136,128]{1,0:T(8,128)S(1)}, f32[136,128]{1,0:T(8,128)S(1)}, u32[]{:S(2)}, u32[]{:S(2)}) collective-permute-start(f32[136,128]{1,0:T(8,128)S(1)} %get-tuple-element.41), channel_id=1, source_target_pairs={{0,3},{1,2},{2,1},{3,0},{4,7},{5,6},{6,5},{7,4},{8,11},{9,10},{10,... | collective-permute-start | bytes 208904 | tf_op jit(solution)/shard_map/ppermute | solution.py:25
  39.8 5.4 %collective-permute-start.8 = (f32[256,128]{1,0:T(8,128)S(1)}, f32[256,128]{1,0:T(8,128)S(1)}, u32[]{:S(2)}, u32[]{:S(2)}) collective-permute-start(f32[256,128]{1,0:T(8,128)S(1)} %get-tuple-element.44), channel_id=1, source_target_pairs={{0,8},{8,16},{16,24},{1,9},{9,17},{17,25},{2,10},{10,18},{18,26},{... | collective-permute-start | bytes 393224 | tf_op jit(solution)/shard_map/ppermute | solution.py:21
  42.5 12.3 %collective-permute-start.14 = (f32[256,128]{1,0:T(8,128)S(1)}, f32[256,128]{1,0:T(8,128)S(1)}, u32[]{:S(2)}, u32[]{:S(2)}) collective-permute-start(f32[256,128]{1,0:T(8,128)S(1)} %get-tuple-element.55), channel_id=1, source_target_pairs={{0,4},{1,5},{2,6},{3,7},{4,0},{5,1},{6,2},{7,3},{8,12},{9,13},{10,... | collective-permute-start | bytes 393224 | tf_op jit(solution)/shard_map/ppermute | solution.py:25
  45.2 12.4 %collective-permute-start.13 = (f32[256,128]{1,0:T(8,128)S(1)}, f32[256,128]{1,0:T(8,128)S(1)}, u32[]{:S(2)}, u32[]{:S(2)}) collective-permute-start(f32[256,128]{1,0:T(8,128)S(1)} %get-tuple-element.57), channel_id=1, source_target_pairs={{0,4},{1,5},{2,6},{3,7},{4,0},{5,1},{6,2},{7,3},{8,12},{9,13},{10,... | collective-permute-start | bytes 393224 | tf_op jit(solution)/shard_map/ppermute | solution.py:25

commit v5 on v3

--- a/solution.py
+++ b/solution.py
@@ -103,11 +103,16 @@
     )(*[pltpu.with_memory_space_constraint(array, pltpu.HBM) for array in arrays])
 
 
+def pick_kernel(window, rows, cols, out):
+    _, column, _ = chosen(1, rows, cols, lax.axis_index("tile") * (2 * window), window)
+    out[...] = jnp.broadcast_to(column.astype(F32), out.shape)
+
+
 def rim_kernel(window, wanted, obj, out):
-    offset = wanted[0]
+    offset = wanted[pl.ds(0, 1), :]
     tiles = window // LANES
     for tile in range(tiles):
-        column = lax.broadcasted_iota(jnp.int32, (window, LANES), 1) + tile * LANES
+        column = (lax.broadcasted_iota(jnp.int32, (window, LANES), 1) + tile * LANES).astype(F32)
         for part in range(2):
             near = obj[pl.ds(tile * 2 + part, window, stride=4 * tiles), :]
             beyond = obj[pl.ds((tiles + tile) * 2 + part, window, stride=4 * tiles), :]
@@ -286,10 +291,11 @@
     tiles = window // LANES
     scalars = (row_offset, col_offset)
 
-    crossing = row_offset[:1] - lax.axis_index("tile") * band_rows > window
-    wanted = shifted(jnp.where(crossing, col_offset[:1], col_offset[1:]), "tile", 1)
+    remote = tuple(pltpu.with_memory_space_constraint(scalar, pltpu.HBM) for scalar in scalars)
+    (wanted,) = kernel_call(functools.partial(pick_kernel, window), "pick", [(8, LANES)], remote, [])
+    wanted = shifted(wanted, "tile", 1)
     obj, ill, amps, table = loaded([linear(object_field), linear(illumination), amplitudes, split_tables(window)])
-    (rim,) = kernel_call(functools.partial(rim_kernel, window), "rim", [(2, window, window)], [wanted], [obj])
+    (rim,) = kernel_call(functools.partial(rim_kernel, window), "rim", [(2, window, window)], (), [wanted, obj])
     rim = shifted(rim, "tile", -1)
 
     def spread(pieces):

time: 54.9 us -> 51 us (0.929)
  between operations: 1.96 us -> 0.14 us
  local copies, waits for them, and re-layouts: 1.35 us -> 0.01 us
  starting transfers between devices: 17.2 us -> 16.5 us
    slice x1 -> x0, local copies, waits for them, and re-layouts: 1.33 us -> none  [on_device(): col_offset[1:]]
    ppermute x3, starting transfers between devices: 6.99 us -> 6.28 us  [shifted(): return lax.ppermute(block, axis, route)]
    pallas_call x5 -> x6, Pallas kernels: 10.7 us -> 10.7 us  [kernel_call(): pl.pallas_call(body, out_shape=[pltpu.VMEM(shape, F32) for shape in out_s...]
  transfers between devices with their start and end apart: 10 -> 10, of which waited for: 5 -> 5; matrix products, arithmetic and copies ran while one was open for 0% -> 0% of each run, Pallas kernels for 21% -> 22%
where the time goes in v5:
time: 51 us; the launch traced here: 50.7 us
  waiting for transfers between devices  20.6 us (40%)
  starting transfers between devices  16.5 us (32%)
  Pallas kernels  12.7 us (25%)
  other arithmetic  0.79 us (2%)
    ppermute x7, waiting for transfers between devices, exchanged(): lax.ppermute(block, axis, [(i, i ^ flip) for i in range(lax.axis_size(axi...  19.5 us
    pallas_call x6, Pallas kernels, kernel_call(): pl.pallas_call(body, out_shape=[pltpu.VMEM(shape, F32) for shape in out_s...  10.7 us
    ppermute x7, starting transfers between devices, exchanged(): lax.ppermute(block, axis, [(i, i ^ flip) for i in range(lax.axis_size(axi...  10.2 us
    ppermute x3, starting transfers between devices, shifted(): return lax.ppermute(block, axis, route)  6.28 us
    pallas_call x1, Pallas kernels, loaded(): pl.pallas_call(functools.partial(load_kernel, len(arrays)), out_shape=[pl...  1.95 us
    ppermute x3, waiting for transfers between devices, shifted(): return lax.ppermute(block, axis, route)  1.13 us
  transfers between devices with their start and end apart: 10, of which 5 were waited for; matrix products, arithmetic and copies ran while one was open for 0% of the time, Pallas kernels for 22%

profile of v5, /device:TPU:0, one launch (start us, length us, event | category | flops | bytes accessed | tf_op | source)
XLA Modules:
  0.0 50.7 jit_solution(9200014179459947981)
XLA Ops:
  0.0 0.7 %pick.1 = f32[8,128]{1,0:T(8,128)S(1)} custom-call(s32[2]{0:T(128)} %rows.5, s32[2]{0:T(128)} %cols.5), custom_call_target="tpu_custom_call" | custom-call | bytes 8192 | tf_op jit(solution)/shard_map/pick/pallas_call | solution.py:67
  0.7 2.4 %collective-permute-start.3 = (f32[8,128]{1,0:T(8,128)S(1)}, f32[8,128]{1,0:T(8,128)S(1)}, u32[]{:S(2)}, u32[]{:S(2)}) collective-permute-start(f32[8,128]{1,0:T(8,128)S(1)} %pick.1), channel_id=1, source_target_pairs={{0,8},{8,16},{16,24},{1,9},{9,17},{17,25},{2,10},{10,18},{18,26},{... | collective-permute-start | bytes 12296 | tf_op jit(solution)/shard_map/ppermute | solution.py:20
  3.1 1.9 %load.1 = (f32[4096,128]{1,0:T(8,128)S(1)}, f32[1024,128]{1,0:T(8,128)S(1)}, bf16[2,256,256]{2,1,0:T(8,128)(2,1)S(1)}, bf16[1024,256]{1,0:T(8,128)(2,1)S(1)}) custom-call(f32[4096,128]{1,0:T(8,128)} %bitcast.15, f32[1024,128]{1,0:T(8,128)} %bitcast.16, bf16[2,256,256]{2,1,0:T(8,128)(2,1)} %refs_2_.1, bf16[1024,256]{1,0:T(8,128)(2,1)} %constant.8.clone.refs_3_), custom_call_target="tpu_custom_call" | custom-call | tf_op jit(solution)/shard_map/load/pallas_call | solution.py:95
  5.1 0.0 copy-start
  5.1 0.0 copy-start.1
  5.1 0.0 collective-permute-done.3.wanted
  5.1 0.2 rim.1
  5.3 1.3 %collective-permute-start.4 = (f32[2,256,256]{2,1,0:T(8,128)S(1)}, f32[2,256,256]{2,1,0:T(8,128)S(1)}, u32[]{:S(2)}, u32[]{:S(2)}) collective-permute-start(f32[2,256,256]{2,1,0:T(8,128)S(1)} %rim.1), channel_id=1, source_target_pairs={{8,0},{16,8},{24,16},{9,1},{17,9},{25,17},{10,2},{18,10},{26,18},{... | collective-permute-start | bytes 1572872 | tf_op jit(solution)/shard_map/ppermute | solution.py:20
  6.6 0.0 copy-done
  6.6 0.0 copy-done.1
  6.6 4.6 %wave0.1 = (f32[136,256]{1,0:T(8,128)S(1)}, f32[136,256]{1,0:T(8,128)S(1)}, f32[136,256]{1,0:T(8,128)S(1)}, f32[136,256]{1,0:T(8,128)S(1)}) custom-call(s32[2]{0:T(128)S(1)} %copy-done, s32[2]{0:T(128)S(1)} %copy-done.1, f32[4096,128]{1,0:T(8,128)S(1)} %get-tuple-element.20.obj, f32[1024,128]{1,0:T(8,128)S(1)} %get-tuple-element.21.ill, ...), custom_call_target="tpu_custom_call" | custom-call | flops 1610612736 | bytes 1114112 | tf_op jit(solution)/shard_map/wave0/pallas_call | solution.py:67
  11.2 2.4 %collective-permute-start = (f32[136,256]{1,0:T(8,128)S(1)}, f32[136,256]{1,0:T(8,128)S(1)}, u32[]{:S(2)}, u32[]{:S(2)}) collective-permute-start(f32[136,256]{1,0:T(8,128)S(1)} %get-tuple-element.25), channel_id=1, source_target_pairs={{0,1},{1,0},{2,3},{3,2},{4,5},{5,4},{6,7},{7,6},{8,9},{9,8},{10,11... | collective-permute-start | bytes 417800 | tf_op jit(solution)/shard_map/ppermute | solution.py:24
  13.6 1.6 %collective-permute-start.1 = (f32[136,256]{1,0:T(8,128)S(1)}, f32[136,256]{1,0:T(8,128)S(1)}, u32[]{:S(2)}, u32[]{:S(2)}) collective-permute-start(f32[136,256]{1,0:T(8,128)S(1)} %get-tuple-element.26), channel_id=1, source_target_pairs={{0,2},{1,3},{2,0},{3,1},{4,6},{5,7},{6,4},{7,5},{8,10},{9,11},{10,... | collective-permute-start | bytes 417800 | tf_op jit(solution)/shard_map/ppermute | solution.py:24
  15.1 0.0 collective-permute-start.2
  15.1 0.0 collective-permute-done.4.refs_0_
  15.2 4.6 %wave1.1 = (f32[136,256]{1,0:T(8,128)S(1)}, f32[136,256]{1,0:T(8,128)S(1)}, f32[136,256]{1,0:T(8,128)S(1)}, f32[136,256]{1,0:T(8,128)S(1)}) custom-call(s32[2]{0:T(128)S(1)} %copy-done, s32[2]{0:T(128)S(1)} %copy-done.1, f32[4096,128]{1,0:T(8,128)S(1)} %get-tuple-element.20.obj, f32[1024,128]{1,0:T(8,128)S(1)} %get-tuple-element.21.ill, ...), custom_call_target="tpu_custom_call" | custom-call | flops 1610612736 | bytes 1114112 | tf_op jit(solution)/shard_map/wave1/pallas_call | solution.py:67
  19.8 2.0 %collective-permute-start.5 = (f32[136,256]{1,0:T(8,128)S(1)}, f32[136,256]{1,0:T(8,128)S(1)}, u32[]{:S(2)}, u32[]{:S(2)}) collective-permute-start(f32[136,256]{1,0:T(8,128)S(1)} %get-tuple-element.29), channel_id=1, source_target_pairs={{0,1},{1,0},{2,3},{3,2},{4,5},{5,4},{6,7},{7,6},{8,9},{9,8},{10,11... | collective-permute-start | bytes 417800 | tf_op jit(solution)/shard_map/ppermute | solution.py:24
  21.8 1.6 %collective-permute-start.6 = (f32[136,256]{1,0:T(8,128)S(1)}, f32[136,256]{1,0:T(8,128)S(1)}, u32[]{:S(2)}, u32[]{:S(2)}) collective-permute-start(f32[136,256]{1,0:T(8,128)S(1)} %get-tuple-element.30), channel_id=1, source_target_pairs={{0,2},{1,3},{2,0},{3,1},{4,6},{5,7},{6,4},{7,5},{8,10},{9,11},{10,... | collective-permute-start | bytes 417800 | tf_op jit(solution)/shard_map/ppermute | solution.py:24
  23.3 0.0 collective-permute-done.refs_1_
  23.3 0.0 collective-permute-start.7
  23.3 0.0 collective-permute-done.1.refs_2_
  23.4 0.0 collective-permute-done.2.refs_3_
  23.4 0.2 sum0.1.acc
  23.6 1.3 %collective-permute-done.5.refs_1_ = f32[136,256]{1,0:T(8,128)S(1)} collective-permute-done((f32[136,256]{1,0:T(8,128)S(1)}, f32[136,256]{1,0:T(8,128)S(1)}, u32[]{:S(2)}, u32[]{:S(2)}) %collective-permute-start.5) | collective-permute-done | bytes 139296 | tf_op jit(solution)/shard_map/ppermute | solution.py:24
  24.9 1.9 %collective-permute-done.6.refs_2_ = f32[136,256]{1,0:T(8,128)S(1)} collective-permute-done((f32[136,256]{1,0:T(8,128)S(1)}, f32[136,256]{1,0:T(8,128)S(1)}, u32[]{:S(2)}, u32[]{:S(2)}) %collective-permute-start.6) | collective-permute-done | bytes 139296 | tf_op jit(solution)/shard_map/ppermute | solution.py:24
  26.8 4.0 %collective-permute-done.7.refs_3_ = f32[136,256]{1,0:T(8,128)S(1)} collective-permute-done((f32[136,256]{1,0:T(8,128)S(1)}, f32[136,256]{1,0:T(8,128)S(1)}, u32[]{:S(2)}, u32[]{:S(2)}) %collective-permute-start.7) | collective-permute-done | bytes 139296 | tf_op jit(solution)/shard_map/ppermute | solution.py:24
  30.8 0.5 sum1.1
  31.2 2.6 %collective-permute-start.8 = (f32[512,128]{1,0:T(8,128)S(1)}, f32[512,128]{1,0:T(8,128)S(1)}, u32[]{:S(2)}, u32[]{:S(2)}) collective-permute-start(f32[512,128]{1,0:T(8,128)S(1)} %get-tuple-element.34), channel_id=1, source_target_pairs={{0,8},{8,16},{16,24},{1,9},{9,17},{17,25},{2,10},{10,18},{18,26},{... | collective-permute-start | bytes 786440 | tf_op jit(solution)/shard_map/ppermute | solution.py:20
  33.8 1.1 %collective-permute-done.8 = f32[512,128]{1,0:T(8,128)S(1)} collective-permute-done((f32[512,128]{1,0:T(8,128)S(1)}, f32[512,128]{1,0:T(8,128)S(1)}, u32[]{:S(2)}, u32[]{:S(2)}) %collective-permute-start.8) | collective-permute-done | bytes 262176 | tf_op jit(solution)/shard_map/ppermute | solution.py:20
  35.0 2.7 %collective-permute-start.9 = (f32[512,128]{1,0:T(8,128)S(1)}, f32[512,128]{1,0:T(8,128)S(1)}, u32[]{:S(2)}, u32[]{:S(2)}) collective-permute-start(f32[512,128]{1,0:T(8,128)S(1)} %broadcast_select_fusion), channel_id=1, source_target_pairs={{0,4},{1,5},{2,6},{3,7},{4,0},{5,1},{6,2},{7,3},{8,12},{9,13},{10,... | collective-permute-start | bytes 786440 | tf_op jit(solution)/shard_map/ppermute | solution.py:24
  37.7 12.3 %collective-permute-done.9 = f32[512,128]{1,0:T(8,128)S(1)} collective-permute-done((f32[512,128]{1,0:T(8,128)S(1)}, f32[512,128]{1,0:T(8,128)S(1)}, u32[]{:S(2)}, u32[]{:S(2)}) %collective-permute-start.9) | collective-permute-done | bytes 262176 | tf_op jit(solution)/shard_map/ppermute | solution.py:24
  50.0 0.8 %select_add_fusion = f32[512,128]{1,0:T(8,128)} fusion(f32[512,128]{1,0:T(8,128)S(1)} %collective-permute-done.9, f32[512,128]{1,0:T(8,128)S(1)} %get-tuple-element.32, pred[]{:T(512)S(6)} %ge.3, f32[512,128]{1,0:T(8,128)S(1)} %get-tuple-element.33, f32[512,128]{1,0:T(8,128)S(1)} %collective-permute-done.8), kind=kLoop, calls=%fused_computation | loop fusion | flops 196608 | bytes 1310721 | tf_op jit(solution)/shard_map/add | solution.py:320
  (1 shorter events, 0.0 us)
Async XLA Ops:
  0.7 4.4 %collective-permute-start.3 = (f32[8,128]{1,0:T(8,128)S(1)}, f32[8,128]{1,0:T(8,128)S(1)}, u32[]{:S(2)}, u32[]{:S(2)}) collective-permute-start(f32[8,128]{1,0:T(8,128)S(1)} %pick.1), channel_id=1, source_target_pairs={{0,8},{8,16},{16,24},{1,9},{9,17},{17,25},{2,10},{10,18},{18,26},{... | collective-permute-start | bytes 12296 | tf_op jit(solution)/shard_map/ppermute | solution.py:20
  5.1 1.5 %copy-start = (s32[2]{0:T(128)S(1)}, s32[2]{0:T(128)}, u32[]{:S(2)}) copy-start(s32[2]{0:T(128)} %rows.5) | copy-start | bytes 28
  5.1 1.5 %copy-start.1 = (s32[2]{0:T(128)S(1)}, s32[2]{0:T(128)}, u32[]{:S(2)}) copy-start(s32[2]{0:T(128)} %cols.5) | copy-start | bytes 28
  5.3 9.9 %collective-permute-start.4 = (f32[2,256,256]{2,1,0:T(8,128)S(1)}, f32[2,256,256]{2,1,0:T(8,128)S(1)}, u32[]{:S(2)}, u32[]{:S(2)}) collective-permute-start(f32[2,256,256]{2,1,0:T(8,128)S(1)} %rim.1), channel_id=1, source_target_pairs={{8,0},{16,8},{24,16},{9,1},{17,9},{25,17},{10,2},{18,10},{26,18},{... | collective-permute-start | bytes 1572872 | tf_op jit(solution)/shard_map/ppermute | solution.py:20
  11.2 12.2 %collective-permute-start = (f32[136,256]{1,0:T(8,128)S(1)}, f32[136,256]{1,0:T(8,128)S(1)}, u32[]{:S(2)}, u32[]{:S(2)}) collective-permute-start(f32[136,256]{1,0:T(8,128)S(1)} %get-tuple-element.25), channel_id=1, source_target_pairs={{0,1},{1,0},{2,3},{3,2},{4,5},{5,4},{6,7},{7,6},{8,9},{9,8},{10,11... | collective-permute-start | bytes 417800 | tf_op jit(solution)/shard_map/ppermute | solution.py:24
  13.6 9.8 %collective-permute-start.1 = (f32[136,256]{1,0:T(8,128)S(1)}, f32[136,256]{1,0:T(8,128)S(1)}, u32[]{:S(2)}, u32[]{:S(2)}) collective-permute-start(f32[136,256]{1,0:T(8,128)S(1)} %get-tuple-element.26), channel_id=1, source_target_pairs={{0,2},{1,3},{2,0},{3,1},{4,6},{5,7},{6,4},{7,5},{8,10},{9,11},{10,... | collective-permute-start | bytes 417800 | tf_op jit(solution)/shard_map/ppermute | solution.py:24
  15.1 8.2 %collective-permute-start.2 = (f32[136,256]{1,0:T(8,128)S(1)}, f32[136,256]{1,0:T(8,128)S(1)}, u32[]{:S(2)}, u32[]{:S(2)}) collective-permute-start(f32[136,256]{1,0:T(8,128)S(1)} %get-tuple-element.27), channel_id=1, source_target_pairs={{0,3},{1,2},{2,1},{3,0},{4,7},{5,6},{6,5},{7,4},{8,11},{9,10},{10,... | collective-permute-start | bytes 417800 | tf_op jit(solution)/shard_map/ppermute | solution.py:24
  19.8 5.1 %collective-permute-start.5 = (f32[136,256]{1,0:T(8,128)S(1)}, f32[136,256]{1,0:T(8,128)S(1)}, u32[]{:S(2)}, u32[]{:S(2)}) collective-permute-start(f32[136,256]{1,0:T(8,128)S(1)} %get-tuple-element.29), channel_id=1, source_target_pairs={{0,1},{1,0},{2,3},{3,2},{4,5},{5,4},{6,7},{7,6},{8,9},{9,8},{10,11... | collective-permute-start | bytes 417800 | tf_op jit(solution)/shard_map/ppermute | solution.py:24
  21.8 5.1 %collective-permute-start.6 = (f32[136,256]{1,0:T(8,128)S(1)}, f32[136,256]{1,0:T(8,128)S(1)}, u32[]{:S(2)}, u32[]{:S(2)}) collective-permute-start(f32[136,256]{1,0:T(8,128)S(1)} %get-tuple-element.30), channel_id=1, source_target_pairs={{0,2},{1,3},{2,0},{3,1},{4,6},{5,7},{6,4},{7,5},{8,10},{9,11},{10,... | collective-permute-start | bytes 417800 | tf_op jit(solution)/shard_map/ppermute | solution.py:24
  23.3 7.4 %collective-permute-start.7 = (f32[136,256]{1,0:T(8,128)S(1)}, f32[136,256]{1,0:T(8,128)S(1)}, u32[]{:S(2)}, u32[]{:S(2)}) collective-permute-start(f32[136,256]{1,0:T(8,128)S(1)} %get-tuple-element.31), channel_id=1, source_target_pairs={{0,3},{1,2},{2,1},{3,0},{4,7},{5,6},{6,5},{7,4},{8,11},{9,10},{10,... | collective-permute-start | bytes 417800 | tf_op jit(solution)/shard_map/ppermute | solution.py:24
  31.2 3.7 %collective-permute-start.8 = (f32[512,128]{1,0:T(8,128)S(1)}, f32[512,128]{1,0:T(8,128)S(1)}, u32[]{:S(2)}, u32[]{:S(2)}) collective-permute-start(f32[512,128]{1,0:T(8,128)S(1)} %get-tuple-element.34), channel_id=1, source_target_pairs={{0,8},{8,16},{16,24},{1,9},{9,17},{17,25},{2,10},{10,18},{18,26},{... | collective-permute-start | bytes 786440 | tf_op jit(solution)/shard_map/ppermute | solution.py:20
  35.0 15.0 %collective-permute-start.9 = (f32[512,128]{1,0:T(8,128)S(1)}, f32[512,128]{1,0:T(8,128)S(1)}, u32[]{:S(2)}, u32[]{:S(2)}) collective-permute-start(f32[512,128]{1,0:T(8,128)S(1)} %broadcast_select_fusion), channel_id=1, source_target_pairs={{0,4},{1,5},{2,6},{3,7},{4,0},{5,1},{6,2},{7,3},{8,12},{9,13},{10,... | collective-permute-start | bytes 786440 | tf_op jit(solution)/shard_map/ppermute | solution.py:24

commit v6 on v5

--- a/solution.py
+++ b/solution.py
@@ -25,13 +25,18 @@
 
 
 def split_tables(length):
-    indices = np.arange(length, dtype=np.int64)
-    angles = (indices[:, None] * indices[None, :] % length) * (2.0 * math.pi / length)
-    factor = 1.0 / math.sqrt(length)
-    whole = np.concatenate([np.cos(angles), np.sin(angles)], axis=0) * factor
-    high = whole.astype(BF16)
-    low = (whole - high.astype(np.float64)).astype(BF16)
-    return jnp.asarray(np.concatenate([high, low], axis=0))
+    half = length // 2
+    n = np.arange(half, dtype=np.int64)
+    even = 2 * n[:, None] * n[None, :]
+    odd = n[:, None] * (2 * n[None, :] + 1)
+    rows = []
+    for product in (even, odd, odd.T):
+        angles = (product % length) * (2.0 * math.pi / length)
+        real, imag = np.cos(angles) / math.sqrt(length), -np.sin(angles) / math.sqrt(length)
+        whole = np.concatenate([real, imag, -imag], axis=1)
+        high = whole.astype(BF16)
+        rows += [high, (whole - high.astype(np.float64)).astype(BF16)]
+    return jnp.asarray(np.concatenate(rows, axis=0))
 
 
 def linear(array):
@@ -123,8 +128,9 @@
     if with_rim:
         rim, refs = refs[0], refs[1:]
     outs, refs = refs[:classes], refs[classes:]
-    doubled, probe, xh, xl, far = refs
-    tiles = window // LANES
+    doubled, probe, xh, xl, yh, yl, far, ordered = refs
+    tiles = window // LANES
+    half = window // 2
     row, column, index = chosen(slot, rows, cols, lax.axis_index("tile") * (2 * window), window)
     own = lax.rem(lax.axis_index("pos"), classes)
     size = 32
@@ -134,16 +140,43 @@
     doubled[pl.ds(whole, size * step), :] = ill[pl.ds(0, size * step), :]
     turn = lax.rem(row, window)
 
-    def store_pair(first, real, imag):
-        here = pl.ds(first, size)
-        below = pl.ds(window + first, size)
-        left, right = pl.ds(0, window), pl.ds(window, window)
-        for part, ref in zip(range(2), (xh, xl)):
-            r, i, n = (halves(v)[part] for v in (real, imag, -real))
-            ref[here, left] = r
-            ref[here, right] = i
-            ref[below, left] = i
-            ref[below, right] = n
+    below = lax.broadcasted_iota(jnp.int32, (window, window), 0)
+    beside = lax.broadcasted_iota(jnp.int32, (window, window), 1)
+
+    def picks(frequency, place):
+        wanted = jnp.where(place < half, 2 * place, 2 * (place - half) + 1)
+        return jnp.where(frequency == wanted, 1.0, 0.0).astype(BF16)
+
+    by_column = jnp.dot(amps[index], picks(below, beside), preferred_element_type=F32).astype(BF16)
+    ordered[...] = jnp.dot(picks(beside, below), by_column, preferred_element_type=F32)
+
+    def block_of(matrix, part, low):
+        return table[pl.ds((2 * matrix + low) * half, half), pl.ds(part * half, half)]
+
+    def factor(matrix, order):
+        return [
+            jnp.concatenate(
+                [
+                    jnp.concatenate([block_of(matrix, part, low) for part in line], axis=1)
+                    for line in order
+                ],
+                axis=0,
+            )
+            for low in range(2)
+        ]
+
+    def from_right(first, matrix):
+        across = pl.ds(first, window)
+        return dot3(xh[:, across], xl[:, across], *factor(matrix, ((0, 1), (2, 0))))
+
+    def from_left(matrix, first):
+        down = pl.ds(first, window)
+        return dot3(*factor(matrix, ((0, 2), (1, 0))), yh[down, :], yl[down, :])
+
+    def keep(high_ref, low_ref, here, across, value):
+        high, low = halves(value)
+        high_ref[here, across] = high
+        low_ref[here, across] = low
 
     for first in range(0, window, size):
         place = lax.broadcasted_iota(jnp.int32, (size, window), 0) + first
@@ -171,38 +204,61 @@
                 seen = jnp.where(place + window < row, rim[part, pl.ds(first, size), :], seen)
             pair.append((rolled, seen))
         (probe_real, obj_real), (probe_imag, obj_imag) = pair
-        store_pair(
-            first,
+        exits = (
             probe_real * obj_real - probe_imag * obj_imag,
             probe_real * obj_imag + probe_imag * obj_real,
         )
-
-    high = table[pl.ds(0, 2 * window), :]
-    low = table[pl.ds(2 * window, 2 * window), :]
-    left_high = jnp.concatenate([table[pl.ds(0, window), :], table[pl.ds(window, window), :]], axis=1)
-    left_low = jnp.concatenate([table[pl.ds(2 * window, window), :], table[pl.ds(3 * window, window), :]], axis=1)
-
-    def both_sides():
-        mid = dot3(xh[...], xl[...], high, low)
-        for first in range(0, window, size):
-            store_pair(first, mid[first : first + size], mid[window + first : window + first + size])
-        far[...] = dot3(left_high, left_low, xh[...], xl[...])
-
-    both_sides()
+        here = pl.ds(first, size)
+        for part, value in enumerate(exits):
+            left, right = value[:, :half], value[:, half:]
+            keep(xh, xl, here, pl.ds(part * half, half), left + right)
+            keep(xh, xl, here, pl.ds(window + part * half, half), left - right)
+
+    for parity in range(2):
+        mid = from_right(parity * window, parity)
+        across = pl.ds(parity * half, half)
+        for first in range(0, half, size):
+            top, bottom = mid[first : first + size], mid[half + first : half + first + size]
+            for line, value in enumerate((top + bottom, top - bottom)):
+                for part in range(2):
+                    here = pl.ds((2 * line + part) * half + first, size)
+                    keep(yh, yl, here, across, value[:, part * half : (part + 1) * half])
+    far[pl.ds(0, window), :] = from_left(0, 0)
+    far[pl.ds(window, window), :] = from_left(2, window)
+
+    for parity in range(2):
+        for first in range(0, half, size):
+            real = far[pl.ds(parity * window + first, size), :]
+            imag = far[pl.ds(parity * window + half + first, size), :]
+            here = pl.ds(parity * half + first, size)
+            inverse = jnp.minimum(lax.rsqrt(real * real + imag * imag), 4.0)
+            scaled = ordered[here, :] * inverse
+            for part, value in enumerate((real * (1.0 - scaled), imag * (scaled - 1.0))):
+                for side in range(2):
+                    across = pl.ds(side * window + part * half, half)
+                    keep(xh, xl, here, across, value[:, side * half : (side + 1) * half])
+
+    even, odd = from_right(0, 0), from_right(window, 2)
     for first in range(0, window, size):
-        real = far[pl.ds(first, size), pl.ds(0, window)]
-        imag = far[pl.ds(first, size), pl.ds(window, window)]
-        inverse = jnp.minimum(lax.rsqrt(real * real + imag * imag), 4.0)
-        scaled = amps[index, pl.ds(first, size), :].astype(F32) * inverse
-        store_pair(first, real * (1.0 - scaled), imag * (scaled - 1.0))
-    both_sides()
+        near, beyond = even[first : first + size], odd[first : first + size]
+        parity, place = first // half, first % half
+        for side, value in enumerate((near + beyond, near - beyond)):
+            for part in range(2):
+                here = pl.ds((2 * parity + part) * half + place, size)
+                keep(yh, yl, here, pl.ds(side * half, half), value[:, part * half : (part + 1) * half])
+    far[pl.ds(0, window), :] = from_left(0, 0)
+    far[pl.ds(window, window), :] = from_left(1, window)
 
     share = window // classes
     for flip in range(classes):
         base = pl.multiple_of((own ^ flip) * share, share)
+        place = pl.multiple_of(lax.rem(base, half), share)
+        sign = jnp.where(base < half, 1.0, -1.0)
+        real, imag = (
+            far[pl.ds(part * half + place, share), :] + sign * far[pl.ds(window + part * half + place, share), :]
+            for part in range(2)
+        )
         here = pl.ds(base, share)
-        real = far[here, pl.ds(0, window)]
-        imag = far[here, pl.ds(window, window)]
         probe_real = probe[0, here, :]
         probe_imag = probe[1, here, :]
         outs[flip][pl.ds(0, share), :] = probe_real * real - probe_imag * imag
@@ -217,9 +273,12 @@
     scratch = [
         pltpu.VMEM(((window + 32) * 2 * tiles + 8, LANES), F32),
         pltpu.VMEM((2, window, window), F32),
-        pltpu.VMEM((2 * window, 2 * window), BF16),
-        pltpu.VMEM((2 * window, 2 * window), BF16),
-        pltpu.VMEM((window, 2 * window), F32),
+        pltpu.VMEM((window, 2 * window), BF16),
+        pltpu.VMEM((window, 2 * window), BF16),
+        pltpu.VMEM((2 * window, window), BF16),
+        pltpu.VMEM((2 * window, window), BF16),
+        pltpu.VMEM((2 * window, window), F32),
+        pltpu.VMEM((window, window), F32),
     ]
     return kernel_call(
         functools.partial(wave_kernel, slot, window, classes, len(arrays) == 5),
@@ -228,7 +287,7 @@
         scalars,
         arrays,
         scratch,
-        96 * window**3,
+        48 * window**3,
     )
 
 

time: 51 us -> 48.8 us (0.957)
  Pallas kernels: 12.7 us -> 9.07 us
  starting transfers between devices: 16.5 us -> 18.7 us
  waiting for transfers between devices: 20.6 us -> 19.9 us
    pallas_call x6, Pallas kernels: 10.7 us -> 7.1 us  [kernel_call(): pl.pallas_call(body, out_shape=[pltpu.VMEM(shape, F32) for shape in out_s...]
    ppermute x3, starting transfers between devices: 6.28 us -> 8.54 us  [shifted(): return lax.ppermute(block, axis, route)]
    ppermute x7, waiting for transfers between devices: 19.5 us -> 18.8 us  [exchanged(): lax.ppermute(block, axis, [(i, i ^ flip) for i in range(lax.axis_size(axi...]
  transfers between devices with their start and end apart: 10 -> 10, of which waited for: 5 -> 6; matrix products, arithmetic and copies ran while one was open for 0% -> 0% of each run, Pallas kernels for 22% -> 16%
where the time goes in v6:
time: 48.8 us; the launch traced here: 48.6 us
  waiting for transfers between devices  19.9 us (41%)
  starting transfers between devices  18.7 us (38%)
  Pallas kernels  9.07 us (19%)
  other arithmetic  0.79 us (2%)
    ppermute x7, waiting for transfers between devices, exchanged(): lax.ppermute(block, axis, [(i, i ^ flip) for i in range(lax.axis_size(axi...  18.8 us
    ppermute x7, starting transfers between devices, exchanged(): lax.ppermute(block, axis, [(i, i ^ flip) for i in range(lax.axis_size(axi...  10.2 us
    ppermute x3, starting transfers between devices, shifted(): return lax.ppermute(block, axis, route)  8.54 us
    pallas_call x6, Pallas kernels, kernel_call(): pl.pallas_call(body, out_shape=[pltpu.VMEM(shape, F32) for shape in out_s...  7.1 us
    pallas_call x1, Pallas kernels, loaded(): pl.pallas_call(functools.partial(load_kernel, len(arrays)), out_shape=[pl...  1.97 us
    ppermute x3, waiting for transfers between devices, shifted(): return lax.ppermute(block, axis, route)  1.13 us
  transfers between devices with their start and end apart: 10, of which 6 were waited for; matrix products, arithmetic and copies ran while one was open for 0% of the time, Pallas kernels for 16%

profile of v6, /device:TPU:0, one launch (start us, length us, event | category | flops | bytes accessed | tf_op | source)
XLA Modules:
  0.0 48.6 jit_solution(11376570067383117126)
XLA Ops:
  0.0 0.7 %pick.1 = f32[8,128]{1,0:T(8,128)S(1)} custom-call(s32[2]{0:T(128)} %rows.5, s32[2]{0:T(128)} %cols.5), custom_call_target="tpu_custom_call" | custom-call | bytes 8192 | tf_op jit(solution)/shard_map/pick/pallas_call | solution.py:72
  0.7 2.4 %collective-permute-start.3 = (f32[8,128]{1,0:T(8,128)S(1)}, f32[8,128]{1,0:T(8,128)S(1)}, u32[]{:S(2)}, u32[]{:S(2)}) collective-permute-start(f32[8,128]{1,0:T(8,128)S(1)} %pick.1), channel_id=1, source_target_pairs={{0,8},{8,16},{16,24},{1,9},{9,17},{17,25},{2,10},{10,18},{18,26},{... | collective-permute-start | bytes 12296 | tf_op jit(solution)/shard_map/ppermute | solution.py:20
  3.1 2.0 %load.1 = (f32[4096,128]{1,0:T(8,128)S(1)}, f32[1024,128]{1,0:T(8,128)S(1)}, bf16[2,256,256]{2,1,0:T(8,128)(2,1)S(1)}, bf16[768,384]{1,0:T(8,128)(2,1)S(1)}) custom-call(f32[4096,128]{1,0:T(8,128)} %bitcast.15, f32[1024,128]{1,0:T(8,128)} %bitcast.16, bf16[2,256,256]{2,1,0:T(8,128)(2,1)} %refs_2_.1, bf16[768,384]{1,0:T(8,128)(2,1)} %constant.8.clone.refs_3_), custom_call_target="tpu_custom_call" | custom-call | tf_op jit(solution)/shard_map/load/pallas_call | solution.py:100
  5.1 0.0 copy-start
  5.1 0.0 copy-start.1
  5.1 0.0 collective-permute-done.3.wanted
  5.1 0.2 rim.1
  5.3 1.3 %collective-permute-start.4 = (f32[2,256,256]{2,1,0:T(8,128)S(1)}, f32[2,256,256]{2,1,0:T(8,128)S(1)}, u32[]{:S(2)}, u32[]{:S(2)}) collective-permute-start(f32[2,256,256]{2,1,0:T(8,128)S(1)} %rim.1), channel_id=1, source_target_pairs={{8,0},{16,8},{24,16},{9,1},{17,9},{25,17},{10,2},{18,10},{26,18},{... | collective-permute-start | bytes 1572872 | tf_op jit(solution)/shard_map/ppermute | solution.py:20
  6.6 0.0 copy-done
  6.6 0.0 copy-done.1
  6.6 2.8 %wave0.1 = (f32[136,256]{1,0:T(8,128)S(1)}, f32[136,256]{1,0:T(8,128)S(1)}, f32[136,256]{1,0:T(8,128)S(1)}, f32[136,256]{1,0:T(8,128)S(1)}) custom-call(s32[2]{0:T(128)S(1)} %copy-done, s32[2]{0:T(128)S(1)} %copy-done.1, f32[4096,128]{1,0:T(8,128)S(1)} %get-tuple-element.20.obj, f32[1024,128]{1,0:T(8,128)S(1)} %get-tuple-element.21.ill, ...), custom_call_target="tpu_custom_call" | custom-call | flops 805306368 | bytes 1114112 | tf_op jit(solution)/shard_map/wave0/pallas_call | solution.py:72
  9.4 2.4 %collective-permute-start = (f32[136,256]{1,0:T(8,128)S(1)}, f32[136,256]{1,0:T(8,128)S(1)}, u32[]{:S(2)}, u32[]{:S(2)}) collective-permute-start(f32[136,256]{1,0:T(8,128)S(1)} %get-tuple-element.25), channel_id=1, source_target_pairs={{0,1},{1,0},{2,3},{3,2},{4,5},{5,4},{6,7},{7,6},{8,9},{9,8},{10,11... | collective-permute-start | bytes 417800 | tf_op jit(solution)/shard_map/ppermute | solution.py:24
  11.8 1.6 %collective-permute-start.1 = (f32[136,256]{1,0:T(8,128)S(1)}, f32[136,256]{1,0:T(8,128)S(1)}, u32[]{:S(2)}, u32[]{:S(2)}) collective-permute-start(f32[136,256]{1,0:T(8,128)S(1)} %get-tuple-element.26), channel_id=1, source_target_pairs={{0,2},{1,3},{2,0},{3,1},{4,6},{5,7},{6,4},{7,5},{8,10},{9,11},{10,... | collective-permute-start | bytes 417800 | tf_op jit(solution)/shard_map/ppermute | solution.py:24
  13.3 0.0 collective-permute-start.2
  13.3 0.0 collective-permute-done.4.refs_0_
  13.4 2.8 %wave1.1 = (f32[136,256]{1,0:T(8,128)S(1)}, f32[136,256]{1,0:T(8,128)S(1)}, f32[136,256]{1,0:T(8,128)S(1)}, f32[136,256]{1,0:T(8,128)S(1)}) custom-call(s32[2]{0:T(128)S(1)} %copy-done, s32[2]{0:T(128)S(1)} %copy-done.1, f32[4096,128]{1,0:T(8,128)S(1)} %get-tuple-element.20.obj, f32[1024,128]{1,0:T(8,128)S(1)} %get-tuple-element.21.ill, ...), custom_call_target="tpu_custom_call" | custom-call | flops 805306368 | bytes 1114112 | tf_op jit(solution)/shard_map/wave1/pallas_call | solution.py:72
  16.2 2.0 %collective-permute-start.5 = (f32[136,256]{1,0:T(8,128)S(1)}, f32[136,256]{1,0:T(8,128)S(1)}, u32[]{:S(2)}, u32[]{:S(2)}) collective-permute-start(f32[136,256]{1,0:T(8,128)S(1)} %get-tuple-element.29), channel_id=1, source_target_pairs={{0,1},{1,0},{2,3},{3,2},{4,5},{5,4},{6,7},{7,6},{8,9},{9,8},{10,11... | collective-permute-start | bytes 417800 | tf_op jit(solution)/shard_map/ppermute | solution.py:24
  18.1 1.6 %collective-permute-start.6 = (f32[136,256]{1,0:T(8,128)S(1)}, f32[136,256]{1,0:T(8,128)S(1)}, u32[]{:S(2)}, u32[]{:S(2)}) collective-permute-start(f32[136,256]{1,0:T(8,128)S(1)} %get-tuple-element.30), channel_id=1, source_target_pairs={{0,2},{1,3},{2,0},{3,1},{4,6},{5,7},{6,4},{7,5},{8,10},{9,11},{10,... | collective-permute-start | bytes 417800 | tf_op jit(solution)/shard_map/ppermute | solution.py:24
  19.7 0.0 collective-permute-done.refs_1_
  19.7 0.0 collective-permute-start.7
  19.7 0.0 collective-permute-done.1.refs_2_
  19.7 0.5 %collective-permute-done.2.refs_3_ = f32[136,256]{1,0:T(8,128)S(1)} collective-permute-done((f32[136,256]{1,0:T(8,128)S(1)}, f32[136,256]{1,0:T(8,128)S(1)}, u32[]{:S(2)}, u32[]{:S(2)}) %collective-permute-start.2) | collective-permute-done | bytes 139296 | tf_op jit(solution)/shard_map/ppermute | solution.py:24
  20.3 0.2 sum0.1.acc
  20.5 2.0 %collective-permute-done.5.refs_1_ = f32[136,256]{1,0:T(8,128)S(1)} collective-permute-done((f32[136,256]{1,0:T(8,128)S(1)}, f32[136,256]{1,0:T(8,128)S(1)}, u32[]{:S(2)}, u32[]{:S(2)}) %collective-permute-start.5) | collective-permute-done | bytes 139296 | tf_op jit(solution)/shard_map/ppermute | solution.py:24
  22.5 0.7 %collective-permute-done.6.refs_2_ = f32[136,256]{1,0:T(8,128)S(1)} collective-permute-done((f32[136,256]{1,0:T(8,128)S(1)}, f32[136,256]{1,0:T(8,128)S(1)}, u32[]{:S(2)}, u32[]{:S(2)}) %collective-permute-start.6) | collective-permute-done | bytes 139296 | tf_op jit(solution)/shard_map/ppermute | solution.py:24
  23.2 2.8 %collective-permute-done.7.refs_3_ = f32[136,256]{1,0:T(8,128)S(1)} collective-permute-done((f32[136,256]{1,0:T(8,128)S(1)}, f32[136,256]{1,0:T(8,128)S(1)}, u32[]{:S(2)}, u32[]{:S(2)}) %collective-permute-start.7) | collective-permute-done | bytes 139296 | tf_op jit(solution)/shard_map/ppermute | solution.py:24
  26.0 0.4 sum1.1
  26.4 4.9 %collective-permute-start.8 = (f32[512,128]{1,0:T(8,128)S(1)}, f32[512,128]{1,0:T(8,128)S(1)}, u32[]{:S(2)}, u32[]{:S(2)}) collective-permute-start(f32[512,128]{1,0:T(8,128)S(1)} %get-tuple-element.34), channel_id=1, source_target_pairs={{0,8},{8,16},{16,24},{1,9},{9,17},{17,25},{2,10},{10,18},{18,26},{... | collective-permute-start | bytes 786440 | tf_op jit(solution)/shard_map/ppermute | solution.py:20
  31.3 1.1 %collective-permute-done.8 = f32[512,128]{1,0:T(8,128)S(1)} collective-permute-done((f32[512,128]{1,0:T(8,128)S(1)}, f32[512,128]{1,0:T(8,128)S(1)}, u32[]{:S(2)}, u32[]{:S(2)}) %collective-permute-start.8) | collective-permute-done | bytes 262176 | tf_op jit(solution)/shard_map/ppermute | solution.py:20
  32.5 2.7 %collective-permute-start.9 = (f32[512,128]{1,0:T(8,128)S(1)}, f32[512,128]{1,0:T(8,128)S(1)}, u32[]{:S(2)}, u32[]{:S(2)}) collective-permute-start(f32[512,128]{1,0:T(8,128)S(1)} %broadcast_select_fusion), channel_id=1, source_target_pairs={{0,4},{1,5},{2,6},{3,7},{4,0},{5,1},{6,2},{7,3},{8,12},{9,13},{10,... | collective-permute-start | bytes 786440 | tf_op jit(solution)/shard_map/ppermute | solution.py:24
  35.1 12.7 %collective-permute-done.9 = f32[512,128]{1,0:T(8,128)S(1)} collective-permute-done((f32[512,128]{1,0:T(8,128)S(1)}, f32[512,128]{1,0:T(8,128)S(1)}, u32[]{:S(2)}, u32[]{:S(2)}) %collective-permute-start.9) | collective-permute-done | bytes 262176 | tf_op jit(solution)/shard_map/ppermute | solution.py:24
  47.8 0.8 %select_add_fusion = f32[512,128]{1,0:T(8,128)} fusion(f32[512,128]{1,0:T(8,128)S(1)} %collective-permute-done.9, f32[512,128]{1,0:T(8,128)S(1)} %get-tuple-element.32, pred[]{:T(512)S(6)} %ge.3, f32[512,128]{1,0:T(8,128)S(1)} %get-tuple-element.33, f32[512,128]{1,0:T(8,128)S(1)} %collective-permute-done.8), kind=kLoop, calls=%fused_computation | loop fusion | flops 196608 | bytes 1310721 | tf_op jit(solution)/shard_map/add | solution.py:379
  (1 shorter events, 0.0 us)
Async XLA Ops:
  0.7 4.4 %collective-permute-start.3 = (f32[8,128]{1,0:T(8,128)S(1)}, f32[8,128]{1,0:T(8,128)S(1)}, u32[]{:S(2)}, u32[]{:S(2)}) collective-permute-start(f32[8,128]{1,0:T(8,128)S(1)} %pick.1), channel_id=1, source_target_pairs={{0,8},{8,16},{16,24},{1,9},{9,17},{17,25},{2,10},{10,18},{18,26},{... | collective-permute-start | bytes 12296 | tf_op jit(solution)/shard_map/ppermute | solution.py:20
  5.1 1.5 %copy-start = (s32[2]{0:T(128)S(1)}, s32[2]{0:T(128)}, u32[]{:S(2)}) copy-start(s32[2]{0:T(128)} %rows.5) | copy-start | bytes 28
  5.1 1.5 %copy-start.1 = (s32[2]{0:T(128)S(1)}, s32[2]{0:T(128)}, u32[]{:S(2)}) copy-start(s32[2]{0:T(128)} %cols.5) | copy-start | bytes 28
  5.3 8.1 %collective-permute-start.4 = (f32[2,256,256]{2,1,0:T(8,128)S(1)}, f32[2,256,256]{2,1,0:T(8,128)S(1)}, u32[]{:S(2)}, u32[]{:S(2)}) collective-permute-start(f32[2,256,256]{2,1,0:T(8,128)S(1)} %rim.1), channel_id=1, source_target_pairs={{8,0},{16,8},{24,16},{9,1},{17,9},{25,17},{10,2},{18,10},{26,18},{... | collective-permute-start | bytes 1572872 | tf_op jit(solution)/shard_map/ppermute | solution.py:20
  9.4 10.3 %collective-permute-start = (f32[136,256]{1,0:T(8,128)S(1)}, f32[136,256]{1,0:T(8,128)S(1)}, u32[]{:S(2)}, u32[]{:S(2)}) collective-permute-start(f32[136,256]{1,0:T(8,128)S(1)} %get-tuple-element.25), channel_id=1, source_target_pairs={{0,1},{1,0},{2,3},{3,2},{4,5},{5,4},{6,7},{7,6},{8,9},{9,8},{10,11... | collective-permute-start | bytes 417800 | tf_op jit(solution)/shard_map/ppermute | solution.py:24
  11.8 8.0 %collective-permute-start.1 = (f32[136,256]{1,0:T(8,128)S(1)}, f32[136,256]{1,0:T(8,128)S(1)}, u32[]{:S(2)}, u32[]{:S(2)}) collective-permute-start(f32[136,256]{1,0:T(8,128)S(1)} %get-tuple-element.26), channel_id=1, source_target_pairs={{0,2},{1,3},{2,0},{3,1},{4,6},{5,7},{6,4},{7,5},{8,10},{9,11},{10,... | collective-permute-start | bytes 417800 | tf_op jit(solution)/shard_map/ppermute | solution.py:24
  13.3 6.9 %collective-permute-start.2 = (f32[136,256]{1,0:T(8,128)S(1)}, f32[136,256]{1,0:T(8,128)S(1)}, u32[]{:S(2)}, u32[]{:S(2)}) collective-permute-start(f32[136,256]{1,0:T(8,128)S(1)} %get-tuple-element.27), channel_id=1, source_target_pairs={{0,3},{1,2},{2,1},{3,0},{4,7},{5,6},{6,5},{7,4},{8,11},{9,10},{10,... | collective-permute-start | bytes 417800 | tf_op jit(solution)/shard_map/ppermute | solution.py:24
  16.2 6.3 %collective-permute-start.5 = (f32[136,256]{1,0:T(8,128)S(1)}, f32[136,256]{1,0:T(8,128)S(1)}, u32[]{:S(2)}, u32[]{:S(2)}) collective-permute-start(f32[136,256]{1,0:T(8,128)S(1)} %get-tuple-element.29), channel_id=1, source_target_pairs={{0,1},{1,0},{2,3},{3,2},{4,5},{5,4},{6,7},{7,6},{8,9},{9,8},{10,11... | collective-permute-start | bytes 417800 | tf_op jit(solution)/shard_map/ppermute | solution.py:24
  18.1 5.1 %collective-permute-start.6 = (f32[136,256]{1,0:T(8,128)S(1)}, f32[136,256]{1,0:T(8,128)S(1)}, u32[]{:S(2)}, u32[]{:S(2)}) collective-permute-start(f32[136,256]{1,0:T(8,128)S(1)} %get-tuple-element.30), channel_id=1, source_target_pairs={{0,2},{1,3},{2,0},{3,1},{4,6},{5,7},{6,4},{7,5},{8,10},{9,11},{10,... | collective-permute-start | bytes 417800 | tf_op jit(solution)/shard_map/ppermute | solution.py:24
  19.7 6.3 %collective-permute-start.7 = (f32[136,256]{1,0:T(8,128)S(1)}, f32[136,256]{1,0:T(8,128)S(1)}, u32[]{:S(2)}, u32[]{:S(2)}) collective-permute-start(f32[136,256]{1,0:T(8,128)S(1)} %get-tuple-element.31), channel_id=1, source_target_pairs={{0,3},{1,2},{2,1},{3,0},{4,7},{5,6},{6,5},{7,4},{8,11},{9,10},{10,... | collective-permute-start | bytes 417800 | tf_op jit(solution)/shard_map/ppermute | solution.py:24
  26.4 6.0 %collective-permute-start.8 = (f32[512,128]{1,0:T(8,128)S(1)}, f32[512,128]{1,0:T(8,128)S(1)}, u32[]{:S(2)}, u32[]{:S(2)}) collective-permute-start(f32[512,128]{1,0:T(8,128)S(1)} %get-tuple-element.34), channel_id=1, source_target_pairs={{0,8},{8,16},{16,24},{1,9},{9,17},{17,25},{2,10},{10,18},{18,26},{... | collective-permute-start | bytes 786440 | tf_op jit(solution)/shard_map/ppermute | solution.py:20
  32.5 15.4 %collective-permute-start.9 = (f32[512,128]{1,0:T(8,128)S(1)}, f32[512,128]{1,0:T(8,128)S(1)}, u32[]{:S(2)}, u32[]{:S(2)}) collective-permute-start(f32[512,128]{1,0:T(8,128)S(1)} %broadcast_select_fusion), channel_id=1, source_target_pairs={{0,4},{1,5},{2,6},{3,7},{4,0},{5,1},{6,2},{7,3},{8,12},{9,13},{10,... | collective-permute-start | bytes 786440 | tf_op jit(solution)/shard_map/ppermute | solution.py:24

commit v7 on v6

--- a/solution.py
+++ b/solution.py
@@ -8,6 +8,7 @@
 from jax.experimental import pallas as pl
 from jax.experimental.pallas import tpu as pltpu
 from jax.sharding import PartitionSpec as P
+
 
 LANES = 128
 F32 = jnp.float32
@@ -65,7 +66,7 @@
     return pltpu.with_memory_space_constraint(array, pltpu.VMEM)
 
 
-def kernel_call(body, name, out_shapes, scalars, arrays, scratch=(), flops=0):
+def kernel_call(body, out_shapes, scalars, arrays, scratch=(), flops=0):
     smem = pl.BlockSpec(memory_space=pltpu.SMEM)
     vmem = pl.BlockSpec(memory_space=pltpu.VMEM)
     moved = sum(4 * math.prod(shape) for shape in out_shapes)
@@ -77,7 +78,6 @@
         scratch_shapes=scratch,
         cost_estimate=pl.CostEstimate(flops=flops, transcendentals=0, bytes_accessed=2 * moved),
         compiler_params=pltpu.CompilerParams(vmem_limit_bytes=16 << 20),
-        name=name,
     )(*scalars, *[in_vmem(array) for array in arrays])
 
 
@@ -282,7 +282,6 @@
     ]
     return kernel_call(
         functools.partial(wave_kernel, slot, window, classes, len(arrays) == 5),
-        "wave" + str(slot),
         [(2 * share + 8, window)] * classes,
         scalars,
         arrays,
@@ -351,10 +350,10 @@
     scalars = (row_offset, col_offset)
 
     remote = tuple(pltpu.with_memory_space_constraint(scalar, pltpu.HBM) for scalar in scalars)
-    (wanted,) = kernel_call(functools.partial(pick_kernel, window), "pick", [(8, LANES)], remote, [])
+    (wanted,) = kernel_call(functools.partial(pick_kernel, window), [(8, LANES)], remote, [])
     wanted = shifted(wanted, "tile", 1)
     obj, ill, amps, table = loaded([linear(object_field), linear(illumination), amplitudes, split_tables(window)])
-    (rim,) = kernel_call(functools.partial(rim_kernel, window), "rim", [(2, window, window)], (), [wanted, obj])
+    (rim,) = kernel_call(functools.partial(rim_kernel, window), [(2, window, window)], (), [wanted, obj])
     rim = shifted(rim, "tile", -1)
 
     def spread(pieces):
@@ -362,21 +361,22 @@
         return [pieces[0]] + [moved[d] for d in range(1, classes)]
 
     near = spread(wave(0, window, classes, scalars, [obj, ill, amps, table]))
-    (acc,) = kernel_call(
-        functools.partial(first_sum_kernel, window, classes), "sum0", [(2, 2, share, columns)], (), near
-    )
+    (acc,) = kernel_call(functools.partial(first_sum_kernel, window, classes), [(2, 2, share, columns)], (), near)
     late = spread(wave(1, window, classes, scalars, [obj, ill, amps, table, rim]))
     top, middle, spilled = kernel_call(
-        functools.partial(second_sum_kernel, window, classes),
-        "sum1",
-        [(share * 4 * tiles, LANES)] * 3,
-        (),
-        [acc, *late],
+        functools.partial(second_sum_kernel, window, classes), [(share * 4 * tiles, LANES)] * 3, (), [acc, *late]
     )
-    top = top + shifted(spilled, "tile", 1)
     is_upper = lax.axis_index("pos") >= classes
-    received = exchanged(jnp.where(is_upper, top, middle), "pos", classes)
-    result = jnp.where(is_upper, middle, top) + received
+    bands = range(lax.axis_size("tile"))
+    arrived = 0.0
+    for group in ((0, 3), (1, 2)):
+        members = [band for band in bands if band % 4 in group]
+        top = top + lax.ppermute(spilled, "tile", [(band - 1, band) for band in members if band > 0])
+        outgoing = jnp.where(is_upper, top, middle)
+        outgoing, spilled = lax.optimization_barrier((outgoing, spilled))
+        route = [(band * ways + i, band * ways + (i ^ classes)) for band in members for i in range(ways)]
+        arrived = arrived + lax.ppermute(outgoing, ("tile", "pos"), route)
+    result = jnp.where(is_upper, middle, top) + arrived
     return unlinear(result, share, columns)
 
 
@@ -389,6 +389,5 @@
         P(("tile", "pos")),
     )
     out_specs = P(("tile", "pos"), None, None)
-    return jax.shard_map(
-        on_device, mesh=mesh, in_specs=in_specs, out_specs=out_specs, check_vma=False
-    )
+
+    return jax.shard_map(on_device, mesh=mesh, in_specs=in_specs, out_specs=out_specs, check_vma=False)

time: 48.8 us -> 50.8 us (1.041)
  the two profiles are of different devices: /device:TPU:0 before, /device:TPU:4 now
where the time goes in v7:
time: 50.8 us; the launch traced here: 50.6 us
  waiting for transfers between devices  21 us (41%)
  starting transfers between devices  19.5 us (38%)
  Pallas kernels  9.08 us (18%)
  other arithmetic  0.86 us (2%)
    ppermute x2, waiting for transfers between devices, on_device(): arrived = arrived + lax.ppermute(outgoing, ('tile', 'pos'), route)  7.46 us
    ppermute x6, starting transfers between devices, exchanged(): lax.ppermute(block, axis, [(i, i ^ flip) for i in range(lax.axis_size(axi...  7.11 us
    pallas_call x6, Pallas kernels, kernel_call(): pl.pallas_call(body, out_shape=[pltpu.VMEM(shape, F32) for shape in out_s...  7.11 us
    ppermute x2, waiting for transfers between devices, on_device(): lax.ppermute(spilled, 'tile', [(band - 1, band) for band in members if ba...  6.83 us
    ppermute x6, waiting for transfers between devices, exchanged(): lax.ppermute(block, axis, [(i, i ^ flip) for i in range(lax.axis_size(axi...  5.39 us
    ppermute x2, starting transfers between devices, on_device(): arrived = arrived + lax.ppermute(outgoing, ('tile', 'pos'), route)  5.18 us
    ppermute x2, starting transfers between devices, shifted(): return lax.ppermute(block, axis, route)  4.58 us
    ppermute x2, starting transfers between devices, on_device(): lax.ppermute(spilled, 'tile', [(band - 1, band) for band in members if ba...  2.6 us
  transfers between devices with their start and end apart: 12, of which 8 were waited for; matrix products, arithmetic and copies ran while one was open for 0% of the time, Pallas kernels for 15%

profile of v7, /device:TPU:4, one launch (start us, length us, event | category | flops | bytes accessed | tf_op | source)
XLA Modules:
  0.0 50.6 jit_solution(17717326999092205562)
XLA Ops:
  0.0 0.7 %shard_map.66 = f32[8,128]{1,0:T(8,128)S(1)} custom-call(s32[2]{0:T(128)} %rows.5, s32[2]{0:T(128)} %cols.5), custom_call_target="tpu_custom_call" | custom-call | bytes 8192 | tf_op jit(solution)/shard_map/pallas_call | solution.py:73
  0.7 1.9 %collective-permute-start.3 = (f32[8,128]{1,0:T(8,128)S(1)}, f32[8,128]{1,0:T(8,128)S(1)}, u32[]{:S(2)}, u32[]{:S(2)}) collective-permute-start(f32[8,128]{1,0:T(8,128)S(1)} %shard_map.66), channel_id=1, source_target_pairs={{0,8},{8,16},{16,24},{1,9},{9,17},{17,25},{2,10},{10,18},{18,26},{... | collective-permute-start | bytes 12296 | tf_op jit(solution)/shard_map/ppermute | solution.py:21
  2.6 2.0 %load.1 = (f32[4096,128]{1,0:T(8,128)S(1)}, f32[1024,128]{1,0:T(8,128)S(1)}, bf16[2,256,256]{2,1,0:T(8,128)(2,1)S(1)}, bf16[768,384]{1,0:T(8,128)(2,1)S(1)}) custom-call(f32[4096,128]{1,0:T(8,128)} %bitcast.15, f32[1024,128]{1,0:T(8,128)} %bitcast.16, bf16[2,256,256]{2,1,0:T(8,128)(2,1)} %refs_2_.1, bf16[768,384]{1,0:T(8,128)(2,1)} %constant.8.clone.refs_3_), custom_call_target="tpu_custom_call" | custom-call | tf_op jit(solution)/shard_map/load/pallas_call | solution.py:100
  4.6 0.0 copy-start
  4.6 0.0 copy-start.1
  4.6 1.0 %collective-permute-done.3.wanted = f32[8,128]{1,0:T(8,128)S(1)} collective-permute-done((f32[8,128]{1,0:T(8,128)S(1)}, f32[8,128]{1,0:T(8,128)S(1)}, u32[]{:S(2)}, u32[]{:S(2)}) %collective-permute-start.3) | collective-permute-done | bytes 4128 | tf_op jit(solution)/shard_map/ppermute | solution.py:21
  5.6 0.2 shard_map.67
  5.8 2.7 %collective-permute-start.4 = (f32[2,256,256]{2,1,0:T(8,128)S(1)}, f32[2,256,256]{2,1,0:T(8,128)S(1)}, u32[]{:S(2)}, u32[]{:S(2)}) collective-permute-start(f32[2,256,256]{2,1,0:T(8,128)S(1)} %shard_map.67), channel_id=1, source_target_pairs={{8,0},{16,8},{24,16},{9,1},{17,9},{25,17},{10,2},{18,10},{26,18},{... | collective-permute-start | bytes 1572872 | tf_op jit(solution)/shard_map/ppermute | solution.py:21
  8.5 2.8 %shard_map.64 = (f32[136,256]{1,0:T(8,128)S(1)}, f32[136,256]{1,0:T(8,128)S(1)}, f32[136,256]{1,0:T(8,128)S(1)}, f32[136,256]{1,0:T(8,128)S(1)}) custom-call(s32[2]{0:T(128)S(1)} %copy-done, s32[2]{0:T(128)S(1)} %copy-done.1, f32[4096,128]{1,0:T(8,128)S(1)} %get-tuple-element.23.obj, f32[1024,128]{1,0:T(8,128)S(1)} %get-tuple-element.24.ill, ...), custom_call_target="tpu_custom_call" | custom-call | flops 805306368 | bytes 1114112 | tf_op jit(solution)/shard_map/pallas_call | solution.py:73
  11.3 1.6 %collective-permute-start = (f32[136,256]{1,0:T(8,128)S(1)}, f32[136,256]{1,0:T(8,128)S(1)}, u32[]{:S(2)}, u32[]{:S(2)}) collective-permute-start(f32[136,256]{1,0:T(8,128)S(1)} %get-tuple-element.28), channel_id=1, source_target_pairs={{0,1},{1,0},{2,3},{3,2},{4,5},{5,4},{6,7},{7,6},{8,9},{9,8},{10,11... | collective-permute-start | bytes 417800 | tf_op jit(solution)/shard_map/ppermute | solution.py:25
  12.8 1.6 %collective-permute-start.1 = (f32[136,256]{1,0:T(8,128)S(1)}, f32[136,256]{1,0:T(8,128)S(1)}, u32[]{:S(2)}, u32[]{:S(2)}) collective-permute-start(f32[136,256]{1,0:T(8,128)S(1)} %get-tuple-element.29), channel_id=1, source_target_pairs={{0,2},{1,3},{2,0},{3,1},{4,6},{5,7},{6,4},{7,5},{8,10},{9,11},{10,... | collective-permute-start | bytes 417800 | tf_op jit(solution)/shard_map/ppermute | solution.py:25
  14.4 0.4 collective-permute-start.2
  14.8 0.3 collective-permute-done.4.refs_0_
  15.1 2.8 %shard_map.68 = (f32[136,256]{1,0:T(8,128)S(1)}, f32[136,256]{1,0:T(8,128)S(1)}, f32[136,256]{1,0:T(8,128)S(1)}, f32[136,256]{1,0:T(8,128)S(1)}) custom-call(s32[2]{0:T(128)S(1)} %copy-done, s32[2]{0:T(128)S(1)} %copy-done.1, f32[4096,128]{1,0:T(8,128)S(1)} %get-tuple-element.23.obj, f32[1024,128]{1,0:T(8,128)S(1)} %get-tuple-element.24.ill, ...), custom_call_target="tpu_custom_call" | custom-call | flops 805306368 | bytes 1114112 | tf_op jit(solution)/shard_map/pallas_call | solution.py:73
  18.0 1.5 %collective-permute-start.5 = (f32[136,256]{1,0:T(8,128)S(1)}, f32[136,256]{1,0:T(8,128)S(1)}, u32[]{:S(2)}, u32[]{:S(2)}) collective-permute-start(f32[136,256]{1,0:T(8,128)S(1)} %get-tuple-element.32), channel_id=1, source_target_pairs={{0,1},{1,0},{2,3},{3,2},{4,5},{5,4},{6,7},{7,6},{8,9},{9,8},{10,11... | collective-permute-start | bytes 417800 | tf_op jit(solution)/shard_map/ppermute | solution.py:25
  19.5 1.6 %collective-permute-start.6 = (f32[136,256]{1,0:T(8,128)S(1)}, f32[136,256]{1,0:T(8,128)S(1)}, u32[]{:S(2)}, u32[]{:S(2)}) collective-permute-start(f32[136,256]{1,0:T(8,128)S(1)} %get-tuple-element.33), channel_id=1, source_target_pairs={{0,2},{1,3},{2,0},{3,1},{4,6},{5,7},{6,4},{7,5},{8,10},{9,11},{10,... | collective-permute-start | bytes 417800 | tf_op jit(solution)/shard_map/ppermute | solution.py:25
  21.1 0.4 collective-permute-start.7
  21.5 0.0 collective-permute-done.1.refs_2_
  21.5 0.0 collective-permute-done.2.refs_3_
  21.5 0.2 shard_map.65.acc
  21.8 3.6 %collective-permute-done.5.refs_1_ = f32[136,256]{1,0:T(8,128)S(1)} collective-permute-done((f32[136,256]{1,0:T(8,128)S(1)}, f32[136,256]{1,0:T(8,128)S(1)}, u32[]{:S(2)}, u32[]{:S(2)}) %collective-permute-start.5) | collective-permute-done | bytes 139296 | tf_op jit(solution)/shard_map/ppermute | solution.py:25
  25.3 0.1 collective-permute-done.6.refs_2_
  25.4 1.7 %collective-permute-done.7.refs_3_ = f32[136,256]{1,0:T(8,128)S(1)} collective-permute-done((f32[136,256]{1,0:T(8,128)S(1)}, f32[136,256]{1,0:T(8,128)S(1)}, u32[]{:S(2)}, u32[]{:S(2)}) %collective-permute-start.7) | collective-permute-done | bytes 139296 | tf_op jit(solution)/shard_map/ppermute | solution.py:25
  27.1 0.4 shard_map.69
  27.6 1.3 %collective-permute-start.8 = (f32[512,128]{1,0:T(8,128)S(1)}, f32[512,128]{1,0:T(8,128)S(1)}, u32[]{:S(2)}, u32[]{:S(2)}) collective-permute-start(f32[512,128]{1,0:T(8,128)S(1)} %get-tuple-element.38), channel_id=1, source_target_pairs={{16,24},{17,25},{18,26},{19,27},{20,28},{21,29},{22,30},{23,31}} | collective-permute-start | bytes 786440 | tf_op jit(solution)/shard_map/ppermute | solution.py:374
  28.9 1.1 %collective-permute-done.8 = f32[512,128]{1,0:T(8,128)S(1)} collective-permute-done((f32[512,128]{1,0:T(8,128)S(1)}, f32[512,128]{1,0:T(8,128)S(1)}, u32[]{:S(2)}, u32[]{:S(2)}) %collective-permute-start.8) | collective-permute-done | bytes 262176 | tf_op jit(solution)/shard_map/ppermute | solution.py:374
  30.1 1.3 %collective-permute-start.9 = (f32[512,128]{1,0:T(8,128)S(1)}, f32[512,128]{1,0:T(8,128)S(1)}, u32[]{:S(2)}, u32[]{:S(2)}) collective-permute-start(f32[512,128]{1,0:T(8,128)S(1)} %get-tuple-element.38), channel_id=1, source_target_pairs={{0,8},{8,16},{1,9},{9,17},{2,10},{10,18},{3,11},{11,19},{4,12},{12... | collective-permute-start | bytes 786440 | tf_op jit(solution)/shard_map/ppermute | solution.py:374
  31.4 0.7 %collective-permute-start.10 = (f32[512,128]{1,0:T(8,128)S(1)}, f32[512,128]{1,0:T(8,128)S(1)}, u32[]{:S(2)}, u32[]{:S(2)}) collective-permute-start(f32[512,128]{1,0:T(8,128)S(1)} %get-tuple-element.39), channel_id=1, source_target_pairs={{0,4},{1,5},{2,6},{3,7},{4,0},{5,1},{6,2},{7,3},{24,28},{25,29},{2... | collective-permute-start | bytes 786440 | tf_op jit(solution)/shard_map/ppermute | solution.py:378
  32.1 5.7 %collective-permute-done.9 = f32[512,128]{1,0:T(8,128)S(1)} collective-permute-done((f32[512,128]{1,0:T(8,128)S(1)}, f32[512,128]{1,0:T(8,128)S(1)}, u32[]{:S(2)}, u32[]{:S(2)}) %collective-permute-start.9) | collective-permute-done | bytes 262176 | tf_op jit(solution)/shard_map/ppermute | solution.py:374
  37.8 4.5 %collective-permute-start.11 = (f32[512,128]{1,0:T(8,128)S(1)}, f32[512,128]{1,0:T(8,128)S(1)}, u32[]{:S(2)}, u32[]{:S(2)}) collective-permute-start(f32[512,128]{1,0:T(8,128)S(1)} %broadcast_select_fusion), channel_id=1, source_target_pairs={{8,12},{9,13},{10,14},{11,15},{12,8},{13,9},{14,10},{15,11},{16,20... | collective-permute-start | bytes 786440 | tf_op jit(solution)/shard_map/ppermute | solution.py:378
  42.3 7.5 %collective-permute-done.11 = f32[512,128]{1,0:T(8,128)S(1)} collective-permute-done((f32[512,128]{1,0:T(8,128)S(1)}, f32[512,128]{1,0:T(8,128)S(1)}, u32[]{:S(2)}, u32[]{:S(2)}) %collective-permute-start.11) | collective-permute-done | bytes 262176 | tf_op jit(solution)/shard_map/ppermute | solution.py:378
  49.8 0.8 %add_add_fusion = f32[512,128]{1,0:T(8,128)} fusion(f32[512,128]{1,0:T(8,128)S(1)} %collective-permute-done.10, f32[512,128]{1,0:T(8,128)S(1)} %collective-permute-done.11, f32[512,128]{1,0:T(8,128)S(1)} %get-tuple-element.35, pred[]{:T(512)S(6)} %ge.3, f32[512,128]{1,0:T(8,128)S(1)} %get-tuple-element.42, f32[512,128]{1,0:T(8,128)S(1)} %collective-permute-done.9), kind=kLoop, calls=%fused_computation | loop fusion | flops 262144 | bytes 1572865 | tf_op jit(solution)/shard_map/add | solution.py:379
  (6 shorter events, 0.1 us)
Async XLA Ops:
  0.7 4.9 %collective-permute-start.3 = (f32[8,128]{1,0:T(8,128)S(1)}, f32[8,128]{1,0:T(8,128)S(1)}, u32[]{:S(2)}, u32[]{:S(2)}) collective-permute-start(f32[8,128]{1,0:T(8,128)S(1)} %shard_map.66), channel_id=1, source_target_pairs={{0,8},{8,16},{16,24},{1,9},{9,17},{17,25},{2,10},{10,18},{18,26},{... | collective-permute-start | bytes 12296 | tf_op jit(solution)/shard_map/ppermute | solution.py:21
  4.6 3.9 %copy-start = (s32[2]{0:T(128)S(1)}, s32[2]{0:T(128)}, u32[]{:S(2)}) copy-start(s32[2]{0:T(128)} %rows.5) | copy-start | bytes 28
  4.6 3.9 %copy-start.1 = (s32[2]{0:T(128)S(1)}, s32[2]{0:T(128)}, u32[]{:S(2)}) copy-start(s32[2]{0:T(128)} %cols.5) | copy-start | bytes 28
  5.8 9.3 %collective-permute-start.4 = (f32[2,256,256]{2,1,0:T(8,128)S(1)}, f32[2,256,256]{2,1,0:T(8,128)S(1)}, u32[]{:S(2)}, u32[]{:S(2)}) collective-permute-start(f32[2,256,256]{2,1,0:T(8,128)S(1)} %shard_map.67), channel_id=1, source_target_pairs={{8,0},{16,8},{24,16},{9,1},{17,9},{25,17},{10,2},{18,10},{26,18},{... | collective-permute-start | bytes 1572872 | tf_op jit(solution)/shard_map/ppermute | solution.py:21
  11.3 9.8 %collective-permute-start = (f32[136,256]{1,0:T(8,128)S(1)}, f32[136,256]{1,0:T(8,128)S(1)}, u32[]{:S(2)}, u32[]{:S(2)}) collective-permute-start(f32[136,256]{1,0:T(8,128)S(1)} %get-tuple-element.28), channel_id=1, source_target_pairs={{0,1},{1,0},{2,3},{3,2},{4,5},{5,4},{6,7},{7,6},{8,9},{9,8},{10,11... | collective-permute-start | bytes 417800 | tf_op jit(solution)/shard_map/ppermute | solution.py:25
  12.8 8.7 %collective-permute-start.1 = (f32[136,256]{1,0:T(8,128)S(1)}, f32[136,256]{1,0:T(8,128)S(1)}, u32[]{:S(2)}, u32[]{:S(2)}) collective-permute-start(f32[136,256]{1,0:T(8,128)S(1)} %get-tuple-element.29), channel_id=1, source_target_pairs={{0,2},{1,3},{2,0},{3,1},{4,6},{5,7},{6,4},{7,5},{8,10},{9,11},{10,... | collective-permute-start | bytes 417800 | tf_op jit(solution)/shard_map/ppermute | solution.py:25
  14.4 7.1 %collective-permute-start.2 = (f32[136,256]{1,0:T(8,128)S(1)}, f32[136,256]{1,0:T(8,128)S(1)}, u32[]{:S(2)}, u32[]{:S(2)}) collective-permute-start(f32[136,256]{1,0:T(8,128)S(1)} %get-tuple-element.30), channel_id=1, source_target_pairs={{0,3},{1,2},{2,1},{3,0},{4,7},{5,6},{6,5},{7,4},{8,11},{9,10},{10,... | collective-permute-start | bytes 417800 | tf_op jit(solution)/shard_map/ppermute | solution.py:25
  18.0 7.4 %collective-permute-start.5 = (f32[136,256]{1,0:T(8,128)S(1)}, f32[136,256]{1,0:T(8,128)S(1)}, u32[]{:S(2)}, u32[]{:S(2)}) collective-permute-start(f32[136,256]{1,0:T(8,128)S(1)} %get-tuple-element.32), channel_id=1, source_target_pairs={{0,1},{1,0},{2,3},{3,2},{4,5},{5,4},{6,7},{7,6},{8,9},{9,8},{10,11... | collective-permute-start | bytes 417800 | tf_op jit(solution)/shard_map/ppermute | solution.py:25
  19.5 5.9 %collective-permute-start.6 = (f32[136,256]{1,0:T(8,128)S(1)}, f32[136,256]{1,0:T(8,128)S(1)}, u32[]{:S(2)}, u32[]{:S(2)}) collective-permute-start(f32[136,256]{1,0:T(8,128)S(1)} %get-tuple-element.33), channel_id=1, source_target_pairs={{0,2},{1,3},{2,0},{3,1},{4,6},{5,7},{6,4},{7,5},{8,10},{9,11},{10,... | collective-permute-start | bytes 417800 | tf_op jit(solution)/shard_map/ppermute | solution.py:25
  21.1 6.0 %collective-permute-start.7 = (f32[136,256]{1,0:T(8,128)S(1)}, f32[136,256]{1,0:T(8,128)S(1)}, u32[]{:S(2)}, u32[]{:S(2)}) collective-permute-start(f32[136,256]{1,0:T(8,128)S(1)} %get-tuple-element.34), channel_id=1, source_target_pairs={{0,3},{1,2},{2,1},{3,0},{4,7},{5,6},{6,5},{7,4},{8,11},{9,10},{10,... | collective-permute-start | bytes 417800 | tf_op jit(solution)/shard_map/ppermute | solution.py:25
  27.6 2.4 %collective-permute-start.8 = (f32[512,128]{1,0:T(8,128)S(1)}, f32[512,128]{1,0:T(8,128)S(1)}, u32[]{:S(2)}, u32[]{:S(2)}) collective-permute-start(f32[512,128]{1,0:T(8,128)S(1)} %get-tuple-element.38), channel_id=1, source_target_pairs={{16,24},{17,25},{18,26},{19,27},{20,28},{21,29},{22,30},{23,31}} | collective-permute-start | bytes 786440 | tf_op jit(solution)/shard_map/ppermute | solution.py:374
  30.1 7.7 %collective-permute-start.9 = (f32[512,128]{1,0:T(8,128)S(1)}, f32[512,128]{1,0:T(8,128)S(1)}, u32[]{:S(2)}, u32[]{:S(2)}) collective-permute-start(f32[512,128]{1,0:T(8,128)S(1)} %get-tuple-element.38), channel_id=1, source_target_pairs={{0,8},{8,16},{1,9},{9,17},{2,10},{10,18},{3,11},{11,19},{4,12},{12... | collective-permute-start | bytes 786440 | tf_op jit(solution)/shard_map/ppermute | solution.py:374
  31.4 10.9 %collective-permute-start.10 = (f32[512,128]{1,0:T(8,128)S(1)}, f32[512,128]{1,0:T(8,128)S(1)}, u32[]{:S(2)}, u32[]{:S(2)}) collective-permute-start(f32[512,128]{1,0:T(8,128)S(1)} %get-tuple-element.39), channel_id=1, source_target_pairs={{0,4},{1,5},{2,6},{3,7},{4,0},{5,1},{6,2},{7,3},{24,28},{25,29},{2... | collective-permute-start | bytes 786440 | tf_op jit(solution)/shard_map/ppermute | solution.py:378
  37.8 12.0 %collective-permute-start.11 = (f32[512,128]{1,0:T(8,128)S(1)}, f32[512,128]{1,0:T(8,128)S(1)}, u32[]{:S(2)}, u32[]{:S(2)}) collective-permute-start(f32[512,128]{1,0:T(8,128)S(1)} %broadcast_select_fusion), channel_id=1, source_target_pairs={{8,12},{9,13},{10,14},{11,15},{12,8},{13,9},{14,10},{15,11},{16,20... | collective-permute-start | bytes 786440 | tf_op jit(solution)/shard_map/ppermute | solution.py:378

commit v8 on v6

--- a/solution.py
+++ b/solution.py
@@ -15,9 +15,8 @@
 
 
 def shifted(block, axis, distance):
-    devices = range(lax.axis_size(axis))
-    route = [(i - distance, i) for i in devices if i - distance in devices]
-    return lax.ppermute(block, axis, route)
+    devices = lax.axis_size(axis)
+    return lax.ppermute(block, axis, [((i - distance) % devices, i) for i in range(devices)])
 
 
 def exchanged(block, axis, flip):

time: 48.8 us -> 47.8 us (0.980)
  starting transfers between devices: 18.7 us -> 12.7 us
  waiting for transfers between devices: 19.9 us -> 25 us
    ppermute x3, starting transfers between devices: 8.54 us -> 1.74 us  [shifted(): lax.ppermute(block, axis, [((i - distance) % devices, i) for i in range(d...]
    ppermute x3, waiting for transfers between devices: 1.13 us -> 6.69 us  [shifted(): lax.ppermute(block, axis, [((i - distance) % devices, i) for i in range(d...]
    ppermute x7, starting transfers between devices: 10.2 us -> 11 us  [exchanged(): lax.ppermute(block, axis, [(i, i ^ flip) for i in range(lax.axis_size(axi...]
    ppermute x7, waiting for transfers between devices: 18.8 us -> 18.3 us  [exchanged(): lax.ppermute(block, axis, [(i, i ^ flip) for i in range(lax.axis_size(axi...]
  transfers between devices with their start and end apart: 10 -> 10, of which waited for: 6 -> 7; matrix products, arithmetic and copies ran while one was open for 0% -> 0% of each run, Pallas kernels for 16% -> 16%
where the time goes in v8:
time: 47.8 us; the launch traced here: 47.6 us
  waiting for transfers between devices  25 us (52%)
  starting transfers between devices  12.7 us (27%)
  Pallas kernels  9.06 us (19%)
  other arithmetic  0.79 us (2%)
    ppermute x7, waiting for transfers between devices, exchanged(): lax.ppermute(block, axis, [(i, i ^ flip) for i in range(lax.axis_size(axi...  18.3 us
    ppermute x7, starting transfers between devices, exchanged(): lax.ppermute(block, axis, [(i, i ^ flip) for i in range(lax.axis_size(axi...  11 us
    pallas_call x6, Pallas kernels, kernel_call(): pl.pallas_call(body, out_shape=[pltpu.VMEM(shape, F32) for shape in out_s...  7.1 us
    ppermute x3, waiting for transfers between devices, shifted(): lax.ppermute(block, axis, [((i - distance) % devices, i) for i in range(d...  6.69 us
    pallas_call x1, Pallas kernels, loaded(): pl.pallas_call(functools.partial(load_kernel, len(arrays)), out_shape=[pl...  1.96 us
    ppermute x3, starting transfers between devices, shifted(): lax.ppermute(block, axis, [((i - distance) % devices, i) for i in range(d...  1.74 us
  transfers between devices with their start and end apart: 10, of which 7 were waited for; matrix products, arithmetic and copies ran while one was open for 0% of the time, Pallas kernels for 16%

profile of v8, /device:TPU:0, one launch (start us, length us, event | category | flops | bytes accessed | tf_op | source)
XLA Modules:
  0.0 47.6 jit_solution(10968272823417421616)
XLA Ops:
  0.0 0.7 %pick.1 = f32[8,128]{1,0:T(8,128)S(1)} custom-call(s32[2]{0:T(128)} %rows.5, s32[2]{0:T(128)} %cols.5), custom_call_target="tpu_custom_call" | custom-call | bytes 8192 | tf_op jit(solution)/shard_map/pick/pallas_call | solution.py:71
  0.7 0.5 %collective-permute-start.3 = (f32[8,128]{1,0:T(8,128)S(1)}, f32[8,128]{1,0:T(8,128)S(1)}, u32[]{:S(2)}, u32[]{:S(2)}) collective-permute-start(f32[8,128]{1,0:T(8,128)S(1)} %pick.1), channel_id=1, source_target_pairs={{24,0},{0,8},{8,16},{16,24},{25,1},{1,9},{9,17},{17,25},{26,2},{2,... | collective-permute-start | bytes 12296 | tf_op jit(solution)/shard_map/ppermute | solution.py:19
  1.2 2.0 %load.1 = (f32[4096,128]{1,0:T(8,128)S(1)}, f32[1024,128]{1,0:T(8,128)S(1)}, bf16[2,256,256]{2,1,0:T(8,128)(2,1)S(1)}, bf16[768,384]{1,0:T(8,128)(2,1)S(1)}) custom-call(f32[4096,128]{1,0:T(8,128)} %bitcast.15, f32[1024,128]{1,0:T(8,128)} %bitcast.16, bf16[2,256,256]{2,1,0:T(8,128)(2,1)} %refs_2_.1, bf16[768,384]{1,0:T(8,128)(2,1)} %constant.8.clone.refs_3_), custom_call_target="tpu_custom_call" | custom-call | tf_op jit(solution)/shard_map/load/pallas_call | solution.py:99
  3.2 0.0 copy-start
  3.2 0.0 copy-start.1
  3.2 1.2 %collective-permute-done.3.wanted = f32[8,128]{1,0:T(8,128)S(1)} collective-permute-done((f32[8,128]{1,0:T(8,128)S(1)}, f32[8,128]{1,0:T(8,128)S(1)}, u32[]{:S(2)}, u32[]{:S(2)}) %collective-permute-start.3) | collective-permute-done | bytes 4128 | tf_op jit(solution)/shard_map/ppermute | solution.py:19
  4.5 0.2 rim.1
  4.7 0.8 %collective-permute-start.4 = (f32[2,256,256]{2,1,0:T(8,128)S(1)}, f32[2,256,256]{2,1,0:T(8,128)S(1)}, u32[]{:S(2)}, u32[]{:S(2)}) collective-permute-start(f32[2,256,256]{2,1,0:T(8,128)S(1)} %rim.1), channel_id=1, source_target_pairs={{8,0},{16,8},{24,16},{0,24},{9,1},{17,9},{25,17},{1,25},{10,2},{18... | collective-permute-start | bytes 1572872 | tf_op jit(solution)/shard_map/ppermute | solution.py:19
  5.4 0.0 copy-done
  5.4 0.0 copy-done.1
  5.4 2.8 %wave0.1 = (f32[136,256]{1,0:T(8,128)S(1)}, f32[136,256]{1,0:T(8,128)S(1)}, f32[136,256]{1,0:T(8,128)S(1)}, f32[136,256]{1,0:T(8,128)S(1)}) custom-call(s32[2]{0:T(128)S(1)} %copy-done, s32[2]{0:T(128)S(1)} %copy-done.1, f32[4096,128]{1,0:T(8,128)S(1)} %get-tuple-element.20.obj, f32[1024,128]{1,0:T(8,128)S(1)} %get-tuple-element.21.ill, ...), custom_call_target="tpu_custom_call" | custom-call | flops 805306368 | bytes 1114112 | tf_op jit(solution)/shard_map/wave0/pallas_call | solution.py:71
  8.2 2.3 %collective-permute-start = (f32[136,256]{1,0:T(8,128)S(1)}, f32[136,256]{1,0:T(8,128)S(1)}, u32[]{:S(2)}, u32[]{:S(2)}) collective-permute-start(f32[136,256]{1,0:T(8,128)S(1)} %get-tuple-element.25), channel_id=1, source_target_pairs={{0,1},{1,0},{2,3},{3,2},{4,5},{5,4},{6,7},{7,6},{8,9},{9,8},{10,11... | collective-permute-start | bytes 417800 | tf_op jit(solution)/shard_map/ppermute | solution.py:23
  10.6 1.6 %collective-permute-start.1 = (f32[136,256]{1,0:T(8,128)S(1)}, f32[136,256]{1,0:T(8,128)S(1)}, u32[]{:S(2)}, u32[]{:S(2)}) collective-permute-start(f32[136,256]{1,0:T(8,128)S(1)} %get-tuple-element.26), channel_id=1, source_target_pairs={{0,2},{1,3},{2,0},{3,1},{4,6},{5,7},{6,4},{7,5},{8,10},{9,11},{10,... | collective-permute-start | bytes 417800 | tf_op jit(solution)/shard_map/ppermute | solution.py:23
  12.1 0.0 collective-permute-start.2
  12.1 0.0 collective-permute-done.4.refs_0_
  12.1 2.8 %wave1.1 = (f32[136,256]{1,0:T(8,128)S(1)}, f32[136,256]{1,0:T(8,128)S(1)}, f32[136,256]{1,0:T(8,128)S(1)}, f32[136,256]{1,0:T(8,128)S(1)}) custom-call(s32[2]{0:T(128)S(1)} %copy-done, s32[2]{0:T(128)S(1)} %copy-done.1, f32[4096,128]{1,0:T(8,128)S(1)} %get-tuple-element.20.obj, f32[1024,128]{1,0:T(8,128)S(1)} %get-tuple-element.21.ill, ...), custom_call_target="tpu_custom_call" | custom-call | flops 805306368 | bytes 1114112 | tf_op jit(solution)/shard_map/wave1/pallas_call | solution.py:71
  15.0 2.3 %collective-permute-start.5 = (f32[136,256]{1,0:T(8,128)S(1)}, f32[136,256]{1,0:T(8,128)S(1)}, u32[]{:S(2)}, u32[]{:S(2)}) collective-permute-start(f32[136,256]{1,0:T(8,128)S(1)} %get-tuple-element.29), channel_id=1, source_target_pairs={{0,1},{1,0},{2,3},{3,2},{4,5},{5,4},{6,7},{7,6},{8,9},{9,8},{10,11... | collective-permute-start | bytes 417800 | tf_op jit(solution)/shard_map/ppermute | solution.py:23
  17.3 1.6 %collective-permute-start.6 = (f32[136,256]{1,0:T(8,128)S(1)}, f32[136,256]{1,0:T(8,128)S(1)}, u32[]{:S(2)}, u32[]{:S(2)}) collective-permute-start(f32[136,256]{1,0:T(8,128)S(1)} %get-tuple-element.30), channel_id=1, source_target_pairs={{0,2},{1,3},{2,0},{3,1},{4,6},{5,7},{6,4},{7,5},{8,10},{9,11},{10,... | collective-permute-start | bytes 417800 | tf_op jit(solution)/shard_map/ppermute | solution.py:23
  18.9 0.0 collective-permute-done.refs_1_
  18.9 0.0 collective-permute-start.7
  18.9 0.0 collective-permute-done.1.refs_2_
  18.9 0.2 collective-permute-done.2.refs_3_
  19.1 0.2 sum0.1.acc
  19.3 1.4 %collective-permute-done.5.refs_1_ = f32[136,256]{1,0:T(8,128)S(1)} collective-permute-done((f32[136,256]{1,0:T(8,128)S(1)}, f32[136,256]{1,0:T(8,128)S(1)}, u32[]{:S(2)}, u32[]{:S(2)}) %collective-permute-start.5) | collective-permute-done | bytes 139296 | tf_op jit(solution)/shard_map/ppermute | solution.py:23
  20.7 2.3 %collective-permute-done.6.refs_2_ = f32[136,256]{1,0:T(8,128)S(1)} collective-permute-done((f32[136,256]{1,0:T(8,128)S(1)}, f32[136,256]{1,0:T(8,128)S(1)}, u32[]{:S(2)}, u32[]{:S(2)}) %collective-permute-start.6) | collective-permute-done | bytes 139296 | tf_op jit(solution)/shard_map/ppermute | solution.py:23
  23.0 2.8 %collective-permute-done.7.refs_3_ = f32[136,256]{1,0:T(8,128)S(1)} collective-permute-done((f32[136,256]{1,0:T(8,128)S(1)}, f32[136,256]{1,0:T(8,128)S(1)}, u32[]{:S(2)}, u32[]{:S(2)}) %collective-permute-start.7) | collective-permute-done | bytes 139296 | tf_op jit(solution)/shard_map/ppermute | solution.py:23
  25.8 0.4 sum1.1
  26.3 0.4 collective-permute-start.8
  26.7 5.4 %collective-permute-done.8 = f32[512,128]{1,0:T(8,128)S(1)} collective-permute-done((f32[512,128]{1,0:T(8,128)S(1)}, f32[512,128]{1,0:T(8,128)S(1)}, u32[]{:S(2)}, u32[]{:S(2)}) %collective-permute-start.8) | collective-permute-done | bytes 262176 | tf_op jit(solution)/shard_map/ppermute | solution.py:19
  32.2 3.1 %collective-permute-start.9 = (f32[512,128]{1,0:T(8,128)S(1)}, f32[512,128]{1,0:T(8,128)S(1)}, u32[]{:S(2)}, u32[]{:S(2)}) collective-permute-start(f32[512,128]{1,0:T(8,128)S(1)} %broadcast_select_fusion), channel_id=1, source_target_pairs={{0,4},{1,5},{2,6},{3,7},{4,0},{5,1},{6,2},{7,3},{8,12},{9,13},{10,... | collective-permute-start | bytes 786440 | tf_op jit(solution)/shard_map/ppermute | solution.py:23
  35.3 11.5 %collective-permute-done.9 = f32[512,128]{1,0:T(8,128)S(1)} collective-permute-done((f32[512,128]{1,0:T(8,128)S(1)}, f32[512,128]{1,0:T(8,128)S(1)}, u32[]{:S(2)}, u32[]{:S(2)}) %collective-permute-start.9) | collective-permute-done | bytes 262176 | tf_op jit(solution)/shard_map/ppermute | solution.py:23
  46.8 0.8 %select_add_fusion = f32[512,128]{1,0:T(8,128)} fusion(f32[512,128]{1,0:T(8,128)S(1)} %collective-permute-done.9, f32[512,128]{1,0:T(8,128)S(1)} %get-tuple-element.32, pred[]{:T(512)S(6)} %ge.3, f32[512,128]{1,0:T(8,128)S(1)} %get-tuple-element.33, f32[512,128]{1,0:T(8,128)S(1)} %collective-permute-done.8), kind=kLoop, calls=%fused_computation | loop fusion | flops 196608 | bytes 1310721 | tf_op jit(solution)/shard_map/add | solution.py:378
  (1 shorter events, 0.0 us)
Async XLA Ops:
  0.7 3.8 %collective-permute-start.3 = (f32[8,128]{1,0:T(8,128)S(1)}, f32[8,128]{1,0:T(8,128)S(1)}, u32[]{:S(2)}, u32[]{:S(2)}) collective-permute-start(f32[8,128]{1,0:T(8,128)S(1)} %pick.1), channel_id=1, source_target_pairs={{24,0},{0,8},{8,16},{16,24},{25,1},{1,9},{9,17},{17,25},{26,2},{2,... | collective-permute-start | bytes 12296 | tf_op jit(solution)/shard_map/ppermute | solution.py:19
  3.2 2.2 %copy-start = (s32[2]{0:T(128)S(1)}, s32[2]{0:T(128)}, u32[]{:S(2)}) copy-start(s32[2]{0:T(128)} %rows.5) | copy-start | bytes 28
  3.2 2.2 %copy-start.1 = (s32[2]{0:T(128)S(1)}, s32[2]{0:T(128)}, u32[]{:S(2)}) copy-start(s32[2]{0:T(128)} %cols.5) | copy-start | bytes 28
  4.7 7.5 %collective-permute-start.4 = (f32[2,256,256]{2,1,0:T(8,128)S(1)}, f32[2,256,256]{2,1,0:T(8,128)S(1)}, u32[]{:S(2)}, u32[]{:S(2)}) collective-permute-start(f32[2,256,256]{2,1,0:T(8,128)S(1)} %rim.1), channel_id=1, source_target_pairs={{8,0},{16,8},{24,16},{0,24},{9,1},{17,9},{25,17},{1,25},{10,2},{18... | collective-permute-start | bytes 1572872 | tf_op jit(solution)/shard_map/ppermute | solution.py:19
  8.2 10.6 %collective-permute-start = (f32[136,256]{1,0:T(8,128)S(1)}, f32[136,256]{1,0:T(8,128)S(1)}, u32[]{:S(2)}, u32[]{:S(2)}) collective-permute-start(f32[136,256]{1,0:T(8,128)S(1)} %get-tuple-element.25), channel_id=1, source_target_pairs={{0,1},{1,0},{2,3},{3,2},{4,5},{5,4},{6,7},{7,6},{8,9},{9,8},{10,11... | collective-permute-start | bytes 417800 | tf_op jit(solution)/shard_map/ppermute | solution.py:23
  10.6 8.3 %collective-permute-start.1 = (f32[136,256]{1,0:T(8,128)S(1)}, f32[136,256]{1,0:T(8,128)S(1)}, u32[]{:S(2)}, u32[]{:S(2)}) collective-permute-start(f32[136,256]{1,0:T(8,128)S(1)} %get-tuple-element.26), channel_id=1, source_target_pairs={{0,2},{1,3},{2,0},{3,1},{4,6},{5,7},{6,4},{7,5},{8,10},{9,11},{10,... | collective-permute-start | bytes 417800 | tf_op jit(solution)/shard_map/ppermute | solution.py:23
  12.1 7.0 %collective-permute-start.2 = (f32[136,256]{1,0:T(8,128)S(1)}, f32[136,256]{1,0:T(8,128)S(1)}, u32[]{:S(2)}, u32[]{:S(2)}) collective-permute-start(f32[136,256]{1,0:T(8,128)S(1)} %get-tuple-element.27), channel_id=1, source_target_pairs={{0,3},{1,2},{2,1},{3,0},{4,7},{5,6},{6,5},{7,4},{8,11},{9,10},{10,... | collective-permute-start | bytes 417800 | tf_op jit(solution)/shard_map/ppermute | solution.py:23
  15.0 5.7 %collective-permute-start.5 = (f32[136,256]{1,0:T(8,128)S(1)}, f32[136,256]{1,0:T(8,128)S(1)}, u32[]{:S(2)}, u32[]{:S(2)}) collective-permute-start(f32[136,256]{1,0:T(8,128)S(1)} %get-tuple-element.29), channel_id=1, source_target_pairs={{0,1},{1,0},{2,3},{3,2},{4,5},{5,4},{6,7},{7,6},{8,9},{9,8},{10,11... | collective-permute-start | bytes 417800 | tf_op jit(solution)/shard_map/ppermute | solution.py:23
  17.3 5.7 %collective-permute-start.6 = (f32[136,256]{1,0:T(8,128)S(1)}, f32[136,256]{1,0:T(8,128)S(1)}, u32[]{:S(2)}, u32[]{:S(2)}) collective-permute-start(f32[136,256]{1,0:T(8,128)S(1)} %get-tuple-element.30), channel_id=1, source_target_pairs={{0,2},{1,3},{2,0},{3,1},{4,6},{5,7},{6,4},{7,5},{8,10},{9,11},{10,... | collective-permute-start | bytes 417800 | tf_op jit(solution)/shard_map/ppermute | solution.py:23
  18.9 7.0 %collective-permute-start.7 = (f32[136,256]{1,0:T(8,128)S(1)}, f32[136,256]{1,0:T(8,128)S(1)}, u32[]{:S(2)}, u32[]{:S(2)}) collective-permute-start(f32[136,256]{1,0:T(8,128)S(1)} %get-tuple-element.31), channel_id=1, source_target_pairs={{0,3},{1,2},{2,1},{3,0},{4,7},{5,6},{6,5},{7,4},{8,11},{9,10},{10,... | collective-permute-start | bytes 417800 | tf_op jit(solution)/shard_map/ppermute | solution.py:23
  26.3 5.8 %collective-permute-start.8 = (f32[512,128]{1,0:T(8,128)S(1)}, f32[512,128]{1,0:T(8,128)S(1)}, u32[]{:S(2)}, u32[]{:S(2)}) collective-permute-start(f32[512,128]{1,0:T(8,128)S(1)} %get-tuple-element.34), channel_id=1, source_target_pairs={{24,0},{0,8},{8,16},{16,24},{25,1},{1,9},{9,17},{17,25},{26,2},{2,... | collective-permute-start | bytes 786440 | tf_op jit(solution)/shard_map/ppermute | solution.py:19
  32.2 14.7 %collective-permute-start.9 = (f32[512,128]{1,0:T(8,128)S(1)}, f32[512,128]{1,0:T(8,128)S(1)}, u32[]{:S(2)}, u32[]{:S(2)}) collective-permute-start(f32[512,128]{1,0:T(8,128)S(1)} %broadcast_select_fusion), channel_id=1, source_target_pairs={{0,4},{1,5},{2,6},{3,7},{4,0},{5,1},{6,2},{7,3},{8,12},{9,13},{10,... | collective-permute-start | bytes 786440 | tf_op jit(solution)/shard_map/ppermute | solution.py:23

commit v9 on v8

--- a/solution.py
+++ b/solution.py
@@ -86,30 +86,30 @@
     return rows[index] - band_start, cols[index], index
 
 
-def load_kernel(number, *refs):
-    sources, targets, sem = refs[:number], refs[number : 2 * number], refs[2 * number]
+def load_kernel(window, number, rows, cols, *refs):
+    sources, targets = refs[:number], refs[number : 2 * number]
+    wanted, sem = refs[2 * number :]
     copies = [pltpu.make_async_copy(a, b, sem.at[i]) for i, (a, b) in enumerate(zip(sources, targets))]
     for copy in copies:
         copy.start()
+    _, column, _ = chosen(1, rows, cols, lax.axis_index("tile") * (2 * window), window)
+    wanted[...] = jnp.broadcast_to(column.astype(F32), wanted.shape)
     for copy in copies:
         copy.wait()
 
 
-def loaded(arrays):
+def loaded(window, scalars, arrays):
+    smem = pl.BlockSpec(memory_space=pltpu.SMEM)
+    vmem = pl.BlockSpec(memory_space=pltpu.VMEM)
     return pl.pallas_call(
-        functools.partial(load_kernel, len(arrays)),
-        out_shape=[pltpu.VMEM(array.shape, array.dtype) for array in arrays],
-        in_specs=[pl.BlockSpec(memory_space=pl.ANY)] * len(arrays),
-        out_specs=[pl.BlockSpec(memory_space=pltpu.VMEM)] * len(arrays),
+        functools.partial(load_kernel, window, len(arrays)),
+        out_shape=[pltpu.VMEM(array.shape, array.dtype) for array in arrays] + [pltpu.VMEM((8, LANES), F32)],
+        in_specs=[smem] * len(scalars) + [pl.BlockSpec(memory_space=pl.ANY)] * len(arrays),
+        out_specs=[vmem] * (len(arrays) + 1),
         scratch_shapes=[pltpu.SemaphoreType.DMA((len(arrays),))],
         compiler_params=pltpu.CompilerParams(vmem_limit_bytes=16 << 20),
         name="load",
-    )(*[pltpu.with_memory_space_constraint(array, pltpu.HBM) for array in arrays])
-
-
-def pick_kernel(window, rows, cols, out):
-    _, column, _ = chosen(1, rows, cols, lax.axis_index("tile") * (2 * window), window)
-    out[...] = jnp.broadcast_to(column.astype(F32), out.shape)
+    )(*[pltpu.with_memory_space_constraint(array, pltpu.HBM) for array in (*scalars, *arrays)])
 
 
 def rim_kernel(window, wanted, obj, out):
@@ -334,9 +334,19 @@
         for k in range(3):
             for half in range(2):
                 for tile in range(tiles):
-                    outs[k][pl.ds((half * tiles + tile) * 2 + part, share, stride=4 * tiles), :] = total[k][half][
+                    outs[3 * tile + k][pl.ds((half * 2 + part) * share, share), :] = total[k][half][
                         :, tile * LANES : (tile + 1) * LANES
                     ]
+
+
+def final_kernel(tiles, share, *refs):
+    kept, received, out = refs[:tiles], refs[tiles : 2 * tiles], refs[2 * tiles]
+    for tile in range(tiles):
+        for half in range(2):
+            for part in range(2):
+                here = pl.ds((half * 2 + part) * share, share)
+                line = (half * tiles + tile) * 2 + part
+                out[pl.ds(line, share, stride=4 * tiles), :] = kept[tile][here, :] + received[tile][here, :]
 
 
 def on_device(object_field, illumination, amplitudes, row_offset, col_offset):
@@ -349,10 +359,9 @@
     tiles = window // LANES
     scalars = (row_offset, col_offset)
 
-    remote = tuple(pltpu.with_memory_space_constraint(scalar, pltpu.HBM) for scalar in scalars)
-    (wanted,) = kernel_call(functools.partial(pick_kernel, window), "pick", [(8, LANES)], remote, [])
+    arrays = [linear(object_field), linear(illumination), amplitudes, split_tables(window)]
+    obj, ill, amps, table, wanted = loaded(window, scalars, arrays)
     wanted = shifted(wanted, "tile", 1)
-    obj, ill, amps, table = loaded([linear(object_field), linear(illumination), amplitudes, split_tables(window)])
     (rim,) = kernel_call(functools.partial(rim_kernel, window), "rim", [(2, window, window)], (), [wanted, obj])
     rim = shifted(rim, "tile", -1)
 
@@ -365,17 +374,31 @@
         functools.partial(first_sum_kernel, window, classes), "sum0", [(2, 2, share, columns)], (), near
     )
     late = spread(wave(1, window, classes, scalars, [obj, ill, amps, table, rim]))
-    top, middle, spilled = kernel_call(
+    sums = kernel_call(
         functools.partial(second_sum_kernel, window, classes),
         "sum1",
-        [(share * 4 * tiles, LANES)] * 3,
+        [(4 * share, LANES)] * (3 * tiles),
         (),
         [acc, *late],
     )
-    top = top + shifted(spilled, "tile", 1)
     is_upper = lax.axis_index("pos") >= classes
-    received = exchanged(jnp.where(is_upper, top, middle), "pos", classes)
-    result = jnp.where(is_upper, middle, top) + received
+    kept, received = [], []
+    for chunk in range(tiles):
+        top, middle, spilled = sums[3 * chunk : 3 * chunk + 3]
+        with jax.named_scope("spill_" + str(chunk)):
+            top = top + shifted(spilled, "tile", 1)
+        outgoing = jnp.where(is_upper, top, middle)
+        with jax.named_scope("halves_" + str(chunk)):
+            received.append(exchanged(outgoing, "pos", classes))
+        kept.append(jnp.where(is_upper, middle, top))
+    result = pl.pallas_call(
+        functools.partial(final_kernel, tiles, share),
+        out_shape=jax.ShapeDtypeStruct((share * 4 * tiles, LANES), F32),
+        in_specs=[pl.BlockSpec(memory_space=pltpu.VMEM)] * (2 * tiles),
+        out_specs=pl.BlockSpec(memory_space=pltpu.VMEM),
+        compiler_params=pltpu.CompilerParams(vmem_limit_bytes=16 << 20),
+        name="final",
+    )(*[in_vmem(array) for array in kept + received])
     return unlinear(result, share, columns)
 
 

time: 47.8 us -> 47.6 us (level)
  waiting for transfers between devices: 25 us -> 22.2 us
  starting transfers between devices: 12.7 us -> 15.3 us
  Pallas kernels: 9.06 us -> 9.83 us
  other arithmetic: 0.79 us -> 0.05 us
    pallas_call x1 -> x2, Pallas kernels: 1.96 us -> 3.4 us  [the longest x1 2.64 us: loaded(): pl.pallas_call(functools.partial(load_kernel, window, len(arrays)), out_s...]
    ppermute x7 -> x8, waiting for transfers between devices: 18.3 us -> 16.9 us  [exchanged(): lax.ppermute(block, axis, [(i, i ^ flip) for i in range(lax.axis_size(axi...]
    ppermute x7 -> x8, starting transfers between devices: 11 us -> 12.3 us  [exchanged(): lax.ppermute(block, axis, [(i, i ^ flip) for i in range(lax.axis_size(axi...]
    ppermute x3 -> x4, waiting for transfers between devices: 6.69 us -> 5.35 us  [shifted(): lax.ppermute(block, axis, [((i - distance) % devices, i) for i in range(d...]
    ppermute x3 -> x4, starting transfers between devices: 1.74 us -> 2.97 us  [shifted(): lax.ppermute(block, axis, [((i - distance) % devices, i) for i in range(d...]
    add x1 -> x0, other arithmetic: 0.75 us -> none  [on_device(): result = jnp.where(is_upper, middle, top) + received]
    pallas_call x6 -> x5, Pallas kernels: 7.1 us -> 6.42 us  [kernel_call(): pl.pallas_call(body, out_shape=[pltpu.VMEM(shape, F32) for shape in out_s...]
  transfers between devices with their start and end apart: 10 -> 12, of which waited for: 7 -> 8; matrix products, arithmetic and copies ran while one was open for 0% -> 0% of each run, Pallas kernels for 16% -> 12%
where the time goes in v9:
time: 47.6 us; the launch traced here: 47.5 us
  waiting for transfers between devices  22.2 us (47%)
  starting transfers between devices  15.3 us (32%)
  Pallas kernels  9.83 us (21%)
    ppermute x8, waiting for transfers between devices, exchanged(): lax.ppermute(block, axis, [(i, i ^ flip) for i in range(lax.axis_size(axi...  16.9 us
    ppermute x8, starting transfers between devices, exchanged(): lax.ppermute(block, axis, [(i, i ^ flip) for i in range(lax.axis_size(axi...  12.3 us
    pallas_call x5, Pallas kernels, kernel_call(): pl.pallas_call(body, out_shape=[pltpu.VMEM(shape, F32) for shape in out_s...  6.42 us
    ppermute x4, waiting for transfers between devices, shifted(): lax.ppermute(block, axis, [((i - distance) % devices, i) for i in range(d...  5.35 us
    ppermute x4, starting transfers between devices, shifted(): lax.ppermute(block, axis, [((i - distance) % devices, i) for i in range(d...  2.97 us
    pallas_call x1, Pallas kernels, loaded(): pl.pallas_call(functools.partial(load_kernel, window, len(arrays)), out_s...  2.64 us
  transfers between devices with their start and end apart: 12, of which 8 were waited for; matrix products, arithmetic and copies ran while one was open for 0% of the time, Pallas kernels for 12%

profile of v9, /device:TPU:0, one launch (start us, length us, event | category | flops | bytes accessed | tf_op | source)
XLA Modules:
  0.0 47.5 jit_solution(9154517872048086897)
XLA Ops:
  0.0 2.6 %load.1 = (f32[4096,128]{1,0:T(8,128)S(1)}, f32[1024,128]{1,0:T(8,128)S(1)}, bf16[2,256,256]{2,1,0:T(8,128)(2,1)S(1)}, bf16[768,384]{1,0:T(8,128)(2,1)S(1)}, f32[8,128]{1,0:T(8,128)S(1)}) custom-call(s32[2]{0:T(128)} %rows.5, s32[2]{0:T(128)} %cols.5, f32[4096,128]{1,0:T(8,128)} %bitcast.15, f32[1024,128]{1,0:T(8,128)} %bitcast.16, ...), custom_call_target="tpu_custom_call" | custom-call | tf_op jit(solution)/shard_map/load/pallas_call | solution.py:104
  2.6 0.0 copy-start
  2.7 0.0 copy-start.1
  2.7 0.5 %collective-permute-start.3 = (f32[8,128]{1,0:T(8,128)S(1)}, f32[8,128]{1,0:T(8,128)S(1)}, u32[]{:S(2)}, u32[]{:S(2)}) collective-permute-start(f32[8,128]{1,0:T(8,128)S(1)} %get-tuple-element.32), channel_id=1, source_target_pairs={{24,0},{0,8},{8,16},{16,24},{25,1},{1,9},{9,17},{17,25},{26,2},{2,... | collective-permute-start | bytes 12296 | tf_op jit(solution)/shard_map/ppermute | solution.py:19
  3.2 3.2 %collective-permute-done.3.wanted = f32[8,128]{1,0:T(8,128)S(1)} collective-permute-done((f32[8,128]{1,0:T(8,128)S(1)}, f32[8,128]{1,0:T(8,128)S(1)}, u32[]{:S(2)}, u32[]{:S(2)}) %collective-permute-start.3) | collective-permute-done | bytes 4128 | tf_op jit(solution)/shard_map/ppermute | solution.py:19
  6.4 0.2 rim.1
  6.6 0.1 collective-permute-start.4
  6.7 2.8 %wave0.1 = (f32[136,256]{1,0:T(8,128)S(1)}, f32[136,256]{1,0:T(8,128)S(1)}, f32[136,256]{1,0:T(8,128)S(1)}, f32[136,256]{1,0:T(8,128)S(1)}) custom-call(s32[2]{0:T(128)S(1)} %copy-done, s32[2]{0:T(128)S(1)} %copy-done.1, f32[4096,128]{1,0:T(8,128)S(1)} %get-tuple-element.24.obj, f32[1024,128]{1,0:T(8,128)S(1)} %get-tuple-element.25.ill, ...), custom_call_target="tpu_custom_call" | custom-call | flops 805306368 | bytes 1114112 | tf_op jit(solution)/shard_map/wave0/pallas_call | solution.py:71
  9.5 2.3 %collective-permute-start = (f32[136,256]{1,0:T(8,128)S(1)}, f32[136,256]{1,0:T(8,128)S(1)}, u32[]{:S(2)}, u32[]{:S(2)}) collective-permute-start(f32[136,256]{1,0:T(8,128)S(1)} %get-tuple-element.29), channel_id=1, source_target_pairs={{0,1},{1,0},{2,3},{3,2},{4,5},{5,4},{6,7},{7,6},{8,9},{9,8},{10,11... | collective-permute-start | bytes 417800 | tf_op jit(solution)/shard_map/ppermute | solution.py:23
  11.9 1.6 %collective-permute-start.1 = (f32[136,256]{1,0:T(8,128)S(1)}, f32[136,256]{1,0:T(8,128)S(1)}, u32[]{:S(2)}, u32[]{:S(2)}) collective-permute-start(f32[136,256]{1,0:T(8,128)S(1)} %get-tuple-element.30), channel_id=1, source_target_pairs={{0,2},{1,3},{2,0},{3,1},{4,6},{5,7},{6,4},{7,5},{8,10},{9,11},{10,... | collective-permute-start | bytes 417800 | tf_op jit(solution)/shard_map/ppermute | solution.py:23
  13.4 0.0 collective-permute-start.2
  13.4 0.0 collective-permute-done.4.refs_0_
  13.4 2.8 %wave1.1 = (f32[136,256]{1,0:T(8,128)S(1)}, f32[136,256]{1,0:T(8,128)S(1)}, f32[136,256]{1,0:T(8,128)S(1)}, f32[136,256]{1,0:T(8,128)S(1)}) custom-call(s32[2]{0:T(128)S(1)} %copy-done, s32[2]{0:T(128)S(1)} %copy-done.1, f32[4096,128]{1,0:T(8,128)S(1)} %get-tuple-element.24.obj, f32[1024,128]{1,0:T(8,128)S(1)} %get-tuple-element.25.ill, ...), custom_call_target="tpu_custom_call" | custom-call | flops 805306368 | bytes 1114112 | tf_op jit(solution)/shard_map/wave1/pallas_call | solution.py:71
  16.3 2.3 %collective-permute-start.5 = (f32[136,256]{1,0:T(8,128)S(1)}, f32[136,256]{1,0:T(8,128)S(1)}, u32[]{:S(2)}, u32[]{:S(2)}) collective-permute-start(f32[136,256]{1,0:T(8,128)S(1)} %get-tuple-element.34), channel_id=1, source_target_pairs={{0,1},{1,0},{2,3},{3,2},{4,5},{5,4},{6,7},{7,6},{8,9},{9,8},{10,11... | collective-permute-start | bytes 417800 | tf_op jit(solution)/shard_map/ppermute | solution.py:23
  18.6 1.6 %collective-permute-start.6 = (f32[136,256]{1,0:T(8,128)S(1)}, f32[136,256]{1,0:T(8,128)S(1)}, u32[]{:S(2)}, u32[]{:S(2)}) collective-permute-start(f32[136,256]{1,0:T(8,128)S(1)} %get-tuple-element.35), channel_id=1, source_target_pairs={{0,2},{1,3},{2,0},{3,1},{4,6},{5,7},{6,4},{7,5},{8,10},{9,11},{10,... | collective-permute-start | bytes 417800 | tf_op jit(solution)/shard_map/ppermute | solution.py:23
  20.1 0.0 collective-permute-done.refs_1_
  20.1 0.0 collective-permute-start.7
  20.1 0.0 collective-permute-done.1.refs_2_
  20.1 0.3 collective-permute-done.2.refs_3_
  20.5 0.2 sum0.1.acc
  20.7 1.4 %collective-permute-done.5.refs_1_ = f32[136,256]{1,0:T(8,128)S(1)} collective-permute-done((f32[136,256]{1,0:T(8,128)S(1)}, f32[136,256]{1,0:T(8,128)S(1)}, u32[]{:S(2)}, u32[]{:S(2)}) %collective-permute-start.5) | collective-permute-done | bytes 139296 | tf_op jit(solution)/shard_map/ppermute | solution.py:23
  22.1 2.2 %collective-permute-done.6.refs_2_ = f32[136,256]{1,0:T(8,128)S(1)} collective-permute-done((f32[136,256]{1,0:T(8,128)S(1)}, f32[136,256]{1,0:T(8,128)S(1)}, u32[]{:S(2)}, u32[]{:S(2)}) %collective-permute-start.6) | collective-permute-done | bytes 139296 | tf_op jit(solution)/shard_map/ppermute | solution.py:23
  24.3 2.8 %collective-permute-done.7.refs_3_ = f32[136,256]{1,0:T(8,128)S(1)} collective-permute-done((f32[136,256]{1,0:T(8,128)S(1)}, f32[136,256]{1,0:T(8,128)S(1)}, u32[]{:S(2)}, u32[]{:S(2)}) %collective-permute-start.7) | collective-permute-done | bytes 139296 | tf_op jit(solution)/shard_map/ppermute | solution.py:23
  27.1 0.4 sum1.1
  27.5 0.4 collective-permute-start.8
  27.9 1.9 %collective-permute-start.9 = (f32[256,128]{1,0:T(8,128)S(1)}, f32[256,128]{1,0:T(8,128)S(1)}, u32[]{:S(2)}, u32[]{:S(2)}) collective-permute-start(f32[256,128]{1,0:T(8,128)S(1)} %get-tuple-element.42), channel_id=1, source_target_pairs={{24,0},{0,8},{8,16},{16,24},{25,1},{1,9},{9,17},{17,25},{26,2},{2,... | collective-permute-start | bytes 393224 | tf_op jit(solution)/shard_map/spill_1/ppermute | solution.py:19
  29.8 2.1 %collective-permute-done.8 = f32[256,128]{1,0:T(8,128)S(1)} collective-permute-done((f32[256,128]{1,0:T(8,128)S(1)}, f32[256,128]{1,0:T(8,128)S(1)}, u32[]{:S(2)}, u32[]{:S(2)}) %collective-permute-start.8) | collective-permute-done | bytes 131104 | tf_op jit(solution)/shard_map/spill_0/ppermute | solution.py:19
  32.0 3.2 %collective-permute-start.10 = (f32[256,128]{1,0:T(8,128)S(1)}, f32[256,128]{1,0:T(8,128)S(1)}, u32[]{:S(2)}, u32[]{:S(2)}) collective-permute-start(f32[256,128]{1,0:T(8,128)S(1)} %get-tuple-element.45), channel_id=1, source_target_pairs={{0,4},{1,5},{2,6},{3,7},{4,0},{5,1},{6,2},{7,3},{8,12},{9,13},{10,... | collective-permute-start | bytes 393224 | tf_op jit(solution)/shard_map/halves_0/ppermute | solution.py:23
  35.2 1.4 %collective-permute-start.11 = (f32[256,128]{1,0:T(8,128)S(1)}, f32[256,128]{1,0:T(8,128)S(1)}, u32[]{:S(2)}, u32[]{:S(2)}) collective-permute-start(f32[256,128]{1,0:T(8,128)S(1)} %get-tuple-element.43), channel_id=1, source_target_pairs={{0,4},{1,5},{2,6},{3,7},{4,0},{5,1},{6,2},{7,3},{8,12},{9,13},{10,... | collective-permute-start | bytes 393224 | tf_op jit(solution)/shard_map/halves_1/ppermute | solution.py:23
  36.5 8.5 %collective-permute-done.10.refs_2_ = f32[256,128]{1,0:T(8,128)S(1)} collective-permute-done((f32[256,128]{1,0:T(8,128)S(1)}, f32[256,128]{1,0:T(8,128)S(1)}, u32[]{:S(2)}, u32[]{:S(2)}) %collective-permute-start.10) | collective-permute-done | bytes 131104 | tf_op jit(solution)/shard_map/halves_0/ppermute | solution.py:23
  45.1 1.7 %collective-permute-done.11.refs_3_ = f32[256,128]{1,0:T(8,128)S(1)} collective-permute-done((f32[256,128]{1,0:T(8,128)S(1)}, f32[256,128]{1,0:T(8,128)S(1)}, u32[]{:S(2)}, u32[]{:S(2)}) %collective-permute-start.11) | collective-permute-done | bytes 131104 | tf_op jit(solution)/shard_map/halves_1/ppermute | solution.py:23
  46.7 0.8 %final.1 = f32[512,128]{1,0:T(8,128)} custom-call(f32[256,128]{1,0:T(8,128)S(1)} %get-tuple-element.46.refs_0_, f32[256,128]{1,0:T(8,128)S(1)} %get-tuple-element.44.refs_1_, f32[256,128]{1,0:T(8,128)S(1)} %collective-permute-done.10.refs_2_, f32[256,128]{1,0:T(8,128)S(1)} %collective-permute-done.11.refs_3_), custom_call_target="tpu_custom_call" | custom-call | tf_op jit(solution)/shard_map/final/pallas_call | solution.py:394
  (5 shorter events, 0.1 us)
Async XLA Ops:
  2.6 4.1 %copy-start = (s32[2]{0:T(128)S(1)}, s32[2]{0:T(128)}, u32[]{:S(2)}) copy-start(s32[2]{0:T(128)} %rows.5) | copy-start | bytes 28
  2.7 4.1 %copy-start.1 = (s32[2]{0:T(128)S(1)}, s32[2]{0:T(128)}, u32[]{:S(2)}) copy-start(s32[2]{0:T(128)} %cols.5) | copy-start | bytes 28
  2.7 3.8 %collective-permute-start.3 = (f32[8,128]{1,0:T(8,128)S(1)}, f32[8,128]{1,0:T(8,128)S(1)}, u32[]{:S(2)}, u32[]{:S(2)}) collective-permute-start(f32[8,128]{1,0:T(8,128)S(1)} %get-tuple-element.32), channel_id=1, source_target_pairs={{24,0},{0,8},{8,16},{16,24},{25,1},{1,9},{9,17},{17,25},{26,2},{2,... | collective-permute-start | bytes 12296 | tf_op jit(solution)/shard_map/ppermute | solution.py:19
  6.6 6.8 %collective-permute-start.4 = (f32[2,256,256]{2,1,0:T(8,128)S(1)}, f32[2,256,256]{2,1,0:T(8,128)S(1)}, u32[]{:S(2)}, u32[]{:S(2)}) collective-permute-start(f32[2,256,256]{2,1,0:T(8,128)S(1)} %rim.1), channel_id=1, source_target_pairs={{8,0},{16,8},{24,16},{0,24},{9,1},{17,9},{25,17},{1,25},{10,2},{18... | collective-permute-start | bytes 1572872 | tf_op jit(solution)/shard_map/ppermute | solution.py:19
  9.5 10.6 %collective-permute-start = (f32[136,256]{1,0:T(8,128)S(1)}, f32[136,256]{1,0:T(8,128)S(1)}, u32[]{:S(2)}, u32[]{:S(2)}) collective-permute-start(f32[136,256]{1,0:T(8,128)S(1)} %get-tuple-element.29), channel_id=1, source_target_pairs={{0,1},{1,0},{2,3},{3,2},{4,5},{5,4},{6,7},{7,6},{8,9},{9,8},{10,11... | collective-permute-start | bytes 417800 | tf_op jit(solution)/shard_map/ppermute | solution.py:23
  11.9 8.3 %collective-permute-start.1 = (f32[136,256]{1,0:T(8,128)S(1)}, f32[136,256]{1,0:T(8,128)S(1)}, u32[]{:S(2)}, u32[]{:S(2)}) collective-permute-start(f32[136,256]{1,0:T(8,128)S(1)} %get-tuple-element.30), channel_id=1, source_target_pairs={{0,2},{1,3},{2,0},{3,1},{4,6},{5,7},{6,4},{7,5},{8,10},{9,11},{10,... | collective-permute-start | bytes 417800 | tf_op jit(solution)/shard_map/ppermute | solution.py:23
  13.4 7.0 %collective-permute-start.2 = (f32[136,256]{1,0:T(8,128)S(1)}, f32[136,256]{1,0:T(8,128)S(1)}, u32[]{:S(2)}, u32[]{:S(2)}) collective-permute-start(f32[136,256]{1,0:T(8,128)S(1)} %get-tuple-element.31), channel_id=1, source_target_pairs={{0,3},{1,2},{2,1},{3,0},{4,7},{5,6},{6,5},{7,4},{8,11},{9,10},{10,... | collective-permute-start | bytes 417800 | tf_op jit(solution)/shard_map/ppermute | solution.py:23
  16.3 5.8 %collective-permute-start.5 = (f32[136,256]{1,0:T(8,128)S(1)}, f32[136,256]{1,0:T(8,128)S(1)}, u32[]{:S(2)}, u32[]{:S(2)}) collective-permute-start(f32[136,256]{1,0:T(8,128)S(1)} %get-tuple-element.34), channel_id=1, source_target_pairs={{0,1},{1,0},{2,3},{3,2},{4,5},{5,4},{6,7},{7,6},{8,9},{9,8},{10,11... | collective-permute-start | bytes 417800 | tf_op jit(solution)/shard_map/ppermute | solution.py:23
  18.6 5.7 %collective-permute-start.6 = (f32[136,256]{1,0:T(8,128)S(1)}, f32[136,256]{1,0:T(8,128)S(1)}, u32[]{:S(2)}, u32[]{:S(2)}) collective-permute-start(f32[136,256]{1,0:T(8,128)S(1)} %get-tuple-element.35), channel_id=1, source_target_pairs={{0,2},{1,3},{2,0},{3,1},{4,6},{5,7},{6,4},{7,5},{8,10},{9,11},{10,... | collective-permute-start | bytes 417800 | tf_op jit(solution)/shard_map/ppermute | solution.py:23
  20.1 6.9 %collective-permute-start.7 = (f32[136,256]{1,0:T(8,128)S(1)}, f32[136,256]{1,0:T(8,128)S(1)}, u32[]{:S(2)}, u32[]{:S(2)}) collective-permute-start(f32[136,256]{1,0:T(8,128)S(1)} %get-tuple-element.36), channel_id=1, source_target_pairs={{0,3},{1,2},{2,1},{3,0},{4,7},{5,6},{6,5},{7,4},{8,11},{9,10},{10,... | collective-permute-start | bytes 417800 | tf_op jit(solution)/shard_map/ppermute | solution.py:23
  27.5 4.4 %collective-permute-start.8 = (f32[256,128]{1,0:T(8,128)S(1)}, f32[256,128]{1,0:T(8,128)S(1)}, u32[]{:S(2)}, u32[]{:S(2)}) collective-permute-start(f32[256,128]{1,0:T(8,128)S(1)} %get-tuple-element.39), channel_id=1, source_target_pairs={{24,0},{0,8},{8,16},{16,24},{25,1},{1,9},{9,17},{17,25},{26,2},{2,... | collective-permute-start | bytes 393224 | tf_op jit(solution)/shard_map/spill_0/ppermute | solution.py:19
  27.9 7.2 %collective-permute-start.9 = (f32[256,128]{1,0:T(8,128)S(1)}, f32[256,128]{1,0:T(8,128)S(1)}, u32[]{:S(2)}, u32[]{:S(2)}) collective-permute-start(f32[256,128]{1,0:T(8,128)S(1)} %get-tuple-element.42), channel_id=1, source_target_pairs={{24,0},{0,8},{8,16},{16,24},{25,1},{1,9},{9,17},{17,25},{26,2},{2,... | collective-permute-start | bytes 393224 | tf_op jit(solution)/shard_map/spill_1/ppermute | solution.py:19
  32.0 13.1 %collective-permute-start.10 = (f32[256,128]{1,0:T(8,128)S(1)}, f32[256,128]{1,0:T(8,128)S(1)}, u32[]{:S(2)}, u32[]{:S(2)}) collective-permute-start(f32[256,128]{1,0:T(8,128)S(1)} %get-tuple-element.45), channel_id=1, source_target_pairs={{0,4},{1,5},{2,6},{3,7},{4,0},{5,1},{6,2},{7,3},{8,12},{9,13},{10,... | collective-permute-start | bytes 393224 | tf_op jit(solution)/shard_map/halves_0/ppermute | solution.py:23
  35.2 11.5 %collective-permute-start.11 = (f32[256,128]{1,0:T(8,128)S(1)}, f32[256,128]{1,0:T(8,128)S(1)}, u32[]{:S(2)}, u32[]{:S(2)}) collective-permute-start(f32[256,128]{1,0:T(8,128)S(1)} %get-tuple-element.43), channel_id=1, source_target_pairs={{0,4},{1,5},{2,6},{3,7},{4,0},{5,1},{6,2},{7,3},{8,12},{9,13},{10,... | collective-permute-start | bytes 393224 | tf_op jit(solution)/shard_map/halves_1/ppermute | solution.py:23

commit v10 on v9

--- a/solution.py
+++ b/solution.py
@@ -86,30 +86,30 @@
     return rows[index] - band_start, cols[index], index
 
 
-def load_kernel(window, number, rows, cols, *refs):
-    sources, targets = refs[:number], refs[number : 2 * number]
-    wanted, sem = refs[2 * number :]
+def load_kernel(number, *refs):
+    sources, targets, sem = refs[:number], refs[number : 2 * number], refs[2 * number]
     copies = [pltpu.make_async_copy(a, b, sem.at[i]) for i, (a, b) in enumerate(zip(sources, targets))]
     for copy in copies:
         copy.start()
-    _, column, _ = chosen(1, rows, cols, lax.axis_index("tile") * (2 * window), window)
-    wanted[...] = jnp.broadcast_to(column.astype(F32), wanted.shape)
     for copy in copies:
         copy.wait()
 
 
-def loaded(window, scalars, arrays):
-    smem = pl.BlockSpec(memory_space=pltpu.SMEM)
-    vmem = pl.BlockSpec(memory_space=pltpu.VMEM)
+def loaded(arrays):
     return pl.pallas_call(
-        functools.partial(load_kernel, window, len(arrays)),
-        out_shape=[pltpu.VMEM(array.shape, array.dtype) for array in arrays] + [pltpu.VMEM((8, LANES), F32)],
-        in_specs=[smem] * len(scalars) + [pl.BlockSpec(memory_space=pl.ANY)] * len(arrays),
-        out_specs=[vmem] * (len(arrays) + 1),
+        functools.partial(load_kernel, len(arrays)),
+        out_shape=[pltpu.VMEM(array.shape, array.dtype) for array in arrays],
+        in_specs=[pl.BlockSpec(memory_space=pl.ANY)] * len(arrays),
+        out_specs=[pl.BlockSpec(memory_space=pltpu.VMEM)] * len(arrays),
         scratch_shapes=[pltpu.SemaphoreType.DMA((len(arrays),))],
         compiler_params=pltpu.CompilerParams(vmem_limit_bytes=16 << 20),
         name="load",
-    )(*[pltpu.with_memory_space_constraint(array, pltpu.HBM) for array in (*scalars, *arrays)])
+    )(*[pltpu.with_memory_space_constraint(array, pltpu.HBM) for array in arrays])
+
+
+def pick_kernel(window, rows, cols, out):
+    _, column, _ = chosen(1, rows, cols, lax.axis_index("tile") * (2 * window), window)
+    out[...] = jnp.broadcast_to(column.astype(F32), out.shape)
 
 
 def rim_kernel(window, wanted, obj, out):
@@ -123,15 +123,10 @@
             out[part, :, pl.ds(tile * LANES, LANES)] = jnp.where(column < offset, beyond, near)
 
 
-def wave_kernel(slot, window, classes, with_rim, rows, cols, obj, ill, amps, table, *refs):
-    if with_rim:
-        rim, refs = refs[0], refs[1:]
-    outs, refs = refs[:classes], refs[classes:]
-    doubled, probe, xh, xl, yh, yl, far, ordered = refs
+def prepare(slot, window, rows, cols, obj, ill, amps, doubled, probe, ordered, emit):
     tiles = window // LANES
     half = window // 2
     row, column, index = chosen(slot, rows, cols, lax.axis_index("tile") * (2 * window), window)
-    own = lax.rem(lax.axis_index("pos"), classes)
     size = 32
     step = 2 * tiles
     whole = window * step
@@ -148,34 +143,6 @@
 
     by_column = jnp.dot(amps[index], picks(below, beside), preferred_element_type=F32).astype(BF16)
     ordered[...] = jnp.dot(picks(beside, below), by_column, preferred_element_type=F32)
-
-    def block_of(matrix, part, low):
-        return table[pl.ds((2 * matrix + low) * half, half), pl.ds(part * half, half)]
-
-    def factor(matrix, order):
-        return [
-            jnp.concatenate(
-                [
-                    jnp.concatenate([block_of(matrix, part, low) for part in line], axis=1)
-                    for line in order
-                ],
-                axis=0,
-            )
-            for low in range(2)
-        ]
-
-    def from_right(first, matrix):
-        across = pl.ds(first, window)
-        return dot3(xh[:, across], xl[:, across], *factor(matrix, ((0, 1), (2, 0))))
-
-    def from_left(matrix, first):
-        down = pl.ds(first, window)
-        return dot3(*factor(matrix, ((0, 2), (1, 0))), yh[down, :], yl[down, :])
-
-    def keep(high_ref, low_ref, here, across, value):
-        high, low = halves(value)
-        high_ref[here, across] = high
-        low_ref[here, across] = low
 
     for first in range(0, window, size):
         place = lax.broadcasted_iota(jnp.int32, (size, window), 0) + first
@@ -198,20 +165,61 @@
                 beyond = jnp.concatenate([tile_at(t + tiles) for t in range(tiles)], axis=1)
                 return jnp.where(across < column, beyond, near)
 
-            seen = jnp.where(place < row, block(window), block(0))
-            if with_rim:
-                seen = jnp.where(place + window < row, rim[part, pl.ds(first, size), :], seen)
-            pair.append((rolled, seen))
-        (probe_real, obj_real), (probe_imag, obj_imag) = pair
-        exits = (
-            probe_real * obj_real - probe_imag * obj_imag,
-            probe_real * obj_imag + probe_imag * obj_real,
-        )
-        here = pl.ds(first, size)
-        for part, value in enumerate(exits):
-            left, right = value[:, :half], value[:, half:]
-            keep(xh, xl, here, pl.ds(part * half, half), left + right)
-            keep(xh, xl, here, pl.ds(window + part * half, half), left - right)
+            pair.append((rolled, jnp.where(place < row, block(window), block(0))))
+        emit(first, size, product(*pair))
+
+
+def product(real_pair, imag_pair):
+    (probe_real, obj_real), (probe_imag, obj_imag) = real_pair, imag_pair
+    return (
+        probe_real * obj_real - probe_imag * obj_imag,
+        probe_real * obj_imag + probe_imag * obj_real,
+    )
+
+
+def keep(high_ref, low_ref, here, across, value):
+    high, low = halves(value)
+    high_ref[here, across] = high
+    low_ref[here, across] = low
+
+
+def keep_exit(xh, xl, first, size, exits):
+    here = pl.ds(first, size)
+    window = exits[0].shape[1]
+    half = window // 2
+    for part, value in enumerate(exits):
+        left, right = value[:, :half], value[:, half:]
+        keep(xh, xl, here, pl.ds(part * half, half), left + right)
+        keep(xh, xl, here, pl.ds(window + part * half, half), left - right)
+
+
+def transforms(window, classes, table, probe, ordered, xh, xl, yh, yl, far, outs):
+    half = window // 2
+    own = lax.rem(lax.axis_index("pos"), classes)
+    size = 32
+
+    def block_of(matrix, part, low):
+        return table[pl.ds((2 * matrix + low) * half, half), pl.ds(part * half, half)]
+
+    def factor(matrix, order):
+        return [
+            jnp.concatenate(
+                [
+                    jnp.concatenate([block_of(matrix, part, low) for part in line], axis=1)
+                    for line in order
+                ],
+                axis=0,
+            )
+            for low in range(2)
+        ]
+
+    def from_right(first, matrix):
+        across = pl.ds(first, window)
+        return dot3(xh[:, across], xl[:, across], *factor(matrix, ((0, 1), (2, 0))))
+
+    def from_left(matrix, first):
+        down = pl.ds(first, window)
+        return dot3(*factor(matrix, ((0, 2), (1, 0))), yh[down, :], yl[down, :])
 
     for parity in range(2):
         mid = from_right(parity * window, parity)
@@ -262,37 +270,63 @@
         probe_imag = probe[1, here, :]
         outs[flip][pl.ds(0, share), :] = probe_real * real - probe_imag * imag
         outs[flip][pl.ds(share, share), :] = -(probe_real * imag + probe_imag * real)
-        line = lax.broadcasted_iota(jnp.int32, (8, window), 0)
-        outs[flip][pl.ds(2 * share, 8), :] = jnp.where(line == 0, row, column).astype(F32)
-
-
-def wave(slot, window, classes, scalars, arrays):
+
+
+def first_wave_kernel(window, classes, rows, cols, obj, ill, amps, table, *refs):
+    outs = refs[:classes]
+    doubled, probe, ordered, xh, xl, yh, yl, far = refs[classes:]
+    emit = functools.partial(keep_exit, xh, xl)
+    prepare(0, window, rows, cols, obj, ill, amps, doubled, probe, ordered, emit)
+    transforms(window, classes, table, probe, ordered, xh, xl, yh, yl, far, outs)
     share = window // classes
+    line = lax.broadcasted_iota(jnp.int32, (8, window), 0)
+    head = jnp.zeros((8, window), jnp.int32)
+    for slot in range(2):
+        row, column, _ = chosen(slot, rows, cols, lax.axis_index("tile") * (2 * window), window)
+        head = jnp.where(line == 2 * slot, row, jnp.where(line == 2 * slot + 1, column, head))
+    for out in outs:
+        out[pl.ds(2 * share, 8), :] = head.astype(F32)
+
+
+def second_start_kernel(window, rows, cols, obj, ill, amps, probe, ordered, exits, doubled):
+    def emit(first, size, values):
+        for part in range(2):
+            exits[part, pl.ds(first, size), :] = values[part]
+
+    prepare(1, window, rows, cols, obj, ill, amps, doubled, probe, ordered, emit)
+
+
+def second_wave_kernel(window, classes, rows, cols, probe, ordered, exits, table, rim, *refs):
+    outs = refs[:classes]
+    xh, xl, yh, yl, far = refs[classes:]
+    row, _, _ = chosen(1, rows, cols, lax.axis_index("tile") * (2 * window), window)
+    size = 32
+    for first in range(0, window, size):
+        here = pl.ds(first, size)
+        beyond = lax.broadcasted_iota(jnp.int32, (size, window), 0) + (first + window) < row
+        edge = product(*[(probe[part, here, :], rim[part, here, :]) for part in range(2)])
+        values = [jnp.where(beyond, edge[part], exits[part, here, :]) for part in range(2)]
+        keep_exit(xh, xl, first, size, values)
+    transforms(window, classes, table, probe, ordered, xh, xl, yh, yl, far, outs)
+
+
+def scratch_of(window):
     tiles = window // LANES
-    scratch = [
-        pltpu.VMEM(((window + 32) * 2 * tiles + 8, LANES), F32),
-        pltpu.VMEM((2, window, window), F32),
+    roll = [pltpu.VMEM(((window + 32) * 2 * tiles + 8, LANES), F32)]
+    state = [pltpu.VMEM((2, window, window), F32), pltpu.VMEM((window, window), F32)]
+    work = [
         pltpu.VMEM((window, 2 * window), BF16),
         pltpu.VMEM((window, 2 * window), BF16),
         pltpu.VMEM((2 * window, window), BF16),
         pltpu.VMEM((2 * window, window), BF16),
         pltpu.VMEM((2 * window, window), F32),
-        pltpu.VMEM((window, window), F32),
     ]
-    return kernel_call(
-        functools.partial(wave_kernel, slot, window, classes, len(arrays) == 5),
-        "wave" + str(slot),
-        [(2 * share + 8, window)] * classes,
-        scalars,
-        arrays,
-        scratch,
-        48 * window**3,
-    )
-
-
-def placed(piece, own, share, window):
-    row = piece[pl.ds(2 * share, 1), :]
-    column = piece[pl.ds(2 * share + 1, 1), :]
+    return roll, state, work
+
+
+def placed(slot, piece, own, share, window):
+    row = piece[pl.ds(2 * share + 2 * slot, 1), :]
+    column = piece[pl.ds(2 * share + 2 * slot + 1, 1), :]
     place = (lax.broadcasted_iota(jnp.int32, (share, window), 0) + own * share).astype(F32)
     across = lax.broadcasted_iota(jnp.int32, (share, window), 1).astype(F32)
     return across < column, place < row, place + float(window) < row
@@ -305,7 +339,7 @@
     for part in range(2):
         total = [[jnp.zeros((share, window), F32) for _ in range(2)] for _ in range(2)]
         for piece in pieces:
-            upper, below, _ = placed(piece, own, share, window)
+            upper, below, _ = placed(0, piece, own, share, window)
             value = piece[pl.ds(part * share, share), :]
             for k, wanted in enumerate((~below, below)):
                 kept = jnp.where(wanted, value, 0.0)
@@ -317,15 +351,15 @@
 
 
 def second_sum_kernel(window, classes, acc, *refs):
-    pieces, outs = refs[:classes], refs[classes:]
+    heads, pieces, outs = refs[:classes], refs[classes : 2 * classes], refs[2 * classes :]
     share = window // classes
     tiles = window // LANES
     own = lax.rem(lax.axis_index("pos"), classes)
     for part in range(2):
         total = [[acc[k, part, :, pl.ds(h * window, window)] for h in range(2)] for k in range(2)]
         total.append([jnp.zeros((share, window), F32) for _ in range(2)])
-        for piece in pieces:
-            upper, below, lowest = placed(piece, own, share, window)
+        for head, piece in zip(heads, pieces):
+            upper, below, lowest = placed(1, head, own, share, window)
             value = piece[pl.ds(part * share, share), :]
             for k, wanted in enumerate((~below, below & ~lowest, lowest)):
                 kept = jnp.where(wanted, value, 0.0)
@@ -360,8 +394,10 @@
     scalars = (row_offset, col_offset)
 
     arrays = [linear(object_field), linear(illumination), amplitudes, split_tables(window)]
-    obj, ill, amps, table, wanted = loaded(window, scalars, arrays)
+    remote = tuple(pltpu.with_memory_space_constraint(scalar, pltpu.HBM) for scalar in scalars)
+    (wanted,) = kernel_call(functools.partial(pick_kernel, window), "pick", [(8, LANES)], remote, [])
     wanted = shifted(wanted, "tile", 1)
+    obj, ill, amps, table = loaded(arrays)
     (rim,) = kernel_call(functools.partial(rim_kernel, window), "rim", [(2, window, window)], (), [wanted, obj])
     rim = shifted(rim, "tile", -1)
 
@@ -369,17 +405,47 @@
         moved = {d: exchanged(pieces[d], "pos", d) for d in reversed(range(1, classes))}
         return [pieces[0]] + [moved[d] for d in range(1, classes)]
 
-    near = spread(wave(0, window, classes, scalars, [obj, ill, amps, table]))
+    roll, state, work = scratch_of(window)
+    near = spread(
+        kernel_call(
+            functools.partial(first_wave_kernel, window, classes),
+            "wave0",
+            [(2 * share + 8, window)] * classes,
+            scalars,
+            [obj, ill, amps, table],
+            roll + state + work,
+            48 * window**3,
+        )
+    )
+    with jax.named_scope("start"):
+        probe, ordered, exits = kernel_call(
+            functools.partial(second_start_kernel, window),
+            "start1",
+            [(2, window, window), (window, window), (2, window, window)],
+            scalars,
+            [obj, ill, amps],
+            roll,
+        )
     (acc,) = kernel_call(
         functools.partial(first_sum_kernel, window, classes), "sum0", [(2, 2, share, columns)], (), near
     )
-    late = spread(wave(1, window, classes, scalars, [obj, ill, amps, table, rim]))
+    late = spread(
+        kernel_call(
+            functools.partial(second_wave_kernel, window, classes),
+            "wave1",
+            [(2 * share, window)] * classes,
+            scalars,
+            [probe, ordered, exits, table, rim],
+            work,
+            48 * window**3,
+        )
+    )
     sums = kernel_call(
         functools.partial(second_sum_kernel, window, classes),
         "sum1",
         [(4 * share, LANES)] * (3 * tiles),
         (),
-        [acc, *late],
+        [acc, *near, *late],
     )
     is_upper = lax.axis_index("pos") >= classes
     kept, received = [], []

time: 47.6 us -> 45.7 us (0.960)
  waiting for transfers between devices: 22.2 us -> 20.6 us
  starting transfers between devices: 15.3 us -> 14.2 us
  Pallas kernels: 9.83 us -> 10.6 us
    pallas_call x5 -> x7, Pallas kernels: 6.42 us -> 7.82 us  [kernel_call(): pl.pallas_call(body, out_shape=[pltpu.VMEM(shape, F32) for shape in out_s...]
    ppermute x8, waiting for transfers between devices: 16.9 us -> 15.9 us  [exchanged(): lax.ppermute(block, axis, [(i, i ^ flip) for i in range(lax.axis_size(axi...]
    ppermute x4, waiting for transfers between devices: 5.35 us -> 4.68 us  [shifted(): lax.ppermute(block, axis, [((i - distance) % devices, i) for i in range(d...]
    pallas_call x1, Pallas kernels: 2.64 us -> 1.96 us  [loaded(): pl.pallas_call(functools.partial(load_kernel, len(arrays)), out_shape=[pl...]
    ppermute x4, starting transfers between devices: 2.97 us -> 2.33 us  [shifted(): lax.ppermute(block, axis, [((i - distance) % devices, i) for i in range(d...]
  transfers between devices with their start and end apart: 12 -> 12, of which waited for: 8 -> 7; matrix products, arithmetic and copies ran while one was open for 0% -> 0% of each run, Pallas kernels for 12% -> 19%
where the time goes in v10:
time: 45.7 us; the launch traced here: 45.5 us
  waiting for transfers between devices  20.6 us (45%)
  starting transfers between devices  14.2 us (31%)
  Pallas kernels  10.6 us (23%)
    ppermute x8, waiting for transfers between devices, exchanged(): lax.ppermute(block, axis, [(i, i ^ flip) for i in range(lax.axis_size(axi...  15.9 us
    ppermute x8, starting transfers between devices, exchanged(): lax.ppermute(block, axis, [(i, i ^ flip) for i in range(lax.axis_size(axi...  11.8 us
    pallas_call x7, Pallas kernels, kernel_call(): pl.pallas_call(body, out_shape=[pltpu.VMEM(shape, F32) for shape in out_s...  7.82 us
    ppermute x4, waiting for transfers between devices, shifted(): lax.ppermute(block, axis, [((i - distance) % devices, i) for i in range(d...  4.68 us
    ppermute x4, starting transfers between devices, shifted(): lax.ppermute(block, axis, [((i - distance) % devices, i) for i in range(d...  2.33 us
    pallas_call x1, Pallas kernels, loaded(): pl.pallas_call(functools.partial(load_kernel, len(arrays)), out_shape=[pl...  1.96 us
  transfers between devices with their start and end apart: 12, of which 7 were waited for; matrix products, arithmetic and copies ran while one was open for 0% of the time, Pallas kernels for 19%

profile of v10, /device:TPU:0, one launch (start us, length us, event | category | flops | bytes accessed | tf_op | source)
XLA Modules:
  0.0 45.5 jit_solution(13943409552227294898)
XLA Ops:
  0.0 0.7 %pick.1 = f32[8,128]{1,0:T(8,128)S(1)} custom-call(s32[2]{0:T(128)} %rows.7, s32[2]{0:T(128)} %cols.7), custom_call_target="tpu_custom_call" | custom-call | bytes 8192 | tf_op jit(solution)/shard_map/pick/pallas_call | solution.py:71
  0.7 0.5 %collective-permute-start.3 = (f32[8,128]{1,0:T(8,128)S(1)}, f32[8,128]{1,0:T(8,128)S(1)}, u32[]{:S(2)}, u32[]{:S(2)}) collective-permute-start(f32[8,128]{1,0:T(8,128)S(1)} %pick.1), channel_id=1, source_target_pairs={{24,0},{0,8},{8,16},{16,24},{25,1},{1,9},{9,17},{17,25},{26,2},{2,... | collective-permute-start | bytes 12296 | tf_op jit(solution)/shard_map/ppermute | solution.py:19
  1.2 2.0 %load.1 = (f32[4096,128]{1,0:T(8,128)S(1)}, f32[1024,128]{1,0:T(8,128)S(1)}, bf16[2,256,256]{2,1,0:T(8,128)(2,1)S(1)}, bf16[768,384]{1,0:T(8,128)(2,1)S(1)}) custom-call(f32[4096,128]{1,0:T(8,128)} %bitcast.15, f32[1024,128]{1,0:T(8,128)} %bitcast.16, bf16[2,256,256]{2,1,0:T(8,128)(2,1)} %refs_2_.1, bf16[768,384]{1,0:T(8,128)(2,1)} %constant.8.clone.refs_3_), custom_call_target="tpu_custom_call" | custom-call | tf_op jit(solution)/shard_map/load/pallas_call | solution.py:99
  3.2 0.0 copy-start
  3.2 0.0 copy-start.1
  3.2 1.2 %collective-permute-done.3.wanted = f32[8,128]{1,0:T(8,128)S(1)} collective-permute-done((f32[8,128]{1,0:T(8,128)S(1)}, f32[8,128]{1,0:T(8,128)S(1)}, u32[]{:S(2)}, u32[]{:S(2)}) %collective-permute-start.3) | collective-permute-done | bytes 4128 | tf_op jit(solution)/shard_map/ppermute | solution.py:19
  4.5 0.2 rim.1
  4.7 0.8 %collective-permute-start.4 = (f32[2,256,256]{2,1,0:T(8,128)S(1)}, f32[2,256,256]{2,1,0:T(8,128)S(1)}, u32[]{:S(2)}, u32[]{:S(2)}) collective-permute-start(f32[2,256,256]{2,1,0:T(8,128)S(1)} %rim.1), channel_id=1, source_target_pairs={{8,0},{16,8},{24,16},{0,24},{9,1},{17,9},{25,17},{1,25},{10,2},{18... | collective-permute-start | bytes 1572872 | tf_op jit(solution)/shard_map/ppermute | solution.py:19
  5.4 2.8 %wave0.1 = (f32[136,256]{1,0:T(8,128)S(1)}, f32[136,256]{1,0:T(8,128)S(1)}, f32[136,256]{1,0:T(8,128)S(1)}, f32[136,256]{1,0:T(8,128)S(1)}) custom-call(s32[2]{0:T(128)S(1)} %copy-done, s32[2]{0:T(128)S(1)} %copy-done.1, f32[4096,128]{1,0:T(8,128)S(1)} %get-tuple-element.26.obj, f32[1024,128]{1,0:T(8,128)S(1)} %get-tuple-element.27.ill, ...), custom_call_target="tpu_custom_call" | custom-call | flops 805306368 | bytes 1114112 | tf_op jit(solution)/shard_map/wave0/pallas_call | solution.py:71
  8.2 2.3 %collective-permute-start = (f32[136,256]{1,0:T(8,128)S(1)}, f32[136,256]{1,0:T(8,128)S(1)}, u32[]{:S(2)}, u32[]{:S(2)}) collective-permute-start(f32[136,256]{1,0:T(8,128)S(1)} %get-tuple-element.31), channel_id=1, source_target_pairs={{0,1},{1,0},{2,3},{3,2},{4,5},{5,4},{6,7},{7,6},{8,9},{9,8},{10,11... | collective-permute-start | bytes 417800 | tf_op jit(solution)/shard_map/ppermute | solution.py:23
  10.6 1.6 %collective-permute-start.1 = (f32[136,256]{1,0:T(8,128)S(1)}, f32[136,256]{1,0:T(8,128)S(1)}, u32[]{:S(2)}, u32[]{:S(2)}) collective-permute-start(f32[136,256]{1,0:T(8,128)S(1)} %get-tuple-element.32), channel_id=1, source_target_pairs={{0,2},{1,3},{2,0},{3,1},{4,6},{5,7},{6,4},{7,5},{8,10},{9,11},{10,... | collective-permute-start | bytes 417800 | tf_op jit(solution)/shard_map/ppermute | solution.py:23
  12.1 0.0 collective-permute-start.2
  12.1 1.1 %start1.1 = (f32[2,256,256]{2,1,0:T(8,128)S(1)}, f32[256,256]{1,0:T(8,128)S(1)}, f32[2,256,256]{2,1,0:T(8,128)S(1)}) custom-call(s32[2]{0:T(128)S(1)} %copy-done, s32[2]{0:T(128)S(1)} %copy-done.1, f32[4096,128]{1,0:T(8,128)S(1)} %get-tuple-element.26.obj, f32[1024,128]{1,0:T(8,128)S(1)} %get-tuple-element.27.ill, ...), custom_call_target="tpu_custom_call" | custom-call | bytes 2621440 | tf_op jit(solution)/shard_map/start/start1/pallas_call | solution.py:71
  13.3 2.5 %wave1.1 = (f32[128,256]{1,0:T(8,128)S(1)}, f32[128,256]{1,0:T(8,128)S(1)}, f32[128,256]{1,0:T(8,128)S(1)}, f32[128,256]{1,0:T(8,128)S(1)}) custom-call(s32[2]{0:T(128)S(1)} %copy-done, s32[2]{0:T(128)S(1)} %copy-done.1, f32[2,256,256]{2,1,0:T(8,128)S(1)} %get-tuple-element.34.probe, f32[256,256]{1,0:T(8,128)S(1)} %get-tuple-element.35.ordered, ...), custom_call_target="tpu_custom_call" | custom-call | flops 805306368 | bytes 1048576 | tf_op jit(solution)/shard_map/wave1/pallas_call | solution.py:71
  15.7 2.0 %collective-permute-start.5 = (f32[128,256]{1,0:T(8,128)S(1)}, f32[128,256]{1,0:T(8,128)S(1)}, u32[]{:S(2)}, u32[]{:S(2)}) collective-permute-start(f32[128,256]{1,0:T(8,128)S(1)} %get-tuple-element.38), channel_id=1, source_target_pairs={{0,1},{1,0},{2,3},{3,2},{4,5},{5,4},{6,7},{7,6},{8,9},{9,8},{10,11... | collective-permute-start | bytes 393224 | tf_op jit(solution)/shard_map/ppermute | solution.py:23
  17.7 1.6 %collective-permute-start.6 = (f32[128,256]{1,0:T(8,128)S(1)}, f32[128,256]{1,0:T(8,128)S(1)}, u32[]{:S(2)}, u32[]{:S(2)}) collective-permute-start(f32[128,256]{1,0:T(8,128)S(1)} %get-tuple-element.39), channel_id=1, source_target_pairs={{0,2},{1,3},{2,0},{3,1},{4,6},{5,7},{6,4},{7,5},{8,10},{9,11},{10,... | collective-permute-start | bytes 393224 | tf_op jit(solution)/shard_map/ppermute | solution.py:23
  19.3 0.0 collective-permute-done.refs_1_
  19.3 0.0 collective-permute-done.2.refs_3_
  19.3 0.2 sum0.1.acc
  19.5 1.8 %collective-permute-done.5.refs_5_ = f32[128,256]{1,0:T(8,128)S(1)} collective-permute-done((f32[128,256]{1,0:T(8,128)S(1)}, f32[128,256]{1,0:T(8,128)S(1)}, u32[]{:S(2)}, u32[]{:S(2)}) %collective-permute-start.5) | collective-permute-done | bytes 131104 | tf_op jit(solution)/shard_map/ppermute | solution.py:23
  21.4 2.6 %collective-permute-done.6.refs_6_ = f32[128,256]{1,0:T(8,128)S(1)} collective-permute-done((f32[128,256]{1,0:T(8,128)S(1)}, f32[128,256]{1,0:T(8,128)S(1)}, u32[]{:S(2)}, u32[]{:S(2)}) %collective-permute-start.6) | collective-permute-done | bytes 131104 | tf_op jit(solution)/shard_map/ppermute | solution.py:23
  24.0 2.4 %collective-permute-done.7.refs_7_ = f32[128,256]{1,0:T(8,128)S(1)} collective-permute-done((f32[128,256]{1,0:T(8,128)S(1)}, f32[128,256]{1,0:T(8,128)S(1)}, u32[]{:S(2)}, u32[]{:S(2)}) %collective-permute-start.7) | collective-permute-done | bytes 131104 | tf_op jit(solution)/shard_map/ppermute | solution.py:23
  26.4 0.4 sum1.1
  26.8 0.1 collective-permute-start.9
  26.9 0.9 %collective-permute-start.8 = (f32[256,128]{1,0:T(8,128)S(1)}, f32[256,128]{1,0:T(8,128)S(1)}, u32[]{:S(2)}, u32[]{:S(2)}) collective-permute-start(f32[256,128]{1,0:T(8,128)S(1)} %get-tuple-element.43), channel_id=1, source_target_pairs={{24,0},{0,8},{8,16},{16,24},{25,1},{1,9},{9,17},{17,25},{26,2},{2,... | collective-permute-start | bytes 393224 | tf_op jit(solution)/shard_map/spill_0/ppermute | solution.py:19
  27.8 3.4 %collective-permute-done.9 = f32[256,128]{1,0:T(8,128)S(1)} collective-permute-done((f32[256,128]{1,0:T(8,128)S(1)}, f32[256,128]{1,0:T(8,128)S(1)}, u32[]{:S(2)}, u32[]{:S(2)}) %collective-permute-start.9) | collective-permute-done | bytes 131104 | tf_op jit(solution)/shard_map/spill_1/ppermute | solution.py:19
  31.3 3.0 %collective-permute-start.11 = (f32[256,128]{1,0:T(8,128)S(1)}, f32[256,128]{1,0:T(8,128)S(1)}, u32[]{:S(2)}, u32[]{:S(2)}) collective-permute-start(f32[256,128]{1,0:T(8,128)S(1)} %get-tuple-element.47), channel_id=1, source_target_pairs={{0,4},{1,5},{2,6},{3,7},{4,0},{5,1},{6,2},{7,3},{8,12},{9,13},{10,... | collective-permute-start | bytes 393224 | tf_op jit(solution)/shard_map/halves_1/ppermute | solution.py:23
  34.3 0.0 collective-permute-done.8
  34.3 1.4 %collective-permute-start.10 = (f32[256,128]{1,0:T(8,128)S(1)}, f32[256,128]{1,0:T(8,128)S(1)}, u32[]{:S(2)}, u32[]{:S(2)}) collective-permute-start(f32[256,128]{1,0:T(8,128)S(1)} %get-tuple-element.49), channel_id=1, source_target_pairs={{0,4},{1,5},{2,6},{3,7},{4,0},{5,1},{6,2},{7,3},{8,12},{9,13},{10,... | collective-permute-start | bytes 393224 | tf_op jit(solution)/shard_map/halves_0/ppermute | solution.py:23
  35.7 7.4 %collective-permute-done.11.refs_3_ = f32[256,128]{1,0:T(8,128)S(1)} collective-permute-done((f32[256,128]{1,0:T(8,128)S(1)}, f32[256,128]{1,0:T(8,128)S(1)}, u32[]{:S(2)}, u32[]{:S(2)}) %collective-permute-start.11) | collective-permute-done | bytes 131104 | tf_op jit(solution)/shard_map/halves_1/ppermute | solution.py:23
  43.1 1.7 %collective-permute-done.10.refs_2_ = f32[256,128]{1,0:T(8,128)S(1)} collective-permute-done((f32[256,128]{1,0:T(8,128)S(1)}, f32[256,128]{1,0:T(8,128)S(1)}, u32[]{:S(2)}, u32[]{:S(2)}) %collective-permute-start.10) | collective-permute-done | bytes 131104 | tf_op jit(solution)/shard_map/halves_0/ppermute | solution.py:23
  44.7 0.8 %final.1 = f32[512,128]{1,0:T(8,128)} custom-call(f32[256,128]{1,0:T(8,128)S(1)} %get-tuple-element.50.refs_0_, f32[256,128]{1,0:T(8,128)S(1)} %get-tuple-element.48.refs_1_, f32[256,128]{1,0:T(8,128)S(1)} %collective-permute-done.10.refs_2_, f32[256,128]{1,0:T(8,128)S(1)} %collective-permute-done.11.refs_3_), custom_call_target="tpu_custom_call" | custom-call | tf_op jit(solution)/shard_map/final/pallas_call | solution.py:460
  (7 shorter events, 0.1 us)
Async XLA Ops:
  0.7 3.8 %collective-permute-start.3 = (f32[8,128]{1,0:T(8,128)S(1)}, f32[8,128]{1,0:T(8,128)S(1)}, u32[]{:S(2)}, u32[]{:S(2)}) collective-permute-start(f32[8,128]{1,0:T(8,128)S(1)} %pick.1), channel_id=1, source_target_pairs={{24,0},{0,8},{8,16},{16,24},{25,1},{1,9},{9,17},{17,25},{26,2},{2,... | collective-permute-start | bytes 12296 | tf_op jit(solution)/shard_map/ppermute | solution.py:19
  3.2 2.2 %copy-start = (s32[2]{0:T(128)S(1)}, s32[2]{0:T(128)}, u32[]{:S(2)}) copy-start(s32[2]{0:T(128)} %rows.7) | copy-start | bytes 28
  3.2 2.2 %copy-start.1 = (s32[2]{0:T(128)S(1)}, s32[2]{0:T(128)}, u32[]{:S(2)}) copy-start(s32[2]{0:T(128)} %cols.7) | copy-start | bytes 28
  4.7 8.6 %collective-permute-start.4 = (f32[2,256,256]{2,1,0:T(8,128)S(1)}, f32[2,256,256]{2,1,0:T(8,128)S(1)}, u32[]{:S(2)}, u32[]{:S(2)}) collective-permute-start(f32[2,256,256]{2,1,0:T(8,128)S(1)} %rim.1), channel_id=1, source_target_pairs={{8,0},{16,8},{24,16},{0,24},{9,1},{17,9},{25,17},{1,25},{10,2},{18... | collective-permute-start | bytes 1572872 | tf_op jit(solution)/shard_map/ppermute | solution.py:19
  8.2 11.0 %collective-permute-start = (f32[136,256]{1,0:T(8,128)S(1)}, f32[136,256]{1,0:T(8,128)S(1)}, u32[]{:S(2)}, u32[]{:S(2)}) collective-permute-start(f32[136,256]{1,0:T(8,128)S(1)} %get-tuple-element.31), channel_id=1, source_target_pairs={{0,1},{1,0},{2,3},{3,2},{4,5},{5,4},{6,7},{7,6},{8,9},{9,8},{10,11... | collective-permute-start | bytes 417800 | tf_op jit(solution)/shard_map/ppermute | solution.py:23
  10.6 8.7 %collective-permute-start.1 = (f32[136,256]{1,0:T(8,128)S(1)}, f32[136,256]{1,0:T(8,128)S(1)}, u32[]{:S(2)}, u32[]{:S(2)}) collective-permute-start(f32[136,256]{1,0:T(8,128)S(1)} %get-tuple-element.32), channel_id=1, source_target_pairs={{0,2},{1,3},{2,0},{3,1},{4,6},{5,7},{6,4},{7,5},{8,10},{9,11},{10,... | collective-permute-start | bytes 417800 | tf_op jit(solution)/shard_map/ppermute | solution.py:23
  12.1 7.2 %collective-permute-start.2 = (f32[136,256]{1,0:T(8,128)S(1)}, f32[136,256]{1,0:T(8,128)S(1)}, u32[]{:S(2)}, u32[]{:S(2)}) collective-permute-start(f32[136,256]{1,0:T(8,128)S(1)} %get-tuple-element.33), channel_id=1, source_target_pairs={{0,3},{1,2},{2,1},{3,0},{4,7},{5,6},{6,5},{7,4},{8,11},{9,10},{10,... | collective-permute-start | bytes 417800 | tf_op jit(solution)/shard_map/ppermute | solution.py:23
  15.7 5.7 %collective-permute-start.5 = (f32[128,256]{1,0:T(8,128)S(1)}, f32[128,256]{1,0:T(8,128)S(1)}, u32[]{:S(2)}, u32[]{:S(2)}) collective-permute-start(f32[128,256]{1,0:T(8,128)S(1)} %get-tuple-element.38), channel_id=1, source_target_pairs={{0,1},{1,0},{2,3},{3,2},{4,5},{5,4},{6,7},{7,6},{8,9},{9,8},{10,11... | collective-permute-start | bytes 393224 | tf_op jit(solution)/shard_map/ppermute | solution.py:23
  17.7 6.3 %collective-permute-start.6 = (f32[128,256]{1,0:T(8,128)S(1)}, f32[128,256]{1,0:T(8,128)S(1)}, u32[]{:S(2)}, u32[]{:S(2)}) collective-permute-start(f32[128,256]{1,0:T(8,128)S(1)} %get-tuple-element.39), channel_id=1, source_target_pairs={{0,2},{1,3},{2,0},{3,1},{4,6},{5,7},{6,4},{7,5},{8,10},{9,11},{10,... | collective-permute-start | bytes 393224 | tf_op jit(solution)/shard_map/ppermute | solution.py:23
  19.3 7.1 %collective-permute-start.7 = (f32[128,256]{1,0:T(8,128)S(1)}, f32[128,256]{1,0:T(8,128)S(1)}, u32[]{:S(2)}, u32[]{:S(2)}) collective-permute-start(f32[128,256]{1,0:T(8,128)S(1)} %get-tuple-element.40), channel_id=1, source_target_pairs={{0,3},{1,2},{2,1},{3,0},{4,7},{5,6},{6,5},{7,4},{8,11},{9,10},{10,... | collective-permute-start | bytes 393224 | tf_op jit(solution)/shard_map/ppermute | solution.py:23
  26.8 4.4 %collective-permute-start.9 = (f32[256,128]{1,0:T(8,128)S(1)}, f32[256,128]{1,0:T(8,128)S(1)}, u32[]{:S(2)}, u32[]{:S(2)}) collective-permute-start(f32[256,128]{1,0:T(8,128)S(1)} %get-tuple-element.46), channel_id=1, source_target_pairs={{24,0},{0,8},{8,16},{16,24},{25,1},{1,9},{9,17},{17,25},{26,2},{2,... | collective-permute-start | bytes 393224 | tf_op jit(solution)/shard_map/spill_1/ppermute | solution.py:19
  26.9 7.4 %collective-permute-start.8 = (f32[256,128]{1,0:T(8,128)S(1)}, f32[256,128]{1,0:T(8,128)S(1)}, u32[]{:S(2)}, u32[]{:S(2)}) collective-permute-start(f32[256,128]{1,0:T(8,128)S(1)} %get-tuple-element.43), channel_id=1, source_target_pairs={{24,0},{0,8},{8,16},{16,24},{25,1},{1,9},{9,17},{17,25},{26,2},{2,... | collective-permute-start | bytes 393224 | tf_op jit(solution)/shard_map/spill_0/ppermute | solution.py:19
  31.3 11.8 %collective-permute-start.11 = (f32[256,128]{1,0:T(8,128)S(1)}, f32[256,128]{1,0:T(8,128)S(1)}, u32[]{:S(2)}, u32[]{:S(2)}) collective-permute-start(f32[256,128]{1,0:T(8,128)S(1)} %get-tuple-element.47), channel_id=1, source_target_pairs={{0,4},{1,5},{2,6},{3,7},{4,0},{5,1},{6,2},{7,3},{8,12},{9,13},{10,... | collective-permute-start | bytes 393224 | tf_op jit(solution)/shard_map/halves_1/ppermute | solution.py:23
  34.3 10.4 %collective-permute-start.10 = (f32[256,128]{1,0:T(8,128)S(1)}, f32[256,128]{1,0:T(8,128)S(1)}, u32[]{:S(2)}, u32[]{:S(2)}) collective-permute-start(f32[256,128]{1,0:T(8,128)S(1)} %get-tuple-element.49), channel_id=1, source_target_pairs={{0,4},{1,5},{2,6},{3,7},{4,0},{5,1},{6,2},{7,3},{8,12},{9,13},{10,... | collective-permute-start | bytes 393224 | tf_op jit(solution)/shard_map/halves_0/ppermute | solution.py:23

commit v11 on v10

--- a/solution.py
+++ b/solution.py
@@ -368,19 +368,19 @@
         for k in range(3):
             for half in range(2):
                 for tile in range(tiles):
-                    outs[3 * tile + k][pl.ds((half * 2 + part) * share, share), :] = total[k][half][
+                    outs[3 * (2 * tile + part) + k][pl.ds(half * share, share), :] = total[k][half][
                         :, tile * LANES : (tile + 1) * LANES
                     ]
 
 
 def final_kernel(tiles, share, *refs):
-    kept, received, out = refs[:tiles], refs[tiles : 2 * tiles], refs[2 * tiles]
-    for tile in range(tiles):
+    chunks = 2 * tiles
+    kept, received, out = refs[:chunks], refs[chunks : 2 * chunks], refs[2 * chunks]
+    for chunk in range(chunks):
         for half in range(2):
-            for part in range(2):
-                here = pl.ds((half * 2 + part) * share, share)
-                line = (half * tiles + tile) * 2 + part
-                out[pl.ds(line, share, stride=4 * tiles), :] = kept[tile][here, :] + received[tile][here, :]
+            here = pl.ds(half * share, share)
+            line = half * chunks + chunk
+            out[pl.ds(line, share, stride=4 * tiles), :] = kept[chunk][here, :] + received[chunk][here, :]
 
 
 def on_device(object_field, illumination, amplitudes, row_offset, col_offset):
@@ -443,13 +443,13 @@
     sums = kernel_call(
         functools.partial(second_sum_kernel, window, classes),
         "sum1",
-        [(4 * share, LANES)] * (3 * tiles),
+        [(2 * share, LANES)] * (6 * tiles),
         (),
         [acc, *near, *late],
     )
     is_upper = lax.axis_index("pos") >= classes
     kept, received = [], []
-    for chunk in range(tiles):
+    for chunk in range(2 * tiles):
         top, middle, spilled = sums[3 * chunk : 3 * chunk + 3]
         with jax.named_scope("spill_" + str(chunk)):
             top = top + shifted(spilled, "tile", 1)
@@ -460,7 +460,7 @@
     result = pl.pallas_call(
         functools.partial(final_kernel, tiles, share),
         out_shape=jax.ShapeDtypeStruct((share * 4 * tiles, LANES), F32),
-        in_specs=[pl.BlockSpec(memory_space=pltpu.VMEM)] * (2 * tiles),
+        in_specs=[pl.BlockSpec(memory_space=pltpu.VMEM)] * (4 * tiles),
         out_specs=pl.BlockSpec(memory_space=pltpu.VMEM),
         compiler_params=pltpu.CompilerParams(vmem_limit_bytes=16 << 20),
         name="final",

time: 45.7 us -> 45.9 us (level)
  starting transfers between devices: 14.2 us -> 17.8 us
  waiting for transfers between devices: 20.6 us -> 17.2 us
    ppermute x8 -> x10, starting transfers between devices: 11.8 us -> 14.2 us  [exchanged(): lax.ppermute(block, axis, [(i, i ^ flip) for i in range(lax.axis_size(axi...]
    ppermute x4 -> x6, waiting for transfers between devices: 4.68 us -> 2.68 us  [shifted(): lax.ppermute(block, axis, [((i - distance) % devices, i) for i in range(d...]
    ppermute x8 -> x10, waiting for transfers between devices: 15.9 us -> 14.5 us  [exchanged(): lax.ppermute(block, axis, [(i, i ^ flip) for i in range(lax.axis_size(axi...]
    ppermute x4 -> x6, starting transfers between devices: 2.33 us -> 3.63 us  [shifted(): lax.ppermute(block, axis, [((i - distance) % devices, i) for i in range(d...]
  transfers between devices with their start and end apart: 12 -> 16, of which waited for: 7 -> 8; matrix products, arithmetic and copies ran while one was open for 0% -> 0% of each run, Pallas kernels for 19% -> 19%
where the time goes in v11:
time: 45.9 us; the launch traced here: 45.7 us
  starting transfers between devices  17.8 us (39%)
  waiting for transfers between devices  17.2 us (37%)
  Pallas kernels  10.6 us (23%)
    ppermute x10, waiting for transfers between devices, exchanged(): lax.ppermute(block, axis, [(i, i ^ flip) for i in range(lax.axis_size(axi...  14.5 us
    ppermute x10, starting transfers between devices, exchanged(): lax.ppermute(block, axis, [(i, i ^ flip) for i in range(lax.axis_size(axi...  14.2 us
    pallas_call x7, Pallas kernels, kernel_call(): pl.pallas_call(body, out_shape=[pltpu.VMEM(shape, F32) for shape in out_s...  7.82 us
    ppermute x6, starting transfers between devices, shifted(): lax.ppermute(block, axis, [((i - distance) % devices, i) for i in range(d...  3.63 us
    ppermute x6, waiting for transfers between devices, shifted(): lax.ppermute(block, axis, [((i - distance) % devices, i) for i in range(d...  2.68 us
    pallas_call x1, Pallas kernels, loaded(): pl.pallas_call(functools.partial(load_kernel, len(arrays)), out_shape=[pl...  1.96 us
  transfers between devices with their start and end apart: 16, of which 8 were waited for; matrix products, arithmetic and copies ran while one was open for 0% of the time, Pallas kernels for 19%

profile of v11, /device:TPU:0, one launch (start us, length us, event | category | flops | bytes accessed | tf_op | source)
XLA Modules:
  0.0 45.7 jit_solution(7599192346657568003)
XLA Ops:
  0.0 0.7 %pick.1 = f32[8,128]{1,0:T(8,128)S(1)} custom-call(s32[2]{0:T(128)} %rows.7, s32[2]{0:T(128)} %cols.7), custom_call_target="tpu_custom_call" | custom-call | bytes 8192 | tf_op jit(solution)/shard_map/pick/pallas_call | solution.py:71
  0.7 0.5 %collective-permute-start.3 = (f32[8,128]{1,0:T(8,128)S(1)}, f32[8,128]{1,0:T(8,128)S(1)}, u32[]{:S(2)}, u32[]{:S(2)}) collective-permute-start(f32[8,128]{1,0:T(8,128)S(1)} %pick.1), channel_id=1, source_target_pairs={{24,0},{0,8},{8,16},{16,24},{25,1},{1,9},{9,17},{17,25},{26,2},{2,... | collective-permute-start | bytes 12296 | tf_op jit(solution)/shard_map/ppermute | solution.py:19
  1.2 2.0 %load.1 = (f32[4096,128]{1,0:T(8,128)S(1)}, f32[1024,128]{1,0:T(8,128)S(1)}, bf16[2,256,256]{2,1,0:T(8,128)(2,1)S(1)}, bf16[768,384]{1,0:T(8,128)(2,1)S(1)}) custom-call(f32[4096,128]{1,0:T(8,128)} %bitcast.15, f32[1024,128]{1,0:T(8,128)} %bitcast.16, bf16[2,256,256]{2,1,0:T(8,128)(2,1)} %refs_2_.1, bf16[768,384]{1,0:T(8,128)(2,1)} %constant.8.clone.refs_3_), custom_call_target="tpu_custom_call" | custom-call | tf_op jit(solution)/shard_map/load/pallas_call | solution.py:99
  3.2 0.0 copy-start
  3.2 1.2 %collective-permute-done.3.wanted = f32[8,128]{1,0:T(8,128)S(1)} collective-permute-done((f32[8,128]{1,0:T(8,128)S(1)}, f32[8,128]{1,0:T(8,128)S(1)}, u32[]{:S(2)}, u32[]{:S(2)}) %collective-permute-start.3) | collective-permute-done | bytes 4128 | tf_op jit(solution)/shard_map/ppermute | solution.py:19
  4.5 0.2 rim.1
  4.7 0.8 %collective-permute-start.4 = (f32[2,256,256]{2,1,0:T(8,128)S(1)}, f32[2,256,256]{2,1,0:T(8,128)S(1)}, u32[]{:S(2)}, u32[]{:S(2)}) collective-permute-start(f32[2,256,256]{2,1,0:T(8,128)S(1)} %rim.1), channel_id=1, source_target_pairs={{8,0},{16,8},{24,16},{0,24},{9,1},{17,9},{25,17},{1,25},{10,2},{18... | collective-permute-start | bytes 1572872 | tf_op jit(solution)/shard_map/ppermute | solution.py:19
  5.4 2.8 %wave0.1 = (f32[136,256]{1,0:T(8,128)S(1)}, f32[136,256]{1,0:T(8,128)S(1)}, f32[136,256]{1,0:T(8,128)S(1)}, f32[136,256]{1,0:T(8,128)S(1)}) custom-call(s32[2]{0:T(128)S(1)} %copy-done, s32[2]{0:T(128)S(1)} %copy-done.1, f32[4096,128]{1,0:T(8,128)S(1)} %get-tuple-element.32.obj, f32[1024,128]{1,0:T(8,128)S(1)} %get-tuple-element.33.ill, ...), custom_call_target="tpu_custom_call" | custom-call | flops 805306368 | bytes 1114112 | tf_op jit(solution)/shard_map/wave0/pallas_call | solution.py:71
  8.2 2.3 %collective-permute-start = (f32[136,256]{1,0:T(8,128)S(1)}, f32[136,256]{1,0:T(8,128)S(1)}, u32[]{:S(2)}, u32[]{:S(2)}) collective-permute-start(f32[136,256]{1,0:T(8,128)S(1)} %get-tuple-element.37), channel_id=1, source_target_pairs={{0,1},{1,0},{2,3},{3,2},{4,5},{5,4},{6,7},{7,6},{8,9},{9,8},{10,11... | collective-permute-start | bytes 417800 | tf_op jit(solution)/shard_map/ppermute | solution.py:23
  10.6 1.6 %collective-permute-start.1 = (f32[136,256]{1,0:T(8,128)S(1)}, f32[136,256]{1,0:T(8,128)S(1)}, u32[]{:S(2)}, u32[]{:S(2)}) collective-permute-start(f32[136,256]{1,0:T(8,128)S(1)} %get-tuple-element.38), channel_id=1, source_target_pairs={{0,2},{1,3},{2,0},{3,1},{4,6},{5,7},{6,4},{7,5},{8,10},{9,11},{10,... | collective-permute-start | bytes 417800 | tf_op jit(solution)/shard_map/ppermute | solution.py:23
  12.1 1.1 %start1.1 = (f32[2,256,256]{2,1,0:T(8,128)S(1)}, f32[256,256]{1,0:T(8,128)S(1)}, f32[2,256,256]{2,1,0:T(8,128)S(1)}) custom-call(s32[2]{0:T(128)S(1)} %copy-done, s32[2]{0:T(128)S(1)} %copy-done.1, f32[4096,128]{1,0:T(8,128)S(1)} %get-tuple-element.32.obj, f32[1024,128]{1,0:T(8,128)S(1)} %get-tuple-element.33.ill, ...), custom_call_target="tpu_custom_call" | custom-call | bytes 2621440 | tf_op jit(solution)/shard_map/start/start1/pallas_call | solution.py:71
  13.3 2.5 %wave1.1 = (f32[128,256]{1,0:T(8,128)S(1)}, f32[128,256]{1,0:T(8,128)S(1)}, f32[128,256]{1,0:T(8,128)S(1)}, f32[128,256]{1,0:T(8,128)S(1)}) custom-call(s32[2]{0:T(128)S(1)} %copy-done, s32[2]{0:T(128)S(1)} %copy-done.1, f32[2,256,256]{2,1,0:T(8,128)S(1)} %get-tuple-element.40.probe, f32[256,256]{1,0:T(8,128)S(1)} %get-tuple-element.41.ordered, ...), custom_call_target="tpu_custom_call" | custom-call | flops 805306368 | bytes 1048576 | tf_op jit(solution)/shard_map/wave1/pallas_call | solution.py:71
  15.7 2.0 %collective-permute-start.5 = (f32[128,256]{1,0:T(8,128)S(1)}, f32[128,256]{1,0:T(8,128)S(1)}, u32[]{:S(2)}, u32[]{:S(2)}) collective-permute-start(f32[128,256]{1,0:T(8,128)S(1)} %get-tuple-element.44), channel_id=1, source_target_pairs={{0,1},{1,0},{2,3},{3,2},{4,5},{5,4},{6,7},{7,6},{8,9},{9,8},{10,11... | collective-permute-start | bytes 393224 | tf_op jit(solution)/shard_map/ppermute | solution.py:23
  17.7 1.6 %collective-permute-start.6 = (f32[128,256]{1,0:T(8,128)S(1)}, f32[128,256]{1,0:T(8,128)S(1)}, u32[]{:S(2)}, u32[]{:S(2)}) collective-permute-start(f32[128,256]{1,0:T(8,128)S(1)} %get-tuple-element.45), channel_id=1, source_target_pairs={{0,2},{1,3},{2,0},{3,1},{4,6},{5,7},{6,4},{7,5},{8,10},{9,11},{10,... | collective-permute-start | bytes 393224 | tf_op jit(solution)/shard_map/ppermute | solution.py:23
  19.3 0.2 sum0.1.acc
  19.5 1.8 %collective-permute-done.5.refs_5_ = f32[128,256]{1,0:T(8,128)S(1)} collective-permute-done((f32[128,256]{1,0:T(8,128)S(1)}, f32[128,256]{1,0:T(8,128)S(1)}, u32[]{:S(2)}, u32[]{:S(2)}) %collective-permute-start.5) | collective-permute-done | bytes 131104 | tf_op jit(solution)/shard_map/ppermute | solution.py:23
  21.4 2.6 %collective-permute-done.6.refs_6_ = f32[128,256]{1,0:T(8,128)S(1)} collective-permute-done((f32[128,256]{1,0:T(8,128)S(1)}, f32[128,256]{1,0:T(8,128)S(1)}, u32[]{:S(2)}, u32[]{:S(2)}) %collective-permute-start.6) | collective-permute-done | bytes 131104 | tf_op jit(solution)/shard_map/ppermute | solution.py:23
  24.0 2.4 %collective-permute-done.7.refs_7_ = f32[128,256]{1,0:T(8,128)S(1)} collective-permute-done((f32[128,256]{1,0:T(8,128)S(1)}, f32[128,256]{1,0:T(8,128)S(1)}, u32[]{:S(2)}, u32[]{:S(2)}) %collective-permute-start.7) | collective-permute-done | bytes 131104 | tf_op jit(solution)/shard_map/ppermute | solution.py:23
  26.4 0.4 sum1.1
  26.8 0.1 collective-permute-start.11
  26.9 0.9 %collective-permute-start.10 = (f32[128,128]{1,0:T(8,128)S(1)}, f32[128,128]{1,0:T(8,128)S(1)}, u32[]{:S(2)}, u32[]{:S(2)}) collective-permute-start(f32[128,128]{1,0:T(8,128)S(1)} %get-tuple-element.55), channel_id=1, source_target_pairs={{24,0},{0,8},{8,16},{16,24},{25,1},{1,9},{9,17},{17,25},{26,2},{2,... | collective-permute-start | bytes 196616 | tf_op jit(solution)/shard_map/spill_2/ppermute | solution.py:19
  27.8 0.1 collective-permute-start.9
  27.9 1.2 %collective-permute-start.8 = (f32[128,128]{1,0:T(8,128)S(1)}, f32[128,128]{1,0:T(8,128)S(1)}, u32[]{:S(2)}, u32[]{:S(2)}) collective-permute-start(f32[128,128]{1,0:T(8,128)S(1)} %get-tuple-element.49), channel_id=1, source_target_pairs={{24,0},{0,8},{8,16},{16,24},{25,1},{1,9},{9,17},{17,25},{26,2},{2,... | collective-permute-start | bytes 196616 | tf_op jit(solution)/shard_map/spill_0/ppermute | solution.py:19
  29.2 1.4 %collective-permute-done.11 = f32[128,128]{1,0:T(8,128)S(1)} collective-permute-done((f32[128,128]{1,0:T(8,128)S(1)}, f32[128,128]{1,0:T(8,128)S(1)}, u32[]{:S(2)}, u32[]{:S(2)}) %collective-permute-start.11) | collective-permute-done | bytes 65568 | tf_op jit(solution)/shard_map/spill_3/ppermute | solution.py:19
  30.6 3.0 %collective-permute-start.15 = (f32[128,128]{1,0:T(8,128)S(1)}, f32[128,128]{1,0:T(8,128)S(1)}, u32[]{:S(2)}, u32[]{:S(2)}) collective-permute-start(f32[128,128]{1,0:T(8,128)S(1)} %get-tuple-element.59), channel_id=1, source_target_pairs={{0,4},{1,5},{2,6},{3,7},{4,0},{5,1},{6,2},{7,3},{8,12},{9,13},{10,... | collective-permute-start | bytes 196616 | tf_op jit(solution)/shard_map/halves_3/ppermute | solution.py:23
  33.6 0.7 %collective-permute-start.14 = (f32[128,128]{1,0:T(8,128)S(1)}, f32[128,128]{1,0:T(8,128)S(1)}, u32[]{:S(2)}, u32[]{:S(2)}) collective-permute-start(f32[128,128]{1,0:T(8,128)S(1)} %get-tuple-element.61), channel_id=1, source_target_pairs={{0,4},{1,5},{2,6},{3,7},{4,0},{5,1},{6,2},{7,3},{8,12},{9,13},{10,... | collective-permute-start | bytes 196616 | tf_op jit(solution)/shard_map/halves_2/ppermute | solution.py:23
  34.3 2.4 %collective-permute-start.13 = (f32[128,128]{1,0:T(8,128)S(1)}, f32[128,128]{1,0:T(8,128)S(1)}, u32[]{:S(2)}, u32[]{:S(2)}) collective-permute-start(f32[128,128]{1,0:T(8,128)S(1)} %get-tuple-element.63), channel_id=1, source_target_pairs={{0,4},{1,5},{2,6},{3,7},{4,0},{5,1},{6,2},{7,3},{8,12},{9,13},{10,... | collective-permute-start | bytes 196616 | tf_op jit(solution)/shard_map/halves_1/ppermute | solution.py:23
  36.7 0.7 %collective-permute-start.12 = (f32[128,128]{1,0:T(8,128)S(1)}, f32[128,128]{1,0:T(8,128)S(1)}, u32[]{:S(2)}, u32[]{:S(2)}) collective-permute-start(f32[128,128]{1,0:T(8,128)S(1)} %get-tuple-element.65), channel_id=1, source_target_pairs={{0,4},{1,5},{2,6},{3,7},{4,0},{5,1},{6,2},{7,3},{8,12},{9,13},{10,... | collective-permute-start | bytes 196616 | tf_op jit(solution)/shard_map/halves_0/ppermute | solution.py:23
  37.4 4.8 %collective-permute-done.14.refs_6_ = f32[128,128]{1,0:T(8,128)S(1)} collective-permute-done((f32[128,128]{1,0:T(8,128)S(1)}, f32[128,128]{1,0:T(8,128)S(1)}, u32[]{:S(2)}, u32[]{:S(2)}) %collective-permute-start.14) | collective-permute-done | bytes 65568 | tf_op jit(solution)/shard_map/halves_2/ppermute | solution.py:23
  42.2 2.1 %collective-permute-done.13.refs_5_ = f32[128,128]{1,0:T(8,128)S(1)} collective-permute-done((f32[128,128]{1,0:T(8,128)S(1)}, f32[128,128]{1,0:T(8,128)S(1)}, u32[]{:S(2)}, u32[]{:S(2)}) %collective-permute-start.13) | collective-permute-done | bytes 65568 | tf_op jit(solution)/shard_map/halves_1/ppermute | solution.py:23
  44.3 0.7 %collective-permute-done.12.refs_4_ = f32[128,128]{1,0:T(8,128)S(1)} collective-permute-done((f32[128,128]{1,0:T(8,128)S(1)}, f32[128,128]{1,0:T(8,128)S(1)}, u32[]{:S(2)}, u32[]{:S(2)}) %collective-permute-start.12) | collective-permute-done | bytes 65568 | tf_op jit(solution)/shard_map/halves_0/ppermute | solution.py:23
  45.0 0.8 %final.1 = f32[512,128]{1,0:T(8,128)} custom-call(f32[128,128]{1,0:T(8,128)S(1)} %get-tuple-element.66.refs_0_, f32[128,128]{1,0:T(8,128)S(1)} %get-tuple-element.64.refs_1_, f32[128,128]{1,0:T(8,128)S(1)} %get-tuple-element.62.refs_2_, f32[128,128]{1,0:T(8,128)S(1)} %get-tuple-element.60.refs_3_, f32[128,128]{1,0:T(8,128)S(1)} %collective-permute-done.12.refs_4_, ...), custom_call_target="tpu_custom_call" | custom-call | tf_op jit(solution)/shard_map/final/pallas_call | solution.py:460
  (17 shorter events, 0.1 us)
Async XLA Ops:
  0.7 3.8 %collective-permute-start.3 = (f32[8,128]{1,0:T(8,128)S(1)}, f32[8,128]{1,0:T(8,128)S(1)}, u32[]{:S(2)}, u32[]{:S(2)}) collective-permute-start(f32[8,128]{1,0:T(8,128)S(1)} %pick.1), channel_id=1, source_target_pairs={{24,0},{0,8},{8,16},{16,24},{25,1},{1,9},{9,17},{17,25},{26,2},{2,... | collective-permute-start | bytes 12296 | tf_op jit(solution)/shard_map/ppermute | solution.py:19
  3.2 2.2 %copy-start = (s32[2]{0:T(128)S(1)}, s32[2]{0:T(128)}, u32[]{:S(2)}) copy-start(s32[2]{0:T(128)} %rows.7) | copy-start | bytes 28
  3.2 2.2 %copy-start.1 = (s32[2]{0:T(128)S(1)}, s32[2]{0:T(128)}, u32[]{:S(2)}) copy-start(s32[2]{0:T(128)} %cols.7) | copy-start | bytes 28
  4.7 8.6 %collective-permute-start.4 = (f32[2,256,256]{2,1,0:T(8,128)S(1)}, f32[2,256,256]{2,1,0:T(8,128)S(1)}, u32[]{:S(2)}, u32[]{:S(2)}) collective-permute-start(f32[2,256,256]{2,1,0:T(8,128)S(1)} %rim.1), channel_id=1, source_target_pairs={{8,0},{16,8},{24,16},{0,24},{9,1},{17,9},{25,17},{1,25},{10,2},{18... | collective-permute-start | bytes 1572872 | tf_op jit(solution)/shard_map/ppermute | solution.py:19
  8.2 11.0 %collective-permute-start = (f32[136,256]{1,0:T(8,128)S(1)}, f32[136,256]{1,0:T(8,128)S(1)}, u32[]{:S(2)}, u32[]{:S(2)}) collective-permute-start(f32[136,256]{1,0:T(8,128)S(1)} %get-tuple-element.37), channel_id=1, source_target_pairs={{0,1},{1,0},{2,3},{3,2},{4,5},{5,4},{6,7},{7,6},{8,9},{9,8},{10,11... | collective-permute-start | bytes 417800 | tf_op jit(solution)/shard_map/ppermute | solution.py:23
  10.6 8.7 %collective-permute-start.1 = (f32[136,256]{1,0:T(8,128)S(1)}, f32[136,256]{1,0:T(8,128)S(1)}, u32[]{:S(2)}, u32[]{:S(2)}) collective-permute-start(f32[136,256]{1,0:T(8,128)S(1)} %get-tuple-element.38), channel_id=1, source_target_pairs={{0,2},{1,3},{2,0},{3,1},{4,6},{5,7},{6,4},{7,5},{8,10},{9,11},{10,... | collective-permute-start | bytes 417800 | tf_op jit(solution)/shard_map/ppermute | solution.py:23
  12.1 7.2 %collective-permute-start.2 = (f32[136,256]{1,0:T(8,128)S(1)}, f32[136,256]{1,0:T(8,128)S(1)}, u32[]{:S(2)}, u32[]{:S(2)}) collective-permute-start(f32[136,256]{1,0:T(8,128)S(1)} %get-tuple-element.39), channel_id=1, source_target_pairs={{0,3},{1,2},{2,1},{3,0},{4,7},{5,6},{6,5},{7,4},{8,11},{9,10},{10,... | collective-permute-start | bytes 417800 | tf_op jit(solution)/shard_map/ppermute | solution.py:23
  15.7 5.7 %collective-permute-start.5 = (f32[128,256]{1,0:T(8,128)S(1)}, f32[128,256]{1,0:T(8,128)S(1)}, u32[]{:S(2)}, u32[]{:S(2)}) collective-permute-start(f32[128,256]{1,0:T(8,128)S(1)} %get-tuple-element.44), channel_id=1, source_target_pairs={{0,1},{1,0},{2,3},{3,2},{4,5},{5,4},{6,7},{7,6},{8,9},{9,8},{10,11... | collective-permute-start | bytes 393224 | tf_op jit(solution)/shard_map/ppermute | solution.py:23
  17.7 6.3 %collective-permute-start.6 = (f32[128,256]{1,0:T(8,128)S(1)}, f32[128,256]{1,0:T(8,128)S(1)}, u32[]{:S(2)}, u32[]{:S(2)}) collective-permute-start(f32[128,256]{1,0:T(8,128)S(1)} %get-tuple-element.45), channel_id=1, source_target_pairs={{0,2},{1,3},{2,0},{3,1},{4,6},{5,7},{6,4},{7,5},{8,10},{9,11},{10,... | collective-permute-start | bytes 393224 | tf_op jit(solution)/shard_map/ppermute | solution.py:23
  19.3 7.1 %collective-permute-start.7 = (f32[128,256]{1,0:T(8,128)S(1)}, f32[128,256]{1,0:T(8,128)S(1)}, u32[]{:S(2)}, u32[]{:S(2)}) collective-permute-start(f32[128,256]{1,0:T(8,128)S(1)} %get-tuple-element.46), channel_id=1, source_target_pairs={{0,3},{1,2},{2,1},{3,0},{4,7},{5,6},{6,5},{7,4},{8,11},{9,10},{10,... | collective-permute-start | bytes 393224 | tf_op jit(solution)/shard_map/ppermute | solution.py:23
  26.8 3.7 %collective-permute-start.11 = (f32[128,128]{1,0:T(8,128)S(1)}, f32[128,128]{1,0:T(8,128)S(1)}, u32[]{:S(2)}, u32[]{:S(2)}) collective-permute-start(f32[128,128]{1,0:T(8,128)S(1)} %get-tuple-element.58), channel_id=1, source_target_pairs={{24,0},{0,8},{8,16},{16,24},{25,1},{1,9},{9,17},{17,25},{26,2},{2,... | collective-permute-start | bytes 196616 | tf_op jit(solution)/shard_map/spill_3/ppermute | solution.py:19
  26.9 6.7 %collective-permute-start.10 = (f32[128,128]{1,0:T(8,128)S(1)}, f32[128,128]{1,0:T(8,128)S(1)}, u32[]{:S(2)}, u32[]{:S(2)}) collective-permute-start(f32[128,128]{1,0:T(8,128)S(1)} %get-tuple-element.55), channel_id=1, source_target_pairs={{24,0},{0,8},{8,16},{16,24},{25,1},{1,9},{9,17},{17,25},{26,2},{2,... | collective-permute-start | bytes 196616 | tf_op jit(solution)/shard_map/spill_2/ppermute | solution.py:19
  27.8 6.5 %collective-permute-start.9 = (f32[128,128]{1,0:T(8,128)S(1)}, f32[128,128]{1,0:T(8,128)S(1)}, u32[]{:S(2)}, u32[]{:S(2)}) collective-permute-start(f32[128,128]{1,0:T(8,128)S(1)} %get-tuple-element.52), channel_id=1, source_target_pairs={{24,0},{0,8},{8,16},{16,24},{25,1},{1,9},{9,17},{17,25},{26,2},{2,... | collective-permute-start | bytes 196616 | tf_op jit(solution)/shard_map/spill_1/ppermute | solution.py:19
  27.9 8.8 %collective-permute-start.8 = (f32[128,128]{1,0:T(8,128)S(1)}, f32[128,128]{1,0:T(8,128)S(1)}, u32[]{:S(2)}, u32[]{:S(2)}) collective-permute-start(f32[128,128]{1,0:T(8,128)S(1)} %get-tuple-element.49), channel_id=1, source_target_pairs={{24,0},{0,8},{8,16},{16,24},{25,1},{1,9},{9,17},{17,25},{26,2},{2,... | collective-permute-start | bytes 196616 | tf_op jit(solution)/shard_map/spill_0/ppermute | solution.py:19
  30.6 6.8 %collective-permute-start.15 = (f32[128,128]{1,0:T(8,128)S(1)}, f32[128,128]{1,0:T(8,128)S(1)}, u32[]{:S(2)}, u32[]{:S(2)}) collective-permute-start(f32[128,128]{1,0:T(8,128)S(1)} %get-tuple-element.59), channel_id=1, source_target_pairs={{0,4},{1,5},{2,6},{3,7},{4,0},{5,1},{6,2},{7,3},{8,12},{9,13},{10,... | collective-permute-start | bytes 196616 | tf_op jit(solution)/shard_map/halves_3/ppermute | solution.py:23
  33.6 8.6 %collective-permute-start.14 = (f32[128,128]{1,0:T(8,128)S(1)}, f32[128,128]{1,0:T(8,128)S(1)}, u32[]{:S(2)}, u32[]{:S(2)}) collective-permute-start(f32[128,128]{1,0:T(8,128)S(1)} %get-tuple-element.61), channel_id=1, source_target_pairs={{0,4},{1,5},{2,6},{3,7},{4,0},{5,1},{6,2},{7,3},{8,12},{9,13},{10,... | collective-permute-start | bytes 196616 | tf_op jit(solution)/shard_map/halves_2/ppermute | solution.py:23
  34.3 9.9 %collective-permute-start.13 = (f32[128,128]{1,0:T(8,128)S(1)}, f32[128,128]{1,0:T(8,128)S(1)}, u32[]{:S(2)}, u32[]{:S(2)}) collective-permute-start(f32[128,128]{1,0:T(8,128)S(1)} %get-tuple-element.63), channel_id=1, source_target_pairs={{0,4},{1,5},{2,6},{3,7},{4,0},{5,1},{6,2},{7,3},{8,12},{9,13},{10,... | collective-permute-start | bytes 196616 | tf_op jit(solution)/shard_map/halves_1/ppermute | solution.py:23
  36.7 8.3 %collective-permute-start.12 = (f32[128,128]{1,0:T(8,128)S(1)}, f32[128,128]{1,0:T(8,128)S(1)}, u32[]{:S(2)}, u32[]{:S(2)}) collective-permute-start(f32[128,128]{1,0:T(8,128)S(1)} %get-tuple-element.65), channel_id=1, source_target_pairs={{0,4},{1,5},{2,6},{3,7},{4,0},{5,1},{6,2},{7,3},{8,12},{9,13},{10,... | collective-permute-start | bytes 196616 | tf_op jit(solution)/shard_map/halves_0/ppermute | solution.py:23

commit v12 on v11

--- a/solution.py
+++ b/solution.py
@@ -348,6 +348,10 @@
         for k in range(2):
             for half in range(2):
                 acc[k, part, :, pl.ds(half * window, window)] = total[k][half]
+
+
+def grouped(tiles):
+    return [(1, 0)] + [(0, strip - 1) for strip in range(1, 2 * tiles)]
 
 
 def second_sum_kernel(window, classes, acc, *refs):
@@ -368,19 +372,18 @@
         for k in range(3):
             for half in range(2):
                 for tile in range(tiles):
-                    outs[3 * (2 * tile + part) + k][pl.ds(half * share, share), :] = total[k][half][
-                        :, tile * LANES : (tile + 1) * LANES
-                    ]
+                    group, place = grouped(tiles)[2 * tile + part]
+                    here = pl.ds((2 * place + half) * share, share)
+                    outs[3 * group + k][here, :] = total[k][half][:, tile * LANES : (tile + 1) * LANES]
 
 
 def final_kernel(tiles, share, *refs):
-    chunks = 2 * tiles
-    kept, received, out = refs[:chunks], refs[chunks : 2 * chunks], refs[2 * chunks]
-    for chunk in range(chunks):
+    kept, received, out = refs[:2], refs[2:4], refs[4]
+    for strip, (group, place) in enumerate(grouped(tiles)):
         for half in range(2):
-            here = pl.ds(half * share, share)
-            line = half * chunks + chunk
-            out[pl.ds(line, share, stride=4 * tiles), :] = kept[chunk][here, :] + received[chunk][here, :]
+            here = pl.ds((2 * place + half) * share, share)
+            line = half * 2 * tiles + strip
+            out[pl.ds(line, share, stride=4 * tiles), :] = kept[group][here, :] + received[group][here, :]
 
 
 def on_device(object_field, illumination, amplitudes, row_offset, col_offset):
@@ -443,13 +446,13 @@
     sums = kernel_call(
         functools.partial(second_sum_kernel, window, classes),
         "sum1",
-        [(2 * share, LANES)] * (6 * tiles),
+        [((2 * tiles - 1) * 2 * share, LANES)] * 3 + [(2 * share, LANES)] * 3,
         (),
         [acc, *near, *late],
     )
     is_upper = lax.axis_index("pos") >= classes
     kept, received = [], []
-    for chunk in range(2 * tiles):
+    for chunk in range(2):
         top, middle, spilled = sums[3 * chunk : 3 * chunk + 3]
         with jax.named_scope("spill_" + str(chunk)):
             top = top + shifted(spilled, "tile", 1)
@@ -460,7 +463,7 @@
     result = pl.pallas_call(
         functools.partial(final_kernel, tiles, share),
         out_shape=jax.ShapeDtypeStruct((share * 4 * tiles, LANES), F32),
-        in_specs=[pl.BlockSpec(memory_space=pltpu.VMEM)] * (4 * tiles),
+        in_specs=[pl.BlockSpec(memory_space=pltpu.VMEM)] * 4,
         out_specs=pl.BlockSpec(memory_space=pltpu.VMEM),
         compiler_params=pltpu.CompilerParams(vmem_limit_bytes=16 << 20),
         name="final",

time: 45.9 us -> 46.3 us (level)
  waiting for transfers between devices: 17.2 us -> 22 us
  starting transfers between devices: 17.8 us -> 13.5 us
    ppermute x10 -> x8, starting transfers between devices: 14.2 us -> 11.1 us  [exchanged(): lax.ppermute(block, axis, [(i, i ^ flip) for i in range(lax.axis_size(axi...]
    ppermute x6 -> x4, waiting for transfers between devices: 2.68 us -> 5.38 us  [shifted(): lax.ppermute(block, axis, [((i - distance) % devices, i) for i in range(d...]
    ppermute x10 -> x8, waiting for transfers between devices: 14.5 us -> 16.6 us  [exchanged(): lax.ppermute(block, axis, [(i, i ^ flip) for i in range(lax.axis_size(axi...]
    ppermute x6 -> x4, starting transfers between devices: 3.63 us -> 2.33 us  [shifted(): lax.ppermute(block, axis, [((i - distance) % devices, i) for i in range(d...]
  transfers between devices with their start and end apart: 16 -> 12, of which waited for: 8 -> 6; matrix products, arithmetic and copies ran while one was open for 0% -> 0% of each run, Pallas kernels for 19% -> 18%
where the time goes in v12:
time: 46.3 us; the launch traced here: 46.2 us
  waiting for transfers between devices  22 us (48%)
  starting transfers between devices  13.5 us (29%)
  Pallas kernels  10.6 us (23%)
    ppermute x8, waiting for transfers between devices, exchanged(): lax.ppermute(block, axis, [(i, i ^ flip) for i in range(lax.axis_size(axi...  16.6 us
    ppermute x8, starting transfers between devices, exchanged(): lax.ppermute(block, axis, [(i, i ^ flip) for i in range(lax.axis_size(axi...  11.1 us
    pallas_call x7, Pallas kernels, kernel_call(): pl.pallas_call(body, out_shape=[pltpu.VMEM(shape, F32) for shape in out_s...  7.82 us
    ppermute x4, waiting for transfers between devices, shifted(): lax.ppermute(block, axis, [((i - distance) % devices, i) for i in range(d...  5.38 us
    ppermute x4, starting transfers between devices, shifted(): lax.ppermute(block, axis, [((i - distance) % devices, i) for i in range(d...  2.33 us
    pallas_call x1, Pallas kernels, loaded(): pl.pallas_call(functools.partial(load_kernel, len(arrays)), out_shape=[pl...  1.96 us
  transfers between devices with their start and end apart: 12, of which 6 were waited for; matrix products, arithmetic and copies ran while one was open for 0% of the time, Pallas kernels for 18%

profile of v12, /device:TPU:0, one launch (start us, length us, event | category | flops | bytes accessed | tf_op | source)
XLA Modules:
  0.0 46.2 jit_solution(6941701828330989169)
XLA Ops:
  0.0 0.7 %pick.1 = f32[8,128]{1,0:T(8,128)S(1)} custom-call(s32[2]{0:T(128)} %rows.7, s32[2]{0:T(128)} %cols.7), custom_call_target="tpu_custom_call" | custom-call | bytes 8192 | tf_op jit(solution)/shard_map/pick/pallas_call | solution.py:71
  0.7 0.5 %collective-permute-start.3 = (f32[8,128]{1,0:T(8,128)S(1)}, f32[8,128]{1,0:T(8,128)S(1)}, u32[]{:S(2)}, u32[]{:S(2)}) collective-permute-start(f32[8,128]{1,0:T(8,128)S(1)} %pick.1), channel_id=1, source_target_pairs={{24,0},{0,8},{8,16},{16,24},{25,1},{1,9},{9,17},{17,25},{26,2},{2,... | collective-permute-start | bytes 12296 | tf_op jit(solution)/shard_map/ppermute | solution.py:19
  1.2 2.0 %load.1 = (f32[4096,128]{1,0:T(8,128)S(1)}, f32[1024,128]{1,0:T(8,128)S(1)}, bf16[2,256,256]{2,1,0:T(8,128)(2,1)S(1)}, bf16[768,384]{1,0:T(8,128)(2,1)S(1)}) custom-call(f32[4096,128]{1,0:T(8,128)} %bitcast.15, f32[1024,128]{1,0:T(8,128)} %bitcast.16, bf16[2,256,256]{2,1,0:T(8,128)(2,1)} %refs_2_.1, bf16[768,384]{1,0:T(8,128)(2,1)} %constant.8.clone.refs_3_), custom_call_target="tpu_custom_call" | custom-call | tf_op jit(solution)/shard_map/load/pallas_call | solution.py:99
  3.2 0.0 copy-start
  3.2 0.0 copy-start.1
  3.2 1.2 %collective-permute-done.3.wanted = f32[8,128]{1,0:T(8,128)S(1)} collective-permute-done((f32[8,128]{1,0:T(8,128)S(1)}, f32[8,128]{1,0:T(8,128)S(1)}, u32[]{:S(2)}, u32[]{:S(2)}) %collective-permute-start.3) | collective-permute-done | bytes 4128 | tf_op jit(solution)/shard_map/ppermute | solution.py:19
  4.5 0.2 rim.1
  4.7 0.8 %collective-permute-start.4 = (f32[2,256,256]{2,1,0:T(8,128)S(1)}, f32[2,256,256]{2,1,0:T(8,128)S(1)}, u32[]{:S(2)}, u32[]{:S(2)}) collective-permute-start(f32[2,256,256]{2,1,0:T(8,128)S(1)} %rim.1), channel_id=1, source_target_pairs={{8,0},{16,8},{24,16},{0,24},{9,1},{17,9},{25,17},{1,25},{10,2},{18... | collective-permute-start | bytes 1572872 | tf_op jit(solution)/shard_map/ppermute | solution.py:19
  5.4 2.8 %wave0.1 = (f32[136,256]{1,0:T(8,128)S(1)}, f32[136,256]{1,0:T(8,128)S(1)}, f32[136,256]{1,0:T(8,128)S(1)}, f32[136,256]{1,0:T(8,128)S(1)}) custom-call(s32[2]{0:T(128)S(1)} %copy-done, s32[2]{0:T(128)S(1)} %copy-done.1, f32[4096,128]{1,0:T(8,128)S(1)} %get-tuple-element.26.obj, f32[1024,128]{1,0:T(8,128)S(1)} %get-tuple-element.27.ill, ...), custom_call_target="tpu_custom_call" | custom-call | flops 805306368 | bytes 1114112 | tf_op jit(solution)/shard_map/wave0/pallas_call | solution.py:71
  8.2 2.3 %collective-permute-start = (f32[136,256]{1,0:T(8,128)S(1)}, f32[136,256]{1,0:T(8,128)S(1)}, u32[]{:S(2)}, u32[]{:S(2)}) collective-permute-start(f32[136,256]{1,0:T(8,128)S(1)} %get-tuple-element.31), channel_id=1, source_target_pairs={{0,1},{1,0},{2,3},{3,2},{4,5},{5,4},{6,7},{7,6},{8,9},{9,8},{10,11... | collective-permute-start | bytes 417800 | tf_op jit(solution)/shard_map/ppermute | solution.py:23
  10.6 1.6 %collective-permute-start.1 = (f32[136,256]{1,0:T(8,128)S(1)}, f32[136,256]{1,0:T(8,128)S(1)}, u32[]{:S(2)}, u32[]{:S(2)}) collective-permute-start(f32[136,256]{1,0:T(8,128)S(1)} %get-tuple-element.32), channel_id=1, source_target_pairs={{0,2},{1,3},{2,0},{3,1},{4,6},{5,7},{6,4},{7,5},{8,10},{9,11},{10,... | collective-permute-start | bytes 417800 | tf_op jit(solution)/shard_map/ppermute | solution.py:23
  12.1 0.0 collective-permute-start.2
  12.1 1.1 %start1.1 = (f32[2,256,256]{2,1,0:T(8,128)S(1)}, f32[256,256]{1,0:T(8,128)S(1)}, f32[2,256,256]{2,1,0:T(8,128)S(1)}) custom-call(s32[2]{0:T(128)S(1)} %copy-done, s32[2]{0:T(128)S(1)} %copy-done.1, f32[4096,128]{1,0:T(8,128)S(1)} %get-tuple-element.26.obj, f32[1024,128]{1,0:T(8,128)S(1)} %get-tuple-element.27.ill, ...), custom_call_target="tpu_custom_call" | custom-call | bytes 2621440 | tf_op jit(solution)/shard_map/start/start1/pallas_call | solution.py:71
  13.3 2.5 %wave1.1 = (f32[128,256]{1,0:T(8,128)S(1)}, f32[128,256]{1,0:T(8,128)S(1)}, f32[128,256]{1,0:T(8,128)S(1)}, f32[128,256]{1,0:T(8,128)S(1)}) custom-call(s32[2]{0:T(128)S(1)} %copy-done, s32[2]{0:T(128)S(1)} %copy-done.1, f32[2,256,256]{2,1,0:T(8,128)S(1)} %get-tuple-element.34.probe, f32[256,256]{1,0:T(8,128)S(1)} %get-tuple-element.35.ordered, ...), custom_call_target="tpu_custom_call" | custom-call | flops 805306368 | bytes 1048576 | tf_op jit(solution)/shard_map/wave1/pallas_call | solution.py:71
  15.7 2.0 %collective-permute-start.5 = (f32[128,256]{1,0:T(8,128)S(1)}, f32[128,256]{1,0:T(8,128)S(1)}, u32[]{:S(2)}, u32[]{:S(2)}) collective-permute-start(f32[128,256]{1,0:T(8,128)S(1)} %get-tuple-element.38), channel_id=1, source_target_pairs={{0,1},{1,0},{2,3},{3,2},{4,5},{5,4},{6,7},{7,6},{8,9},{9,8},{10,11... | collective-permute-start | bytes 393224 | tf_op jit(solution)/shard_map/ppermute | solution.py:23
  17.7 1.6 %collective-permute-start.6 = (f32[128,256]{1,0:T(8,128)S(1)}, f32[128,256]{1,0:T(8,128)S(1)}, u32[]{:S(2)}, u32[]{:S(2)}) collective-permute-start(f32[128,256]{1,0:T(8,128)S(1)} %get-tuple-element.39), channel_id=1, source_target_pairs={{0,2},{1,3},{2,0},{3,1},{4,6},{5,7},{6,4},{7,5},{8,10},{9,11},{10,... | collective-permute-start | bytes 393224 | tf_op jit(solution)/shard_map/ppermute | solution.py:23
  19.3 0.0 collective-permute-done.refs_1_
  19.3 0.0 collective-permute-done.2.refs_3_
  19.3 0.2 sum0.1.acc
  19.5 1.8 %collective-permute-done.5.refs_5_ = f32[128,256]{1,0:T(8,128)S(1)} collective-permute-done((f32[128,256]{1,0:T(8,128)S(1)}, f32[128,256]{1,0:T(8,128)S(1)}, u32[]{:S(2)}, u32[]{:S(2)}) %collective-permute-start.5) | collective-permute-done | bytes 131104 | tf_op jit(solution)/shard_map/ppermute | solution.py:23
  21.4 2.6 %collective-permute-done.6.refs_6_ = f32[128,256]{1,0:T(8,128)S(1)} collective-permute-done((f32[128,256]{1,0:T(8,128)S(1)}, f32[128,256]{1,0:T(8,128)S(1)}, u32[]{:S(2)}, u32[]{:S(2)}) %collective-permute-start.6) | collective-permute-done | bytes 131104 | tf_op jit(solution)/shard_map/ppermute | solution.py:23
  24.0 2.4 %collective-permute-done.7.refs_7_ = f32[128,256]{1,0:T(8,128)S(1)} collective-permute-done((f32[128,256]{1,0:T(8,128)S(1)}, f32[128,256]{1,0:T(8,128)S(1)}, u32[]{:S(2)}, u32[]{:S(2)}) %collective-permute-start.7) | collective-permute-done | bytes 131104 | tf_op jit(solution)/shard_map/ppermute | solution.py:23
  26.4 0.4 sum1.1
  26.8 0.1 collective-permute-start.8
  26.9 0.9 %collective-permute-start.9 = (f32[128,128]{1,0:T(8,128)S(1)}, f32[128,128]{1,0:T(8,128)S(1)}, u32[]{:S(2)}, u32[]{:S(2)}) collective-permute-start(f32[128,128]{1,0:T(8,128)S(1)} %get-tuple-element.46), channel_id=1, source_target_pairs={{24,0},{0,8},{8,16},{16,24},{25,1},{1,9},{9,17},{17,25},{26,2},{2,... | collective-permute-start | bytes 196616 | tf_op jit(solution)/shard_map/spill_1/ppermute | solution.py:19
  27.8 4.1 %collective-permute-done.8 = f32[384,128]{1,0:T(8,128)S(1)} collective-permute-done((f32[384,128]{1,0:T(8,128)S(1)}, f32[384,128]{1,0:T(8,128)S(1)}, u32[]{:S(2)}, u32[]{:S(2)}) %collective-permute-start.8) | collective-permute-done | bytes 196640 | tf_op jit(solution)/shard_map/spill_0/ppermute | solution.py:19
  32.0 3.0 %collective-permute-start.10 = (f32[384,128]{1,0:T(8,128)S(1)}, f32[384,128]{1,0:T(8,128)S(1)}, u32[]{:S(2)}, u32[]{:S(2)}) collective-permute-start(f32[384,128]{1,0:T(8,128)S(1)} %get-tuple-element.47), channel_id=1, source_target_pairs={{0,4},{1,5},{2,6},{3,7},{4,0},{5,1},{6,2},{7,3},{8,12},{9,13},{10,... | collective-permute-start | bytes 589832 | tf_op jit(solution)/shard_map/halves_0/ppermute | solution.py:23
  35.0 0.0 collective-permute-done.9
  35.1 0.7 %collective-permute-start.11 = (f32[128,128]{1,0:T(8,128)S(1)}, f32[128,128]{1,0:T(8,128)S(1)}, u32[]{:S(2)}, u32[]{:S(2)}) collective-permute-start(f32[128,128]{1,0:T(8,128)S(1)} %get-tuple-element.49), channel_id=1, source_target_pairs={{0,4},{1,5},{2,6},{3,7},{4,0},{5,1},{6,2},{7,3},{8,12},{9,13},{10,... | collective-permute-start | bytes 196616 | tf_op jit(solution)/shard_map/halves_1/ppermute | solution.py:23
  35.7 9.7 %collective-permute-done.11.refs_3_ = f32[128,128]{1,0:T(8,128)S(1)} collective-permute-done((f32[128,128]{1,0:T(8,128)S(1)}, f32[128,128]{1,0:T(8,128)S(1)}, u32[]{:S(2)}, u32[]{:S(2)}) %collective-permute-start.11) | collective-permute-done | bytes 65568 | tf_op jit(solution)/shard_map/halves_1/ppermute | solution.py:23
  45.4 0.0 collective-permute-done.10.refs_2_
  45.4 0.8 %final.1 = f32[512,128]{1,0:T(8,128)} custom-call(f32[384,128]{1,0:T(8,128)S(1)} %get-tuple-element.48.refs_0_, f32[128,128]{1,0:T(8,128)S(1)} %get-tuple-element.50.refs_1_, f32[384,128]{1,0:T(8,128)S(1)} %collective-permute-done.10.refs_2_, f32[128,128]{1,0:T(8,128)S(1)} %collective-permute-done.11.refs_3_), custom_call_target="tpu_custom_call" | custom-call | tf_op jit(solution)/shard_map/final/pallas_call | solution.py:463
  (7 shorter events, 0.1 us)
Async XLA Ops:
  0.7 3.8 %collective-permute-start.3 = (f32[8,128]{1,0:T(8,128)S(1)}, f32[8,128]{1,0:T(8,128)S(1)}, u32[]{:S(2)}, u32[]{:S(2)}) collective-permute-start(f32[8,128]{1,0:T(8,128)S(1)} %pick.1), channel_id=1, source_target_pairs={{24,0},{0,8},{8,16},{16,24},{25,1},{1,9},{9,17},{17,25},{26,2},{2,... | collective-permute-start | bytes 12296 | tf_op jit(solution)/shard_map/ppermute | solution.py:19
  3.2 2.2 %copy-start = (s32[2]{0:T(128)S(1)}, s32[2]{0:T(128)}, u32[]{:S(2)}) copy-start(s32[2]{0:T(128)} %rows.7) | copy-start | bytes 28
  3.2 2.2 %copy-start.1 = (s32[2]{0:T(128)S(1)}, s32[2]{0:T(128)}, u32[]{:S(2)}) copy-start(s32[2]{0:T(128)} %cols.7) | copy-start | bytes 28
  4.7 8.6 %collective-permute-start.4 = (f32[2,256,256]{2,1,0:T(8,128)S(1)}, f32[2,256,256]{2,1,0:T(8,128)S(1)}, u32[]{:S(2)}, u32[]{:S(2)}) collective-permute-start(f32[2,256,256]{2,1,0:T(8,128)S(1)} %rim.1), channel_id=1, source_target_pairs={{8,0},{16,8},{24,16},{0,24},{9,1},{17,9},{25,17},{1,25},{10,2},{18... | collective-permute-start | bytes 1572872 | tf_op jit(solution)/shard_map/ppermute | solution.py:19
  8.2 11.0 %collective-permute-start = (f32[136,256]{1,0:T(8,128)S(1)}, f32[136,256]{1,0:T(8,128)S(1)}, u32[]{:S(2)}, u32[]{:S(2)}) collective-permute-start(f32[136,256]{1,0:T(8,128)S(1)} %get-tuple-element.31), channel_id=1, source_target_pairs={{0,1},{1,0},{2,3},{3,2},{4,5},{5,4},{6,7},{7,6},{8,9},{9,8},{10,11... | collective-permute-start | bytes 417800 | tf_op jit(solution)/shard_map/ppermute | solution.py:23
  10.6 8.7 %collective-permute-start.1 = (f32[136,256]{1,0:T(8,128)S(1)}, f32[136,256]{1,0:T(8,128)S(1)}, u32[]{:S(2)}, u32[]{:S(2)}) collective-permute-start(f32[136,256]{1,0:T(8,128)S(1)} %get-tuple-element.32), channel_id=1, source_target_pairs={{0,2},{1,3},{2,0},{3,1},{4,6},{5,7},{6,4},{7,5},{8,10},{9,11},{10,... | collective-permute-start | bytes 417800 | tf_op jit(solution)/shard_map/ppermute | solution.py:23
  12.1 7.2 %collective-permute-start.2 = (f32[136,256]{1,0:T(8,128)S(1)}, f32[136,256]{1,0:T(8,128)S(1)}, u32[]{:S(2)}, u32[]{:S(2)}) collective-permute-start(f32[136,256]{1,0:T(8,128)S(1)} %get-tuple-element.33), channel_id=1, source_target_pairs={{0,3},{1,2},{2,1},{3,0},{4,7},{5,6},{6,5},{7,4},{8,11},{9,10},{10,... | collective-permute-start | bytes 417800 | tf_op jit(solution)/shard_map/ppermute | solution.py:23
  15.7 5.7 %collective-permute-start.5 = (f32[128,256]{1,0:T(8,128)S(1)}, f32[128,256]{1,0:T(8,128)S(1)}, u32[]{:S(2)}, u32[]{:S(2)}) collective-permute-start(f32[128,256]{1,0:T(8,128)S(1)} %get-tuple-element.38), channel_id=1, source_target_pairs={{0,1},{1,0},{2,3},{3,2},{4,5},{5,4},{6,7},{7,6},{8,9},{9,8},{10,11... | collective-permute-start | bytes 393224 | tf_op jit(solution)/shard_map/ppermute | solution.py:23
  17.7 6.3 %collective-permute-start.6 = (f32[128,256]{1,0:T(8,128)S(1)}, f32[128,256]{1,0:T(8,128)S(1)}, u32[]{:S(2)}, u32[]{:S(2)}) collective-permute-start(f32[128,256]{1,0:T(8,128)S(1)} %get-tuple-element.39), channel_id=1, source_target_pairs={{0,2},{1,3},{2,0},{3,1},{4,6},{5,7},{6,4},{7,5},{8,10},{9,11},{10,... | collective-permute-start | bytes 393224 | tf_op jit(solution)/shard_map/ppermute | solution.py:23
  19.3 7.1 %collective-permute-start.7 = (f32[128,256]{1,0:T(8,128)S(1)}, f32[128,256]{1,0:T(8,128)S(1)}, u32[]{:S(2)}, u32[]{:S(2)}) collective-permute-start(f32[128,256]{1,0:T(8,128)S(1)} %get-tuple-element.40), channel_id=1, source_target_pairs={{0,3},{1,2},{2,1},{3,0},{4,7},{5,6},{6,5},{7,4},{8,11},{9,10},{10,... | collective-permute-start | bytes 393224 | tf_op jit(solution)/shard_map/ppermute | solution.py:23
  26.8 5.1 %collective-permute-start.8 = (f32[384,128]{1,0:T(8,128)S(1)}, f32[384,128]{1,0:T(8,128)S(1)}, u32[]{:S(2)}, u32[]{:S(2)}) collective-permute-start(f32[384,128]{1,0:T(8,128)S(1)} %get-tuple-element.43), channel_id=1, source_target_pairs={{24,0},{0,8},{8,16},{16,24},{25,1},{1,9},{9,17},{17,25},{26,2},{2,... | collective-permute-start | bytes 589832 | tf_op jit(solution)/shard_map/spill_0/ppermute | solution.py:19
  26.9 8.1 %collective-permute-start.9 = (f32[128,128]{1,0:T(8,128)S(1)}, f32[128,128]{1,0:T(8,128)S(1)}, u32[]{:S(2)}, u32[]{:S(2)}) collective-permute-start(f32[128,128]{1,0:T(8,128)S(1)} %get-tuple-element.46), channel_id=1, source_target_pairs={{24,0},{0,8},{8,16},{16,24},{25,1},{1,9},{9,17},{17,25},{26,2},{2,... | collective-permute-start | bytes 196616 | tf_op jit(solution)/shard_map/spill_1/ppermute | solution.py:19
  32.0 13.4 %collective-permute-start.10 = (f32[384,128]{1,0:T(8,128)S(1)}, f32[384,128]{1,0:T(8,128)S(1)}, u32[]{:S(2)}, u32[]{:S(2)}) collective-permute-start(f32[384,128]{1,0:T(8,128)S(1)} %get-tuple-element.47), channel_id=1, source_target_pairs={{0,4},{1,5},{2,6},{3,7},{4,0},{5,1},{6,2},{7,3},{8,12},{9,13},{10,... | collective-permute-start | bytes 589832 | tf_op jit(solution)/shard_map/halves_0/ppermute | solution.py:23
  35.1 10.4 %collective-permute-start.11 = (f32[128,128]{1,0:T(8,128)S(1)}, f32[128,128]{1,0:T(8,128)S(1)}, u32[]{:S(2)}, u32[]{:S(2)}) collective-permute-start(f32[128,128]{1,0:T(8,128)S(1)} %get-tuple-element.49), channel_id=1, source_target_pairs={{0,4},{1,5},{2,6},{3,7},{4,0},{5,1},{6,2},{7,3},{8,12},{9,13},{10,... | collective-permute-start | bytes 196616 | tf_op jit(solution)/shard_map/halves_1/ppermute | solution.py:23

commit v13 on v12

--- a/solution.py
+++ b/solution.py
@@ -8,6 +8,7 @@
 from jax.experimental import pallas as pl
 from jax.experimental.pallas import tpu as pltpu
 from jax.sharding import PartitionSpec as P
+
 
 LANES = 128
 F32 = jnp.float32
@@ -64,7 +65,7 @@
     return pltpu.with_memory_space_constraint(array, pltpu.VMEM)
 
 
-def kernel_call(body, name, out_shapes, scalars, arrays, scratch=(), flops=0):
+def kernel_call(body, out_shapes, scalars, arrays, scratch=(), flops=0):
     smem = pl.BlockSpec(memory_space=pltpu.SMEM)
     vmem = pl.BlockSpec(memory_space=pltpu.VMEM)
     moved = sum(4 * math.prod(shape) for shape in out_shapes)
@@ -76,7 +77,6 @@
         scratch_shapes=scratch,
         cost_estimate=pl.CostEstimate(flops=flops, transcendentals=0, bytes_accessed=2 * moved),
         compiler_params=pltpu.CompilerParams(vmem_limit_bytes=16 << 20),
-        name=name,
     )(*scalars, *[in_vmem(array) for array in arrays])
 
 
@@ -398,10 +398,10 @@
 
     arrays = [linear(object_field), linear(illumination), amplitudes, split_tables(window)]
     remote = tuple(pltpu.with_memory_space_constraint(scalar, pltpu.HBM) for scalar in scalars)
-    (wanted,) = kernel_call(functools.partial(pick_kernel, window), "pick", [(8, LANES)], remote, [])
+    (wanted,) = kernel_call(functools.partial(pick_kernel, window), [(8, LANES)], remote, [])
     wanted = shifted(wanted, "tile", 1)
     obj, ill, amps, table = loaded(arrays)
-    (rim,) = kernel_call(functools.partial(rim_kernel, window), "rim", [(2, window, window)], (), [wanted, obj])
+    (rim,) = kernel_call(functools.partial(rim_kernel, window), [(2, window, window)], (), [wanted, obj])
     rim = shifted(rim, "tile", -1)
 
     def spread(pieces):
@@ -412,7 +412,6 @@
     near = spread(
         kernel_call(
             functools.partial(first_wave_kernel, window, classes),
-            "wave0",
             [(2 * share + 8, window)] * classes,
             scalars,
             [obj, ill, amps, table],
@@ -420,22 +419,17 @@
             48 * window**3,
         )
     )
-    with jax.named_scope("start"):
-        probe, ordered, exits = kernel_call(
-            functools.partial(second_start_kernel, window),
-            "start1",
-            [(2, window, window), (window, window), (2, window, window)],
-            scalars,
-            [obj, ill, amps],
-            roll,
-        )
-    (acc,) = kernel_call(
-        functools.partial(first_sum_kernel, window, classes), "sum0", [(2, 2, share, columns)], (), near
-    )
+    probe, ordered, exits = kernel_call(
+        functools.partial(second_start_kernel, window),
+        [(2, window, window), (window, window), (2, window, window)],
+        scalars,
+        [obj, ill, amps],
+        roll,
+    )
+    (acc,) = kernel_call(functools.partial(first_sum_kernel, window, classes), [(2, 2, share, columns)], (), near)
     late = spread(
         kernel_call(
             functools.partial(second_wave_kernel, window, classes),
-            "wave1",
             [(2 * share, window)] * classes,
             scalars,
             [probe, ordered, exits, table, rim],
@@ -445,7 +439,6 @@
     )
     sums = kernel_call(
         functools.partial(second_sum_kernel, window, classes),
-        "sum1",
         [((2 * tiles - 1) * 2 * share, LANES)] * 3 + [(2 * share, LANES)] * 3,
         (),
         [acc, *near, *late],
@@ -454,11 +447,9 @@
     kept, received = [], []
     for chunk in range(2):
         top, middle, spilled = sums[3 * chunk : 3 * chunk + 3]
-        with jax.named_scope("spill_" + str(chunk)):
-            top = top + shifted(spilled, "tile", 1)
+        top = top + shifted(spilled, "tile", 1)
         outgoing = jnp.where(is_upper, top, middle)
-        with jax.named_scope("halves_" + str(chunk)):
-            received.append(exchanged(outgoing, "pos", classes))
+        received.append(exchanged(outgoing, "pos", classes))
         kept.append(jnp.where(is_upper, middle, top))
     result = pl.pallas_call(
         functools.partial(final_kernel, tiles, share),
@@ -480,6 +471,5 @@
         P(("tile", "pos")),
     )
     out_specs = P(("tile", "pos"), None, None)
-    return jax.shard_map(
-        on_device, mesh=mesh, in_specs=in_specs, out_specs=out_specs, check_vma=False
-    )
+
+    return jax.shard_map(on_device, mesh=mesh, in_specs=in_specs, out_specs=out_specs, check_vma=False)

time: 46.3 us -> 46.3 us (level)
  no operation moved by 1% of the time
where the time goes in v13:
time: 46.3 us; the launch traced here: 46.2 us
  waiting for transfers between devices  22 us (48%)
  starting transfers between devices  13.5 us (29%)
  Pallas kernels  10.6 us (23%)
    ppermute x8, waiting for transfers between devices, exchanged(): lax.ppermute(block, axis, [(i, i ^ flip) for i in range(lax.axis_size(axi...  16.6 us
    ppermute x8, starting transfers between devices, exchanged(): lax.ppermute(block, axis, [(i, i ^ flip) for i in range(lax.axis_size(axi...  11.1 us
    pallas_call x7, Pallas kernels, kernel_call(): pl.pallas_call(body, out_shape=[pltpu.VMEM(shape, F32) for shape in out_s...  7.82 us
    ppermute x4, waiting for transfers between devices, shifted(): lax.ppermute(block, axis, [((i - distance) % devices, i) for i in range(d...  5.38 us
    ppermute x4, starting transfers between devices, shifted(): lax.ppermute(block, axis, [((i - distance) % devices, i) for i in range(d...  2.33 us
    pallas_call x1, Pallas kernels, loaded(): pl.pallas_call(functools.partial(load_kernel, len(arrays)), out_shape=[pl...  1.96 us
  transfers between devices with their start and end apart: 12, of which 6 were waited for; matrix products, arithmetic and copies ran while one was open for 0% of the time, Pallas kernels for 18%

profile of v13, /device:TPU:0, one launch (start us, length us, event | category | flops | bytes accessed | tf_op | source)
XLA Modules:
  0.0 46.2 jit_solution(6941701828330989169)
XLA Ops:
  0.0 0.7 %shard_map.67 = f32[8,128]{1,0:T(8,128)S(1)} custom-call(s32[2]{0:T(128)} %rows.7, s32[2]{0:T(128)} %cols.7), custom_call_target="tpu_custom_call" | custom-call | bytes 8192 | tf_op jit(solution)/shard_map/pallas_call | solution.py:72
  0.7 0.5 %collective-permute-start.3 = (f32[8,128]{1,0:T(8,128)S(1)}, f32[8,128]{1,0:T(8,128)S(1)}, u32[]{:S(2)}, u32[]{:S(2)}) collective-permute-start(f32[8,128]{1,0:T(8,128)S(1)} %shard_map.67), channel_id=1, source_target_pairs={{24,0},{0,8},{8,16},{16,24},{25,1},{1,9},{9,17},{17,25},{26,2},{2,... | collective-permute-start | bytes 12296 | tf_op jit(solution)/shard_map/ppermute | solution.py:20
  1.2 2.0 %load.1 = (f32[4096,128]{1,0:T(8,128)S(1)}, f32[1024,128]{1,0:T(8,128)S(1)}, bf16[2,256,256]{2,1,0:T(8,128)(2,1)S(1)}, bf16[768,384]{1,0:T(8,128)(2,1)S(1)}) custom-call(f32[4096,128]{1,0:T(8,128)} %bitcast.15, f32[1024,128]{1,0:T(8,128)} %bitcast.16, bf16[2,256,256]{2,1,0:T(8,128)(2,1)} %refs_2_.1, bf16[768,384]{1,0:T(8,128)(2,1)} %constant.8.clone.refs_3_), custom_call_target="tpu_custom_call" | custom-call | tf_op jit(solution)/shard_map/load/pallas_call | solution.py:99
  3.2 0.0 copy-start
  3.2 0.0 copy-start.1
  3.2 1.2 %collective-permute-done.3.wanted = f32[8,128]{1,0:T(8,128)S(1)} collective-permute-done((f32[8,128]{1,0:T(8,128)S(1)}, f32[8,128]{1,0:T(8,128)S(1)}, u32[]{:S(2)}, u32[]{:S(2)}) %collective-permute-start.3) | collective-permute-done | bytes 4128 | tf_op jit(solution)/shard_map/ppermute | solution.py:20
  4.5 0.2 shard_map.68
  4.7 0.8 %collective-permute-start.4 = (f32[2,256,256]{2,1,0:T(8,128)S(1)}, f32[2,256,256]{2,1,0:T(8,128)S(1)}, u32[]{:S(2)}, u32[]{:S(2)}) collective-permute-start(f32[2,256,256]{2,1,0:T(8,128)S(1)} %shard_map.68), channel_id=1, source_target_pairs={{8,0},{16,8},{24,16},{0,24},{9,1},{17,9},{25,17},{1,25},{10,2},{18... | collective-permute-start | bytes 1572872 | tf_op jit(solution)/shard_map/ppermute | solution.py:20
  5.4 2.8 %shard_map.64 = (f32[136,256]{1,0:T(8,128)S(1)}, f32[136,256]{1,0:T(8,128)S(1)}, f32[136,256]{1,0:T(8,128)S(1)}, f32[136,256]{1,0:T(8,128)S(1)}) custom-call(s32[2]{0:T(128)S(1)} %copy-done, s32[2]{0:T(128)S(1)} %copy-done.1, f32[4096,128]{1,0:T(8,128)S(1)} %get-tuple-element.26.obj, f32[1024,128]{1,0:T(8,128)S(1)} %get-tuple-element.27.ill, ...), custom_call_target="tpu_custom_call" | custom-call | flops 805306368 | bytes 1114112 | tf_op jit(solution)/shard_map/pallas_call | solution.py:72
  8.2 2.3 %collective-permute-start = (f32[136,256]{1,0:T(8,128)S(1)}, f32[136,256]{1,0:T(8,128)S(1)}, u32[]{:S(2)}, u32[]{:S(2)}) collective-permute-start(f32[136,256]{1,0:T(8,128)S(1)} %get-tuple-element.31), channel_id=1, source_target_pairs={{0,1},{1,0},{2,3},{3,2},{4,5},{5,4},{6,7},{7,6},{8,9},{9,8},{10,11... | collective-permute-start | bytes 417800 | tf_op jit(solution)/shard_map/ppermute | solution.py:24
  10.6 1.6 %collective-permute-start.1 = (f32[136,256]{1,0:T(8,128)S(1)}, f32[136,256]{1,0:T(8,128)S(1)}, u32[]{:S(2)}, u32[]{:S(2)}) collective-permute-start(f32[136,256]{1,0:T(8,128)S(1)} %get-tuple-element.32), channel_id=1, source_target_pairs={{0,2},{1,3},{2,0},{3,1},{4,6},{5,7},{6,4},{7,5},{8,10},{9,11},{10,... | collective-permute-start | bytes 417800 | tf_op jit(solution)/shard_map/ppermute | solution.py:24
  12.1 0.0 collective-permute-start.2
  12.1 1.1 %shard_map.66 = (f32[2,256,256]{2,1,0:T(8,128)S(1)}, f32[256,256]{1,0:T(8,128)S(1)}, f32[2,256,256]{2,1,0:T(8,128)S(1)}) custom-call(s32[2]{0:T(128)S(1)} %copy-done, s32[2]{0:T(128)S(1)} %copy-done.1, f32[4096,128]{1,0:T(8,128)S(1)} %get-tuple-element.26.obj, f32[1024,128]{1,0:T(8,128)S(1)} %get-tuple-element.27.ill, ...), custom_call_target="tpu_custom_call" | custom-call | bytes 2621440 | tf_op jit(solution)/shard_map/pallas_call | solution.py:72
  13.3 2.5 %shard_map.69 = (f32[128,256]{1,0:T(8,128)S(1)}, f32[128,256]{1,0:T(8,128)S(1)}, f32[128,256]{1,0:T(8,128)S(1)}, f32[128,256]{1,0:T(8,128)S(1)}) custom-call(s32[2]{0:T(128)S(1)} %copy-done, s32[2]{0:T(128)S(1)} %copy-done.1, f32[2,256,256]{2,1,0:T(8,128)S(1)} %get-tuple-element.34.probe, f32[256,256]{1,0:T(8,128)S(1)} %get-tuple-element.35.ordered, ...), custom_call_target="tpu_custom_call" | custom-call | flops 805306368 | bytes 1048576 | tf_op jit(solution)/shard_map/pallas_call | solution.py:72
  15.7 2.0 %collective-permute-start.5 = (f32[128,256]{1,0:T(8,128)S(1)}, f32[128,256]{1,0:T(8,128)S(1)}, u32[]{:S(2)}, u32[]{:S(2)}) collective-permute-start(f32[128,256]{1,0:T(8,128)S(1)} %get-tuple-element.38), channel_id=1, source_target_pairs={{0,1},{1,0},{2,3},{3,2},{4,5},{5,4},{6,7},{7,6},{8,9},{9,8},{10,11... | collective-permute-start | bytes 393224 | tf_op jit(solution)/shard_map/ppermute | solution.py:24
  17.7 1.6 %collective-permute-start.6 = (f32[128,256]{1,0:T(8,128)S(1)}, f32[128,256]{1,0:T(8,128)S(1)}, u32[]{:S(2)}, u32[]{:S(2)}) collective-permute-start(f32[128,256]{1,0:T(8,128)S(1)} %get-tuple-element.39), channel_id=1, source_target_pairs={{0,2},{1,3},{2,0},{3,1},{4,6},{5,7},{6,4},{7,5},{8,10},{9,11},{10,... | collective-permute-start | bytes 393224 | tf_op jit(solution)/shard_map/ppermute | solution.py:24
  19.3 0.0 collective-permute-done.refs_1_
  19.3 0.0 collective-permute-done.2.refs_3_
  19.3 0.2 shard_map.65.acc
  19.5 1.8 %collective-permute-done.5.refs_5_ = f32[128,256]{1,0:T(8,128)S(1)} collective-permute-done((f32[128,256]{1,0:T(8,128)S(1)}, f32[128,256]{1,0:T(8,128)S(1)}, u32[]{:S(2)}, u32[]{:S(2)}) %collective-permute-start.5) | collective-permute-done | bytes 131104 | tf_op jit(solution)/shard_map/ppermute | solution.py:24
  21.4 2.6 %collective-permute-done.6.refs_6_ = f32[128,256]{1,0:T(8,128)S(1)} collective-permute-done((f32[128,256]{1,0:T(8,128)S(1)}, f32[128,256]{1,0:T(8,128)S(1)}, u32[]{:S(2)}, u32[]{:S(2)}) %collective-permute-start.6) | collective-permute-done | bytes 131104 | tf_op jit(solution)/shard_map/ppermute | solution.py:24
  24.0 2.4 %collective-permute-done.7.refs_7_ = f32[128,256]{1,0:T(8,128)S(1)} collective-permute-done((f32[128,256]{1,0:T(8,128)S(1)}, f32[128,256]{1,0:T(8,128)S(1)}, u32[]{:S(2)}, u32[]{:S(2)}) %collective-permute-start.7) | collective-permute-done | bytes 131104 | tf_op jit(solution)/shard_map/ppermute | solution.py:24
  26.4 0.4 shard_map.70
  26.8 0.1 collective-permute-start.8
  26.9 0.9 %collective-permute-start.9 = (f32[128,128]{1,0:T(8,128)S(1)}, f32[128,128]{1,0:T(8,128)S(1)}, u32[]{:S(2)}, u32[]{:S(2)}) collective-permute-start(f32[128,128]{1,0:T(8,128)S(1)} %get-tuple-element.46), channel_id=1, source_target_pairs={{24,0},{0,8},{8,16},{16,24},{25,1},{1,9},{9,17},{17,25},{26,2},{2,... | collective-permute-start | bytes 196616 | tf_op jit(solution)/shard_map/ppermute | solution.py:20
  27.8 4.1 %collective-permute-done.8 = f32[384,128]{1,0:T(8,128)S(1)} collective-permute-done((f32[384,128]{1,0:T(8,128)S(1)}, f32[384,128]{1,0:T(8,128)S(1)}, u32[]{:S(2)}, u32[]{:S(2)}) %collective-permute-start.8) | collective-permute-done | bytes 196640 | tf_op jit(solution)/shard_map/ppermute | solution.py:20
  32.0 3.0 %collective-permute-start.10 = (f32[384,128]{1,0:T(8,128)S(1)}, f32[384,128]{1,0:T(8,128)S(1)}, u32[]{:S(2)}, u32[]{:S(2)}) collective-permute-start(f32[384,128]{1,0:T(8,128)S(1)} %get-tuple-element.47), channel_id=1, source_target_pairs={{0,4},{1,5},{2,6},{3,7},{4,0},{5,1},{6,2},{7,3},{8,12},{9,13},{10,... | collective-permute-start | bytes 589832 | tf_op jit(solution)/shard_map/ppermute | solution.py:24
  35.0 0.0 collective-permute-done.9
  35.1 0.7 %collective-permute-start.11 = (f32[128,128]{1,0:T(8,128)S(1)}, f32[128,128]{1,0:T(8,128)S(1)}, u32[]{:S(2)}, u32[]{:S(2)}) collective-permute-start(f32[128,128]{1,0:T(8,128)S(1)} %get-tuple-element.49), channel_id=1, source_target_pairs={{0,4},{1,5},{2,6},{3,7},{4,0},{5,1},{6,2},{7,3},{8,12},{9,13},{10,... | collective-permute-start | bytes 196616 | tf_op jit(solution)/shard_map/ppermute | solution.py:24
  35.7 9.7 %collective-permute-done.11.refs_3_ = f32[128,128]{1,0:T(8,128)S(1)} collective-permute-done((f32[128,128]{1,0:T(8,128)S(1)}, f32[128,128]{1,0:T(8,128)S(1)}, u32[]{:S(2)}, u32[]{:S(2)}) %collective-permute-start.11) | collective-permute-done | bytes 65568 | tf_op jit(solution)/shard_map/ppermute | solution.py:24
  45.4 0.0 collective-permute-done.10.refs_2_
  45.4 0.8 %final.1 = f32[512,128]{1,0:T(8,128)} custom-call(f32[384,128]{1,0:T(8,128)S(1)} %get-tuple-element.48.refs_0_, f32[128,128]{1,0:T(8,128)S(1)} %get-tuple-element.50.refs_1_, f32[384,128]{1,0:T(8,128)S(1)} %collective-permute-done.10.refs_2_, f32[128,128]{1,0:T(8,128)S(1)} %collective-permute-done.11.refs_3_), custom_call_target="tpu_custom_call" | custom-call | tf_op jit(solution)/shard_map/final/pallas_call | solution.py:454
  (7 shorter events, 0.1 us)
Async XLA Ops:
  0.7 3.8 %collective-permute-start.3 = (f32[8,128]{1,0:T(8,128)S(1)}, f32[8,128]{1,0:T(8,128)S(1)}, u32[]{:S(2)}, u32[]{:S(2)}) collective-permute-start(f32[8,128]{1,0:T(8,128)S(1)} %shard_map.67), channel_id=1, source_target_pairs={{24,0},{0,8},{8,16},{16,24},{25,1},{1,9},{9,17},{17,25},{26,2},{2,... | collective-permute-start | bytes 12296 | tf_op jit(solution)/shard_map/ppermute | solution.py:20
  3.2 2.2 %copy-start = (s32[2]{0:T(128)S(1)}, s32[2]{0:T(128)}, u32[]{:S(2)}) copy-start(s32[2]{0:T(128)} %rows.7) | copy-start | bytes 28
  3.2 2.2 %copy-start.1 = (s32[2]{0:T(128)S(1)}, s32[2]{0:T(128)}, u32[]{:S(2)}) copy-start(s32[2]{0:T(128)} %cols.7) | copy-start | bytes 28
  4.7 8.6 %collective-permute-start.4 = (f32[2,256,256]{2,1,0:T(8,128)S(1)}, f32[2,256,256]{2,1,0:T(8,128)S(1)}, u32[]{:S(2)}, u32[]{:S(2)}) collective-permute-start(f32[2,256,256]{2,1,0:T(8,128)S(1)} %shard_map.68), channel_id=1, source_target_pairs={{8,0},{16,8},{24,16},{0,24},{9,1},{17,9},{25,17},{1,25},{10,2},{18... | collective-permute-start | bytes 1572872 | tf_op jit(solution)/shard_map/ppermute | solution.py:20
  8.2 11.0 %collective-permute-start = (f32[136,256]{1,0:T(8,128)S(1)}, f32[136,256]{1,0:T(8,128)S(1)}, u32[]{:S(2)}, u32[]{:S(2)}) collective-permute-start(f32[136,256]{1,0:T(8,128)S(1)} %get-tuple-element.31), channel_id=1, source_target_pairs={{0,1},{1,0},{2,3},{3,2},{4,5},{5,4},{6,7},{7,6},{8,9},{9,8},{10,11... | collective-permute-start | bytes 417800 | tf_op jit(solution)/shard_map/ppermute | solution.py:24
  10.6 8.7 %collective-permute-start.1 = (f32[136,256]{1,0:T(8,128)S(1)}, f32[136,256]{1,0:T(8,128)S(1)}, u32[]{:S(2)}, u32[]{:S(2)}) collective-permute-start(f32[136,256]{1,0:T(8,128)S(1)} %get-tuple-element.32), channel_id=1, source_target_pairs={{0,2},{1,3},{2,0},{3,1},{4,6},{5,7},{6,4},{7,5},{8,10},{9,11},{10,... | collective-permute-start | bytes 417800 | tf_op jit(solution)/shard_map/ppermute | solution.py:24
  12.1 7.2 %collective-permute-start.2 = (f32[136,256]{1,0:T(8,128)S(1)}, f32[136,256]{1,0:T(8,128)S(1)}, u32[]{:S(2)}, u32[]{:S(2)}) collective-permute-start(f32[136,256]{1,0:T(8,128)S(1)} %get-tuple-element.33), channel_id=1, source_target_pairs={{0,3},{1,2},{2,1},{3,0},{4,7},{5,6},{6,5},{7,4},{8,11},{9,10},{10,... | collective-permute-start | bytes 417800 | tf_op jit(solution)/shard_map/ppermute | solution.py:24
  15.7 5.7 %collective-permute-start.5 = (f32[128,256]{1,0:T(8,128)S(1)}, f32[128,256]{1,0:T(8,128)S(1)}, u32[]{:S(2)}, u32[]{:S(2)}) collective-permute-start(f32[128,256]{1,0:T(8,128)S(1)} %get-tuple-element.38), channel_id=1, source_target_pairs={{0,1},{1,0},{2,3},{3,2},{4,5},{5,4},{6,7},{7,6},{8,9},{9,8},{10,11... | collective-permute-start | bytes 393224 | tf_op jit(solution)/shard_map/ppermute | solution.py:24
  17.7 6.3 %collective-permute-start.6 = (f32[128,256]{1,0:T(8,128)S(1)}, f32[128,256]{1,0:T(8,128)S(1)}, u32[]{:S(2)}, u32[]{:S(2)}) collective-permute-start(f32[128,256]{1,0:T(8,128)S(1)} %get-tuple-element.39), channel_id=1, source_target_pairs={{0,2},{1,3},{2,0},{3,1},{4,6},{5,7},{6,4},{7,5},{8,10},{9,11},{10,... | collective-permute-start | bytes 393224 | tf_op jit(solution)/shard_map/ppermute | solution.py:24
  19.3 7.1 %collective-permute-start.7 = (f32[128,256]{1,0:T(8,128)S(1)}, f32[128,256]{1,0:T(8,128)S(1)}, u32[]{:S(2)}, u32[]{:S(2)}) collective-permute-start(f32[128,256]{1,0:T(8,128)S(1)} %get-tuple-element.40), channel_id=1, source_target_pairs={{0,3},{1,2},{2,1},{3,0},{4,7},{5,6},{6,5},{7,4},{8,11},{9,10},{10,... | collective-permute-start | bytes 393224 | tf_op jit(solution)/shard_map/ppermute | solution.py:24
  26.8 5.1 %collective-permute-start.8 = (f32[384,128]{1,0:T(8,128)S(1)}, f32[384,128]{1,0:T(8,128)S(1)}, u32[]{:S(2)}, u32[]{:S(2)}) collective-permute-start(f32[384,128]{1,0:T(8,128)S(1)} %get-tuple-element.43), channel_id=1, source_target_pairs={{24,0},{0,8},{8,16},{16,24},{25,1},{1,9},{9,17},{17,25},{26,2},{2,... | collective-permute-start | bytes 589832 | tf_op jit(solution)/shard_map/ppermute | solution.py:20
  26.9 8.1 %collective-permute-start.9 = (f32[128,128]{1,0:T(8,128)S(1)}, f32[128,128]{1,0:T(8,128)S(1)}, u32[]{:S(2)}, u32[]{:S(2)}) collective-permute-start(f32[128,128]{1,0:T(8,128)S(1)} %get-tuple-element.46), channel_id=1, source_target_pairs={{24,0},{0,8},{8,16},{16,24},{25,1},{1,9},{9,17},{17,25},{26,2},{2,... | collective-permute-start | bytes 196616 | tf_op jit(solution)/shard_map/ppermute | solution.py:20
  32.0 13.4 %collective-permute-start.10 = (f32[384,128]{1,0:T(8,128)S(1)}, f32[384,128]{1,0:T(8,128)S(1)}, u32[]{:S(2)}, u32[]{:S(2)}) collective-permute-start(f32[384,128]{1,0:T(8,128)S(1)} %get-tuple-element.47), channel_id=1, source_target_pairs={{0,4},{1,5},{2,6},{3,7},{4,0},{5,1},{6,2},{7,3},{8,12},{9,13},{10,... | collective-permute-start | bytes 589832 | tf_op jit(solution)/shard_map/ppermute | solution.py:24
  35.1 10.4 %collective-permute-start.11 = (f32[128,128]{1,0:T(8,128)S(1)}, f32[128,128]{1,0:T(8,128)S(1)}, u32[]{:S(2)}, u32[]{:S(2)}) collective-permute-start(f32[128,128]{1,0:T(8,128)S(1)} %get-tuple-element.49), channel_id=1, source_target_pairs={{0,4},{1,5},{2,6},{3,7},{4,0},{5,1},{6,2},{7,3},{8,12},{9,13},{10,... | collective-permute-start | bytes 196616 | tf_op jit(solution)/shard_map/ppermute | solution.py:24

commit v14 on v10

--- a/solution.py
+++ b/solution.py
@@ -107,16 +107,13 @@
     )(*[pltpu.with_memory_space_constraint(array, pltpu.HBM) for array in arrays])
 
 
-def pick_kernel(window, rows, cols, out):
-    _, column, _ = chosen(1, rows, cols, lax.axis_index("tile") * (2 * window), window)
-    out[...] = jnp.broadcast_to(column.astype(F32), out.shape)
-
-
-def rim_kernel(window, wanted, obj, out):
-    offset = wanted[pl.ds(0, 1), :]
+def rim_kernel(window, rows, cols, obj, out):
+    band_start = (lax.axis_index("tile") - 1) * (2 * window)
+    crossing = rows[:, 0:1] - band_start > window
+    offset = jnp.where(crossing, cols[:, 0:1], cols[:, 1:2])
     tiles = window // LANES
     for tile in range(tiles):
-        column = (lax.broadcasted_iota(jnp.int32, (window, LANES), 1) + tile * LANES).astype(F32)
+        column = lax.broadcasted_iota(jnp.int32, (window, LANES), 1) + tile * LANES
         for part in range(2):
             near = obj[pl.ds(tile * 2 + part, window, stride=4 * tiles), :]
             beyond = obj[pl.ds((tiles + tile) * 2 + part, window, stride=4 * tiles), :]
@@ -394,11 +391,9 @@
     scalars = (row_offset, col_offset)
 
     arrays = [linear(object_field), linear(illumination), amplitudes, split_tables(window)]
-    remote = tuple(pltpu.with_memory_space_constraint(scalar, pltpu.HBM) for scalar in scalars)
-    (wanted,) = kernel_call(functools.partial(pick_kernel, window), "pick", [(8, LANES)], remote, [])
-    wanted = shifted(wanted, "tile", 1)
+    wanted = [shifted(scalar, "tile", 1).reshape(1, 2) for scalar in scalars]
     obj, ill, amps, table = loaded(arrays)
-    (rim,) = kernel_call(functools.partial(rim_kernel, window), "rim", [(2, window, window)], (), [wanted, obj])
+    (rim,) = kernel_call(functools.partial(rim_kernel, window), "rim", [(2, window, window)], (), [*wanted, obj])
     rim = shifted(rim, "tile", -1)
 
     def spread(pieces):

time: 45.7 us -> 45 us (0.985)
  waiting for transfers between devices: 20.6 us -> 19.6 us
  Pallas kernels: 10.6 us -> 9.94 us
  starting transfers between devices: 14.2 us -> 14.8 us
    ppermute x4 -> x5, starting transfers between devices: 2.33 us -> 3.72 us  [shifted(): lax.ppermute(block, axis, [((i - distance) % devices, i) for i in range(d...]
    ppermute x4 -> x5, waiting for transfers between devices: 4.68 us -> 3.91 us  [shifted(): lax.ppermute(block, axis, [((i - distance) % devices, i) for i in range(d...]
    ppermute x8, starting transfers between devices: 11.8 us -> 11.1 us  [exchanged(): lax.ppermute(block, axis, [(i, i ^ flip) for i in range(lax.axis_size(axi...]
    pallas_call x7 -> x6, Pallas kernels: 7.82 us -> 7.21 us  [kernel_call(): pl.pallas_call(body, out_shape=[pltpu.VMEM(shape, F32) for shape in out_s...]
  transfers between devices with their start and end apart: 12 -> 13, of which waited for: 7 -> 6; matrix products, arithmetic and copies ran while one was open for 0% -> 0% of each run, Pallas kernels for 19% -> 19%
where the time goes in v14:
time: 45 us; the launch traced here: 44.9 us
  waiting for transfers between devices  19.6 us (44%)
  starting transfers between devices  14.8 us (33%)
  Pallas kernels  9.94 us (22%)
    ppermute x8, waiting for transfers between devices, exchanged(): lax.ppermute(block, axis, [(i, i ^ flip) for i in range(lax.axis_size(axi...  15.7 us
    ppermute x8, starting transfers between devices, exchanged(): lax.ppermute(block, axis, [(i, i ^ flip) for i in range(lax.axis_size(axi...  11.1 us
    pallas_call x6, Pallas kernels, kernel_call(): pl.pallas_call(body, out_shape=[pltpu.VMEM(shape, F32) for shape in out_s...  7.21 us
    ppermute x5, waiting for transfers between devices, shifted(): lax.ppermute(block, axis, [((i - distance) % devices, i) for i in range(d...  3.91 us
    ppermute x5, starting transfers between devices, shifted(): lax.ppermute(block, axis, [((i - distance) % devices, i) for i in range(d...  3.72 us
    pallas_call x1, Pallas kernels, loaded(): pl.pallas_call(functools.partial(load_kernel, len(arrays)), out_shape=[pl...  1.96 us
  transfers between devices with their start and end apart: 13, of which 6 were waited for; matrix products, arithmetic and copies ran while one was open for 0% of the time, Pallas kernels for 19%

profile of v14, /device:TPU:0, one launch (start us, length us, event | category | flops | bytes accessed | tf_op | source)
XLA Modules:
  0.0 44.9 jit_solution(12334554584513527501)
XLA Ops:
  0.0 0.5 %collective-permute-start.3 = (s32[2]{0:T(128)}, s32[2]{0:T(128)S(1)}, u32[]{:S(2)}, u32[]{:S(2)}) collective-permute-start(s32[2]{0:T(128)} %rows.5), channel_id=1, source_target_pairs={{24,0},{0,8},{8,16},{16,24},{25,1},{1,9},{9,17},{17,25},{26,2},{2,... | collective-permute-start | bytes 32 | tf_op jit(solution)/shard_map/ppermute | solution.py:19
  0.5 2.6 %collective-permute-start.4 = (s32[2]{0:T(128)}, s32[2]{0:T(128)S(1)}, u32[]{:S(2)}, u32[]{:S(2)}) collective-permute-start(s32[2]{0:T(128)} %cols.5), channel_id=1, source_target_pairs={{24,0},{0,8},{8,16},{16,24},{25,1},{1,9},{9,17},{17,25},{26,2},{2,... | collective-permute-start | bytes 32 | tf_op jit(solution)/shard_map/ppermute | solution.py:19
  3.1 2.0 %load.1 = (f32[4096,128]{1,0:T(8,128)S(1)}, f32[1024,128]{1,0:T(8,128)S(1)}, bf16[2,256,256]{2,1,0:T(8,128)(2,1)S(1)}, bf16[768,384]{1,0:T(8,128)(2,1)S(1)}) custom-call(f32[4096,128]{1,0:T(8,128)} %bitcast.19, f32[1024,128]{1,0:T(8,128)} %bitcast.20, bf16[2,256,256]{2,1,0:T(8,128)(2,1)} %refs_2_.1, bf16[768,384]{1,0:T(8,128)(2,1)} %constant.8.clone.refs_3_), custom_call_target="tpu_custom_call" | custom-call | tf_op jit(solution)/shard_map/load/pallas_call | solution.py:99
  5.1 0.0 copy-start
  5.1 0.0 copy-start.1
  5.1 0.0 collective-permute-done.4
  5.1 0.3 rim.1
  5.4 0.1 collective-permute-start.5
  5.5 0.3 copy-done
  5.7 0.0 copy-done.1
  5.8 2.8 %wave0.1 = (f32[136,256]{1,0:T(8,128)S(1)}, f32[136,256]{1,0:T(8,128)S(1)}, f32[136,256]{1,0:T(8,128)S(1)}, f32[136,256]{1,0:T(8,128)S(1)}) custom-call(s32[2]{0:T(128)S(1)} %copy-done, s32[2]{0:T(128)S(1)} %copy-done.1, f32[4096,128]{1,0:T(8,128)S(1)} %get-tuple-element.26.obj, f32[1024,128]{1,0:T(8,128)S(1)} %get-tuple-element.27.ill, ...), custom_call_target="tpu_custom_call" | custom-call | flops 805306368 | bytes 1114112 | tf_op jit(solution)/shard_map/wave0/pallas_call | solution.py:71
  8.5 1.6 %collective-permute-start = (f32[136,256]{1,0:T(8,128)S(1)}, f32[136,256]{1,0:T(8,128)S(1)}, u32[]{:S(2)}, u32[]{:S(2)}) collective-permute-start(f32[136,256]{1,0:T(8,128)S(1)} %get-tuple-element.31), channel_id=1, source_target_pairs={{0,1},{1,0},{2,3},{3,2},{4,5},{5,4},{6,7},{7,6},{8,9},{9,8},{10,11... | collective-permute-start | bytes 417800 | tf_op jit(solution)/shard_map/ppermute | solution.py:23
  10.1 1.6 %collective-permute-start.1 = (f32[136,256]{1,0:T(8,128)S(1)}, f32[136,256]{1,0:T(8,128)S(1)}, u32[]{:S(2)}, u32[]{:S(2)}) collective-permute-start(f32[136,256]{1,0:T(8,128)S(1)} %get-tuple-element.32), channel_id=1, source_target_pairs={{0,2},{1,3},{2,0},{3,1},{4,6},{5,7},{6,4},{7,5},{8,10},{9,11},{10,... | collective-permute-start | bytes 417800 | tf_op jit(solution)/shard_map/ppermute | solution.py:23
  11.7 0.4 collective-permute-start.2
  12.1 1.1 %start1.1 = (f32[2,256,256]{2,1,0:T(8,128)S(1)}, f32[256,256]{1,0:T(8,128)S(1)}, f32[2,256,256]{2,1,0:T(8,128)S(1)}) custom-call(s32[2]{0:T(128)S(1)} %copy-done, s32[2]{0:T(128)S(1)} %copy-done.1, f32[4096,128]{1,0:T(8,128)S(1)} %get-tuple-element.26.obj, f32[1024,128]{1,0:T(8,128)S(1)} %get-tuple-element.27.ill, ...), custom_call_target="tpu_custom_call" | custom-call | bytes 2621440 | tf_op jit(solution)/shard_map/start/start1/pallas_call | solution.py:71
  13.2 2.5 %wave1.1 = (f32[128,256]{1,0:T(8,128)S(1)}, f32[128,256]{1,0:T(8,128)S(1)}, f32[128,256]{1,0:T(8,128)S(1)}, f32[128,256]{1,0:T(8,128)S(1)}) custom-call(s32[2]{0:T(128)S(1)} %copy-done, s32[2]{0:T(128)S(1)} %copy-done.1, f32[2,256,256]{2,1,0:T(8,128)S(1)} %get-tuple-element.34.probe, f32[256,256]{1,0:T(8,128)S(1)} %get-tuple-element.35.ordered, ...), custom_call_target="tpu_custom_call" | custom-call | flops 805306368 | bytes 1048576 | tf_op jit(solution)/shard_map/wave1/pallas_call | solution.py:71
  15.7 1.6 %collective-permute-start.6 = (f32[128,256]{1,0:T(8,128)S(1)}, f32[128,256]{1,0:T(8,128)S(1)}, u32[]{:S(2)}, u32[]{:S(2)}) collective-permute-start(f32[128,256]{1,0:T(8,128)S(1)} %get-tuple-element.38), channel_id=1, source_target_pairs={{0,1},{1,0},{2,3},{3,2},{4,5},{5,4},{6,7},{7,6},{8,9},{9,8},{10,11... | collective-permute-start | bytes 393224 | tf_op jit(solution)/shard_map/ppermute | solution.py:23
  17.2 1.6 %collective-permute-start.7 = (f32[128,256]{1,0:T(8,128)S(1)}, f32[128,256]{1,0:T(8,128)S(1)}, u32[]{:S(2)}, u32[]{:S(2)}) collective-permute-start(f32[128,256]{1,0:T(8,128)S(1)} %get-tuple-element.39), channel_id=1, source_target_pairs={{0,2},{1,3},{2,0},{3,1},{4,6},{5,7},{6,4},{7,5},{8,10},{9,11},{10,... | collective-permute-start | bytes 393224 | tf_op jit(solution)/shard_map/ppermute | solution.py:23
  18.8 0.4 collective-permute-start.8
  19.2 0.2 sum0.1.acc
  19.5 2.5 %collective-permute-done.6.refs_5_ = f32[128,256]{1,0:T(8,128)S(1)} collective-permute-done((f32[128,256]{1,0:T(8,128)S(1)}, f32[128,256]{1,0:T(8,128)S(1)}, u32[]{:S(2)}, u32[]{:S(2)}) %collective-permute-start.6) | collective-permute-done | bytes 131104 | tf_op jit(solution)/shard_map/ppermute | solution.py:23
  21.9 1.7 %collective-permute-done.7.refs_6_ = f32[128,256]{1,0:T(8,128)S(1)} collective-permute-done((f32[128,256]{1,0:T(8,128)S(1)}, f32[128,256]{1,0:T(8,128)S(1)}, u32[]{:S(2)}, u32[]{:S(2)}) %collective-permute-start.7) | collective-permute-done | bytes 131104 | tf_op jit(solution)/shard_map/ppermute | solution.py:23
  23.6 2.7 %collective-permute-done.8.refs_7_ = f32[128,256]{1,0:T(8,128)S(1)} collective-permute-done((f32[128,256]{1,0:T(8,128)S(1)}, f32[128,256]{1,0:T(8,128)S(1)}, u32[]{:S(2)}, u32[]{:S(2)}) %collective-permute-start.8) | collective-permute-done | bytes 131104 | tf_op jit(solution)/shard_map/ppermute | solution.py:23
  26.3 0.4 sum1.1
  26.7 0.1 collective-permute-start.10
  26.8 0.5 %collective-permute-start.9 = (f32[256,128]{1,0:T(8,128)S(1)}, f32[256,128]{1,0:T(8,128)S(1)}, u32[]{:S(2)}, u32[]{:S(2)}) collective-permute-start(f32[256,128]{1,0:T(8,128)S(1)} %get-tuple-element.43), channel_id=1, source_target_pairs={{24,0},{0,8},{8,16},{16,24},{25,1},{1,9},{9,17},{17,25},{26,2},{2,... | collective-permute-start | bytes 393224 | tf_op jit(solution)/shard_map/spill_0/ppermute | solution.py:19
  27.3 3.9 %collective-permute-done.10 = f32[256,128]{1,0:T(8,128)S(1)} collective-permute-done((f32[256,128]{1,0:T(8,128)S(1)}, f32[256,128]{1,0:T(8,128)S(1)}, u32[]{:S(2)}, u32[]{:S(2)}) %collective-permute-start.10) | collective-permute-done | bytes 131104 | tf_op jit(solution)/shard_map/spill_1/ppermute | solution.py:19
  31.2 2.7 %collective-permute-start.12 = (f32[256,128]{1,0:T(8,128)S(1)}, f32[256,128]{1,0:T(8,128)S(1)}, u32[]{:S(2)}, u32[]{:S(2)}) collective-permute-start(f32[256,128]{1,0:T(8,128)S(1)} %get-tuple-element.47), channel_id=1, source_target_pairs={{0,4},{1,5},{2,6},{3,7},{4,0},{5,1},{6,2},{7,3},{8,12},{9,13},{10,... | collective-permute-start | bytes 393224 | tf_op jit(solution)/shard_map/halves_1/ppermute | solution.py:23
  33.9 1.4 %collective-permute-start.11 = (f32[256,128]{1,0:T(8,128)S(1)}, f32[256,128]{1,0:T(8,128)S(1)}, u32[]{:S(2)}, u32[]{:S(2)}) collective-permute-start(f32[256,128]{1,0:T(8,128)S(1)} %get-tuple-element.49), channel_id=1, source_target_pairs={{0,4},{1,5},{2,6},{3,7},{4,0},{5,1},{6,2},{7,3},{8,12},{9,13},{10,... | collective-permute-start | bytes 393224 | tf_op jit(solution)/shard_map/halves_0/ppermute | solution.py:23
  35.2 7.5 %collective-permute-done.12.refs_3_ = f32[256,128]{1,0:T(8,128)S(1)} collective-permute-done((f32[256,128]{1,0:T(8,128)S(1)}, f32[256,128]{1,0:T(8,128)S(1)}, u32[]{:S(2)}, u32[]{:S(2)}) %collective-permute-start.12) | collective-permute-done | bytes 131104 | tf_op jit(solution)/shard_map/halves_1/ppermute | solution.py:23
  42.7 1.4 %collective-permute-done.11.refs_2_ = f32[256,128]{1,0:T(8,128)S(1)} collective-permute-done((f32[256,128]{1,0:T(8,128)S(1)}, f32[256,128]{1,0:T(8,128)S(1)}, u32[]{:S(2)}, u32[]{:S(2)}) %collective-permute-start.11) | collective-permute-done | bytes 131104 | tf_op jit(solution)/shard_map/halves_0/ppermute | solution.py:23
  44.1 0.8 %final.1 = f32[512,128]{1,0:T(8,128)} custom-call(f32[256,128]{1,0:T(8,128)S(1)} %get-tuple-element.50.refs_0_, f32[256,128]{1,0:T(8,128)S(1)} %get-tuple-element.48.refs_1_, f32[256,128]{1,0:T(8,128)S(1)} %collective-permute-done.11.refs_2_, f32[256,128]{1,0:T(8,128)S(1)} %collective-permute-done.12.refs_3_), custom_call_target="tpu_custom_call" | custom-call | tf_op jit(solution)/shard_map/final/pallas_call | solution.py:455
  (8 shorter events, 0.1 us)
Async XLA Ops:
  0.0 5.1 %collective-permute-start.3 = (s32[2]{0:T(128)}, s32[2]{0:T(128)S(1)}, u32[]{:S(2)}, u32[]{:S(2)}) collective-permute-start(s32[2]{0:T(128)} %rows.5), channel_id=1, source_target_pairs={{24,0},{0,8},{8,16},{16,24},{25,1},{1,9},{9,17},{17,25},{26,2},{2,... | collective-permute-start | bytes 32 | tf_op jit(solution)/shard_map/ppermute | solution.py:19
  0.5 4.6 %collective-permute-start.4 = (s32[2]{0:T(128)}, s32[2]{0:T(128)S(1)}, u32[]{:S(2)}, u32[]{:S(2)}) collective-permute-start(s32[2]{0:T(128)} %cols.5), channel_id=1, source_target_pairs={{24,0},{0,8},{8,16},{16,24},{25,1},{1,9},{9,17},{17,25},{26,2},{2,... | collective-permute-start | bytes 32 | tf_op jit(solution)/shard_map/ppermute | solution.py:19
  5.1 0.7 %copy-start = (s32[2]{0:T(128)S(1)}, s32[2]{0:T(128)}, u32[]{:S(2)}) copy-start(s32[2]{0:T(128)} %rows.5) | copy-start | bytes 28
  5.1 0.7 %copy-start.1 = (s32[2]{0:T(128)S(1)}, s32[2]{0:T(128)}, u32[]{:S(2)}) copy-start(s32[2]{0:T(128)} %cols.5) | copy-start | bytes 28
  5.4 7.8 %collective-permute-start.5 = (f32[2,256,256]{2,1,0:T(8,128)S(1)}, f32[2,256,256]{2,1,0:T(8,128)S(1)}, u32[]{:S(2)}, u32[]{:S(2)}) collective-permute-start(f32[2,256,256]{2,1,0:T(8,128)S(1)} %rim.1), channel_id=1, source_target_pairs={{8,0},{16,8},{24,16},{0,24},{9,1},{17,9},{25,17},{1,25},{10,2},{18... | collective-permute-start | bytes 1572872 | tf_op jit(solution)/shard_map/ppermute | solution.py:19
  8.5 10.3 %collective-permute-start = (f32[136,256]{1,0:T(8,128)S(1)}, f32[136,256]{1,0:T(8,128)S(1)}, u32[]{:S(2)}, u32[]{:S(2)}) collective-permute-start(f32[136,256]{1,0:T(8,128)S(1)} %get-tuple-element.31), channel_id=1, source_target_pairs={{0,1},{1,0},{2,3},{3,2},{4,5},{5,4},{6,7},{7,6},{8,9},{9,8},{10,11... | collective-permute-start | bytes 417800 | tf_op jit(solution)/shard_map/ppermute | solution.py:23
  10.1 9.1 %collective-permute-start.1 = (f32[136,256]{1,0:T(8,128)S(1)}, f32[136,256]{1,0:T(8,128)S(1)}, u32[]{:S(2)}, u32[]{:S(2)}) collective-permute-start(f32[136,256]{1,0:T(8,128)S(1)} %get-tuple-element.32), channel_id=1, source_target_pairs={{0,2},{1,3},{2,0},{3,1},{4,6},{5,7},{6,4},{7,5},{8,10},{9,11},{10,... | collective-permute-start | bytes 417800 | tf_op jit(solution)/shard_map/ppermute | solution.py:23
  11.7 7.6 %collective-permute-start.2 = (f32[136,256]{1,0:T(8,128)S(1)}, f32[136,256]{1,0:T(8,128)S(1)}, u32[]{:S(2)}, u32[]{:S(2)}) collective-permute-start(f32[136,256]{1,0:T(8,128)S(1)} %get-tuple-element.33), channel_id=1, source_target_pairs={{0,3},{1,2},{2,1},{3,0},{4,7},{5,6},{6,5},{7,4},{8,11},{9,10},{10,... | collective-permute-start | bytes 417800 | tf_op jit(solution)/shard_map/ppermute | solution.py:23
  15.7 6.2 %collective-permute-start.6 = (f32[128,256]{1,0:T(8,128)S(1)}, f32[128,256]{1,0:T(8,128)S(1)}, u32[]{:S(2)}, u32[]{:S(2)}) collective-permute-start(f32[128,256]{1,0:T(8,128)S(1)} %get-tuple-element.38), channel_id=1, source_target_pairs={{0,1},{1,0},{2,3},{3,2},{4,5},{5,4},{6,7},{7,6},{8,9},{9,8},{10,11... | collective-permute-start | bytes 393224 | tf_op jit(solution)/shard_map/ppermute | solution.py:23
  17.2 6.4 %collective-permute-start.7 = (f32[128,256]{1,0:T(8,128)S(1)}, f32[128,256]{1,0:T(8,128)S(1)}, u32[]{:S(2)}, u32[]{:S(2)}) collective-permute-start(f32[128,256]{1,0:T(8,128)S(1)} %get-tuple-element.39), channel_id=1, source_target_pairs={{0,2},{1,3},{2,0},{3,1},{4,6},{5,7},{6,4},{7,5},{8,10},{9,11},{10,... | collective-permute-start | bytes 393224 | tf_op jit(solution)/shard_map/ppermute | solution.py:23
  18.8 7.5 %collective-permute-start.8 = (f32[128,256]{1,0:T(8,128)S(1)}, f32[128,256]{1,0:T(8,128)S(1)}, u32[]{:S(2)}, u32[]{:S(2)}) collective-permute-start(f32[128,256]{1,0:T(8,128)S(1)} %get-tuple-element.40), channel_id=1, source_target_pairs={{0,3},{1,2},{2,1},{3,0},{4,7},{5,6},{6,5},{7,4},{8,11},{9,10},{10,... | collective-permute-start | bytes 393224 | tf_op jit(solution)/shard_map/ppermute | solution.py:23
  26.7 4.4 %collective-permute-start.10 = (f32[256,128]{1,0:T(8,128)S(1)}, f32[256,128]{1,0:T(8,128)S(1)}, u32[]{:S(2)}, u32[]{:S(2)}) collective-permute-start(f32[256,128]{1,0:T(8,128)S(1)} %get-tuple-element.46), channel_id=1, source_target_pairs={{24,0},{0,8},{8,16},{16,24},{25,1},{1,9},{9,17},{17,25},{26,2},{2,... | collective-permute-start | bytes 393224 | tf_op jit(solution)/shard_map/spill_1/ppermute | solution.py:19
  26.8 7.1 %collective-permute-start.9 = (f32[256,128]{1,0:T(8,128)S(1)}, f32[256,128]{1,0:T(8,128)S(1)}, u32[]{:S(2)}, u32[]{:S(2)}) collective-permute-start(f32[256,128]{1,0:T(8,128)S(1)} %get-tuple-element.43), channel_id=1, source_target_pairs={{24,0},{0,8},{8,16},{16,24},{25,1},{1,9},{9,17},{17,25},{26,2},{2,... | collective-permute-start | bytes 393224 | tf_op jit(solution)/shard_map/spill_0/ppermute | solution.py:19
  31.2 11.5 %collective-permute-start.12 = (f32[256,128]{1,0:T(8,128)S(1)}, f32[256,128]{1,0:T(8,128)S(1)}, u32[]{:S(2)}, u32[]{:S(2)}) collective-permute-start(f32[256,128]{1,0:T(8,128)S(1)} %get-tuple-element.47), channel_id=1, source_target_pairs={{0,4},{1,5},{2,6},{3,7},{4,0},{5,1},{6,2},{7,3},{8,12},{9,13},{10,... | collective-permute-start | bytes 393224 | tf_op jit(solution)/shard_map/halves_1/ppermute | solution.py:23
  33.9 10.2 %collective-permute-start.11 = (f32[256,128]{1,0:T(8,128)S(1)}, f32[256,128]{1,0:T(8,128)S(1)}, u32[]{:S(2)}, u32[]{:S(2)}) collective-permute-start(f32[256,128]{1,0:T(8,128)S(1)} %get-tuple-element.49), channel_id=1, source_target_pairs={{0,4},{1,5},{2,6},{3,7},{4,0},{5,1},{6,2},{7,3},{8,12},{9,13},{10,... | collective-permute-start | bytes 393224 | tf_op jit(solution)/shard_map/halves_0/ppermute | solution.py:23

commit v15 on v14

--- a/solution.py
+++ b/solution.py
@@ -8,6 +8,7 @@
 from jax.experimental import pallas as pl
 from jax.experimental.pallas import tpu as pltpu
 from jax.sharding import PartitionSpec as P
+
 
 LANES = 128
 F32 = jnp.float32
@@ -64,7 +65,7 @@
     return pltpu.with_memory_space_constraint(array, pltpu.VMEM)
 
 
-def kernel_call(body, name, out_shapes, scalars, arrays, scratch=(), flops=0):
+def kernel_call(body, out_shapes, scalars, arrays, scratch=(), flops=0):
     smem = pl.BlockSpec(memory_space=pltpu.SMEM)
     vmem = pl.BlockSpec(memory_space=pltpu.VMEM)
     moved = sum(4 * math.prod(shape) for shape in out_shapes)
@@ -76,7 +77,6 @@
         scratch_shapes=scratch,
         cost_estimate=pl.CostEstimate(flops=flops, transcendentals=0, bytes_accessed=2 * moved),
         compiler_params=pltpu.CompilerParams(vmem_limit_bytes=16 << 20),
-        name=name,
     )(*scalars, *[in_vmem(array) for array in arrays])
 
 
@@ -87,36 +87,40 @@
 
 
 def load_kernel(number, *refs):
-    sources, targets, sem = refs[:number], refs[number : 2 * number], refs[2 * number]
-    copies = [pltpu.make_async_copy(a, b, sem.at[i]) for i, (a, b) in enumerate(zip(sources, targets))]
+    sources, targets, sem = refs[:number], refs[number : 2 * number + 1], refs[2 * number + 1]
+    strip = sources[0].at[pl.ds(0, targets[-1].shape[0])]
+    copies = [pltpu.make_async_copy(a, b, sem.at[i]) for i, (a, b) in enumerate(zip((strip, *sources), (targets[-1], *targets)))]
     for copy in copies:
         copy.start()
     for copy in copies:
         copy.wait()
 
 
-def loaded(arrays):
+def loaded(arrays, strip_rows):
+    outputs = [pltpu.VMEM(array.shape, array.dtype) for array in arrays] + [pltpu.VMEM((strip_rows, LANES), F32)]
     return pl.pallas_call(
         functools.partial(load_kernel, len(arrays)),
-        out_shape=[pltpu.VMEM(array.shape, array.dtype) for array in arrays],
+        out_shape=outputs,
         in_specs=[pl.BlockSpec(memory_space=pl.ANY)] * len(arrays),
-        out_specs=[pl.BlockSpec(memory_space=pltpu.VMEM)] * len(arrays),
-        scratch_shapes=[pltpu.SemaphoreType.DMA((len(arrays),))],
+        out_specs=[pl.BlockSpec(memory_space=pltpu.VMEM)] * len(outputs),
+        scratch_shapes=[pltpu.SemaphoreType.DMA((len(outputs),))],
         compiler_params=pltpu.CompilerParams(vmem_limit_bytes=16 << 20),
         name="load",
     )(*[pltpu.with_memory_space_constraint(array, pltpu.HBM) for array in arrays])
 
 
-def rim_kernel(window, rows, cols, obj, out):
+def rim_kernel(window, skipped, rows, cols, obj, out):
     band_start = (lax.axis_index("tile") - 1) * (2 * window)
     crossing = rows[:, 0:1] - band_start > window
     offset = jnp.where(crossing, cols[:, 0:1], cols[:, 1:2])
     tiles = window // LANES
+    number = window - skipped
+    base = skipped * 4 * tiles
     for tile in range(tiles):
-        column = lax.broadcasted_iota(jnp.int32, (window, LANES), 1) + tile * LANES
+        column = lax.broadcasted_iota(jnp.int32, (number, LANES), 1) + tile * LANES
         for part in range(2):
-            near = obj[pl.ds(tile * 2 + part, window, stride=4 * tiles), :]
-            beyond = obj[pl.ds((tiles + tile) * 2 + part, window, stride=4 * tiles), :]
+            near = obj[pl.ds(base + tile * 2 + part, number, stride=4 * tiles), :]
+            beyond = obj[pl.ds(base + (tiles + tile) * 2 + part, number, stride=4 * tiles), :]
             out[part, :, pl.ds(tile * LANES, LANES)] = jnp.where(column < offset, beyond, near)
 
 
@@ -293,15 +297,30 @@
     prepare(1, window, rows, cols, obj, ill, amps, doubled, probe, ordered, emit)
 
 
-def second_wave_kernel(window, classes, rows, cols, probe, ordered, exits, table, rim, *refs):
+def second_wave_kernel(window, classes, rows, cols, probe, ordered, exits, table, strip, rim, *refs):
     outs = refs[:classes]
     xh, xl, yh, yl, far = refs[classes:]
-    row, _, _ = chosen(1, rows, cols, lax.axis_index("tile") * (2 * window), window)
+    row, column, _ = chosen(1, rows, cols, lax.axis_index("tile") * (2 * window), window)
     size = 32
+    tiles = window // LANES
+    skipped = window - rim.shape[1]
+    across = lax.broadcasted_iota(jnp.int32, (size, window), 1)
+
+    def rim_rows(first, part):
+        if first >= skipped:
+            return rim[part, pl.ds(first - skipped, size), :]
+
+        def tile_at(tile):
+            return strip[pl.ds(first * 4 * tiles + tile * 2 + part, size, stride=4 * tiles), :]
+
+        near = jnp.concatenate([tile_at(t) for t in range(tiles)], axis=1)
+        beyond = jnp.concatenate([tile_at(t + tiles) for t in range(tiles)], axis=1)
+        return jnp.where(across < column, beyond, near)
+
     for first in range(0, window, size):
         here = pl.ds(first, size)
         beyond = lax.broadcasted_iota(jnp.int32, (size, window), 0) + (first + window) < row
-        edge = product(*[(probe[part, here, :], rim[part, here, :]) for part in range(2)])
+        edge = product(*[(probe[part, here, :], rim_rows(first, part)) for part in range(2)])
         values = [jnp.where(beyond, edge[part], exits[part, here, :]) for part in range(2)]
         keep_exit(xh, xl, first, size, values)
     transforms(window, classes, table, probe, ordered, xh, xl, yh, yl, far, outs)
@@ -391,9 +410,12 @@
     scalars = (row_offset, col_offset)
 
     arrays = [linear(object_field), linear(illumination), amplitudes, split_tables(window)]
+    skipped = window // 4
     wanted = [shifted(scalar, "tile", 1).reshape(1, 2) for scalar in scalars]
-    obj, ill, amps, table = loaded(arrays)
-    (rim,) = kernel_call(functools.partial(rim_kernel, window), "rim", [(2, window, window)], (), [*wanted, obj])
+    obj, ill, amps, table, strip = loaded(arrays, skipped * 4 * tiles)
+    strip = shifted(strip, "tile", -1)
+    rim_body = functools.partial(rim_kernel, window, skipped)
+    (rim,) = kernel_call(rim_body, [(2, window - skipped, window)], (), [*wanted, obj])
     rim = shifted(rim, "tile", -1)
 
     def spread(pieces):
@@ -404,7 +426,6 @@
     near = spread(
         kernel_call(
             functools.partial(first_wave_kernel, window, classes),
-            "wave0",
             [(2 * share + 8, window)] * classes,
             scalars,
             [obj, ill, amps, table],
@@ -412,32 +433,26 @@
             48 * window**3,
         )
     )
-    with jax.named_scope("start"):
-        probe, ordered, exits = kernel_call(
-            functools.partial(second_start_kernel, window),
-            "start1",
-            [(2, window, window), (window, window), (2, window, window)],
-            scalars,
-            [obj, ill, amps],
-            roll,
-        )
-    (acc,) = kernel_call(
-        functools.partial(first_sum_kernel, window, classes), "sum0", [(2, 2, share, columns)], (), near
-    )
+    probe, ordered, exits = kernel_call(
+        functools.partial(second_start_kernel, window),
+        [(2, window, window), (window, window), (2, window, window)],
+        scalars,
+        [obj, ill, amps],
+        roll,
+    )
+    (acc,) = kernel_call(functools.partial(first_sum_kernel, window, classes), [(2, 2, share, columns)], (), near)
     late = spread(
         kernel_call(
             functools.partial(second_wave_kernel, window, classes),
-            "wave1",
             [(2 * share, window)] * classes,
             scalars,
-            [probe, ordered, exits, table, rim],
+            [probe, ordered, exits, table, strip, rim],
             work,
             48 * window**3,
         )
     )
     sums = kernel_call(
         functools.partial(second_sum_kernel, window, classes),
-        "sum1",
         [(4 * share, LANES)] * (3 * tiles),
         (),
         [acc, *near, *late],
@@ -446,11 +461,9 @@
     kept, received = [], []
     for chunk in range(tiles):
         top, middle, spilled = sums[3 * chunk : 3 * chunk + 3]
-        with jax.named_scope("spill_" + str(chunk)):
-            top = top + shifted(spilled, "tile", 1)
+        top = top + shifted(spilled, "tile", 1)
         outgoing = jnp.where(is_upper, top, middle)
-        with jax.named_scope("halves_" + str(chunk)):
-            received.append(exchanged(outgoing, "pos", classes))
+        received.append(exchanged(outgoing, "pos", classes))
         kept.append(jnp.where(is_upper, middle, top))
     result = pl.pallas_call(
         functools.partial(final_kernel, tiles, share),
@@ -472,6 +485,5 @@
         P(("tile", "pos")),
     )
     out_specs = P(("tile", "pos"), None, None)
-    return jax.shard_map(
-        on_device, mesh=mesh, in_specs=in_specs, out_specs=out_specs, check_vma=False
-    )
+
+    return jax.shard_map(on_device, mesh=mesh, in_specs=in_specs, out_specs=out_specs, check_vma=False)

time: 45 us -> 46.5 us (1.033)
  starting transfers between devices: 14.8 us -> 16.8 us
    ppermute x5 -> x6, starting transfers between devices: 3.72 us -> 5.61 us  [shifted(): lax.ppermute(block, axis, [((i - distance) % devices, i) for i in range(d...]
    ppermute x5 -> x6, waiting for transfers between devices: 3.91 us -> 3.12 us  [shifted(): lax.ppermute(block, axis, [((i - distance) % devices, i) for i in range(d...]
    ppermute x8, waiting for transfers between devices: 15.7 us -> 16.3 us  [exchanged(): lax.ppermute(block, axis, [(i, i ^ flip) for i in range(lax.axis_size(axi...]
  transfers between devices with their start and end apart: 13 -> 14, of which waited for: 6 -> 6; matrix products, arithmetic and copies ran while one was open for 0% -> 0% of each run, Pallas kernels for 19% -> 19%
where the time goes in v15:
time: 46.5 us; the launch traced here: 46.3 us
  waiting for transfers between devices  19.4 us (42%)
  starting transfers between devices  16.8 us (36%)
  Pallas kernels  10 us (22%)
    ppermute x8, waiting for transfers between devices, exchanged(): lax.ppermute(block, axis, [(i, i ^ flip) for i in range(lax.axis_size(axi...  16.3 us
    ppermute x8, starting transfers between devices, exchanged(): lax.ppermute(block, axis, [(i, i ^ flip) for i in range(lax.axis_size(axi...  11.1 us
    pallas_call x6, Pallas kernels, kernel_call(): pl.pallas_call(body, out_shape=[pltpu.VMEM(shape, F32) for shape in out_s...  7.19 us
    ppermute x6, starting transfers between devices, shifted(): lax.ppermute(block, axis, [((i - distance) % devices, i) for i in range(d...  5.61 us
    ppermute x6, waiting for transfers between devices, shifted(): lax.ppermute(block, axis, [((i - distance) % devices, i) for i in range(d...  3.12 us
    pallas_call x1, Pallas kernels, loaded(): pl.pallas_call(functools.partial(load_kernel, len(arrays)), out_shape=out...  2.06 us
  transfers between devices with their start and end apart: 14, of which 6 were waited for; matrix products, arithmetic and copies ran while one was open for 0% of the time, Pallas kernels for 19%

profile of v15, /device:TPU:0, one launch (start us, length us, event | category | flops | bytes accessed | tf_op | source)
XLA Modules:
  0.0 46.3 jit_solution(3986416284450144219)
XLA Ops:
  0.0 0.5 %collective-permute-start.4 = (s32[2]{0:T(128)}, s32[2]{0:T(128)S(1)}, u32[]{:S(2)}, u32[]{:S(2)}) collective-permute-start(s32[2]{0:T(128)} %rows.5), channel_id=1, source_target_pairs={{24,0},{0,8},{8,16},{16,24},{25,1},{1,9},{9,17},{17,25},{26,2},{2,... | collective-permute-start | bytes 32 | tf_op jit(solution)/shard_map/ppermute | solution.py:20
  0.5 2.6 %collective-permute-start.5 = (s32[2]{0:T(128)}, s32[2]{0:T(128)S(1)}, u32[]{:S(2)}, u32[]{:S(2)}) collective-permute-start(s32[2]{0:T(128)} %cols.5), channel_id=1, source_target_pairs={{24,0},{0,8},{8,16},{16,24},{25,1},{1,9},{9,17},{17,25},{26,2},{2,... | collective-permute-start | bytes 32 | tf_op jit(solution)/shard_map/ppermute | solution.py:20
  3.1 2.1 %load.1 = (f32[4096,128]{1,0:T(8,128)S(1)}, f32[1024,128]{1,0:T(8,128)S(1)}, bf16[2,256,256]{2,1,0:T(8,128)(2,1)S(1)}, bf16[768,384]{1,0:T(8,128)(2,1)S(1)}, f32[512,128]{1,0:T(8,128)S(1)}) custom-call(f32[4096,128]{1,0:T(8,128)} %bitcast.19, f32[1024,128]{1,0:T(8,128)} %bitcast.20, bf16[2,256,256]{2,1,0:T(8,128)(2,1)} %refs_2_.1, ...), custom_call_target="tpu_custom_call" | custom-call | tf_op jit(solution)/shard_map/load/pallas_call | solution.py:101
  5.2 0.0 copy-start
  5.2 0.0 copy-start.1
  5.2 0.0 collective-permute-done.4
  5.2 0.2 shard_map.67
  5.5 0.1 collective-permute-start.6
  5.5 1.1 %collective-permute-start.3 = (f32[512,128]{1,0:T(8,128)S(1)}, f32[512,128]{1,0:T(8,128)S(1)}, u32[]{:S(2)}, u32[]{:S(2)}) collective-permute-start(f32[512,128]{1,0:T(8,128)S(1)} %get-tuple-element.38), channel_id=1, source_target_pairs={{8,0},{16,8},{24,16},{0,24},{9,1},{17,9},{25,17},{1,25},{10,2},{18... | collective-permute-start | bytes 786440 | tf_op jit(solution)/shard_map/ppermute | solution.py:20
  6.6 2.8 %shard_map.64 = (f32[136,256]{1,0:T(8,128)S(1)}, f32[136,256]{1,0:T(8,128)S(1)}, f32[136,256]{1,0:T(8,128)S(1)}, f32[136,256]{1,0:T(8,128)S(1)}) custom-call(s32[2]{0:T(128)S(1)} %copy-done, s32[2]{0:T(128)S(1)} %copy-done.1, f32[4096,128]{1,0:T(8,128)S(1)} %get-tuple-element.27.obj, f32[1024,128]{1,0:T(8,128)S(1)} %get-tuple-element.28.ill, ...), custom_call_target="tpu_custom_call" | custom-call | flops 805306368 | bytes 1114112 | tf_op jit(solution)/shard_map/pallas_call | solution.py:72
  9.4 1.6 %collective-permute-start = (f32[136,256]{1,0:T(8,128)S(1)}, f32[136,256]{1,0:T(8,128)S(1)}, u32[]{:S(2)}, u32[]{:S(2)}) collective-permute-start(f32[136,256]{1,0:T(8,128)S(1)} %get-tuple-element.32), channel_id=1, source_target_pairs={{0,1},{1,0},{2,3},{3,2},{4,5},{5,4},{6,7},{7,6},{8,9},{9,8},{10,11... | collective-permute-start | bytes 417800 | tf_op jit(solution)/shard_map/ppermute | solution.py:24
  11.0 1.6 %collective-permute-start.1 = (f32[136,256]{1,0:T(8,128)S(1)}, f32[136,256]{1,0:T(8,128)S(1)}, u32[]{:S(2)}, u32[]{:S(2)}) collective-permute-start(f32[136,256]{1,0:T(8,128)S(1)} %get-tuple-element.33), channel_id=1, source_target_pairs={{0,2},{1,3},{2,0},{3,1},{4,6},{5,7},{6,4},{7,5},{8,10},{9,11},{10,... | collective-permute-start | bytes 417800 | tf_op jit(solution)/shard_map/ppermute | solution.py:24
  12.6 0.4 collective-permute-start.2
  13.0 1.1 %shard_map.66 = (f32[2,256,256]{2,1,0:T(8,128)S(1)}, f32[256,256]{1,0:T(8,128)S(1)}, f32[2,256,256]{2,1,0:T(8,128)S(1)}) custom-call(s32[2]{0:T(128)S(1)} %copy-done, s32[2]{0:T(128)S(1)} %copy-done.1, f32[4096,128]{1,0:T(8,128)S(1)} %get-tuple-element.27.obj, f32[1024,128]{1,0:T(8,128)S(1)} %get-tuple-element.28.ill, ...), custom_call_target="tpu_custom_call" | custom-call | bytes 2621440 | tf_op jit(solution)/shard_map/pallas_call | solution.py:72
  14.1 0.0 collective-permute-done.3.strip
  14.1 2.5 %shard_map.68 = (f32[128,256]{1,0:T(8,128)S(1)}, f32[128,256]{1,0:T(8,128)S(1)}, f32[128,256]{1,0:T(8,128)S(1)}, f32[128,256]{1,0:T(8,128)S(1)}) custom-call(s32[2]{0:T(128)S(1)} %copy-done, s32[2]{0:T(128)S(1)} %copy-done.1, f32[2,256,256]{2,1,0:T(8,128)S(1)} %get-tuple-element.35.probe, f32[256,256]{1,0:T(8,128)S(1)} %get-tuple-element.36.ordered, ...), custom_call_target="tpu_custom_call" | custom-call | flops 805306368 | bytes 1048576 | tf_op jit(solution)/shard_map/pallas_call | solution.py:72
  16.6 1.6 %collective-permute-start.7 = (f32[128,256]{1,0:T(8,128)S(1)}, f32[128,256]{1,0:T(8,128)S(1)}, u32[]{:S(2)}, u32[]{:S(2)}) collective-permute-start(f32[128,256]{1,0:T(8,128)S(1)} %get-tuple-element.40), channel_id=1, source_target_pairs={{0,1},{1,0},{2,3},{3,2},{4,5},{5,4},{6,7},{7,6},{8,9},{9,8},{10,11... | collective-permute-start | bytes 393224 | tf_op jit(solution)/shard_map/ppermute | solution.py:24
  18.1 1.6 %collective-permute-start.8 = (f32[128,256]{1,0:T(8,128)S(1)}, f32[128,256]{1,0:T(8,128)S(1)}, u32[]{:S(2)}, u32[]{:S(2)}) collective-permute-start(f32[128,256]{1,0:T(8,128)S(1)} %get-tuple-element.41), channel_id=1, source_target_pairs={{0,2},{1,3},{2,0},{3,1},{4,6},{5,7},{6,4},{7,5},{8,10},{9,11},{10,... | collective-permute-start | bytes 393224 | tf_op jit(solution)/shard_map/ppermute | solution.py:24
  19.7 0.4 collective-permute-start.9
  20.1 0.2 shard_map.65.acc
  20.4 1.9 %collective-permute-done.7.refs_5_ = f32[128,256]{1,0:T(8,128)S(1)} collective-permute-done((f32[128,256]{1,0:T(8,128)S(1)}, f32[128,256]{1,0:T(8,128)S(1)}, u32[]{:S(2)}, u32[]{:S(2)}) %collective-permute-start.7) | collective-permute-done | bytes 131104 | tf_op jit(solution)/shard_map/ppermute | solution.py:24
  22.2 1.8 %collective-permute-done.8.refs_6_ = f32[128,256]{1,0:T(8,128)S(1)} collective-permute-done((f32[128,256]{1,0:T(8,128)S(1)}, f32[128,256]{1,0:T(8,128)S(1)}, u32[]{:S(2)}, u32[]{:S(2)}) %collective-permute-start.8) | collective-permute-done | bytes 131104 | tf_op jit(solution)/shard_map/ppermute | solution.py:24
  24.0 3.0 %collective-permute-done.9.refs_7_ = f32[128,256]{1,0:T(8,128)S(1)} collective-permute-done((f32[128,256]{1,0:T(8,128)S(1)}, f32[128,256]{1,0:T(8,128)S(1)}, u32[]{:S(2)}, u32[]{:S(2)}) %collective-permute-start.9) | collective-permute-done | bytes 131104 | tf_op jit(solution)/shard_map/ppermute | solution.py:24
  27.0 0.4 shard_map.69
  27.4 0.2 collective-permute-start.10
  27.6 1.2 %collective-permute-start.11 = (f32[256,128]{1,0:T(8,128)S(1)}, f32[256,128]{1,0:T(8,128)S(1)}, u32[]{:S(2)}, u32[]{:S(2)}) collective-permute-start(f32[256,128]{1,0:T(8,128)S(1)} %get-tuple-element.48), channel_id=1, source_target_pairs={{24,0},{0,8},{8,16},{16,24},{25,1},{1,9},{9,17},{17,25},{26,2},{2,... | collective-permute-start | bytes 393224 | tf_op jit(solution)/shard_map/ppermute | solution.py:20
  28.7 3.1 %collective-permute-done.10 = f32[256,128]{1,0:T(8,128)S(1)} collective-permute-done((f32[256,128]{1,0:T(8,128)S(1)}, f32[256,128]{1,0:T(8,128)S(1)}, u32[]{:S(2)}, u32[]{:S(2)}) %collective-permute-start.10) | collective-permute-done | bytes 131104 | tf_op jit(solution)/shard_map/ppermute | solution.py:20
  31.9 2.7 %collective-permute-start.12 = (f32[256,128]{1,0:T(8,128)S(1)}, f32[256,128]{1,0:T(8,128)S(1)}, u32[]{:S(2)}, u32[]{:S(2)}) collective-permute-start(f32[256,128]{1,0:T(8,128)S(1)} %get-tuple-element.51), channel_id=1, source_target_pairs={{0,4},{1,5},{2,6},{3,7},{4,0},{5,1},{6,2},{7,3},{8,12},{9,13},{10,... | collective-permute-start | bytes 393224 | tf_op jit(solution)/shard_map/ppermute | solution.py:24
  34.6 1.4 %collective-permute-start.13 = (f32[256,128]{1,0:T(8,128)S(1)}, f32[256,128]{1,0:T(8,128)S(1)}, u32[]{:S(2)}, u32[]{:S(2)}) collective-permute-start(f32[256,128]{1,0:T(8,128)S(1)} %get-tuple-element.49), channel_id=1, source_target_pairs={{0,4},{1,5},{2,6},{3,7},{4,0},{5,1},{6,2},{7,3},{8,12},{9,13},{10,... | collective-permute-start | bytes 393224 | tf_op jit(solution)/shard_map/ppermute | solution.py:24
  35.9 8.0 %collective-permute-done.12.refs_2_ = f32[256,128]{1,0:T(8,128)S(1)} collective-permute-done((f32[256,128]{1,0:T(8,128)S(1)}, f32[256,128]{1,0:T(8,128)S(1)}, u32[]{:S(2)}, u32[]{:S(2)}) %collective-permute-start.12) | collective-permute-done | bytes 131104 | tf_op jit(solution)/shard_map/ppermute | solution.py:24
  43.9 1.7 %collective-permute-done.13.refs_3_ = f32[256,128]{1,0:T(8,128)S(1)} collective-permute-done((f32[256,128]{1,0:T(8,128)S(1)}, f32[256,128]{1,0:T(8,128)S(1)}, u32[]{:S(2)}, u32[]{:S(2)}) %collective-permute-start.13) | collective-permute-done | bytes 131104 | tf_op jit(solution)/shard_map/ppermute | solution.py:24
  45.6 0.8 %final.1 = f32[512,128]{1,0:T(8,128)} custom-call(f32[256,128]{1,0:T(8,128)S(1)} %get-tuple-element.52.refs_0_, f32[256,128]{1,0:T(8,128)S(1)} %get-tuple-element.50.refs_1_, f32[256,128]{1,0:T(8,128)S(1)} %collective-permute-done.12.refs_2_, f32[256,128]{1,0:T(8,128)S(1)} %collective-permute-done.13.refs_3_), custom_call_target="tpu_custom_call" | custom-call | tf_op jit(solution)/shard_map/final/pallas_call | solution.py:468
  (10 shorter events, 0.1 us)
Async XLA Ops:
  0.0 5.2 %collective-permute-start.4 = (s32[2]{0:T(128)}, s32[2]{0:T(128)S(1)}, u32[]{:S(2)}, u32[]{:S(2)}) collective-permute-start(s32[2]{0:T(128)} %rows.5), channel_id=1, source_target_pairs={{24,0},{0,8},{8,16},{16,24},{25,1},{1,9},{9,17},{17,25},{26,2},{2,... | collective-permute-start | bytes 32 | tf_op jit(solution)/shard_map/ppermute | solution.py:20
  0.5 4.7 %collective-permute-start.5 = (s32[2]{0:T(128)}, s32[2]{0:T(128)S(1)}, u32[]{:S(2)}, u32[]{:S(2)}) collective-permute-start(s32[2]{0:T(128)} %cols.5), channel_id=1, source_target_pairs={{24,0},{0,8},{8,16},{16,24},{25,1},{1,9},{9,17},{17,25},{26,2},{2,... | collective-permute-start | bytes 32 | tf_op jit(solution)/shard_map/ppermute | solution.py:20
  5.2 1.4 %copy-start = (s32[2]{0:T(128)S(1)}, s32[2]{0:T(128)}, u32[]{:S(2)}) copy-start(s32[2]{0:T(128)} %rows.5) | copy-start | bytes 28
  5.2 1.4 %copy-start.1 = (s32[2]{0:T(128)S(1)}, s32[2]{0:T(128)}, u32[]{:S(2)}) copy-start(s32[2]{0:T(128)} %cols.5) | copy-start | bytes 28
  5.5 8.6 %collective-permute-start.6 = (f32[2,192,256]{2,1,0:T(8,128)S(1)}, f32[2,192,256]{2,1,0:T(8,128)S(1)}, u32[]{:S(2)}, u32[]{:S(2)}) collective-permute-start(f32[2,192,256]{2,1,0:T(8,128)S(1)} %shard_map.67), channel_id=1, source_target_pairs={{8,0},{16,8},{24,16},{0,24},{9,1},{17,9},{25,17},{1,25},{10,2},{18... | collective-permute-start | bytes 1179656 | tf_op jit(solution)/shard_map/ppermute | solution.py:20
  5.5 8.6 %collective-permute-start.3 = (f32[512,128]{1,0:T(8,128)S(1)}, f32[512,128]{1,0:T(8,128)S(1)}, u32[]{:S(2)}, u32[]{:S(2)}) collective-permute-start(f32[512,128]{1,0:T(8,128)S(1)} %get-tuple-element.38), channel_id=1, source_target_pairs={{8,0},{16,8},{24,16},{0,24},{9,1},{17,9},{25,17},{1,25},{10,2},{18... | collective-permute-start | bytes 786440 | tf_op jit(solution)/shard_map/ppermute | solution.py:20
  9.4 10.3 %collective-permute-start = (f32[136,256]{1,0:T(8,128)S(1)}, f32[136,256]{1,0:T(8,128)S(1)}, u32[]{:S(2)}, u32[]{:S(2)}) collective-permute-start(f32[136,256]{1,0:T(8,128)S(1)} %get-tuple-element.32), channel_id=1, source_target_pairs={{0,1},{1,0},{2,3},{3,2},{4,5},{5,4},{6,7},{7,6},{8,9},{9,8},{10,11... | collective-permute-start | bytes 417800 | tf_op jit(solution)/shard_map/ppermute | solution.py:24
  11.0 9.2 %collective-permute-start.1 = (f32[136,256]{1,0:T(8,128)S(1)}, f32[136,256]{1,0:T(8,128)S(1)}, u32[]{:S(2)}, u32[]{:S(2)}) collective-permute-start(f32[136,256]{1,0:T(8,128)S(1)} %get-tuple-element.33), channel_id=1, source_target_pairs={{0,2},{1,3},{2,0},{3,1},{4,6},{5,7},{6,4},{7,5},{8,10},{9,11},{10,... | collective-permute-start | bytes 417800 | tf_op jit(solution)/shard_map/ppermute | solution.py:24
  12.6 7.6 %collective-permute-start.2 = (f32[136,256]{1,0:T(8,128)S(1)}, f32[136,256]{1,0:T(8,128)S(1)}, u32[]{:S(2)}, u32[]{:S(2)}) collective-permute-start(f32[136,256]{1,0:T(8,128)S(1)} %get-tuple-element.34), channel_id=1, source_target_pairs={{0,3},{1,2},{2,1},{3,0},{4,7},{5,6},{6,5},{7,4},{8,11},{9,10},{10,... | collective-permute-start | bytes 417800 | tf_op jit(solution)/shard_map/ppermute | solution.py:24
  16.6 5.7 %collective-permute-start.7 = (f32[128,256]{1,0:T(8,128)S(1)}, f32[128,256]{1,0:T(8,128)S(1)}, u32[]{:S(2)}, u32[]{:S(2)}) collective-permute-start(f32[128,256]{1,0:T(8,128)S(1)} %get-tuple-element.40), channel_id=1, source_target_pairs={{0,1},{1,0},{2,3},{3,2},{4,5},{5,4},{6,7},{7,6},{8,9},{9,8},{10,11... | collective-permute-start | bytes 393224 | tf_op jit(solution)/shard_map/ppermute | solution.py:24
  18.1 5.9 %collective-permute-start.8 = (f32[128,256]{1,0:T(8,128)S(1)}, f32[128,256]{1,0:T(8,128)S(1)}, u32[]{:S(2)}, u32[]{:S(2)}) collective-permute-start(f32[128,256]{1,0:T(8,128)S(1)} %get-tuple-element.41), channel_id=1, source_target_pairs={{0,2},{1,3},{2,0},{3,1},{4,6},{5,7},{6,4},{7,5},{8,10},{9,11},{10,... | collective-permute-start | bytes 393224 | tf_op jit(solution)/shard_map/ppermute | solution.py:24
  19.7 7.3 %collective-permute-start.9 = (f32[128,256]{1,0:T(8,128)S(1)}, f32[128,256]{1,0:T(8,128)S(1)}, u32[]{:S(2)}, u32[]{:S(2)}) collective-permute-start(f32[128,256]{1,0:T(8,128)S(1)} %get-tuple-element.42), channel_id=1, source_target_pairs={{0,3},{1,2},{2,1},{3,0},{4,7},{5,6},{6,5},{7,4},{8,11},{9,10},{10,... | collective-permute-start | bytes 393224 | tf_op jit(solution)/shard_map/ppermute | solution.py:24
  27.4 4.4 %collective-permute-start.10 = (f32[256,128]{1,0:T(8,128)S(1)}, f32[256,128]{1,0:T(8,128)S(1)}, u32[]{:S(2)}, u32[]{:S(2)}) collective-permute-start(f32[256,128]{1,0:T(8,128)S(1)} %get-tuple-element.45), channel_id=1, source_target_pairs={{24,0},{0,8},{8,16},{16,24},{25,1},{1,9},{9,17},{17,25},{26,2},{2,... | collective-permute-start | bytes 393224 | tf_op jit(solution)/shard_map/ppermute | solution.py:20
  27.6 7.0 %collective-permute-start.11 = (f32[256,128]{1,0:T(8,128)S(1)}, f32[256,128]{1,0:T(8,128)S(1)}, u32[]{:S(2)}, u32[]{:S(2)}) collective-permute-start(f32[256,128]{1,0:T(8,128)S(1)} %get-tuple-element.48), channel_id=1, source_target_pairs={{24,0},{0,8},{8,16},{16,24},{25,1},{1,9},{9,17},{17,25},{26,2},{2,... | collective-permute-start | bytes 393224 | tf_op jit(solution)/shard_map/ppermute | solution.py:20
  31.9 12.1 %collective-permute-start.12 = (f32[256,128]{1,0:T(8,128)S(1)}, f32[256,128]{1,0:T(8,128)S(1)}, u32[]{:S(2)}, u32[]{:S(2)}) collective-permute-start(f32[256,128]{1,0:T(8,128)S(1)} %get-tuple-element.51), channel_id=1, source_target_pairs={{0,4},{1,5},{2,6},{3,7},{4,0},{5,1},{6,2},{7,3},{8,12},{9,13},{10,... | collective-permute-start | bytes 393224 | tf_op jit(solution)/shard_map/ppermute | solution.py:24
  34.6 11.0 %collective-permute-start.13 = (f32[256,128]{1,0:T(8,128)S(1)}, f32[256,128]{1,0:T(8,128)S(1)}, u32[]{:S(2)}, u32[]{:S(2)}) collective-permute-start(f32[256,128]{1,0:T(8,128)S(1)} %get-tuple-element.49), channel_id=1, source_target_pairs={{0,4},{1,5},{2,6},{3,7},{4,0},{5,1},{6,2},{7,3},{8,12},{9,13},{10,... | collective-permute-start | bytes 393224 | tf_op jit(solution)/shard_map/ppermute | solution.py:24

commit v16 on v14

--- a/solution.py
+++ b/solution.py
@@ -397,7 +397,7 @@
     rim = shifted(rim, "tile", -1)
 
     def spread(pieces):
-        moved = {d: exchanged(pieces[d], "pos", d) for d in reversed(range(1, classes))}
+        moved = {d: exchanged(pieces[d], "pos", d) for d in range(1, classes)}
         return [pieces[0]] + [moved[d] for d in range(1, classes)]
 
     roll, state, work = scratch_of(window)

time: 45 us -> 45 us (level)
  no operation moved by 1% of the time
where the time goes in v16:
time: 45 us; the launch traced here: 44.9 us
  waiting for transfers between devices  19.6 us (44%)
  starting transfers between devices  14.8 us (33%)
  Pallas kernels  9.94 us (22%)
    ppermute x8, waiting for transfers between devices, exchanged(): lax.ppermute(block, axis, [(i, i ^ flip) for i in range(lax.axis_size(axi...  15.7 us
    ppermute x8, starting transfers between devices, exchanged(): lax.ppermute(block, axis, [(i, i ^ flip) for i in range(lax.axis_size(axi...  11.1 us
    pallas_call x6, Pallas kernels, kernel_call(): pl.pallas_call(body, out_shape=[pltpu.VMEM(shape, F32) for shape in out_s...  7.21 us
    ppermute x5, waiting for transfers between devices, shifted(): lax.ppermute(block, axis, [((i - distance) % devices, i) for i in range(d...  3.91 us
    ppermute x5, starting transfers between devices, shifted(): lax.ppermute(block, axis, [((i - distance) % devices, i) for i in range(d...  3.72 us
    pallas_call x1, Pallas kernels, loaded(): pl.pallas_call(functools.partial(load_kernel, len(arrays)), out_shape=[pl...  1.96 us
  transfers between devices with their start and end apart: 13, of which 6 were waited for; matrix products, arithmetic and copies ran while one was open for 0% of the time, Pallas kernels for 19%

profile of v16, /device:TPU:0, one launch (start us, length us, event | category | flops | bytes accessed | tf_op | source)
XLA Modules:
  0.0 44.9 jit_solution(12334554584513527501)
XLA Ops:
  0.0 0.5 %collective-permute-start.3 = (s32[2]{0:T(128)}, s32[2]{0:T(128)S(1)}, u32[]{:S(2)}, u32[]{:S(2)}) collective-permute-start(s32[2]{0:T(128)} %rows.5), channel_id=1, source_target_pairs={{24,0},{0,8},{8,16},{16,24},{25,1},{1,9},{9,17},{17,25},{26,2},{2,... | collective-permute-start | bytes 32 | tf_op jit(solution)/shard_map/ppermute | solution.py:19
  0.5 2.6 %collective-permute-start.4 = (s32[2]{0:T(128)}, s32[2]{0:T(128)S(1)}, u32[]{:S(2)}, u32[]{:S(2)}) collective-permute-start(s32[2]{0:T(128)} %cols.5), channel_id=1, source_target_pairs={{24,0},{0,8},{8,16},{16,24},{25,1},{1,9},{9,17},{17,25},{26,2},{2,... | collective-permute-start | bytes 32 | tf_op jit(solution)/shard_map/ppermute | solution.py:19
  3.1 2.0 %load.1 = (f32[4096,128]{1,0:T(8,128)S(1)}, f32[1024,128]{1,0:T(8,128)S(1)}, bf16[2,256,256]{2,1,0:T(8,128)(2,1)S(1)}, bf16[768,384]{1,0:T(8,128)(2,1)S(1)}) custom-call(f32[4096,128]{1,0:T(8,128)} %bitcast.19, f32[1024,128]{1,0:T(8,128)} %bitcast.20, bf16[2,256,256]{2,1,0:T(8,128)(2,1)} %refs_2_.1, bf16[768,384]{1,0:T(8,128)(2,1)} %constant.8.clone.refs_3_), custom_call_target="tpu_custom_call" | custom-call | tf_op jit(solution)/shard_map/load/pallas_call | solution.py:99
  5.1 0.0 copy-start
  5.1 0.0 copy-start.1
  5.1 0.0 collective-permute-done.4
  5.1 0.3 rim.1
  5.4 0.1 collective-permute-start.5
  5.5 0.3 copy-done
  5.7 0.0 copy-done.1
  5.8 2.8 %wave0.1 = (f32[136,256]{1,0:T(8,128)S(1)}, f32[136,256]{1,0:T(8,128)S(1)}, f32[136,256]{1,0:T(8,128)S(1)}, f32[136,256]{1,0:T(8,128)S(1)}) custom-call(s32[2]{0:T(128)S(1)} %copy-done, s32[2]{0:T(128)S(1)} %copy-done.1, f32[4096,128]{1,0:T(8,128)S(1)} %get-tuple-element.26.obj, f32[1024,128]{1,0:T(8,128)S(1)} %get-tuple-element.27.ill, ...), custom_call_target="tpu_custom_call" | custom-call | flops 805306368 | bytes 1114112 | tf_op jit(solution)/shard_map/wave0/pallas_call | solution.py:71
  8.5 1.6 %collective-permute-start = (f32[136,256]{1,0:T(8,128)S(1)}, f32[136,256]{1,0:T(8,128)S(1)}, u32[]{:S(2)}, u32[]{:S(2)}) collective-permute-start(f32[136,256]{1,0:T(8,128)S(1)} %get-tuple-element.31), channel_id=1, source_target_pairs={{0,1},{1,0},{2,3},{3,2},{4,5},{5,4},{6,7},{7,6},{8,9},{9,8},{10,11... | collective-permute-start | bytes 417800 | tf_op jit(solution)/shard_map/ppermute | solution.py:23
  10.1 1.6 %collective-permute-start.1 = (f32[136,256]{1,0:T(8,128)S(1)}, f32[136,256]{1,0:T(8,128)S(1)}, u32[]{:S(2)}, u32[]{:S(2)}) collective-permute-start(f32[136,256]{1,0:T(8,128)S(1)} %get-tuple-element.32), channel_id=1, source_target_pairs={{0,2},{1,3},{2,0},{3,1},{4,6},{5,7},{6,4},{7,5},{8,10},{9,11},{10,... | collective-permute-start | bytes 417800 | tf_op jit(solution)/shard_map/ppermute | solution.py:23
  11.7 0.4 collective-permute-start.2
  12.1 1.1 %start1.1 = (f32[2,256,256]{2,1,0:T(8,128)S(1)}, f32[256,256]{1,0:T(8,128)S(1)}, f32[2,256,256]{2,1,0:T(8,128)S(1)}) custom-call(s32[2]{0:T(128)S(1)} %copy-done, s32[2]{0:T(128)S(1)} %copy-done.1, f32[4096,128]{1,0:T(8,128)S(1)} %get-tuple-element.26.obj, f32[1024,128]{1,0:T(8,128)S(1)} %get-tuple-element.27.ill, ...), custom_call_target="tpu_custom_call" | custom-call | bytes 2621440 | tf_op jit(solution)/shard_map/start/start1/pallas_call | solution.py:71
  13.2 2.5 %wave1.1 = (f32[128,256]{1,0:T(8,128)S(1)}, f32[128,256]{1,0:T(8,128)S(1)}, f32[128,256]{1,0:T(8,128)S(1)}, f32[128,256]{1,0:T(8,128)S(1)}) custom-call(s32[2]{0:T(128)S(1)} %copy-done, s32[2]{0:T(128)S(1)} %copy-done.1, f32[2,256,256]{2,1,0:T(8,128)S(1)} %get-tuple-element.34.probe, f32[256,256]{1,0:T(8,128)S(1)} %get-tuple-element.35.ordered, ...), custom_call_target="tpu_custom_call" | custom-call | flops 805306368 | bytes 1048576 | tf_op jit(solution)/shard_map/wave1/pallas_call | solution.py:71
  15.7 1.6 %collective-permute-start.6 = (f32[128,256]{1,0:T(8,128)S(1)}, f32[128,256]{1,0:T(8,128)S(1)}, u32[]{:S(2)}, u32[]{:S(2)}) collective-permute-start(f32[128,256]{1,0:T(8,128)S(1)} %get-tuple-element.38), channel_id=1, source_target_pairs={{0,1},{1,0},{2,3},{3,2},{4,5},{5,4},{6,7},{7,6},{8,9},{9,8},{10,11... | collective-permute-start | bytes 393224 | tf_op jit(solution)/shard_map/ppermute | solution.py:23
  17.2 1.6 %collective-permute-start.7 = (f32[128,256]{1,0:T(8,128)S(1)}, f32[128,256]{1,0:T(8,128)S(1)}, u32[]{:S(2)}, u32[]{:S(2)}) collective-permute-start(f32[128,256]{1,0:T(8,128)S(1)} %get-tuple-element.39), channel_id=1, source_target_pairs={{0,2},{1,3},{2,0},{3,1},{4,6},{5,7},{6,4},{7,5},{8,10},{9,11},{10,... | collective-permute-start | bytes 393224 | tf_op jit(solution)/shard_map/ppermute | solution.py:23
  18.8 0.4 collective-permute-start.8
  19.2 0.2 sum0.1.acc
  19.5 2.5 %collective-permute-done.6.refs_5_ = f32[128,256]{1,0:T(8,128)S(1)} collective-permute-done((f32[128,256]{1,0:T(8,128)S(1)}, f32[128,256]{1,0:T(8,128)S(1)}, u32[]{:S(2)}, u32[]{:S(2)}) %collective-permute-start.6) | collective-permute-done | bytes 131104 | tf_op jit(solution)/shard_map/ppermute | solution.py:23
  21.9 1.7 %collective-permute-done.7.refs_6_ = f32[128,256]{1,0:T(8,128)S(1)} collective-permute-done((f32[128,256]{1,0:T(8,128)S(1)}, f32[128,256]{1,0:T(8,128)S(1)}, u32[]{:S(2)}, u32[]{:S(2)}) %collective-permute-start.7) | collective-permute-done | bytes 131104 | tf_op jit(solution)/shard_map/ppermute | solution.py:23
  23.6 2.7 %collective-permute-done.8.refs_7_ = f32[128,256]{1,0:T(8,128)S(1)} collective-permute-done((f32[128,256]{1,0:T(8,128)S(1)}, f32[128,256]{1,0:T(8,128)S(1)}, u32[]{:S(2)}, u32[]{:S(2)}) %collective-permute-start.8) | collective-permute-done | bytes 131104 | tf_op jit(solution)/shard_map/ppermute | solution.py:23
  26.3 0.4 sum1.1
  26.7 0.1 collective-permute-start.10
  26.8 0.5 %collective-permute-start.9 = (f32[256,128]{1,0:T(8,128)S(1)}, f32[256,128]{1,0:T(8,128)S(1)}, u32[]{:S(2)}, u32[]{:S(2)}) collective-permute-start(f32[256,128]{1,0:T(8,128)S(1)} %get-tuple-element.43), channel_id=1, source_target_pairs={{24,0},{0,8},{8,16},{16,24},{25,1},{1,9},{9,17},{17,25},{26,2},{2,... | collective-permute-start | bytes 393224 | tf_op jit(solution)/shard_map/spill_0/ppermute | solution.py:19
  27.3 3.9 %collective-permute-done.10 = f32[256,128]{1,0:T(8,128)S(1)} collective-permute-done((f32[256,128]{1,0:T(8,128)S(1)}, f32[256,128]{1,0:T(8,128)S(1)}, u32[]{:S(2)}, u32[]{:S(2)}) %collective-permute-start.10) | collective-permute-done | bytes 131104 | tf_op jit(solution)/shard_map/spill_1/ppermute | solution.py:19
  31.2 2.7 %collective-permute-start.12 = (f32[256,128]{1,0:T(8,128)S(1)}, f32[256,128]{1,0:T(8,128)S(1)}, u32[]{:S(2)}, u32[]{:S(2)}) collective-permute-start(f32[256,128]{1,0:T(8,128)S(1)} %get-tuple-element.47), channel_id=1, source_target_pairs={{0,4},{1,5},{2,6},{3,7},{4,0},{5,1},{6,2},{7,3},{8,12},{9,13},{10,... | collective-permute-start | bytes 393224 | tf_op jit(solution)/shard_map/halves_1/ppermute | solution.py:23
  33.9 1.4 %collective-permute-start.11 = (f32[256,128]{1,0:T(8,128)S(1)}, f32[256,128]{1,0:T(8,128)S(1)}, u32[]{:S(2)}, u32[]{:S(2)}) collective-permute-start(f32[256,128]{1,0:T(8,128)S(1)} %get-tuple-element.49), channel_id=1, source_target_pairs={{0,4},{1,5},{2,6},{3,7},{4,0},{5,1},{6,2},{7,3},{8,12},{9,13},{10,... | collective-permute-start | bytes 393224 | tf_op jit(solution)/shard_map/halves_0/ppermute | solution.py:23
  35.2 7.5 %collective-permute-done.12.refs_3_ = f32[256,128]{1,0:T(8,128)S(1)} collective-permute-done((f32[256,128]{1,0:T(8,128)S(1)}, f32[256,128]{1,0:T(8,128)S(1)}, u32[]{:S(2)}, u32[]{:S(2)}) %collective-permute-start.12) | collective-permute-done | bytes 131104 | tf_op jit(solution)/shard_map/halves_1/ppermute | solution.py:23
  42.7 1.4 %collective-permute-done.11.refs_2_ = f32[256,128]{1,0:T(8,128)S(1)} collective-permute-done((f32[256,128]{1,0:T(8,128)S(1)}, f32[256,128]{1,0:T(8,128)S(1)}, u32[]{:S(2)}, u32[]{:S(2)}) %collective-permute-start.11) | collective-permute-done | bytes 131104 | tf_op jit(solution)/shard_map/halves_0/ppermute | solution.py:23
  44.1 0.8 %final.1 = f32[512,128]{1,0:T(8,128)} custom-call(f32[256,128]{1,0:T(8,128)S(1)} %get-tuple-element.50.refs_0_, f32[256,128]{1,0:T(8,128)S(1)} %get-tuple-element.48.refs_1_, f32[256,128]{1,0:T(8,128)S(1)} %collective-permute-done.11.refs_2_, f32[256,128]{1,0:T(8,128)S(1)} %collective-permute-done.12.refs_3_), custom_call_target="tpu_custom_call" | custom-call | tf_op jit(solution)/shard_map/final/pallas_call | solution.py:455
  (8 shorter events, 0.1 us)
Async XLA Ops:
  0.0 5.1 %collective-permute-start.3 = (s32[2]{0:T(128)}, s32[2]{0:T(128)S(1)}, u32[]{:S(2)}, u32[]{:S(2)}) collective-permute-start(s32[2]{0:T(128)} %rows.5), channel_id=1, source_target_pairs={{24,0},{0,8},{8,16},{16,24},{25,1},{1,9},{9,17},{17,25},{26,2},{2,... | collective-permute-start | bytes 32 | tf_op jit(solution)/shard_map/ppermute | solution.py:19
  0.5 4.6 %collective-permute-start.4 = (s32[2]{0:T(128)}, s32[2]{0:T(128)S(1)}, u32[]{:S(2)}, u32[]{:S(2)}) collective-permute-start(s32[2]{0:T(128)} %cols.5), channel_id=1, source_target_pairs={{24,0},{0,8},{8,16},{16,24},{25,1},{1,9},{9,17},{17,25},{26,2},{2,... | collective-permute-start | bytes 32 | tf_op jit(solution)/shard_map/ppermute | solution.py:19
  5.1 0.7 %copy-start = (s32[2]{0:T(128)S(1)}, s32[2]{0:T(128)}, u32[]{:S(2)}) copy-start(s32[2]{0:T(128)} %rows.5) | copy-start | bytes 28
  5.1 0.7 %copy-start.1 = (s32[2]{0:T(128)S(1)}, s32[2]{0:T(128)}, u32[]{:S(2)}) copy-start(s32[2]{0:T(128)} %cols.5) | copy-start | bytes 28
  5.4 7.8 %collective-permute-start.5 = (f32[2,256,256]{2,1,0:T(8,128)S(1)}, f32[2,256,256]{2,1,0:T(8,128)S(1)}, u32[]{:S(2)}, u32[]{:S(2)}) collective-permute-start(f32[2,256,256]{2,1,0:T(8,128)S(1)} %rim.1), channel_id=1, source_target_pairs={{8,0},{16,8},{24,16},{0,24},{9,1},{17,9},{25,17},{1,25},{10,2},{18... | collective-permute-start | bytes 1572872 | tf_op jit(solution)/shard_map/ppermute | solution.py:19
  8.5 10.3 %collective-permute-start = (f32[136,256]{1,0:T(8,128)S(1)}, f32[136,256]{1,0:T(8,128)S(1)}, u32[]{:S(2)}, u32[]{:S(2)}) collective-permute-start(f32[136,256]{1,0:T(8,128)S(1)} %get-tuple-element.31), channel_id=1, source_target_pairs={{0,1},{1,0},{2,3},{3,2},{4,5},{5,4},{6,7},{7,6},{8,9},{9,8},{10,11... | collective-permute-start | bytes 417800 | tf_op jit(solution)/shard_map/ppermute | solution.py:23
  10.1 9.1 %collective-permute-start.1 = (f32[136,256]{1,0:T(8,128)S(1)}, f32[136,256]{1,0:T(8,128)S(1)}, u32[]{:S(2)}, u32[]{:S(2)}) collective-permute-start(f32[136,256]{1,0:T(8,128)S(1)} %get-tuple-element.32), channel_id=1, source_target_pairs={{0,2},{1,3},{2,0},{3,1},{4,6},{5,7},{6,4},{7,5},{8,10},{9,11},{10,... | collective-permute-start | bytes 417800 | tf_op jit(solution)/shard_map/ppermute | solution.py:23
  11.7 7.6 %collective-permute-start.2 = (f32[136,256]{1,0:T(8,128)S(1)}, f32[136,256]{1,0:T(8,128)S(1)}, u32[]{:S(2)}, u32[]{:S(2)}) collective-permute-start(f32[136,256]{1,0:T(8,128)S(1)} %get-tuple-element.33), channel_id=1, source_target_pairs={{0,3},{1,2},{2,1},{3,0},{4,7},{5,6},{6,5},{7,4},{8,11},{9,10},{10,... | collective-permute-start | bytes 417800 | tf_op jit(solution)/shard_map/ppermute | solution.py:23
  15.7 6.2 %collective-permute-start.6 = (f32[128,256]{1,0:T(8,128)S(1)}, f32[128,256]{1,0:T(8,128)S(1)}, u32[]{:S(2)}, u32[]{:S(2)}) collective-permute-start(f32[128,256]{1,0:T(8,128)S(1)} %get-tuple-element.38), channel_id=1, source_target_pairs={{0,1},{1,0},{2,3},{3,2},{4,5},{5,4},{6,7},{7,6},{8,9},{9,8},{10,11... | collective-permute-start | bytes 393224 | tf_op jit(solution)/shard_map/ppermute | solution.py:23
  17.2 6.4 %collective-permute-start.7 = (f32[128,256]{1,0:T(8,128)S(1)}, f32[128,256]{1,0:T(8,128)S(1)}, u32[]{:S(2)}, u32[]{:S(2)}) collective-permute-start(f32[128,256]{1,0:T(8,128)S(1)} %get-tuple-element.39), channel_id=1, source_target_pairs={{0,2},{1,3},{2,0},{3,1},{4,6},{5,7},{6,4},{7,5},{8,10},{9,11},{10,... | collective-permute-start | bytes 393224 | tf_op jit(solution)/shard_map/ppermute | solution.py:23
  18.8 7.5 %collective-permute-start.8 = (f32[128,256]{1,0:T(8,128)S(1)}, f32[128,256]{1,0:T(8,128)S(1)}, u32[]{:S(2)}, u32[]{:S(2)}) collective-permute-start(f32[128,256]{1,0:T(8,128)S(1)} %get-tuple-element.40), channel_id=1, source_target_pairs={{0,3},{1,2},{2,1},{3,0},{4,7},{5,6},{6,5},{7,4},{8,11},{9,10},{10,... | collective-permute-start | bytes 393224 | tf_op jit(solution)/shard_map/ppermute | solution.py:23
  26.7 4.4 %collective-permute-start.10 = (f32[256,128]{1,0:T(8,128)S(1)}, f32[256,128]{1,0:T(8,128)S(1)}, u32[]{:S(2)}, u32[]{:S(2)}) collective-permute-start(f32[256,128]{1,0:T(8,128)S(1)} %get-tuple-element.46), channel_id=1, source_target_pairs={{24,0},{0,8},{8,16},{16,24},{25,1},{1,9},{9,17},{17,25},{26,2},{2,... | collective-permute-start | bytes 393224 | tf_op jit(solution)/shard_map/spill_1/ppermute | solution.py:19
  26.8 7.1 %collective-permute-start.9 = (f32[256,128]{1,0:T(8,128)S(1)}, f32[256,128]{1,0:T(8,128)S(1)}, u32[]{:S(2)}, u32[]{:S(2)}) collective-permute-start(f32[256,128]{1,0:T(8,128)S(1)} %get-tuple-element.43), channel_id=1, source_target_pairs={{24,0},{0,8},{8,16},{16,24},{25,1},{1,9},{9,17},{17,25},{26,2},{2,... | collective-permute-start | bytes 393224 | tf_op jit(solution)/shard_map/spill_0/ppermute | solution.py:19
  31.2 11.5 %collective-permute-start.12 = (f32[256,128]{1,0:T(8,128)S(1)}, f32[256,128]{1,0:T(8,128)S(1)}, u32[]{:S(2)}, u32[]{:S(2)}) collective-permute-start(f32[256,128]{1,0:T(8,128)S(1)} %get-tuple-element.47), channel_id=1, source_target_pairs={{0,4},{1,5},{2,6},{3,7},{4,0},{5,1},{6,2},{7,3},{8,12},{9,13},{10,... | collective-permute-start | bytes 393224 | tf_op jit(solution)/shard_map/halves_1/ppermute | solution.py:23
  33.9 10.2 %collective-permute-start.11 = (f32[256,128]{1,0:T(8,128)S(1)}, f32[256,128]{1,0:T(8,128)S(1)}, u32[]{:S(2)}, u32[]{:S(2)}) collective-permute-start(f32[256,128]{1,0:T(8,128)S(1)} %get-tuple-element.49), channel_id=1, source_target_pairs={{0,4},{1,5},{2,6},{3,7},{4,0},{5,1},{6,2},{7,3},{8,12},{9,13},{10,... | collective-permute-start | bytes 393224 | tf_op jit(solution)/shard_map/halves_0/ppermute | solution.py:23

commit v17 on v16

--- a/solution.py
+++ b/solution.py
@@ -77,7 +77,7 @@
         cost_estimate=pl.CostEstimate(flops=flops, transcendentals=0, bytes_accessed=2 * moved),
         compiler_params=pltpu.CompilerParams(vmem_limit_bytes=16 << 20),
         name=name,
-    )(*scalars, *[in_vmem(array) for array in arrays])
+    )(*[pltpu.with_memory_space_constraint(scalar, pltpu.HBM) for scalar in scalars], *[in_vmem(array) for array in arrays])
 
 
 def chosen(slot, rows, cols, band_start, window):

time: 45 us -> 45.1 us (level)
  transfers between devices with their start and end apart: 13 -> 13, of which waited for: 6 -> 6; matrix products, arithmetic and copies ran while one was open for 0% -> 0% of each run, Pallas kernels for 19% -> 20%
where the time goes in v17:
time: 45.1 us; the launch traced here: 44.9 us
  waiting for transfers between devices  19.7 us (44%)
  starting transfers between devices  14.9 us (33%)
  Pallas kernels  10.3 us (23%)
    ppermute x8, waiting for transfers between devices, exchanged(): lax.ppermute(block, axis, [(i, i ^ flip) for i in range(lax.axis_size(axi...  15.7 us
    ppermute x8, starting transfers between devices, exchanged(): lax.ppermute(block, axis, [(i, i ^ flip) for i in range(lax.axis_size(axi...  11.1 us
    pallas_call x6, Pallas kernels, kernel_call(): pl.pallas_call(body, out_shape=[pltpu.VMEM(shape, F32) for shape in out_s...  7.55 us
    ppermute x5, waiting for transfers between devices, shifted(): lax.ppermute(block, axis, [((i - distance) % devices, i) for i in range(d...  3.91 us
    ppermute x5, starting transfers between devices, shifted(): lax.ppermute(block, axis, [((i - distance) % devices, i) for i in range(d...  3.72 us
    pallas_call x1, Pallas kernels, loaded(): pl.pallas_call(functools.partial(load_kernel, len(arrays)), out_shape=[pl...  1.96 us
  transfers between devices with their start and end apart: 13, of which 6 were waited for; matrix products, arithmetic and copies ran while one was open for 0% of the time, Pallas kernels for 20%

profile of v17, /device:TPU:0, one launch (start us, length us, event | category | flops | bytes accessed | tf_op | source)
XLA Modules:
  0.0 44.9 jit_solution(3565171575619107405)
XLA Ops:
  0.0 0.5 %collective-permute-start.3 = (s32[2]{0:T(128)}, s32[2]{0:T(128)S(1)}, u32[]{:S(2)}, u32[]{:S(2)}) collective-permute-start(s32[2]{0:T(128)} %rows.5), channel_id=1, source_target_pairs={{24,0},{0,8},{8,16},{16,24},{25,1},{1,9},{9,17},{17,25},{26,2},{2,... | collective-permute-start | bytes 32 | tf_op jit(solution)/shard_map/ppermute | solution.py:19
  0.5 2.6 %collective-permute-start.4 = (s32[2]{0:T(128)}, s32[2]{0:T(128)S(1)}, u32[]{:S(2)}, u32[]{:S(2)}) collective-permute-start(s32[2]{0:T(128)} %cols.5), channel_id=1, source_target_pairs={{24,0},{0,8},{8,16},{16,24},{25,1},{1,9},{9,17},{17,25},{26,2},{2,... | collective-permute-start | bytes 32 | tf_op jit(solution)/shard_map/ppermute | solution.py:19
  3.1 2.0 %load.1 = (f32[4096,128]{1,0:T(8,128)S(1)}, f32[1024,128]{1,0:T(8,128)S(1)}, bf16[2,256,256]{2,1,0:T(8,128)(2,1)S(1)}, bf16[768,384]{1,0:T(8,128)(2,1)S(1)}) custom-call(f32[4096,128]{1,0:T(8,128)} %bitcast.19, f32[1024,128]{1,0:T(8,128)} %bitcast.20, bf16[2,256,256]{2,1,0:T(8,128)(2,1)} %refs_2_.1, bf16[768,384]{1,0:T(8,128)(2,1)} %constant.8.clone.refs_3_), custom_call_target="tpu_custom_call" | custom-call | tf_op jit(solution)/shard_map/load/pallas_call | solution.py:99
  5.1 0.0 collective-permute-done.3
  5.1 0.0 collective-permute-done.4
  5.1 0.3 rim.1
  5.4 0.1 collective-permute-start.5
  5.4 2.9 %wave0.1 = (f32[136,256]{1,0:T(8,128)S(1)}, f32[136,256]{1,0:T(8,128)S(1)}, f32[136,256]{1,0:T(8,128)S(1)}, f32[136,256]{1,0:T(8,128)S(1)}) custom-call(s32[2]{0:T(128)} %rows.5, s32[2]{0:T(128)} %cols.5, f32[4096,128]{1,0:T(8,128)S(1)} %get-tuple-element.26.obj, f32[1024,128]{1,0:T(8,128)S(1)} %get-tuple-element.27.ill, ...), custom_call_target="tpu_custom_call" | custom-call | flops 805306368 | bytes 1114112 | tf_op jit(solution)/shard_map/wave0/pallas_call | solution.py:71
  8.3 1.7 %collective-permute-start = (f32[136,256]{1,0:T(8,128)S(1)}, f32[136,256]{1,0:T(8,128)S(1)}, u32[]{:S(2)}, u32[]{:S(2)}) collective-permute-start(f32[136,256]{1,0:T(8,128)S(1)} %get-tuple-element.31), channel_id=1, source_target_pairs={{0,1},{1,0},{2,3},{3,2},{4,5},{5,4},{6,7},{7,6},{8,9},{9,8},{10,11... | collective-permute-start | bytes 417800 | tf_op jit(solution)/shard_map/ppermute | solution.py:23
  10.0 1.6 %collective-permute-start.1 = (f32[136,256]{1,0:T(8,128)S(1)}, f32[136,256]{1,0:T(8,128)S(1)}, u32[]{:S(2)}, u32[]{:S(2)}) collective-permute-start(f32[136,256]{1,0:T(8,128)S(1)} %get-tuple-element.32), channel_id=1, source_target_pairs={{0,2},{1,3},{2,0},{3,1},{4,6},{5,7},{6,4},{7,5},{8,10},{9,11},{10,... | collective-permute-start | bytes 417800 | tf_op jit(solution)/shard_map/ppermute | solution.py:23
  11.6 0.3 collective-permute-start.2
  11.9 1.2 %start1.1 = (f32[2,256,256]{2,1,0:T(8,128)S(1)}, f32[256,256]{1,0:T(8,128)S(1)}, f32[2,256,256]{2,1,0:T(8,128)S(1)}) custom-call(s32[2]{0:T(128)} %rows.5, s32[2]{0:T(128)} %cols.5, f32[4096,128]{1,0:T(8,128)S(1)} %get-tuple-element.26.obj, f32[1024,128]{1,0:T(8,128)S(1)} %get-tuple-element.27.ill, bf16[2,256,256]{2,1,0:T(8,128)(2,1)S(1)} %get-tuple-element.28.amps), custom_call_target="tpu_custom_call" | custom-call | bytes 2621440 | tf_op jit(solution)/shard_map/start/start1/pallas_call | solution.py:71
  13.1 0.0 collective-permute-done.5.rim
  13.1 2.6 %wave1.1 = (f32[128,256]{1,0:T(8,128)S(1)}, f32[128,256]{1,0:T(8,128)S(1)}, f32[128,256]{1,0:T(8,128)S(1)}, f32[128,256]{1,0:T(8,128)S(1)}) custom-call(s32[2]{0:T(128)} %rows.5, s32[2]{0:T(128)} %cols.5, f32[2,256,256]{2,1,0:T(8,128)S(1)} %get-tuple-element.34.probe, f32[256,256]{1,0:T(8,128)S(1)} %get-tuple-element.35.ordered, ...), custom_call_target="tpu_custom_call" | custom-call | flops 805306368 | bytes 1048576 | tf_op jit(solution)/shard_map/wave1/pallas_call | solution.py:71
  15.7 1.7 %collective-permute-start.6 = (f32[128,256]{1,0:T(8,128)S(1)}, f32[128,256]{1,0:T(8,128)S(1)}, u32[]{:S(2)}, u32[]{:S(2)}) collective-permute-start(f32[128,256]{1,0:T(8,128)S(1)} %get-tuple-element.38), channel_id=1, source_target_pairs={{0,1},{1,0},{2,3},{3,2},{4,5},{5,4},{6,7},{7,6},{8,9},{9,8},{10,11... | collective-permute-start | bytes 393224 | tf_op jit(solution)/shard_map/ppermute | solution.py:23
  17.4 1.6 %collective-permute-start.7 = (f32[128,256]{1,0:T(8,128)S(1)}, f32[128,256]{1,0:T(8,128)S(1)}, u32[]{:S(2)}, u32[]{:S(2)}) collective-permute-start(f32[128,256]{1,0:T(8,128)S(1)} %get-tuple-element.39), channel_id=1, source_target_pairs={{0,2},{1,3},{2,0},{3,1},{4,6},{5,7},{6,4},{7,5},{8,10},{9,11},{10,... | collective-permute-start | bytes 393224 | tf_op jit(solution)/shard_map/ppermute | solution.py:23
  18.9 0.0 collective-permute-done.refs_1_
  19.0 0.3 collective-permute-start.8
  19.3 0.0 collective-permute-done.2.refs_3_
  19.3 0.2 sum0.1.acc
  19.5 2.4 %collective-permute-done.6.refs_5_ = f32[128,256]{1,0:T(8,128)S(1)} collective-permute-done((f32[128,256]{1,0:T(8,128)S(1)}, f32[128,256]{1,0:T(8,128)S(1)}, u32[]{:S(2)}, u32[]{:S(2)}) %collective-permute-start.6) | collective-permute-done | bytes 131104 | tf_op jit(solution)/shard_map/ppermute | solution.py:23
  21.9 1.8 %collective-permute-done.7.refs_6_ = f32[128,256]{1,0:T(8,128)S(1)} collective-permute-done((f32[128,256]{1,0:T(8,128)S(1)}, f32[128,256]{1,0:T(8,128)S(1)}, u32[]{:S(2)}, u32[]{:S(2)}) %collective-permute-start.7) | collective-permute-done | bytes 131104 | tf_op jit(solution)/shard_map/ppermute | solution.py:23
  23.7 2.6 %collective-permute-done.8.refs_7_ = f32[128,256]{1,0:T(8,128)S(1)} collective-permute-done((f32[128,256]{1,0:T(8,128)S(1)}, f32[128,256]{1,0:T(8,128)S(1)}, u32[]{:S(2)}, u32[]{:S(2)}) %collective-permute-start.8) | collective-permute-done | bytes 131104 | tf_op jit(solution)/shard_map/ppermute | solution.py:23
  26.4 0.4 sum1.1
  26.8 0.1 collective-permute-start.10
  26.9 0.4 collective-permute-start.9
  27.3 3.9 %collective-permute-done.10 = f32[256,128]{1,0:T(8,128)S(1)} collective-permute-done((f32[256,128]{1,0:T(8,128)S(1)}, f32[256,128]{1,0:T(8,128)S(1)}, u32[]{:S(2)}, u32[]{:S(2)}) %collective-permute-start.10) | collective-permute-done | bytes 131104 | tf_op jit(solution)/shard_map/spill_1/ppermute | solution.py:19
  31.2 2.7 %collective-permute-start.12 = (f32[256,128]{1,0:T(8,128)S(1)}, f32[256,128]{1,0:T(8,128)S(1)}, u32[]{:S(2)}, u32[]{:S(2)}) collective-permute-start(f32[256,128]{1,0:T(8,128)S(1)} %get-tuple-element.47), channel_id=1, source_target_pairs={{0,4},{1,5},{2,6},{3,7},{4,0},{5,1},{6,2},{7,3},{8,12},{9,13},{10,... | collective-permute-start | bytes 393224 | tf_op jit(solution)/shard_map/halves_1/ppermute | solution.py:23
  33.9 1.4 %collective-permute-start.11 = (f32[256,128]{1,0:T(8,128)S(1)}, f32[256,128]{1,0:T(8,128)S(1)}, u32[]{:S(2)}, u32[]{:S(2)}) collective-permute-start(f32[256,128]{1,0:T(8,128)S(1)} %get-tuple-element.49), channel_id=1, source_target_pairs={{0,4},{1,5},{2,6},{3,7},{4,0},{5,1},{6,2},{7,3},{8,12},{9,13},{10,... | collective-permute-start | bytes 393224 | tf_op jit(solution)/shard_map/halves_0/ppermute | solution.py:23
  35.3 7.5 %collective-permute-done.12.refs_3_ = f32[256,128]{1,0:T(8,128)S(1)} collective-permute-done((f32[256,128]{1,0:T(8,128)S(1)}, f32[256,128]{1,0:T(8,128)S(1)}, u32[]{:S(2)}, u32[]{:S(2)}) %collective-permute-start.12) | collective-permute-done | bytes 131104 | tf_op jit(solution)/shard_map/halves_1/ppermute | solution.py:23
  42.8 1.4 %collective-permute-done.11.refs_2_ = f32[256,128]{1,0:T(8,128)S(1)} collective-permute-done((f32[256,128]{1,0:T(8,128)S(1)}, f32[256,128]{1,0:T(8,128)S(1)}, u32[]{:S(2)}, u32[]{:S(2)}) %collective-permute-start.11) | collective-permute-done | bytes 131104 | tf_op jit(solution)/shard_map/halves_0/ppermute | solution.py:23
  44.2 0.8 %final.1 = f32[512,128]{1,0:T(8,128)} custom-call(f32[256,128]{1,0:T(8,128)S(1)} %get-tuple-element.50.refs_0_, f32[256,128]{1,0:T(8,128)S(1)} %get-tuple-element.48.refs_1_, f32[256,128]{1,0:T(8,128)S(1)} %collective-permute-done.11.refs_2_, f32[256,128]{1,0:T(8,128)S(1)} %collective-permute-done.12.refs_3_), custom_call_target="tpu_custom_call" | custom-call | tf_op jit(solution)/shard_map/final/pallas_call | solution.py:455
  (4 shorter events, 0.1 us)
Async XLA Ops:
  0.0 5.1 %collective-permute-start.3 = (s32[2]{0:T(128)}, s32[2]{0:T(128)S(1)}, u32[]{:S(2)}, u32[]{:S(2)}) collective-permute-start(s32[2]{0:T(128)} %rows.5), channel_id=1, source_target_pairs={{24,0},{0,8},{8,16},{16,24},{25,1},{1,9},{9,17},{17,25},{26,2},{2,... | collective-permute-start | bytes 32 | tf_op jit(solution)/shard_map/ppermute | solution.py:19
  0.5 4.6 %collective-permute-start.4 = (s32[2]{0:T(128)}, s32[2]{0:T(128)S(1)}, u32[]{:S(2)}, u32[]{:S(2)}) collective-permute-start(s32[2]{0:T(128)} %cols.5), channel_id=1, source_target_pairs={{24,0},{0,8},{8,16},{16,24},{25,1},{1,9},{9,17},{17,25},{26,2},{2,... | collective-permute-start | bytes 32 | tf_op jit(solution)/shard_map/ppermute | solution.py:19
  5.4 7.7 %collective-permute-start.5 = (f32[2,256,256]{2,1,0:T(8,128)S(1)}, f32[2,256,256]{2,1,0:T(8,128)S(1)}, u32[]{:S(2)}, u32[]{:S(2)}) collective-permute-start(f32[2,256,256]{2,1,0:T(8,128)S(1)} %rim.1), channel_id=1, source_target_pairs={{8,0},{16,8},{24,16},{0,24},{9,1},{17,9},{25,17},{1,25},{10,2},{18... | collective-permute-start | bytes 1572872 | tf_op jit(solution)/shard_map/ppermute | solution.py:19
  8.3 10.6 %collective-permute-start = (f32[136,256]{1,0:T(8,128)S(1)}, f32[136,256]{1,0:T(8,128)S(1)}, u32[]{:S(2)}, u32[]{:S(2)}) collective-permute-start(f32[136,256]{1,0:T(8,128)S(1)} %get-tuple-element.31), channel_id=1, source_target_pairs={{0,1},{1,0},{2,3},{3,2},{4,5},{5,4},{6,7},{7,6},{8,9},{9,8},{10,11... | collective-permute-start | bytes 417800 | tf_op jit(solution)/shard_map/ppermute | solution.py:23
  10.0 9.3 %collective-permute-start.1 = (f32[136,256]{1,0:T(8,128)S(1)}, f32[136,256]{1,0:T(8,128)S(1)}, u32[]{:S(2)}, u32[]{:S(2)}) collective-permute-start(f32[136,256]{1,0:T(8,128)S(1)} %get-tuple-element.32), channel_id=1, source_target_pairs={{0,2},{1,3},{2,0},{3,1},{4,6},{5,7},{6,4},{7,5},{8,10},{9,11},{10,... | collective-permute-start | bytes 417800 | tf_op jit(solution)/shard_map/ppermute | solution.py:23
  11.6 7.7 %collective-permute-start.2 = (f32[136,256]{1,0:T(8,128)S(1)}, f32[136,256]{1,0:T(8,128)S(1)}, u32[]{:S(2)}, u32[]{:S(2)}) collective-permute-start(f32[136,256]{1,0:T(8,128)S(1)} %get-tuple-element.33), channel_id=1, source_target_pairs={{0,3},{1,2},{2,1},{3,0},{4,7},{5,6},{6,5},{7,4},{8,11},{9,10},{10,... | collective-permute-start | bytes 417800 | tf_op jit(solution)/shard_map/ppermute | solution.py:23
  15.7 6.2 %collective-permute-start.6 = (f32[128,256]{1,0:T(8,128)S(1)}, f32[128,256]{1,0:T(8,128)S(1)}, u32[]{:S(2)}, u32[]{:S(2)}) collective-permute-start(f32[128,256]{1,0:T(8,128)S(1)} %get-tuple-element.38), channel_id=1, source_target_pairs={{0,1},{1,0},{2,3},{3,2},{4,5},{5,4},{6,7},{7,6},{8,9},{9,8},{10,11... | collective-permute-start | bytes 393224 | tf_op jit(solution)/shard_map/ppermute | solution.py:23
  17.4 6.4 %collective-permute-start.7 = (f32[128,256]{1,0:T(8,128)S(1)}, f32[128,256]{1,0:T(8,128)S(1)}, u32[]{:S(2)}, u32[]{:S(2)}) collective-permute-start(f32[128,256]{1,0:T(8,128)S(1)} %get-tuple-element.39), channel_id=1, source_target_pairs={{0,2},{1,3},{2,0},{3,1},{4,6},{5,7},{6,4},{7,5},{8,10},{9,11},{10,... | collective-permute-start | bytes 393224 | tf_op jit(solution)/shard_map/ppermute | solution.py:23
  19.0 7.4 %collective-permute-start.8 = (f32[128,256]{1,0:T(8,128)S(1)}, f32[128,256]{1,0:T(8,128)S(1)}, u32[]{:S(2)}, u32[]{:S(2)}) collective-permute-start(f32[128,256]{1,0:T(8,128)S(1)} %get-tuple-element.40), channel_id=1, source_target_pairs={{0,3},{1,2},{2,1},{3,0},{4,7},{5,6},{6,5},{7,4},{8,11},{9,10},{10,... | collective-permute-start | bytes 393224 | tf_op jit(solution)/shard_map/ppermute | solution.py:23
  26.8 4.4 %collective-permute-start.10 = (f32[256,128]{1,0:T(8,128)S(1)}, f32[256,128]{1,0:T(8,128)S(1)}, u32[]{:S(2)}, u32[]{:S(2)}) collective-permute-start(f32[256,128]{1,0:T(8,128)S(1)} %get-tuple-element.46), channel_id=1, source_target_pairs={{24,0},{0,8},{8,16},{16,24},{25,1},{1,9},{9,17},{17,25},{26,2},{2,... | collective-permute-start | bytes 393224 | tf_op jit(solution)/shard_map/spill_1/ppermute | solution.py:19
  26.9 7.0 %collective-permute-start.9 = (f32[256,128]{1,0:T(8,128)S(1)}, f32[256,128]{1,0:T(8,128)S(1)}, u32[]{:S(2)}, u32[]{:S(2)}) collective-permute-start(f32[256,128]{1,0:T(8,128)S(1)} %get-tuple-element.43), channel_id=1, source_target_pairs={{24,0},{0,8},{8,16},{16,24},{25,1},{1,9},{9,17},{17,25},{26,2},{2,... | collective-permute-start | bytes 393224 | tf_op jit(solution)/shard_map/spill_0/ppermute | solution.py:19
  31.2 11.5 %collective-permute-start.12 = (f32[256,128]{1,0:T(8,128)S(1)}, f32[256,128]{1,0:T(8,128)S(1)}, u32[]{:S(2)}, u32[]{:S(2)}) collective-permute-start(f32[256,128]{1,0:T(8,128)S(1)} %get-tuple-element.47), channel_id=1, source_target_pairs={{0,4},{1,5},{2,6},{3,7},{4,0},{5,1},{6,2},{7,3},{8,12},{9,13},{10,... | collective-permute-start | bytes 393224 | tf_op jit(solution)/shard_map/halves_1/ppermute | solution.py:23
  33.9 10.2 %collective-permute-start.11 = (f32[256,128]{1,0:T(8,128)S(1)}, f32[256,128]{1,0:T(8,128)S(1)}, u32[]{:S(2)}, u32[]{:S(2)}) collective-permute-start(f32[256,128]{1,0:T(8,128)S(1)} %get-tuple-element.49), channel_id=1, source_target_pairs={{0,4},{1,5},{2,6},{3,7},{4,0},{5,1},{6,2},{7,3},{8,12},{9,13},{10,... | collective-permute-start | bytes 393224 | tf_op jit(solution)/shard_map/halves_0/ppermute | solution.py:23

commit v18 on v16

--- a/solution.py
+++ b/solution.py
@@ -397,7 +397,7 @@
     rim = shifted(rim, "tile", -1)
 
     def spread(pieces):
-        moved = {d: exchanged(pieces[d], "pos", d) for d in range(1, classes)}
+        moved = {d: exchanged(pieces[d], "pos", d) for d in (*range(1, classes, 2), *range(2, classes, 2))}
         return [pieces[0]] + [moved[d] for d in range(1, classes)]
 
     roll, state, work = scratch_of(window)

time: 45 us -> 45 us (level)
  no operation moved by 1% of the time
where the time goes in v18:
time: 45 us; the launch traced here: 44.9 us
  waiting for transfers between devices  19.6 us (44%)
  starting transfers between devices  14.8 us (33%)
  Pallas kernels  9.94 us (22%)
    ppermute x8, waiting for transfers between devices, exchanged(): lax.ppermute(block, axis, [(i, i ^ flip) for i in range(lax.axis_size(axi...  15.7 us
    ppermute x8, starting transfers between devices, exchanged(): lax.ppermute(block, axis, [(i, i ^ flip) for i in range(lax.axis_size(axi...  11.1 us
    pallas_call x6, Pallas kernels, kernel_call(): pl.pallas_call(body, out_shape=[pltpu.VMEM(shape, F32) for shape in out_s...  7.21 us
    ppermute x5, waiting for transfers between devices, shifted(): lax.ppermute(block, axis, [((i - distance) % devices, i) for i in range(d...  3.91 us
    ppermute x5, starting transfers between devices, shifted(): lax.ppermute(block, axis, [((i - distance) % devices, i) for i in range(d...  3.72 us
    pallas_call x1, Pallas kernels, loaded(): pl.pallas_call(functools.partial(load_kernel, len(arrays)), out_shape=[pl...  1.96 us
  transfers between devices with their start and end apart: 13, of which 6 were waited for; matrix products, arithmetic and copies ran while one was open for 0% of the time, Pallas kernels for 19%

profile of v18, /device:TPU:0, one launch (start us, length us, event | category | flops | bytes accessed | tf_op | source)
XLA Modules:
  0.0 44.9 jit_solution(12334554584513527501)
XLA Ops:
  0.0 0.5 %collective-permute-start.3 = (s32[2]{0:T(128)}, s32[2]{0:T(128)S(1)}, u32[]{:S(2)}, u32[]{:S(2)}) collective-permute-start(s32[2]{0:T(128)} %rows.5), channel_id=1, source_target_pairs={{24,0},{0,8},{8,16},{16,24},{25,1},{1,9},{9,17},{17,25},{26,2},{2,... | collective-permute-start | bytes 32 | tf_op jit(solution)/shard_map/ppermute | solution.py:19
  0.5 2.6 %collective-permute-start.4 = (s32[2]{0:T(128)}, s32[2]{0:T(128)S(1)}, u32[]{:S(2)}, u32[]{:S(2)}) collective-permute-start(s32[2]{0:T(128)} %cols.5), channel_id=1, source_target_pairs={{24,0},{0,8},{8,16},{16,24},{25,1},{1,9},{9,17},{17,25},{26,2},{2,... | collective-permute-start | bytes 32 | tf_op jit(solution)/shard_map/ppermute | solution.py:19
  3.1 2.0 %load.1 = (f32[4096,128]{1,0:T(8,128)S(1)}, f32[1024,128]{1,0:T(8,128)S(1)}, bf16[2,256,256]{2,1,0:T(8,128)(2,1)S(1)}, bf16[768,384]{1,0:T(8,128)(2,1)S(1)}) custom-call(f32[4096,128]{1,0:T(8,128)} %bitcast.19, f32[1024,128]{1,0:T(8,128)} %bitcast.20, bf16[2,256,256]{2,1,0:T(8,128)(2,1)} %refs_2_.1, bf16[768,384]{1,0:T(8,128)(2,1)} %constant.8.clone.refs_3_), custom_call_target="tpu_custom_call" | custom-call | tf_op jit(solution)/shard_map/load/pallas_call | solution.py:99
  5.1 0.0 copy-start
  5.1 0.0 copy-start.1
  5.1 0.0 collective-permute-done.4
  5.1 0.3 rim.1
  5.4 0.1 collective-permute-start.5
  5.5 0.3 copy-done
  5.7 0.0 copy-done.1
  5.8 2.8 %wave0.1 = (f32[136,256]{1,0:T(8,128)S(1)}, f32[136,256]{1,0:T(8,128)S(1)}, f32[136,256]{1,0:T(8,128)S(1)}, f32[136,256]{1,0:T(8,128)S(1)}) custom-call(s32[2]{0:T(128)S(1)} %copy-done, s32[2]{0:T(128)S(1)} %copy-done.1, f32[4096,128]{1,0:T(8,128)S(1)} %get-tuple-element.26.obj, f32[1024,128]{1,0:T(8,128)S(1)} %get-tuple-element.27.ill, ...), custom_call_target="tpu_custom_call" | custom-call | flops 805306368 | bytes 1114112 | tf_op jit(solution)/shard_map/wave0/pallas_call | solution.py:71
  8.5 1.6 %collective-permute-start = (f32[136,256]{1,0:T(8,128)S(1)}, f32[136,256]{1,0:T(8,128)S(1)}, u32[]{:S(2)}, u32[]{:S(2)}) collective-permute-start(f32[136,256]{1,0:T(8,128)S(1)} %get-tuple-element.31), channel_id=1, source_target_pairs={{0,1},{1,0},{2,3},{3,2},{4,5},{5,4},{6,7},{7,6},{8,9},{9,8},{10,11... | collective-permute-start | bytes 417800 | tf_op jit(solution)/shard_map/ppermute | solution.py:23
  10.1 1.6 %collective-permute-start.1 = (f32[136,256]{1,0:T(8,128)S(1)}, f32[136,256]{1,0:T(8,128)S(1)}, u32[]{:S(2)}, u32[]{:S(2)}) collective-permute-start(f32[136,256]{1,0:T(8,128)S(1)} %get-tuple-element.32), channel_id=1, source_target_pairs={{0,2},{1,3},{2,0},{3,1},{4,6},{5,7},{6,4},{7,5},{8,10},{9,11},{10,... | collective-permute-start | bytes 417800 | tf_op jit(solution)/shard_map/ppermute | solution.py:23
  11.7 0.4 collective-permute-start.2
  12.1 1.1 %start1.1 = (f32[2,256,256]{2,1,0:T(8,128)S(1)}, f32[256,256]{1,0:T(8,128)S(1)}, f32[2,256,256]{2,1,0:T(8,128)S(1)}) custom-call(s32[2]{0:T(128)S(1)} %copy-done, s32[2]{0:T(128)S(1)} %copy-done.1, f32[4096,128]{1,0:T(8,128)S(1)} %get-tuple-element.26.obj, f32[1024,128]{1,0:T(8,128)S(1)} %get-tuple-element.27.ill, ...), custom_call_target="tpu_custom_call" | custom-call | bytes 2621440 | tf_op jit(solution)/shard_map/start/start1/pallas_call | solution.py:71
  13.2 2.5 %wave1.1 = (f32[128,256]{1,0:T(8,128)S(1)}, f32[128,256]{1,0:T(8,128)S(1)}, f32[128,256]{1,0:T(8,128)S(1)}, f32[128,256]{1,0:T(8,128)S(1)}) custom-call(s32[2]{0:T(128)S(1)} %copy-done, s32[2]{0:T(128)S(1)} %copy-done.1, f32[2,256,256]{2,1,0:T(8,128)S(1)} %get-tuple-element.34.probe, f32[256,256]{1,0:T(8,128)S(1)} %get-tuple-element.35.ordered, ...), custom_call_target="tpu_custom_call" | custom-call | flops 805306368 | bytes 1048576 | tf_op jit(solution)/shard_map/wave1/pallas_call | solution.py:71
  15.7 1.6 %collective-permute-start.6 = (f32[128,256]{1,0:T(8,128)S(1)}, f32[128,256]{1,0:T(8,128)S(1)}, u32[]{:S(2)}, u32[]{:S(2)}) collective-permute-start(f32[128,256]{1,0:T(8,128)S(1)} %get-tuple-element.38), channel_id=1, source_target_pairs={{0,1},{1,0},{2,3},{3,2},{4,5},{5,4},{6,7},{7,6},{8,9},{9,8},{10,11... | collective-permute-start | bytes 393224 | tf_op jit(solution)/shard_map/ppermute | solution.py:23
  17.2 1.6 %collective-permute-start.7 = (f32[128,256]{1,0:T(8,128)S(1)}, f32[128,256]{1,0:T(8,128)S(1)}, u32[]{:S(2)}, u32[]{:S(2)}) collective-permute-start(f32[128,256]{1,0:T(8,128)S(1)} %get-tuple-element.39), channel_id=1, source_target_pairs={{0,2},{1,3},{2,0},{3,1},{4,6},{5,7},{6,4},{7,5},{8,10},{9,11},{10,... | collective-permute-start | bytes 393224 | tf_op jit(solution)/shard_map/ppermute | solution.py:23
  18.8 0.4 collective-permute-start.8
  19.2 0.2 sum0.1.acc
  19.5 2.5 %collective-permute-done.6.refs_5_ = f32[128,256]{1,0:T(8,128)S(1)} collective-permute-done((f32[128,256]{1,0:T(8,128)S(1)}, f32[128,256]{1,0:T(8,128)S(1)}, u32[]{:S(2)}, u32[]{:S(2)}) %collective-permute-start.6) | collective-permute-done | bytes 131104 | tf_op jit(solution)/shard_map/ppermute | solution.py:23
  21.9 1.7 %collective-permute-done.7.refs_6_ = f32[128,256]{1,0:T(8,128)S(1)} collective-permute-done((f32[128,256]{1,0:T(8,128)S(1)}, f32[128,256]{1,0:T(8,128)S(1)}, u32[]{:S(2)}, u32[]{:S(2)}) %collective-permute-start.7) | collective-permute-done | bytes 131104 | tf_op jit(solution)/shard_map/ppermute | solution.py:23
  23.6 2.7 %collective-permute-done.8.refs_7_ = f32[128,256]{1,0:T(8,128)S(1)} collective-permute-done((f32[128,256]{1,0:T(8,128)S(1)}, f32[128,256]{1,0:T(8,128)S(1)}, u32[]{:S(2)}, u32[]{:S(2)}) %collective-permute-start.8) | collective-permute-done | bytes 131104 | tf_op jit(solution)/shard_map/ppermute | solution.py:23
  26.3 0.4 sum1.1
  26.7 0.1 collective-permute-start.10
  26.8 0.5 %collective-permute-start.9 = (f32[256,128]{1,0:T(8,128)S(1)}, f32[256,128]{1,0:T(8,128)S(1)}, u32[]{:S(2)}, u32[]{:S(2)}) collective-permute-start(f32[256,128]{1,0:T(8,128)S(1)} %get-tuple-element.43), channel_id=1, source_target_pairs={{24,0},{0,8},{8,16},{16,24},{25,1},{1,9},{9,17},{17,25},{26,2},{2,... | collective-permute-start | bytes 393224 | tf_op jit(solution)/shard_map/spill_0/ppermute | solution.py:19
  27.3 3.9 %collective-permute-done.10 = f32[256,128]{1,0:T(8,128)S(1)} collective-permute-done((f32[256,128]{1,0:T(8,128)S(1)}, f32[256,128]{1,0:T(8,128)S(1)}, u32[]{:S(2)}, u32[]{:S(2)}) %collective-permute-start.10) | collective-permute-done | bytes 131104 | tf_op jit(solution)/shard_map/spill_1/ppermute | solution.py:19
  31.2 2.7 %collective-permute-start.12 = (f32[256,128]{1,0:T(8,128)S(1)}, f32[256,128]{1,0:T(8,128)S(1)}, u32[]{:S(2)}, u32[]{:S(2)}) collective-permute-start(f32[256,128]{1,0:T(8,128)S(1)} %get-tuple-element.47), channel_id=1, source_target_pairs={{0,4},{1,5},{2,6},{3,7},{4,0},{5,1},{6,2},{7,3},{8,12},{9,13},{10,... | collective-permute-start | bytes 393224 | tf_op jit(solution)/shard_map/halves_1/ppermute | solution.py:23
  33.9 1.4 %collective-permute-start.11 = (f32[256,128]{1,0:T(8,128)S(1)}, f32[256,128]{1,0:T(8,128)S(1)}, u32[]{:S(2)}, u32[]{:S(2)}) collective-permute-start(f32[256,128]{1,0:T(8,128)S(1)} %get-tuple-element.49), channel_id=1, source_target_pairs={{0,4},{1,5},{2,6},{3,7},{4,0},{5,1},{6,2},{7,3},{8,12},{9,13},{10,... | collective-permute-start | bytes 393224 | tf_op jit(solution)/shard_map/halves_0/ppermute | solution.py:23
  35.2 7.5 %collective-permute-done.12.refs_3_ = f32[256,128]{1,0:T(8,128)S(1)} collective-permute-done((f32[256,128]{1,0:T(8,128)S(1)}, f32[256,128]{1,0:T(8,128)S(1)}, u32[]{:S(2)}, u32[]{:S(2)}) %collective-permute-start.12) | collective-permute-done | bytes 131104 | tf_op jit(solution)/shard_map/halves_1/ppermute | solution.py:23
  42.7 1.4 %collective-permute-done.11.refs_2_ = f32[256,128]{1,0:T(8,128)S(1)} collective-permute-done((f32[256,128]{1,0:T(8,128)S(1)}, f32[256,128]{1,0:T(8,128)S(1)}, u32[]{:S(2)}, u32[]{:S(2)}) %collective-permute-start.11) | collective-permute-done | bytes 131104 | tf_op jit(solution)/shard_map/halves_0/ppermute | solution.py:23
  44.1 0.8 %final.1 = f32[512,128]{1,0:T(8,128)} custom-call(f32[256,128]{1,0:T(8,128)S(1)} %get-tuple-element.50.refs_0_, f32[256,128]{1,0:T(8,128)S(1)} %get-tuple-element.48.refs_1_, f32[256,128]{1,0:T(8,128)S(1)} %collective-permute-done.11.refs_2_, f32[256,128]{1,0:T(8,128)S(1)} %collective-permute-done.12.refs_3_), custom_call_target="tpu_custom_call" | custom-call | tf_op jit(solution)/shard_map/final/pallas_call | solution.py:455
  (8 shorter events, 0.1 us)
Async XLA Ops:
  0.0 5.1 %collective-permute-start.3 = (s32[2]{0:T(128)}, s32[2]{0:T(128)S(1)}, u32[]{:S(2)}, u32[]{:S(2)}) collective-permute-start(s32[2]{0:T(128)} %rows.5), channel_id=1, source_target_pairs={{24,0},{0,8},{8,16},{16,24},{25,1},{1,9},{9,17},{17,25},{26,2},{2,... | collective-permute-start | bytes 32 | tf_op jit(solution)/shard_map/ppermute | solution.py:19
  0.5 4.6 %collective-permute-start.4 = (s32[2]{0:T(128)}, s32[2]{0:T(128)S(1)}, u32[]{:S(2)}, u32[]{:S(2)}) collective-permute-start(s32[2]{0:T(128)} %cols.5), channel_id=1, source_target_pairs={{24,0},{0,8},{8,16},{16,24},{25,1},{1,9},{9,17},{17,25},{26,2},{2,... | collective-permute-start | bytes 32 | tf_op jit(solution)/shard_map/ppermute | solution.py:19
  5.1 0.7 %copy-start = (s32[2]{0:T(128)S(1)}, s32[2]{0:T(128)}, u32[]{:S(2)}) copy-start(s32[2]{0:T(128)} %rows.5) | copy-start | bytes 28
  5.1 0.7 %copy-start.1 = (s32[2]{0:T(128)S(1)}, s32[2]{0:T(128)}, u32[]{:S(2)}) copy-start(s32[2]{0:T(128)} %cols.5) | copy-start | bytes 28
  5.4 7.8 %collective-permute-start.5 = (f32[2,256,256]{2,1,0:T(8,128)S(1)}, f32[2,256,256]{2,1,0:T(8,128)S(1)}, u32[]{:S(2)}, u32[]{:S(2)}) collective-permute-start(f32[2,256,256]{2,1,0:T(8,128)S(1)} %rim.1), channel_id=1, source_target_pairs={{8,0},{16,8},{24,16},{0,24},{9,1},{17,9},{25,17},{1,25},{10,2},{18... | collective-permute-start | bytes 1572872 | tf_op jit(solution)/shard_map/ppermute | solution.py:19
  8.5 10.3 %collective-permute-start = (f32[136,256]{1,0:T(8,128)S(1)}, f32[136,256]{1,0:T(8,128)S(1)}, u32[]{:S(2)}, u32[]{:S(2)}) collective-permute-start(f32[136,256]{1,0:T(8,128)S(1)} %get-tuple-element.31), channel_id=1, source_target_pairs={{0,1},{1,0},{2,3},{3,2},{4,5},{5,4},{6,7},{7,6},{8,9},{9,8},{10,11... | collective-permute-start | bytes 417800 | tf_op jit(solution)/shard_map/ppermute | solution.py:23
  10.1 9.1 %collective-permute-start.1 = (f32[136,256]{1,0:T(8,128)S(1)}, f32[136,256]{1,0:T(8,128)S(1)}, u32[]{:S(2)}, u32[]{:S(2)}) collective-permute-start(f32[136,256]{1,0:T(8,128)S(1)} %get-tuple-element.32), channel_id=1, source_target_pairs={{0,2},{1,3},{2,0},{3,1},{4,6},{5,7},{6,4},{7,5},{8,10},{9,11},{10,... | collective-permute-start | bytes 417800 | tf_op jit(solution)/shard_map/ppermute | solution.py:23
  11.7 7.6 %collective-permute-start.2 = (f32[136,256]{1,0:T(8,128)S(1)}, f32[136,256]{1,0:T(8,128)S(1)}, u32[]{:S(2)}, u32[]{:S(2)}) collective-permute-start(f32[136,256]{1,0:T(8,128)S(1)} %get-tuple-element.33), channel_id=1, source_target_pairs={{0,3},{1,2},{2,1},{3,0},{4,7},{5,6},{6,5},{7,4},{8,11},{9,10},{10,... | collective-permute-start | bytes 417800 | tf_op jit(solution)/shard_map/ppermute | solution.py:23
  15.7 6.2 %collective-permute-start.6 = (f32[128,256]{1,0:T(8,128)S(1)}, f32[128,256]{1,0:T(8,128)S(1)}, u32[]{:S(2)}, u32[]{:S(2)}) collective-permute-start(f32[128,256]{1,0:T(8,128)S(1)} %get-tuple-element.38), channel_id=1, source_target_pairs={{0,1},{1,0},{2,3},{3,2},{4,5},{5,4},{6,7},{7,6},{8,9},{9,8},{10,11... | collective-permute-start | bytes 393224 | tf_op jit(solution)/shard_map/ppermute | solution.py:23
  17.2 6.4 %collective-permute-start.7 = (f32[128,256]{1,0:T(8,128)S(1)}, f32[128,256]{1,0:T(8,128)S(1)}, u32[]{:S(2)}, u32[]{:S(2)}) collective-permute-start(f32[128,256]{1,0:T(8,128)S(1)} %get-tuple-element.39), channel_id=1, source_target_pairs={{0,2},{1,3},{2,0},{3,1},{4,6},{5,7},{6,4},{7,5},{8,10},{9,11},{10,... | collective-permute-start | bytes 393224 | tf_op jit(solution)/shard_map/ppermute | solution.py:23
  18.8 7.5 %collective-permute-start.8 = (f32[128,256]{1,0:T(8,128)S(1)}, f32[128,256]{1,0:T(8,128)S(1)}, u32[]{:S(2)}, u32[]{:S(2)}) collective-permute-start(f32[128,256]{1,0:T(8,128)S(1)} %get-tuple-element.40), channel_id=1, source_target_pairs={{0,3},{1,2},{2,1},{3,0},{4,7},{5,6},{6,5},{7,4},{8,11},{9,10},{10,... | collective-permute-start | bytes 393224 | tf_op jit(solution)/shard_map/ppermute | solution.py:23
  26.7 4.4 %collective-permute-start.10 = (f32[256,128]{1,0:T(8,128)S(1)}, f32[256,128]{1,0:T(8,128)S(1)}, u32[]{:S(2)}, u32[]{:S(2)}) collective-permute-start(f32[256,128]{1,0:T(8,128)S(1)} %get-tuple-element.46), channel_id=1, source_target_pairs={{24,0},{0,8},{8,16},{16,24},{25,1},{1,9},{9,17},{17,25},{26,2},{2,... | collective-permute-start | bytes 393224 | tf_op jit(solution)/shard_map/spill_1/ppermute | solution.py:19
  26.8 7.1 %collective-permute-start.9 = (f32[256,128]{1,0:T(8,128)S(1)}, f32[256,128]{1,0:T(8,128)S(1)}, u32[]{:S(2)}, u32[]{:S(2)}) collective-permute-start(f32[256,128]{1,0:T(8,128)S(1)} %get-tuple-element.43), channel_id=1, source_target_pairs={{24,0},{0,8},{8,16},{16,24},{25,1},{1,9},{9,17},{17,25},{26,2},{2,... | collective-permute-start | bytes 393224 | tf_op jit(solution)/shard_map/spill_0/ppermute | solution.py:19
  31.2 11.5 %collective-permute-start.12 = (f32[256,128]{1,0:T(8,128)S(1)}, f32[256,128]{1,0:T(8,128)S(1)}, u32[]{:S(2)}, u32[]{:S(2)}) collective-permute-start(f32[256,128]{1,0:T(8,128)S(1)} %get-tuple-element.47), channel_id=1, source_target_pairs={{0,4},{1,5},{2,6},{3,7},{4,0},{5,1},{6,2},{7,3},{8,12},{9,13},{10,... | collective-permute-start | bytes 393224 | tf_op jit(solution)/shard_map/halves_1/ppermute | solution.py:23
  33.9 10.2 %collective-permute-start.11 = (f32[256,128]{1,0:T(8,128)S(1)}, f32[256,128]{1,0:T(8,128)S(1)}, u32[]{:S(2)}, u32[]{:S(2)}) collective-permute-start(f32[256,128]{1,0:T(8,128)S(1)} %get-tuple-element.49), channel_id=1, source_target_pairs={{0,4},{1,5},{2,6},{3,7},{4,0},{5,1},{6,2},{7,3},{8,12},{9,13},{10,... | collective-permute-start | bytes 393224 | tf_op jit(solution)/shard_map/halves_0/ppermute | solution.py:23
